TPU v7x, 128 devices: a whole 4x4x4 slice. The times are simulated.
128 devices in a mesh: ray: 8 (over z, core), cell: 16 (over x, y).
Axes of the slice: x: 4, y: 4, z: 4, core: 2. Of those that a mesh axis runs over, the one named last changes fastest.
Arguments:
- right_side: float32 [8, 16384], P(None, 'ray'), may hold values from -6 to 6
- tiles: bfloat16 [64, 64, 256, 256], P('ray', 'cell'), may hold values from -0.375 to 0.375
- pattern: int32 [64, 64], P('ray', 'cell'), may hold values from 0 to 31, as said below
- counts: int32 [64, 16], P('ray', 'cell'), may hold values from 1 to 4, as said below
Outputs:
- solution: float32 [8, 131072], P(None, 'cell')
- misfit: float32 [8], replicated
Inputs may be any that keep to these rules, and one draw needn't show every extreme that they name: `pattern`: each entry indexes a block within the slot's group of 32 cell blocks; a bundle may name a block more than once. Ragged counts; some bundle has all 4 slots live in some group, and some has one.
All inputs are finite; a program needn't handle non-finite values.
Results may differ from a plain program's by a relative error of at most 0.0014.
Values may be sent and summed in bfloat16 or wider, within the bound.
No kernel may reach another device: no remote copies, remote signals or barrier semaphores. Data moves between devices by JAX's collectives and lax.ppermute only.
A program may use at most 64 MiB of HBM per device.

v0:
```python
import jax
import jax.numpy as jnp
from jax import lax
from jax.sharding import PartitionSpec as P

BLK_DEV = 32
ITERS = 4


def norm_rows(local_sq):
    total = lax.psum(local_sq, "ray")
    return jnp.sqrt(total + 1e-06)


def norm_cols(local_sq):
    total = lax.psum(local_sq, "cell")
    return jnp.sqrt(total + 1e-06)


def local(right_side, tiles, pattern, counts):
    nrhs = right_side.shape[0]
    bundles = tiles.shape[0]
    slots = tiles.shape[1]
    ray_rows = tiles.shape[2]
    block_cells = tiles.shape[3]
    blocks = BLK_DEV
    live = lax.broadcasted_iota(jnp.int32, pattern.shape, 1) < counts
    live_bf = live.astype(jnp.bfloat16)
    selector = (
        (pattern[:, :, None] == lax.broadcasted_iota(jnp.int32, (bundles, slots, blocks), 2))
        & live[:, :, None]
    ).astype(jnp.float32)

    def adjoint(vector_bf):
        rows = vector_bf.reshape(nrhs, bundles, ray_rows)
        per = jnp.einsum("bsrc,nbr->bsnc", tiles, rows, preferred_element_type=jnp.float32)
        total = jnp.einsum("bsk,bsnc->nkc", selector, per, precision=lax.Precision.HIGHEST)
        return total.reshape(nrhs, blocks * block_cells)

    u_state = right_side
    beta = norm_rows(jnp.sum(u_state * u_state, axis=1))
    u_state = u_state / beta[:, None]

    def rows_bf(state):
        return state.astype(jnp.bfloat16)

    def cols_reduce(adj_terms):
        return lax.psum(adj_terms, "ray")

    v_state = cols_reduce(adjoint(rows_bf(u_state)))
    alpha = norm_cols(jnp.sum(v_state * v_state, axis=1))
    v_state = v_state / alpha[:, None]
    w_state = v_state
    x_state = jnp.zeros_like(v_state)
    phibar = beta
    rhobar = alpha
    for step in range(ITERS):
        vblocks = v_state.astype(jnp.bfloat16).reshape(nrhs, blocks, block_cells)
        picked = vblocks[:, pattern] * live_bf[None, :, :, None]
        partial_value = jnp.einsum(
            "bsrc,nbsc->nbr", tiles, picked, preferred_element_type=jnp.float32
        )
        partial_value = partial_value.reshape(nrhs, bundles * ray_rows)
        summed = lax.psum(partial_value, "cell")
        u_state = summed - alpha[:, None] * u_state
        beta = norm_rows(jnp.sum(u_state * u_state, axis=1))
        u_state = u_state / beta[:, None]
        v_state = cols_reduce(adjoint(rows_bf(u_state))) - beta[:, None] * v_state
        alpha = norm_cols(jnp.sum(v_state * v_state, axis=1))
        v_state = v_state / alpha[:, None]
        rho = jnp.sqrt(rhobar * rhobar + beta * beta)
        cosine = rhobar / rho
        sine = beta / rho
        theta = sine * alpha
        rhobar = -cosine * alpha
        phi = cosine * phibar
        phibar = sine * phibar
        x_state = x_state + (phi / rho)[:, None] * w_state
        w_state = v_state - (theta / rho)[:, None] * w_state
    return (x_state, phibar)


def solution(mesh):
    in_specs = (P(None, "ray"), P("ray", "cell", None, None), P("ray", "cell"), P("ray", "cell"))
    out_specs = (P(None, "cell"), P())
    return jax.shard_map(local, mesh=mesh, in_specs=in_specs, out_specs=out_specs, check_vma=False)
```

profile of v0, /device:TPU:0, one launch (start us, length us, event | category | flops | bytes accessed | tf_op | source)
XLA Modules:
  0.0 825.7 jit_solution(12070884797289773276)
XLA Ops:
  8.2 16.0 %psum.119 = f32[8]{0:T(128)S(1)} all-reduce(f32[8]{0:T(128)S(1)} %multiply_reduce_fusion.8), channel_id=1, replica_groups=mesh['ray'=8,'cell'=16] {'ray'}, use_global_device_ids=true, to_apply=%region_1.0 | all-reduce | flops 8 | bytes 64 | tf_op jit(solution)/shard_map/psum | solution.py:11
  25.9 2.8 fusion.51
  30.3 58.9 %all-reduce.9.cloned.1.call-done = f32[8,8192]{1,0:T(8,128)} async-done(((f32[8,8192]{1,0:T(8,128)}), f32[8,8192]{1,0:T(8,128)}) %all-reduce.9.cloned.1.call-update) | async-done | bytes 262160 | tf_op jit(solution)/shard_map/psum | solution.py:48
  89.2 1.1 multiply_reduce_fusion.3
  90.4 40.3 %psum.121 = f32[8]{0:T(128)S(1)} all-reduce(f32[8]{0:T(128)S(1)} %multiply_reduce_fusion.3), channel_id=1, replica_groups=mesh['ray'=8,'cell'=16] {'cell'}, use_global_device_ids=true, to_apply=%region_4.0 | all-reduce | flops 8 | bytes 64 | tf_op jit(solution)/shard_map/psum | solution.py:16
  132.3 4.1 fusion.14
  136.5 74.6 %all-reduce.11.cloned.1.call-done = f32[8,2048]{1,0:T(8,128)} async-done(((f32[8,2048]{1,0:T(8,128)}), f32[8,2048]{1,0:T(8,128)}) %all-reduce.11.cloned.1.call-update) | async-done | bytes 65552 | tf_op jit(solution)/shard_map/psum | solution.py:64
  212.1 13.2 %psum.123 = f32[8]{0:T(128)S(1)} all-reduce(f32[8]{0:T(128)S(1)} %get-tuple-element.21), channel_id=1, replica_groups=mesh['ray'=8,'cell'=16] {'ray'}, use_global_device_ids=true, to_apply=%region_7.0 | all-reduce | flops 8 | bytes 64 | tf_op jit(solution)/shard_map/psum | solution.py:11
  225.4 2.9 fusion.52
  229.6 56.8 %all-reduce.13.cloned.1.call-done = f32[8,8192]{1,0:T(8,128)} async-done(((f32[8,8192]{1,0:T(8,128)}), f32[8,8192]{1,0:T(8,128)}) %all-reduce.13.cloned.1.call-update) | async-done | bytes 262160 | tf_op jit(solution)/shard_map/psum | solution.py:48
  286.5 1.2 multiply_reduce_fusion.2
  287.7 40.3 %psum.125 = f32[8]{0:T(128)S(1)} all-reduce(f32[8]{0:T(128)S(1)} %multiply_reduce_fusion.2), channel_id=1, replica_groups=mesh['ray'=8,'cell'=16] {'cell'}, use_global_device_ids=true, to_apply=%region_10.0 | all-reduce | flops 8 | bytes 64 | tf_op jit(solution)/shard_map/psum | solution.py:16
  328.0 1.1 fusion.50
  329.7 4.0 fusion.12
  333.8 74.6 %all-reduce.15.cloned.1.call-done = f32[8,2048]{1,0:T(8,128)} async-done(((f32[8,2048]{1,0:T(8,128)}), f32[8,2048]{1,0:T(8,128)}) %all-reduce.15.cloned.1.call-update) | async-done | bytes 65552 | tf_op jit(solution)/shard_map/psum | solution.py:64
  409.4 13.2 %psum.127 = f32[8]{0:T(128)S(1)} all-reduce(f32[8]{0:T(128)S(1)} %get-tuple-element.17), channel_id=1, replica_groups=mesh['ray'=8,'cell'=16] {'ray'}, use_global_device_ids=true, to_apply=%region_13.0 | all-reduce | flops 8 | bytes 64 | tf_op jit(solution)/shard_map/psum | solution.py:11
  422.7 2.9 fusion.53
  426.9 56.8 %all-reduce.17.cloned.1.call-done = f32[8,8192]{1,0:T(8,128)} async-done(((f32[8,8192]{1,0:T(8,128)}), f32[8,8192]{1,0:T(8,128)}) %all-reduce.17.cloned.1.call-update) | async-done | bytes 262160 | tf_op jit(solution)/shard_map/psum | solution.py:48
  483.8 1.2 multiply_reduce_fusion.1
  485.0 40.3 %psum.129 = f32[8]{0:T(128)S(1)} all-reduce(f32[8]{0:T(128)S(1)} %multiply_reduce_fusion.1), channel_id=1, replica_groups=mesh['ray'=8,'cell'=16] {'cell'}, use_global_device_ids=true, to_apply=%region_16.0 | all-reduce | flops 8 | bytes 64 | tf_op jit(solution)/shard_map/psum | solution.py:16
  525.3 1.1 fusion.49
  527.0 4.0 fusion.10
  531.1 74.6 %all-reduce.19.cloned.1.call-done = f32[8,2048]{1,0:T(8,128)} async-done(((f32[8,2048]{1,0:T(8,128)}), f32[8,2048]{1,0:T(8,128)}) %all-reduce.19.cloned.1.call-update) | async-done | bytes 65552 | tf_op jit(solution)/shard_map/psum | solution.py:64
  606.7 13.2 %psum.131 = f32[8]{0:T(128)S(1)} all-reduce(f32[8]{0:T(128)S(1)} %get-tuple-element.13), channel_id=1, replica_groups=mesh['ray'=8,'cell'=16] {'ray'}, use_global_device_ids=true, to_apply=%region_19.0 | all-reduce | flops 8 | bytes 64 | tf_op jit(solution)/shard_map/psum | solution.py:11
  620.0 2.9 fusion.54
  624.2 56.8 %all-reduce.21.cloned.1.call-done = f32[8,8192]{1,0:T(8,128)} async-done(((f32[8,8192]{1,0:T(8,128)}), f32[8,8192]{1,0:T(8,128)}) %all-reduce.21.cloned.1.call-update) | async-done | bytes 262160 | tf_op jit(solution)/shard_map/psum | solution.py:48
  681.1 1.3 multiply_reduce_fusion
  682.4 40.3 %psum.133 = f32[8]{0:T(128)S(1)} all-reduce(f32[8]{0:T(128)S(1)} %multiply_reduce_fusion), channel_id=1, replica_groups=mesh['ray'=8,'cell'=16] {'cell'}, use_global_device_ids=true, to_apply=%region_22.0 | all-reduce | flops 8 | bytes 64 | tf_op jit(solution)/shard_map/psum | solution.py:16
  722.7 1.1 fusion.24
  724.3 4.0 fusion.8
  728.4 74.6 %all-reduce.23.cloned.1.call-done = f32[8,2048]{1,0:T(8,128)} async-done(((f32[8,2048]{1,0:T(8,128)}), f32[8,2048]{1,0:T(8,128)}) %all-reduce.23.cloned.1.call-update) | async-done | bytes 65552 | tf_op jit(solution)/shard_map/psum | solution.py:64
  804.0 13.2 %psum.135 = f32[8]{0:T(128)S(1)} all-reduce(f32[8]{0:T(128)S(1)} %multiply_reduce_fusion.4), channel_id=1, replica_groups=mesh['ray'=8,'cell'=16] {'ray'}, use_global_device_ids=true, to_apply=%region_25.0 | all-reduce | flops 8 | bytes 64 | tf_op jit(solution)/shard_map/psum | solution.py:11
  (63 shorter events, 18.0 us)
Async XLA Ops:
  7.2 21.6 %copy-start.3 = (s32[8,4]{0,1:T(4,128)S(1)}, s32[8,4]{0,1:T(4,128)}, u32[]{:S(2)}) copy-start(s32[8,4]{0,1:T(4,128)} %param.6) | copy-start | bytes 388
  7.2 82.1 %all-reduce.9.cloned.1.call-start = ((), (), s32[]{:S(2)}) async-start(), calls=%async_computation | async-start | bytes 524288 | tf_op jit(solution)/shard_map/psum | solution.py:48
  28.8 182.3 %copy-start.2 = (f32[8,2048]{1,0:T(8,128)S(1)}, f32[8,2048]{1,0:T(8,128)}, u32[]{:S(2)}) copy-start(f32[8,2048]{1,0:T(8,128)} %param.4) | copy-start | bytes 196612
  30.1 180.9 %all-reduce.11.cloned.1.call-start = ((), (), s32[]{:S(2)}) async-start(), calls=%async_computation.1 | async-start | bytes 131072 | tf_op jit(solution)/shard_map/psum | solution.py:64
  132.3 154.2 %copy-start = (f32[8,8192]{1,0:T(8,128)S(1)}, f32[8,8192]{1,0:T(8,128)}, u32[]{:S(2)}) copy-start(f32[8,8192]{1,0:T(8,128)} %all-reduce.9.cloned.1.call-done) | copy-start | bytes 786436
  136.4 150.1 %all-reduce.13.cloned.1.call-start = ((), (), s32[]{:S(2)}) async-start(), calls=%async_computation.2 | async-start | bytes 524288 | tf_op jit(solution)/shard_map/psum | solution.py:48
  229.6 178.7 %all-reduce.15.cloned.1.call-start = ((), (), s32[]{:S(2)}) async-start(), calls=%async_computation.3 | async-start | bytes 131072 | tf_op jit(solution)/shard_map/psum | solution.py:64
  333.7 150.1 %all-reduce.17.cloned.1.call-start = ((), (), s32[]{:S(2)}) async-start(), calls=%async_computation.4 | async-start | bytes 524288 | tf_op jit(solution)/shard_map/psum | solution.py:48
  426.9 178.7 %all-reduce.19.cloned.1.call-start = ((), (), s32[]{:S(2)}) async-start(), calls=%async_computation.5 | async-start | bytes 131072 | tf_op jit(solution)/shard_map/psum | solution.py:64
  531.0 150.1 %all-reduce.21.cloned.1.call-start = ((), (), s32[]{:S(2)}) async-start(), calls=%async_computation.6 | async-start | bytes 524288 | tf_op jit(solution)/shard_map/psum | solution.py:48
  624.2 178.8 %all-reduce.23.cloned.1.call-start = ((), (), s32[]{:S(2)}) async-start(), calls=%async_computation.7 | async-start | bytes 131072 | tf_op jit(solution)/shard_map/psum | solution.py:64
  681.1 136.8 %copy-start.1 = (f32[8,8192]{1,0:T(8,128)S(1)}, f32[8,8192]{1,0:T(8,128)}, u32[]{:S(2)}) copy-start(f32[8,8192]{1,0:T(8,128)} %all-reduce.21.cloned.1.call-done) | copy-start | bytes 786436
Sparse Core Ops, SparseCore 0:
  30.2 58.9 all-reduce.8
  136.5 74.4 all-reduce.10
  229.7 56.7 all-reduce.12
  333.8 74.4 all-reduce.14
  427.0 56.7 all-reduce.16
  531.1 74.4 all-reduce.18
  624.3 56.7 all-reduce.20
  728.5 74.4 all-reduce.22
where the time goes:
time: 827 us; the launch traced here: 826 us
  waiting for transfers between devices  528 us (64%)
  blocking collectives  230 us (28%)
  matrix products  29.4 us (4%)
  other arithmetic  17.7 us (2%)
  between operations  14.3 us (2%)
    psum x4, waiting for transfers between devices, local(): summed = lax.psum(partial_value, 'cell')  298 us
    psum x4, waiting for transfers between devices, cols_reduce(): return lax.psum(adj_terms, 'ray')  229 us
    psum x4, blocking collectives, norm_cols(): total = lax.psum(local_sq, 'cell')  161 us
    psum x5, blocking collectives, norm_rows(): total = lax.psum(local_sq, 'ray')  68.9 us
  transfers between devices with their start and end apart: 8, of which 8 were waited for; matrix products, arithmetic and copies ran while one was open for 0% of the time, Pallas kernels for 0%

commit v1 on v0

v1 whole, which is shorter than its diff:
```python
import functools

import jax
import jax.numpy as jnp
from jax import lax
from jax.experimental import pallas as pl
from jax.experimental.pallas import tpu as pltpu
from jax.sharding import Mesh, PartitionSpec as P

BLK_DEV = 32
ITERS = 4
EPS = 1e-06
F32 = jnp.float32
BF16 = jnp.bfloat16

VMEM = pl.BlockSpec(memory_space=pltpu.VMEM)
SMEM = pl.BlockSpec(memory_space=pltpu.SMEM)


def lane_sum(x):
    return jnp.sum(x, axis=1, keepdims=True)


def fold_sq(x, width):
    total = None
    for at in range(0, x.shape[1], width):
        piece = x[:, at : at + width]
        total = piece * piece if total is None else total + piece * piece
    return total


def wide(x):
    return jnp.broadcast_to(x, (x.shape[0], 128))


def scatter_products(u, place_ref, tiles_ref, keep_ref, send_ref, acc_ref):
    bundles, slots, rays, cells = tiles_ref.shape
    half = keep_ref.shape[1]
    acc_ref[...] = jnp.zeros_like(acc_ref)
    low = u.astype(BF16)
    for b in range(bundles):
        rows = low[:, b * rays : (b + 1) * rays]
        for s in range(slots):
            part = jnp.dot(rows, tiles_ref[b, s], preferred_element_type=F32)
            at = pl.multiple_of(place_ref[b * slots + s] * cells, cells)
            acc_ref[:, pl.ds(at, cells)] += part
    squares = fold_sq(u, cells)
    for out_ref, at in ((keep_ref, 0), (send_ref, half)):
        out_ref[:, : half - cells] = acc_ref[:, at : at + half - cells]
        out_ref[:, half - cells :] = squares


def first_adjoint(place_ref, right_ref, tiles_ref, keep_ref, send_ref, acc_ref):
    scatter_products(right_ref[...], place_ref, tiles_ref, keep_ref, send_ref, acc_ref)


def ray_vector(own_ref, left_ref, right_ref, far_ref, prev_ref, beta_ref):
    total = (own_ref[...] + far_ref[...]) + (left_ref[...] + right_ref[...])
    rows = prev_ref.shape[1]
    alpha = jnp.sqrt(lane_sum(total[:, rows:]) + EPS)
    u = total[:, :rows] / alpha - (alpha / beta_ref[:, :1]) * prev_ref[...]
    return u, alpha


def next_adjoint(
    place_ref, own_ref, left_ref, right_ref, far_ref, prev_ref, beta_ref, tiles_ref,
    keep_ref, send_ref, u_ref, alpha_ref, acc_ref,
):
    u, alpha = ray_vector(own_ref, left_ref, right_ref, far_ref, prev_ref, beta_ref)
    u_ref[...] = u
    alpha_ref[...] = wide(alpha)
    scatter_products(u, place_ref, tiles_ref, keep_ref, send_ref, acc_ref)


def last_norm(
    own_ref, left_ref, right_ref, far_ref, prev_ref, beta_ref, out_ref, alpha_ref
):
    u, alpha = ray_vector(own_ref, left_ref, right_ref, far_ref, prev_ref, beta_ref)
    alpha_ref[...] = wide(alpha)
    out_ref[...] = fold_sq(u, 128)


def cell_vector(
    first, own_ref, left_ref, right_ref, far_ref, prev_ref, alpha_ref, v_ref, beta_ref
):
    total = (own_ref[...] + far_ref[...]) + (left_ref[...] + right_ref[...])
    width = v_ref.shape[1]
    beta = jnp.sqrt(lane_sum(total[:, width:]) + EPS)
    v = total[:, :width] / beta
    if not first:
        v = v - (beta / alpha_ref[:, :1]) * prev_ref[...]
    v_ref[...] = v
    beta_ref[...] = wide(beta)


def forward(place_ref, own_ref, other_ref, tiles_ref, out_ref, low_ref):
    bundles, slots, rays, cells = tiles_ref.shape
    width = own_ref.shape[1]
    own, other = own_ref[...], other_ref[...]
    low_ref[:, :width] = own.astype(BF16)
    low_ref[:, width : 2 * width] = other.astype(BF16)
    low_ref[:, 2 * width :] = jnp.zeros((own.shape[0], cells), BF16)
    base = bundles * slots
    for b in range(bundles):
        acc = None
        for s in range(slots):
            at = pl.multiple_of(place_ref[base + b * slots + s] * cells, cells)
            part = lax.dot_general(
                low_ref[:, pl.ds(at, cells)], tiles_ref[b, s],
                (((1,), (1,)), ((), ())), preferred_element_type=F32,
            )
            acc = part if acc is None else acc + part
        out_ref[:, b * rays : (b + 1) * rays] = acc
    out_ref[:, bundles * rays :] = fold_sq(own, cells) + fold_sq(other, cells)


def finish(place_ref, own_ref, left_ref, right_ref, far_ref, *rest):
    count = ITERS
    own_refs, other_refs = rest[:count], rest[count : 2 * count]
    alpha_refs, beta_refs = rest[2 * count : 3 * count], rest[3 * count : 4 * count]
    x_ref, misfit_ref = rest[4 * count :]
    width = own_refs[0].shape[1]
    total = (own_ref[...] + far_ref[...]) + (left_ref[...] + right_ref[...])
    last_beta = jnp.sqrt(lane_sum(total) + EPS)
    alphas = [ref[:, :1] for ref in alpha_refs]
    betas = [ref[:, :1] for ref in beta_refs] + [last_beta]
    phibar, rhobar = betas[0], alphas[0]
    steps, turns = [], []
    for k in range(count):
        beta = betas[k + 1]
        rho = jnp.sqrt(rhobar * rhobar + beta * beta)
        cosine, sine = rhobar / rho, beta / rho
        phi = cosine * phibar
        phibar = sine * phibar
        steps.append(phi / rho)
        if k + 1 < count:
            theta = sine * alphas[k + 1]
            rhobar = -cosine * alphas[k + 1]
            turns.append(theta / rho)
    core = place_ref[place_ref.shape[0] - 1]
    for refs, half in ((own_refs, core), (other_refs, 1 - core)):
        w = refs[0][...] / alphas[0]
        x = steps[0] * w
        for k in range(1, count):
            w = refs[k][...] / alphas[k] - turns[k - 1] * w
            x = x + steps[k] * w
        x_ref[:, pl.ds(pl.multiple_of(half * width, width), width)] = x
    misfit_ref[...] = wide(phibar)


def call(body, outs, specs, args, scratch=()):
    return pl.pallas_call(
        body,
        out_shape=outs,
        in_specs=specs,
        out_specs=[VMEM] * len(outs),
        scratch_shapes=list(scratch),
        compiler_params=pltpu.CompilerParams(vmem_limit_bytes=40 << 20),
    )(*args)


def local(right_side, tiles, pattern, counts):
    nrhs, rows = right_side.shape
    bundles, slots, rays, cells = tiles.shape
    blocks = BLK_DEV // 2
    half = blocks * cells
    core = lax.axis_index("core")
    live = lax.broadcasted_iota(jnp.int32, pattern.shape, 1) < counts
    mine = pattern // blocks == core
    within = pattern % blocks
    put = jnp.where(live, jnp.where(mine, within, blocks + 1 + within), blocks)
    get = jnp.where(live, jnp.where(mine, within, blocks + within), BLK_DEV)
    place = jnp.concatenate([put.reshape(-1), get.reshape(-1), core.astype(jnp.int32).reshape(1)])

    def shape(columns, dtype=F32):
        return jax.ShapeDtypeStruct((nrhs, columns), dtype)

    def spread(value, axis):
        n = lax.axis_size(axis)
        moved = [
            lax.ppermute(value, axis, [(i, (i + by) % n) for i in range(n)]) for by in (1, 3, 2)
        ]
        return [value] + moved

    def swap(value):
        return lax.ppermute(value, "core", [(0, 1), (1, 0)])

    def over_cell(partial):
        own, left, right, far = spread(partial, "x")
        return spread((own + far) + (left + right), "y")

    halves = [shape(half + cells)] * 2
    store = [pltpu.VMEM((nrhs, 2 * (half + cells)), F32)]
    keep, send = call(
        first_adjoint, halves, [SMEM, VMEM, VMEM], (place, right_side, tiles), store
    )
    u = right_side
    owns, others, alphas, betas = [], [], [], []
    for step in range(ITERS):
        prev = (owns[-1], alphas[-1]) if step else (right_side, right_side)
        v, beta = call(
            functools.partial(cell_vector, step == 0), [shape(half), shape(128)], [VMEM] * 6,
            (*spread(keep + swap(send), "z"), *prev),
        )
        other = swap(v)
        owns.append(v)
        others.append(other)
        betas.append(beta)
        products, = call(
            forward, [shape(rows + cells)], [SMEM] + [VMEM] * 3, (place, v, other, tiles),
            [pltpu.VMEM((nrhs, 2 * half + cells), BF16)],
        )
        rows_in = over_cell(products)
        if step + 1 < ITERS:
            keep, send, u, alpha = call(
                next_adjoint, halves + [shape(rows), shape(128)], [SMEM] + [VMEM] * 7,
                (place, *rows_in, u, beta, tiles), store,
            )
        else:
            squares, alpha = call(
                last_norm, [shape(128), shape(128)], [VMEM] * 6, (*rows_in, u, beta)
            )
        alphas.append(alpha)
    x, misfit = call(
        finish, [shape(2 * half), shape(128)], [SMEM] + [VMEM] * (4 + 4 * ITERS),
        (place, *spread(squares + swap(squares), "z"), *owns, *others, *alphas, *betas),
    )
    return x, misfit[:, 0]


def solution(mesh):
    parts = Mesh(mesh.devices.reshape(4, 2, 4, 4), ("z", "core", "x", "y"))
    ray, cell = ("z", "core"), ("x", "y")
    in_specs = (P(None, ray), P(ray, cell, None, None), P(ray, cell), P(ray, cell))
    out_specs = (P(None, cell), P())
    return jax.shard_map(local, mesh=parts, in_specs=in_specs, out_specs=out_specs, check_vma=False)
```

time: 827 us -> 154 us (0.19)
  waiting for transfers between devices: 528 us -> 80.4 us
  blocking collectives: 230 us -> 0 us
  starting transfers between devices: 0.33 us -> 53.3 us
  matrix products: 29.4 us -> 0 us
  other arithmetic: 17.7 us -> 0.95 us
  Pallas kernels: 0 us -> 14.6 us
  between operations: 14.3 us -> 0.86 us
    psum x8 -> x0, waiting for transfers between devices: 528 us -> none  [the longest x4 298 us: local(): summed = lax.psum(partial_value, 'cell')]
    psum x9 -> x0, blocking collectives: 230 us -> none  [the longest x4 161 us: norm_cols(): total = lax.psum(local_sq, 'cell')]
    ppermute x0 -> x48, waiting for transfers between devices: none -> 80.4 us  [the longest x39 68.6 us: spread(): lax.ppermute(value, axis, [(i, (i + by) % n) for i in range(n)])]
    ppermute x0 -> x48, starting transfers between devices: none -> 53.3 us  [the longest x39 52.3 us: spread(): lax.ppermute(value, axis, [(i, (i + by) % n) for i in range(n)])]
    dot_general x12 -> x0, matrix products: 29.4 us -> none  [the longest x4 16.1 us: local(): jnp.einsum('bsrc,nbsc->nbr', tiles, picked, preferred_element_type=jnp.fl...]
    pallas_call x0 -> x14, Pallas kernels: none -> 14.6 us  [call(): pl.pallas_call(body, out_shape=outs, in_specs=specs, out_specs=[VMEM] * l...]
    reduce_sum x9 -> x0, other arithmetic: 9.93 us -> none  [the longest x5 5.13 us: local(): beta = norm_rows(jnp.sum(u_state * u_state, axis=1))]
  transfers between devices with their start and end apart: 8 -> 48, of which waited for: 8 -> 39; matrix products, arithmetic and copies ran while one was open for 0% -> 0% of each run, Pallas kernels for 0% -> 0%
where the time goes in v1:
time: 154 us
  waiting for transfers between devices  80.4 us (52%)
  starting transfers between devices  53.3 us (35%)
  Pallas kernels  14.6 us (9%)
  local copies, waits for them, and re-layouts  3.99 us (3%)
    ppermute x39, waiting for transfers between devices, spread(): lax.ppermute(value, axis, [(i, (i + by) % n) for i in range(n)])  68.6 us
    ppermute x39, starting transfers between devices, spread(): lax.ppermute(value, axis, [(i, (i + by) % n) for i in range(n)])  52.3 us
    pallas_call x14, Pallas kernels, call(): pl.pallas_call(body, out_shape=outs, in_specs=specs, out_specs=[VMEM] * l...  14.6 us
    ppermute x9, waiting for transfers between devices, swap(): return lax.ppermute(value, 'core', [(0, 1), (1, 0)])  11.9 us
  transfers between devices with their start and end apart: 48, of which 39 were waited for; matrix products, arithmetic and copies ran while one was open for 0% of the time, Pallas kernels for 0%

profile of v1, /device:TPU:0, one launch (start us, length us, event | category | flops | bytes accessed | tf_op | source)
XLA Modules:
  0.0 154.1 jit_solution(10168624154925457298)
XLA Ops:
  1.8 2.2 %copy-done = bf16[8,4,256,256]{3,2,1,0:T(8,128)(2,1)S(1)} copy-done((bf16[8,4,256,256]{3,2,1,0:T(8,128)(2,1)S(1)}, bf16[8,4,256,256]{3,2,1,0:T(8,128)(2,1)}, u32[]{:S(2)}) %copy-start) | copy-done | bytes 4194328
  7.5 4.0 %collective-permute-start.3 = (f32[8,4352]{1,0:T(8,128)S(1)}, f32[8,4352]{1,0:T(8,128)S(1)}, u32[]{:S(2)}, u32[]{:S(2)}) collective-permute-start(f32[8,4352]{1,0:T(8,128)S(1)} %add.72.own_ref), channel_id=1, source_target_pairs={{0,64},{32,96},{64,0},{96,32},{1,65},{33,97},{65,1},{97,33},{2,66}... | collective-permute-start | bytes 417800 | tf_op jit(solution)/shard_map/ppermute | solution.py:181
  13.6 2.4 %collective-permute-done.3.far_ref = f32[8,4352]{1,0:T(8,128)S(1)} collective-permute-done((f32[8,4352]{1,0:T(8,128)S(1)}, f32[8,4352]{1,0:T(8,128)S(1)}, u32[]{:S(2)}, u32[]{:S(2)}) %collective-permute-start.3) | collective-permute-done | bytes 139296 | tf_op jit(solution)/shard_map/ppermute | solution.py:181
  15.9 3.4 %collective-permute-done.2.right_ref = f32[8,4352]{1,0:T(8,128)S(1)} collective-permute-done((f32[8,4352]{1,0:T(8,128)S(1)}, f32[8,4352]{1,0:T(8,128)S(1)}, u32[]{:S(2)}, u32[]{:S(2)}) %collective-permute-start.2) | collective-permute-done | bytes 139296 | tf_op jit(solution)/shard_map/ppermute | solution.py:181
  20.8 1.7 %shard_map.61 = f32[8,2304]{1,0:T(8,128)S(1)} custom-call(s32[65]{0:T(128)S(1)} %pad_add_fusion.place_ref, f32[8,4096]{1,0:T(8,128)S(1)} %get-tuple-element.30.own_ref.prev_ref.rest_0_, f32[8,4096]{1,0:T(8,128)S(1)} %collective-permute-done.4.other_ref.rest_4_, bf16[8,4,256,256]{3,2,1,0:T(8,128)(2,1)S(1)} %copy-done.1), custom_call_target="tpu_custom_call" | custom-call | tf_op jit(solution)/shard_map/pallas_call | solution.py:152
  22.6 2.8 %collective-permute-start.7 = (f32[8,2304]{1,0:T(8,128)S(1)}, f32[8,2304]{1,0:T(8,128)S(1)}, u32[]{:S(2)}, u32[]{:S(2)}) collective-permute-start(f32[8,2304]{1,0:T(8,128)S(1)} %shard_map.61), channel_id=1, source_target_pairs={{0,12},{4,0},{8,4},{12,8},{1,13},{5,1},{9,5},{13,9},{2,14},{6,2},{... | collective-permute-start | bytes 221192 | tf_op jit(solution)/shard_map/ppermute | solution.py:181
  25.3 2.3 %collective-permute-start.5 = (f32[8,2304]{1,0:T(8,128)S(1)}, f32[8,2304]{1,0:T(8,128)S(1)}, u32[]{:S(2)}, u32[]{:S(2)}) collective-permute-start(f32[8,2304]{1,0:T(8,128)S(1)} %shard_map.61), channel_id=1, source_target_pairs={{0,8},{4,12},{8,0},{12,4},{1,9},{5,13},{9,1},{13,5},{2,10},{6,14},... | collective-permute-start | bytes 221192 | tf_op jit(solution)/shard_map/ppermute | solution.py:181
  27.6 4.5 %collective-permute-done.6 = f32[8,2304]{1,0:T(8,128)S(1)} collective-permute-done((f32[8,2304]{1,0:T(8,128)S(1)}, f32[8,2304]{1,0:T(8,128)S(1)}, u32[]{:S(2)}, u32[]{:S(2)}) %collective-permute-start.6) | collective-permute-done | bytes 73760 | tf_op jit(solution)/shard_map/ppermute | solution.py:181
  32.2 3.3 %collective-permute-start.10 = (f32[8,2304]{1,0:T(8,128)S(1)}, f32[8,2304]{1,0:T(8,128)S(1)}, u32[]{:S(2)}, u32[]{:S(2)}) collective-permute-start(f32[8,2304]{1,0:T(8,128)S(1)} %add_add_fusion.3.own_ref), channel_id=1, source_target_pairs={{0,2},{1,3},{2,0},{3,1},{4,6},{5,7},{6,4},{7,5},{8,10},{9,11},{10,... | collective-permute-start | bytes 221192 | tf_op jit(solution)/shard_map/ppermute | solution.py:181
  39.8 2.3 %collective-permute-done.8.left_ref = f32[8,2304]{1,0:T(8,128)S(1)} collective-permute-done((f32[8,2304]{1,0:T(8,128)S(1)}, f32[8,2304]{1,0:T(8,128)S(1)}, u32[]{:S(2)}, u32[]{:S(2)}) %collective-permute-start.8) | collective-permute-done | bytes 73760 | tf_op jit(solution)/shard_map/ppermute | solution.py:181
  44.9 2.5 %collective-permute-start.14 = (f32[8,4352]{1,0:T(8,128)S(1)}, f32[8,4352]{1,0:T(8,128)S(1)}, u32[]{:S(2)}, u32[]{:S(2)}) collective-permute-start(f32[8,4352]{1,0:T(8,128)S(1)} %add.76.own_ref), channel_id=1, source_target_pairs={{0,64},{32,96},{64,0},{96,32},{1,65},{33,97},{65,1},{97,33},{2,66}... | collective-permute-start | bytes 417800 | tf_op jit(solution)/shard_map/ppermute | solution.py:181
  49.5 3.5 %collective-permute-done.14.far_ref = f32[8,4352]{1,0:T(8,128)S(1)} collective-permute-done((f32[8,4352]{1,0:T(8,128)S(1)}, f32[8,4352]{1,0:T(8,128)S(1)}, u32[]{:S(2)}, u32[]{:S(2)}) %collective-permute-start.14) | collective-permute-done | bytes 139296 | tf_op jit(solution)/shard_map/ppermute | solution.py:181
  53.0 2.1 %collective-permute-done.13.right_ref = f32[8,4352]{1,0:T(8,128)S(1)} collective-permute-done((f32[8,4352]{1,0:T(8,128)S(1)}, f32[8,4352]{1,0:T(8,128)S(1)}, u32[]{:S(2)}, u32[]{:S(2)}) %collective-permute-start.13) | collective-permute-done | bytes 139296 | tf_op jit(solution)/shard_map/ppermute | solution.py:181
  57.1 1.7 %shard_map.64 = f32[8,2304]{1,0:T(8,128)S(1)} custom-call(s32[65]{0:T(128)S(1)} %pad_add_fusion.place_ref, f32[8,4096]{1,0:T(8,128)S(1)} %get-tuple-element.35.own_ref.prev_ref.rest_1_, f32[8,4096]{1,0:T(8,128)S(1)} %collective-permute-done.15.other_ref.rest_5_, bf16[8,4,256,256]{3,2,1,0:T(8,128)(2,1)S(1)} %copy-done.1), custom_call_target="tpu_custom_call" | custom-call | tf_op jit(solution)/shard_map/pallas_call | solution.py:152
  58.9 2.3 %collective-permute-start.18 = (f32[8,2304]{1,0:T(8,128)S(1)}, f32[8,2304]{1,0:T(8,128)S(1)}, u32[]{:S(2)}, u32[]{:S(2)}) collective-permute-start(f32[8,2304]{1,0:T(8,128)S(1)} %shard_map.64), channel_id=1, source_target_pairs={{0,12},{4,0},{8,4},{12,8},{1,13},{5,1},{9,5},{13,9},{2,14},{6,2},{... | collective-permute-start | bytes 221192 | tf_op jit(solution)/shard_map/ppermute | solution.py:181
  63.2 4.7 %collective-permute-done.17 = f32[8,2304]{1,0:T(8,128)S(1)} collective-permute-done((f32[8,2304]{1,0:T(8,128)S(1)}, f32[8,2304]{1,0:T(8,128)S(1)}, u32[]{:S(2)}, u32[]{:S(2)}) %collective-permute-start.17) | collective-permute-done | bytes 73760 | tf_op jit(solution)/shard_map/ppermute | solution.py:181
  68.6 2.0 %collective-permute-start.20 = (f32[8,2304]{1,0:T(8,128)S(1)}, f32[8,2304]{1,0:T(8,128)S(1)}, u32[]{:S(2)}, u32[]{:S(2)}) collective-permute-start(f32[8,2304]{1,0:T(8,128)S(1)} %add_add_fusion.2.own_ref), channel_id=1, source_target_pairs={{0,3},{1,0},{2,1},{3,2},{4,7},{5,4},{6,5},{7,6},{8,11},{9,8},{10,9... | collective-permute-start | bytes 221192 | tf_op jit(solution)/shard_map/ppermute | solution.py:181
  70.6 3.9 %collective-permute-done.21.far_ref = f32[8,2304]{1,0:T(8,128)S(1)} collective-permute-done((f32[8,2304]{1,0:T(8,128)S(1)}, f32[8,2304]{1,0:T(8,128)S(1)}, u32[]{:S(2)}, u32[]{:S(2)}) %collective-permute-start.21) | collective-permute-done | bytes 73760 | tf_op jit(solution)/shard_map/ppermute | solution.py:181
  78.9 2.3 %collective-permute-start.25 = (f32[8,4352]{1,0:T(8,128)S(1)}, f32[8,4352]{1,0:T(8,128)S(1)}, u32[]{:S(2)}, u32[]{:S(2)}) collective-permute-start(f32[8,4352]{1,0:T(8,128)S(1)} %add.80.own_ref), channel_id=1, source_target_pairs={{0,64},{32,96},{64,0},{96,32},{1,65},{33,97},{65,1},{97,33},{2,66}... | collective-permute-start | bytes 417800 | tf_op jit(solution)/shard_map/ppermute | solution.py:181
  83.2 3.8 %collective-permute-done.25.far_ref = f32[8,4352]{1,0:T(8,128)S(1)} collective-permute-done((f32[8,4352]{1,0:T(8,128)S(1)}, f32[8,4352]{1,0:T(8,128)S(1)}, u32[]{:S(2)}, u32[]{:S(2)}) %collective-permute-start.25) | collective-permute-done | bytes 139296 | tf_op jit(solution)/shard_map/ppermute | solution.py:181
  87.0 1.9 %collective-permute-done.24.right_ref = f32[8,4352]{1,0:T(8,128)S(1)} collective-permute-done((f32[8,4352]{1,0:T(8,128)S(1)}, f32[8,4352]{1,0:T(8,128)S(1)}, u32[]{:S(2)}, u32[]{:S(2)}) %collective-permute-start.24) | collective-permute-done | bytes 139296 | tf_op jit(solution)/shard_map/ppermute | solution.py:181
  92.9 2.3 %collective-permute-start.29 = (f32[8,2304]{1,0:T(8,128)S(1)}, f32[8,2304]{1,0:T(8,128)S(1)}, u32[]{:S(2)}, u32[]{:S(2)}) collective-permute-start(f32[8,2304]{1,0:T(8,128)S(1)} %shard_map.67), channel_id=1, source_target_pairs={{0,12},{4,0},{8,4},{12,8},{1,13},{5,1},{9,5},{13,9},{2,14},{6,2},{... | collective-permute-start | bytes 221192 | tf_op jit(solution)/shard_map/ppermute | solution.py:181
  97.3 4.7 %collective-permute-done.28 = f32[8,2304]{1,0:T(8,128)S(1)} collective-permute-done((f32[8,2304]{1,0:T(8,128)S(1)}, f32[8,2304]{1,0:T(8,128)S(1)}, u32[]{:S(2)}, u32[]{:S(2)}) %collective-permute-start.28) | collective-permute-done | bytes 73760 | tf_op jit(solution)/shard_map/ppermute | solution.py:181
  104.2 4.3 %collective-permute-done.32.far_ref = f32[8,2304]{1,0:T(8,128)S(1)} collective-permute-done((f32[8,2304]{1,0:T(8,128)S(1)}, f32[8,2304]{1,0:T(8,128)S(1)}, u32[]{:S(2)}, u32[]{:S(2)}) %collective-permute-start.32) | collective-permute-done | bytes 73760 | tf_op jit(solution)/shard_map/ppermute | solution.py:181
  112.1 2.1 %collective-permute-start.36 = (f32[8,4352]{1,0:T(8,128)S(1)}, f32[8,4352]{1,0:T(8,128)S(1)}, u32[]{:S(2)}, u32[]{:S(2)}) collective-permute-start(f32[8,4352]{1,0:T(8,128)S(1)} %add.84.own_ref), channel_id=1, source_target_pairs={{0,64},{32,96},{64,0},{96,32},{1,65},{33,97},{65,1},{97,33},{2,66}... | collective-permute-start | bytes 417800 | tf_op jit(solution)/shard_map/ppermute | solution.py:181
  116.2 4.0 %collective-permute-done.36.far_ref = f32[8,4352]{1,0:T(8,128)S(1)} collective-permute-done((f32[8,4352]{1,0:T(8,128)S(1)}, f32[8,4352]{1,0:T(8,128)S(1)}, u32[]{:S(2)}, u32[]{:S(2)}) %collective-permute-start.36) | collective-permute-done | bytes 139296 | tf_op jit(solution)/shard_map/ppermute | solution.py:181
  124.1 1.7 %shard_map.70 = f32[8,2304]{1,0:T(8,128)S(1)} custom-call(s32[65]{0:T(128)S(1)} %pad_add_fusion.place_ref, f32[8,4096]{1,0:T(8,128)S(1)} %get-tuple-element.47.own_ref.rest_3_, f32[8,4096]{1,0:T(8,128)S(1)} %collective-permute-done.37.other_ref.rest_7_, bf16[8,4,256,256]{3,2,1,0:T(8,128)(2,1)S(1)} %copy-done.1), custom_call_target="tpu_custom_call" | custom-call | tf_op jit(solution)/shard_map/pallas_call | solution.py:152
  125.8 2.2 %collective-permute-start.40 = (f32[8,2304]{1,0:T(8,128)S(1)}, f32[8,2304]{1,0:T(8,128)S(1)}, u32[]{:S(2)}, u32[]{:S(2)}) collective-permute-start(f32[8,2304]{1,0:T(8,128)S(1)} %shard_map.70), channel_id=1, source_target_pairs={{0,12},{4,0},{8,4},{12,8},{1,13},{5,1},{9,5},{13,9},{2,14},{6,2},{... | collective-permute-start | bytes 221192 | tf_op jit(solution)/shard_map/ppermute | solution.py:181
  130.2 4.7 %collective-permute-done.39 = f32[8,2304]{1,0:T(8,128)S(1)} collective-permute-done((f32[8,2304]{1,0:T(8,128)S(1)}, f32[8,2304]{1,0:T(8,128)S(1)}, u32[]{:S(2)}, u32[]{:S(2)}) %collective-permute-start.39) | collective-permute-done | bytes 73760 | tf_op jit(solution)/shard_map/ppermute | solution.py:181
  137.8 3.6 %collective-permute-done.43.far_ref = f32[8,2304]{1,0:T(8,128)S(1)} collective-permute-done((f32[8,2304]{1,0:T(8,128)S(1)}, f32[8,2304]{1,0:T(8,128)S(1)}, u32[]{:S(2)}, u32[]{:S(2)}) %collective-permute-start.43) | collective-permute-done | bytes 73760 | tf_op jit(solution)/shard_map/ppermute | solution.py:181
  144.0 2.0 %collective-permute-start.47 = (f32[8,128]{1,0:T(8,128)S(1)}, f32[8,128]{1,0:T(8,128)S(1)}, u32[]{:S(2)}, u32[]{:S(2)}) collective-permute-start(f32[8,128]{1,0:T(8,128)S(1)} %add.88.own_ref), channel_id=1, source_target_pairs={{0,64},{32,96},{64,0},{96,32},{1,65},{33,97},{65,1},{97,33},{2,66}... | collective-permute-start | bytes 12296 | tf_op jit(solution)/shard_map/ppermute | solution.py:181
  149.6 2.4 %collective-permute-done.45.left_ref = f32[8,128]{1,0:T(8,128)S(1)} collective-permute-done((f32[8,128]{1,0:T(8,128)S(1)}, f32[8,128]{1,0:T(8,128)S(1)}, u32[]{:S(2)}, u32[]{:S(2)}) %collective-permute-start.45) | collective-permute-done | bytes 4128 | tf_op jit(solution)/shard_map/ppermute | solution.py:181
  (102 shorter events, 59.7 us)
Async XLA Ops:
  7.5 8.4 %collective-permute-start.3 = (f32[8,4352]{1,0:T(8,128)S(1)}, f32[8,4352]{1,0:T(8,128)S(1)}, u32[]{:S(2)}, u32[]{:S(2)}) collective-permute-start(f32[8,4352]{1,0:T(8,128)S(1)} %add.72.own_ref), channel_id=1, source_target_pairs={{0,64},{32,96},{64,0},{96,32},{1,65},{33,97},{65,1},{97,33},{2,66}... | collective-permute-start | bytes 417800 | tf_op jit(solution)/shard_map/ppermute | solution.py:181
  11.5 7.7 %collective-permute-start.2 = (f32[8,4352]{1,0:T(8,128)S(1)}, f32[8,4352]{1,0:T(8,128)S(1)}, u32[]{:S(2)}, u32[]{:S(2)}) collective-permute-start(f32[8,4352]{1,0:T(8,128)S(1)} %add.72.own_ref), channel_id=1, source_target_pairs={{0,96},{32,0},{64,32},{96,64},{1,97},{33,1},{65,33},{97,65},{2,98}... | collective-permute-start | bytes 417800 | tf_op jit(solution)/shard_map/ppermute | solution.py:181
  12.2 7.0 %collective-permute-start.1 = (f32[8,4352]{1,0:T(8,128)S(1)}, f32[8,4352]{1,0:T(8,128)S(1)}, u32[]{:S(2)}, u32[]{:S(2)}) collective-permute-start(f32[8,4352]{1,0:T(8,128)S(1)} %add.72.own_ref), channel_id=1, source_target_pairs={{0,32},{32,64},{64,96},{96,0},{1,33},{33,65},{65,97},{97,1},{2,34}... | collective-permute-start | bytes 417800 | tf_op jit(solution)/shard_map/ppermute | solution.py:181
  25.3 6.8 %collective-permute-start.6 = (f32[8,2304]{1,0:T(8,128)S(1)}, f32[8,2304]{1,0:T(8,128)S(1)}, u32[]{:S(2)}, u32[]{:S(2)}) collective-permute-start(f32[8,2304]{1,0:T(8,128)S(1)} %shard_map.61), channel_id=1, source_target_pairs={{0,4},{4,8},{8,12},{12,0},{1,5},{5,9},{9,13},{13,1},{2,6},{6,10},{... | collective-permute-start | bytes 221192 | tf_op jit(solution)/shard_map/ppermute | solution.py:181
  25.3 6.8 %collective-permute-start.5 = (f32[8,2304]{1,0:T(8,128)S(1)}, f32[8,2304]{1,0:T(8,128)S(1)}, u32[]{:S(2)}, u32[]{:S(2)}) collective-permute-start(f32[8,2304]{1,0:T(8,128)S(1)} %shard_map.61), channel_id=1, source_target_pairs={{0,8},{4,12},{8,0},{12,4},{1,9},{5,13},{9,1},{13,5},{2,10},{6,14},... | collective-permute-start | bytes 221192 | tf_op jit(solution)/shard_map/ppermute | solution.py:181
  32.2 6.7 %collective-permute-start.10 = (f32[8,2304]{1,0:T(8,128)S(1)}, f32[8,2304]{1,0:T(8,128)S(1)}, u32[]{:S(2)}, u32[]{:S(2)}) collective-permute-start(f32[8,2304]{1,0:T(8,128)S(1)} %add_add_fusion.3.own_ref), channel_id=1, source_target_pairs={{0,2},{1,3},{2,0},{3,1},{4,6},{5,7},{6,4},{7,5},{8,10},{9,11},{10,... | collective-permute-start | bytes 221192 | tf_op jit(solution)/shard_map/ppermute | solution.py:181
  36.5 5.6 %collective-permute-start.8 = (f32[8,2304]{1,0:T(8,128)S(1)}, f32[8,2304]{1,0:T(8,128)S(1)}, u32[]{:S(2)}, u32[]{:S(2)}) collective-permute-start(f32[8,2304]{1,0:T(8,128)S(1)} %add_add_fusion.3.own_ref), channel_id=1, source_target_pairs={{0,1},{1,2},{2,3},{3,0},{4,5},{5,6},{6,7},{7,4},{8,9},{9,10},{10,1... | collective-permute-start | bytes 221192 | tf_op jit(solution)/shard_map/ppermute | solution.py:181
  44.9 8.1 %collective-permute-start.14 = (f32[8,4352]{1,0:T(8,128)S(1)}, f32[8,4352]{1,0:T(8,128)S(1)}, u32[]{:S(2)}, u32[]{:S(2)}) collective-permute-start(f32[8,4352]{1,0:T(8,128)S(1)} %add.76.own_ref), channel_id=1, source_target_pairs={{0,64},{32,96},{64,0},{96,32},{1,65},{33,97},{65,1},{97,33},{2,66}... | collective-permute-start | bytes 417800 | tf_op jit(solution)/shard_map/ppermute | solution.py:181
  47.5 7.7 %collective-permute-start.13 = (f32[8,4352]{1,0:T(8,128)S(1)}, f32[8,4352]{1,0:T(8,128)S(1)}, u32[]{:S(2)}, u32[]{:S(2)}) collective-permute-start(f32[8,4352]{1,0:T(8,128)S(1)} %add.76.own_ref), channel_id=1, source_target_pairs={{0,96},{32,0},{64,32},{96,64},{1,97},{33,1},{65,33},{97,65},{2,98}... | collective-permute-start | bytes 417800 | tf_op jit(solution)/shard_map/ppermute | solution.py:181
  48.6 6.9 %collective-permute-start.12 = (f32[8,4352]{1,0:T(8,128)S(1)}, f32[8,4352]{1,0:T(8,128)S(1)}, u32[]{:S(2)}, u32[]{:S(2)}) collective-permute-start(f32[8,4352]{1,0:T(8,128)S(1)} %add.76.own_ref), channel_id=1, source_target_pairs={{0,32},{32,64},{64,96},{96,0},{1,33},{33,65},{65,97},{97,1},{2,34}... | collective-permute-start | bytes 417800 | tf_op jit(solution)/shard_map/ppermute | solution.py:181
  61.1 6.8 %collective-permute-start.17 = (f32[8,2304]{1,0:T(8,128)S(1)}, f32[8,2304]{1,0:T(8,128)S(1)}, u32[]{:S(2)}, u32[]{:S(2)}) collective-permute-start(f32[8,2304]{1,0:T(8,128)S(1)} %shard_map.64), channel_id=1, source_target_pairs={{0,4},{4,8},{8,12},{12,0},{1,5},{5,9},{9,13},{13,1},{2,6},{6,10},{... | collective-permute-start | bytes 221192 | tf_op jit(solution)/shard_map/ppermute | solution.py:181
  61.1 6.8 %collective-permute-start.16 = (f32[8,2304]{1,0:T(8,128)S(1)}, f32[8,2304]{1,0:T(8,128)S(1)}, u32[]{:S(2)}, u32[]{:S(2)}) collective-permute-start(f32[8,2304]{1,0:T(8,128)S(1)} %shard_map.64), channel_id=1, source_target_pairs={{0,8},{4,12},{8,0},{12,4},{1,9},{5,13},{9,1},{13,5},{2,10},{6,14},... | collective-permute-start | bytes 221192 | tf_op jit(solution)/shard_map/ppermute | solution.py:181
  68.0 6.5 %collective-permute-start.21 = (f32[8,2304]{1,0:T(8,128)S(1)}, f32[8,2304]{1,0:T(8,128)S(1)}, u32[]{:S(2)}, u32[]{:S(2)}) collective-permute-start(f32[8,2304]{1,0:T(8,128)S(1)} %add_add_fusion.2.own_ref), channel_id=1, source_target_pairs={{0,2},{1,3},{2,0},{3,1},{4,6},{5,7},{6,4},{7,5},{8,10},{9,11},{10,... | collective-permute-start | bytes 221192 | tf_op jit(solution)/shard_map/ppermute | solution.py:181
  68.6 6.0 %collective-permute-start.20 = (f32[8,2304]{1,0:T(8,128)S(1)}, f32[8,2304]{1,0:T(8,128)S(1)}, u32[]{:S(2)}, u32[]{:S(2)}) collective-permute-start(f32[8,2304]{1,0:T(8,128)S(1)} %add_add_fusion.2.own_ref), channel_id=1, source_target_pairs={{0,3},{1,0},{2,1},{3,2},{4,7},{5,4},{6,5},{7,6},{8,11},{9,8},{10,9... | collective-permute-start | bytes 221192 | tf_op jit(solution)/shard_map/ppermute | solution.py:181
  70.5 5.6 %collective-permute-start.19 = (f32[8,2304]{1,0:T(8,128)S(1)}, f32[8,2304]{1,0:T(8,128)S(1)}, u32[]{:S(2)}, u32[]{:S(2)}) collective-permute-start(f32[8,2304]{1,0:T(8,128)S(1)} %add_add_fusion.2.own_ref), channel_id=1, source_target_pairs={{0,1},{1,2},{2,3},{3,0},{4,5},{5,6},{6,7},{7,4},{8,9},{9,10},{10,1... | collective-permute-start | bytes 221192 | tf_op jit(solution)/shard_map/ppermute | solution.py:181
  78.9 8.1 %collective-permute-start.25 = (f32[8,4352]{1,0:T(8,128)S(1)}, f32[8,4352]{1,0:T(8,128)S(1)}, u32[]{:S(2)}, u32[]{:S(2)}) collective-permute-start(f32[8,4352]{1,0:T(8,128)S(1)} %add.80.own_ref), channel_id=1, source_target_pairs={{0,64},{32,96},{64,0},{96,32},{1,65},{33,97},{65,1},{97,33},{2,66}... | collective-permute-start | bytes 417800 | tf_op jit(solution)/shard_map/ppermute | solution.py:181
  81.2 7.7 %collective-permute-start.24 = (f32[8,4352]{1,0:T(8,128)S(1)}, f32[8,4352]{1,0:T(8,128)S(1)}, u32[]{:S(2)}, u32[]{:S(2)}) collective-permute-start(f32[8,4352]{1,0:T(8,128)S(1)} %add.80.own_ref), channel_id=1, source_target_pairs={{0,96},{32,0},{64,32},{96,64},{1,97},{33,1},{65,33},{97,65},{2,98}... | collective-permute-start | bytes 417800 | tf_op jit(solution)/shard_map/ppermute | solution.py:181
  82.3 7.0 %collective-permute-start.23 = (f32[8,4352]{1,0:T(8,128)S(1)}, f32[8,4352]{1,0:T(8,128)S(1)}, u32[]{:S(2)}, u32[]{:S(2)}) collective-permute-start(f32[8,4352]{1,0:T(8,128)S(1)} %add.80.own_ref), channel_id=1, source_target_pairs={{0,32},{32,64},{64,96},{96,0},{1,33},{33,65},{65,97},{97,1},{2,34}... | collective-permute-start | bytes 417800 | tf_op jit(solution)/shard_map/ppermute | solution.py:181
  95.2 6.8 %collective-permute-start.28 = (f32[8,2304]{1,0:T(8,128)S(1)}, f32[8,2304]{1,0:T(8,128)S(1)}, u32[]{:S(2)}, u32[]{:S(2)}) collective-permute-start(f32[8,2304]{1,0:T(8,128)S(1)} %shard_map.67), channel_id=1, source_target_pairs={{0,4},{4,8},{8,12},{12,0},{1,5},{5,9},{9,13},{13,1},{2,6},{6,10},{... | collective-permute-start | bytes 221192 | tf_op jit(solution)/shard_map/ppermute | solution.py:181
  95.2 6.8 %collective-permute-start.27 = (f32[8,2304]{1,0:T(8,128)S(1)}, f32[8,2304]{1,0:T(8,128)S(1)}, u32[]{:S(2)}, u32[]{:S(2)}) collective-permute-start(f32[8,2304]{1,0:T(8,128)S(1)} %shard_map.67), channel_id=1, source_target_pairs={{0,8},{4,12},{8,0},{12,4},{1,9},{5,13},{9,1},{13,5},{2,10},{6,14},... | collective-permute-start | bytes 221192 | tf_op jit(solution)/shard_map/ppermute | solution.py:181
  102.0 6.5 %collective-permute-start.32 = (f32[8,2304]{1,0:T(8,128)S(1)}, f32[8,2304]{1,0:T(8,128)S(1)}, u32[]{:S(2)}, u32[]{:S(2)}) collective-permute-start(f32[8,2304]{1,0:T(8,128)S(1)} %add_add_fusion.1.own_ref), channel_id=1, source_target_pairs={{0,2},{1,3},{2,0},{3,1},{4,6},{5,7},{6,4},{7,5},{8,10},{9,11},{10,... | collective-permute-start | bytes 221192 | tf_op jit(solution)/shard_map/ppermute | solution.py:181
  102.1 6.4 %collective-permute-start.31 = (f32[8,2304]{1,0:T(8,128)S(1)}, f32[8,2304]{1,0:T(8,128)S(1)}, u32[]{:S(2)}, u32[]{:S(2)}) collective-permute-start(f32[8,2304]{1,0:T(8,128)S(1)} %add_add_fusion.1.own_ref), channel_id=1, source_target_pairs={{0,3},{1,0},{2,1},{3,2},{4,7},{5,4},{6,5},{7,6},{8,11},{9,8},{10,9... | collective-permute-start | bytes 221192 | tf_op jit(solution)/shard_map/ppermute | solution.py:181
  103.6 5.6 %collective-permute-start.30 = (f32[8,2304]{1,0:T(8,128)S(1)}, f32[8,2304]{1,0:T(8,128)S(1)}, u32[]{:S(2)}, u32[]{:S(2)}) collective-permute-start(f32[8,2304]{1,0:T(8,128)S(1)} %add_add_fusion.1.own_ref), channel_id=1, source_target_pairs={{0,1},{1,2},{2,3},{3,0},{4,5},{5,6},{6,7},{7,4},{8,9},{9,10},{10,1... | collective-permute-start | bytes 221192 | tf_op jit(solution)/shard_map/ppermute | solution.py:181
  112.1 8.1 %collective-permute-start.36 = (f32[8,4352]{1,0:T(8,128)S(1)}, f32[8,4352]{1,0:T(8,128)S(1)}, u32[]{:S(2)}, u32[]{:S(2)}) collective-permute-start(f32[8,4352]{1,0:T(8,128)S(1)} %add.84.own_ref), channel_id=1, source_target_pairs={{0,64},{32,96},{64,0},{96,32},{1,65},{33,97},{65,1},{97,33},{2,66}... | collective-permute-start | bytes 417800 | tf_op jit(solution)/shard_map/ppermute | solution.py:181
  114.2 7.7 %collective-permute-start.35 = (f32[8,4352]{1,0:T(8,128)S(1)}, f32[8,4352]{1,0:T(8,128)S(1)}, u32[]{:S(2)}, u32[]{:S(2)}) collective-permute-start(f32[8,4352]{1,0:T(8,128)S(1)} %add.84.own_ref), channel_id=1, source_target_pairs={{0,96},{32,0},{64,32},{96,64},{1,97},{33,1},{65,33},{97,65},{2,98}... | collective-permute-start | bytes 417800 | tf_op jit(solution)/shard_map/ppermute | solution.py:181
  115.4 7.1 %collective-permute-start.34 = (f32[8,4352]{1,0:T(8,128)S(1)}, f32[8,4352]{1,0:T(8,128)S(1)}, u32[]{:S(2)}, u32[]{:S(2)}) collective-permute-start(f32[8,4352]{1,0:T(8,128)S(1)} %add.84.own_ref), channel_id=1, source_target_pairs={{0,32},{32,64},{64,96},{96,0},{1,33},{33,65},{65,97},{97,1},{2,34}... | collective-permute-start | bytes 417800 | tf_op jit(solution)/shard_map/ppermute | solution.py:181
  128.0 6.8 %collective-permute-start.39 = (f32[8,2304]{1,0:T(8,128)S(1)}, f32[8,2304]{1,0:T(8,128)S(1)}, u32[]{:S(2)}, u32[]{:S(2)}) collective-permute-start(f32[8,2304]{1,0:T(8,128)S(1)} %shard_map.70), channel_id=1, source_target_pairs={{0,4},{4,8},{8,12},{12,0},{1,5},{5,9},{9,13},{13,1},{2,6},{6,10},{... | collective-permute-start | bytes 221192 | tf_op jit(solution)/shard_map/ppermute | solution.py:181
  128.0 6.8 %collective-permute-start.38 = (f32[8,2304]{1,0:T(8,128)S(1)}, f32[8,2304]{1,0:T(8,128)S(1)}, u32[]{:S(2)}, u32[]{:S(2)}) collective-permute-start(f32[8,2304]{1,0:T(8,128)S(1)} %shard_map.70), channel_id=1, source_target_pairs={{0,8},{4,12},{8,0},{12,4},{1,9},{5,13},{9,1},{13,5},{2,10},{6,14},... | collective-permute-start | bytes 221192 | tf_op jit(solution)/shard_map/ppermute | solution.py:181
  134.9 6.5 %collective-permute-start.43 = (f32[8,2304]{1,0:T(8,128)S(1)}, f32[8,2304]{1,0:T(8,128)S(1)}, u32[]{:S(2)}, u32[]{:S(2)}) collective-permute-start(f32[8,2304]{1,0:T(8,128)S(1)} %add_add_fusion.own_ref), channel_id=1, source_target_pairs={{0,2},{1,3},{2,0},{3,1},{4,6},{5,7},{6,4},{7,5},{8,10},{9,11},{10,... | collective-permute-start | bytes 221192 | tf_op jit(solution)/shard_map/ppermute | solution.py:181
  135.8 5.7 %collective-permute-start.42 = (f32[8,2304]{1,0:T(8,128)S(1)}, f32[8,2304]{1,0:T(8,128)S(1)}, u32[]{:S(2)}, u32[]{:S(2)}) collective-permute-start(f32[8,2304]{1,0:T(8,128)S(1)} %add_add_fusion.own_ref), channel_id=1, source_target_pairs={{0,3},{1,0},{2,1},{3,2},{4,7},{5,4},{6,5},{7,6},{8,11},{9,8},{10,9... | collective-permute-start | bytes 221192 | tf_op jit(solution)/shard_map/ppermute | solution.py:181
  137.0 5.6 %collective-permute-start.41 = (f32[8,2304]{1,0:T(8,128)S(1)}, f32[8,2304]{1,0:T(8,128)S(1)}, u32[]{:S(2)}, u32[]{:S(2)}) collective-permute-start(f32[8,2304]{1,0:T(8,128)S(1)} %add_add_fusion.own_ref), channel_id=1, source_target_pairs={{0,1},{1,2},{2,3},{3,0},{4,5},{5,6},{6,7},{7,4},{8,9},{9,10},{10,1... | collective-permute-start | bytes 221192 | tf_op jit(solution)/shard_map/ppermute | solution.py:181
  144.0 5.1 %collective-permute-start.47 = (f32[8,128]{1,0:T(8,128)S(1)}, f32[8,128]{1,0:T(8,128)S(1)}, u32[]{:S(2)}, u32[]{:S(2)}) collective-permute-start(f32[8,128]{1,0:T(8,128)S(1)} %add.88.own_ref), channel_id=1, source_target_pairs={{0,64},{32,96},{64,0},{96,32},{1,65},{33,97},{65,1},{97,33},{2,66}... | collective-permute-start | bytes 12296 | tf_op jit(solution)/shard_map/ppermute | solution.py:181
  (20 other events, 77.5 us)

commit v2 on v1

--- a/solution.py
+++ b/solution.py
@@ -15,6 +15,7 @@
 
 VMEM = pl.BlockSpec(memory_space=pltpu.VMEM)
 SMEM = pl.BlockSpec(memory_space=pltpu.SMEM)
+HBM = pl.BlockSpec(memory_space=pltpu.HBM)
 
 
 def lane_sum(x):
@@ -33,12 +34,14 @@
     return jnp.broadcast_to(x, (x.shape[0], 128))
 
 
-def scatter_products(u, place_ref, tiles_ref, keep_ref, send_ref, acc_ref):
+def scatter_products(u, place_ref, tiles_ref, keep_ref, send_ref, acc_ref, copies=None):
     bundles, slots, rays, cells = tiles_ref.shape
     half = keep_ref.shape[1]
     acc_ref[...] = jnp.zeros_like(acc_ref)
     low = u.astype(BF16)
     for b in range(bundles):
+        if copies:
+            copies[b].wait()
         rows = low[:, b * rays : (b + 1) * rays]
         for s in range(slots):
             part = jnp.dot(rows, tiles_ref[b, s], preferred_element_type=F32)
@@ -50,8 +53,16 @@
         out_ref[:, half - cells :] = squares
 
 
-def first_adjoint(place_ref, right_ref, tiles_ref, keep_ref, send_ref, acc_ref):
-    scatter_products(right_ref[...], place_ref, tiles_ref, keep_ref, send_ref, acc_ref)
+def first_adjoint(
+    place_ref, right_ref, source_ref, keep_ref, send_ref, tiles_ref, acc_ref, sem
+):
+    copies = [
+        pltpu.make_async_copy(source_ref.at[b], tiles_ref.at[b], sem.at[b])
+        for b in range(source_ref.shape[0])
+    ]
+    for copy in copies:
+        copy.start()
+    scatter_products(right_ref[...], place_ref, tiles_ref, keep_ref, send_ref, acc_ref, copies)
 
 
 def ray_vector(own_ref, left_ref, right_ref, far_ref, prev_ref, beta_ref):
@@ -155,7 +166,7 @@
         in_specs=specs,
         out_specs=[VMEM] * len(outs),
         scratch_shapes=list(scratch),
-        compiler_params=pltpu.CompilerParams(vmem_limit_bytes=40 << 20),
+        compiler_params=pltpu.CompilerParams(vmem_limit_bytes=12 << 20),
     )(*args)
 
 
@@ -178,7 +189,7 @@
     def spread(value, axis):
         n = lax.axis_size(axis)
         moved = [
-            lax.ppermute(value, axis, [(i, (i + by) % n) for i in range(n)]) for by in (1, 3, 2)
+            lax.ppermute(value, axis, [(i, i ^ by) for i in range(n)]) for by in (1, 3, 2)
         ]
         return [value] + moved
 
@@ -191,8 +202,10 @@
 
     halves = [shape(half + cells)] * 2
     store = [pltpu.VMEM((nrhs, 2 * (half + cells)), F32)]
-    keep, send = call(
-        first_adjoint, halves, [SMEM, VMEM, VMEM], (place, right_side, tiles), store
+    keep, send, tiles = call(
+        first_adjoint, halves + [jax.ShapeDtypeStruct(tiles.shape, tiles.dtype)],
+        [SMEM, VMEM, HBM], (place, right_side, tiles),
+        store + [pltpu.SemaphoreType.DMA((bundles,))],
     )
     u = right_side
     owns, others, alphas, betas = [], [], [], []

time: 154 us -> 150 us (0.974)
  waiting for transfers between devices: 80.4 us -> 73.1 us
    ppermute x39, waiting for transfers between devices: 68.6 us -> 61.3 us  [spread(): lax.ppermute(value, axis, [(i, i ^ by) for i in range(n)])]
    ppermute x39, starting transfers between devices: 52.3 us -> 53.9 us  [spread(): lax.ppermute(value, axis, [(i, i ^ by) for i in range(n)])]
  transfers between devices with their start and end apart: 48 -> 48, of which waited for: 39 -> 41; matrix products, arithmetic and copies ran while one was open for 0% -> 0% of each run, Pallas kernels for 0% -> 0%
where the time goes in v2:
time: 150 us
  waiting for transfers between devices  73.1 us (49%)
  starting transfers between devices  54.7 us (36%)
  Pallas kernels  15.9 us (11%)
  local copies, waits for them, and re-layouts  3.99 us (3%)
    ppermute x39, waiting for transfers between devices, spread(): lax.ppermute(value, axis, [(i, i ^ by) for i in range(n)])  61.3 us
    ppermute x39, starting transfers between devices, spread(): lax.ppermute(value, axis, [(i, i ^ by) for i in range(n)])  53.9 us
    pallas_call x14, Pallas kernels, call(): pl.pallas_call(body, out_shape=outs, in_specs=specs, out_specs=[VMEM] * l...  15.9 us
    ppermute x9, waiting for transfers between devices, swap(): return lax.ppermute(value, 'core', [(0, 1), (1, 0)])  11.9 us
    unnamed x6, local copies, waits for them, and re-layouts  3.04 us
  transfers between devices with their start and end apart: 48, of which 41 were waited for; matrix products, arithmetic and copies ran while one was open for 0% of the time, Pallas kernels for 0%

profile of v2, /device:TPU:0, one launch (start us, length us, event | category | flops | bytes accessed | tf_op | source)
XLA Modules:
  0.0 149.5 jit_solution(1875173483053109366)
XLA Ops:
  1.8 2.2 %copy-done = bf16[8,4,256,256]{3,2,1,0:T(8,128)(2,1)S(1)} copy-done((bf16[8,4,256,256]{3,2,1,0:T(8,128)(2,1)S(1)}, bf16[8,4,256,256]{3,2,1,0:T(8,128)(2,1)}, u32[]{:S(2)}) %copy-start) | copy-done | bytes 4194328
  4.8 2.5 %shard_map.59 = (f32[8,4352]{1,0:T(8,128)S(1)}, f32[8,4352]{1,0:T(8,128)S(1)}, bf16[8,4,256,256]{3,2,1,0:T(8,128)(2,1)S(1)}) custom-call(s32[65]{0:T(128)S(1)} %pad_add_fusion.place_ref, f32[8,2048]{1,0:T(8,128)S(1)} %copy-done.1, bf16[8,4,256,256]{3,2,1,0:T(8,128)(2,1)S(1)} %copy-done), custom_call_target="tpu_custom_call" | custom-call | tf_op jit(solution)/shard_map/pallas_call | solution.py:163
  8.7 4.0 %collective-permute-start.3 = (f32[8,4352]{1,0:T(8,128)S(1)}, f32[8,4352]{1,0:T(8,128)S(1)}, u32[]{:S(2)}, u32[]{:S(2)}) collective-permute-start(f32[8,4352]{1,0:T(8,128)S(1)} %add.72.own_ref), channel_id=1, source_target_pairs={{0,64},{32,96},{64,0},{96,32},{1,65},{33,97},{65,1},{97,33},{2,66}... | collective-permute-start | bytes 417800 | tf_op jit(solution)/shard_map/ppermute | solution.py:192
  13.8 3.1 %collective-permute-done.3.far_ref = f32[8,4352]{1,0:T(8,128)S(1)} collective-permute-done((f32[8,4352]{1,0:T(8,128)S(1)}, f32[8,4352]{1,0:T(8,128)S(1)}, u32[]{:S(2)}, u32[]{:S(2)}) %collective-permute-start.3) | collective-permute-done | bytes 139296 | tf_op jit(solution)/shard_map/ppermute | solution.py:192
  16.8 2.9 %collective-permute-done.2.right_ref = f32[8,4352]{1,0:T(8,128)S(1)} collective-permute-done((f32[8,4352]{1,0:T(8,128)S(1)}, f32[8,4352]{1,0:T(8,128)S(1)}, u32[]{:S(2)}, u32[]{:S(2)}) %collective-permute-start.2) | collective-permute-done | bytes 139296 | tf_op jit(solution)/shard_map/ppermute | solution.py:192
  22.1 1.7 %shard_map.61 = f32[8,2304]{1,0:T(8,128)S(1)} custom-call(s32[65]{0:T(128)S(1)} %pad_add_fusion.place_ref, f32[8,4096]{1,0:T(8,128)S(1)} %get-tuple-element.31.own_ref.prev_ref.rest_0_, f32[8,4096]{1,0:T(8,128)S(1)} %collective-permute-done.4.other_ref.rest_4_, bf16[8,4,256,256]{3,2,1,0:T(8,128)(2,1)S(1)} %get-tuple-element.32.tiles_ref), custom_call_target="tpu_custom_call" | custom-call | tf_op jit(solution)/shard_map/pallas_call | solution.py:163
  23.8 2.8 %collective-permute-start.7 = (f32[8,2304]{1,0:T(8,128)S(1)}, f32[8,2304]{1,0:T(8,128)S(1)}, u32[]{:S(2)}, u32[]{:S(2)}) collective-permute-start(f32[8,2304]{1,0:T(8,128)S(1)} %shard_map.61), channel_id=1, source_target_pairs={{0,12},{4,8},{8,4},{12,0},{1,13},{5,9},{9,5},{13,1},{2,14},{6,10},... | collective-permute-start | bytes 221192 | tf_op jit(solution)/shard_map/ppermute | solution.py:192
  26.8 1.7 %collective-permute-start.5 = (f32[8,2304]{1,0:T(8,128)S(1)}, f32[8,2304]{1,0:T(8,128)S(1)}, u32[]{:S(2)}, u32[]{:S(2)}) collective-permute-start(f32[8,2304]{1,0:T(8,128)S(1)} %shard_map.61), channel_id=1, source_target_pairs={{0,8},{4,12},{8,0},{12,4},{1,9},{5,13},{9,1},{13,5},{2,10},{6,14},... | collective-permute-start | bytes 221192 | tf_op jit(solution)/shard_map/ppermute | solution.py:192
  29.4 2.0 %collective-permute-done.6 = f32[8,2304]{1,0:T(8,128)S(1)} collective-permute-done((f32[8,2304]{1,0:T(8,128)S(1)}, f32[8,2304]{1,0:T(8,128)S(1)}, u32[]{:S(2)}, u32[]{:S(2)}) %collective-permute-start.6) | collective-permute-done | bytes 73760 | tf_op jit(solution)/shard_map/ppermute | solution.py:192
  32.7 3.3 %collective-permute-start.10 = (f32[8,2304]{1,0:T(8,128)S(1)}, f32[8,2304]{1,0:T(8,128)S(1)}, u32[]{:S(2)}, u32[]{:S(2)}) collective-permute-start(f32[8,2304]{1,0:T(8,128)S(1)} %add_add_fusion.3.own_ref), channel_id=1, source_target_pairs={{0,2},{1,3},{2,0},{3,1},{4,6},{5,7},{6,4},{7,5},{8,10},{9,11},{10,... | collective-permute-start | bytes 221192 | tf_op jit(solution)/shard_map/ppermute | solution.py:192
  38.6 2.9 %collective-permute-done.9.right_ref = f32[8,2304]{1,0:T(8,128)S(1)} collective-permute-done((f32[8,2304]{1,0:T(8,128)S(1)}, f32[8,2304]{1,0:T(8,128)S(1)}, u32[]{:S(2)}, u32[]{:S(2)}) %collective-permute-start.9) | collective-permute-done | bytes 73760 | tf_op jit(solution)/shard_map/ppermute | solution.py:192
  44.3 2.1 %collective-permute-start.14 = (f32[8,4352]{1,0:T(8,128)S(1)}, f32[8,4352]{1,0:T(8,128)S(1)}, u32[]{:S(2)}, u32[]{:S(2)}) collective-permute-start(f32[8,4352]{1,0:T(8,128)S(1)} %add.76.own_ref), channel_id=1, source_target_pairs={{0,64},{32,96},{64,0},{96,32},{1,65},{33,97},{65,1},{97,33},{2,66}... | collective-permute-start | bytes 417800 | tf_op jit(solution)/shard_map/ppermute | solution.py:192
  48.1 3.8 %collective-permute-done.14.far_ref = f32[8,4352]{1,0:T(8,128)S(1)} collective-permute-done((f32[8,4352]{1,0:T(8,128)S(1)}, f32[8,4352]{1,0:T(8,128)S(1)}, u32[]{:S(2)}, u32[]{:S(2)}) %collective-permute-start.14) | collective-permute-done | bytes 139296 | tf_op jit(solution)/shard_map/ppermute | solution.py:192
  51.9 2.7 %collective-permute-done.13.right_ref = f32[8,4352]{1,0:T(8,128)S(1)} collective-permute-done((f32[8,4352]{1,0:T(8,128)S(1)}, f32[8,4352]{1,0:T(8,128)S(1)}, u32[]{:S(2)}, u32[]{:S(2)}) %collective-permute-start.13) | collective-permute-done | bytes 139296 | tf_op jit(solution)/shard_map/ppermute | solution.py:192
  58.0 2.2 %collective-permute-start.18 = (f32[8,2304]{1,0:T(8,128)S(1)}, f32[8,2304]{1,0:T(8,128)S(1)}, u32[]{:S(2)}, u32[]{:S(2)}) collective-permute-start(f32[8,2304]{1,0:T(8,128)S(1)} %shard_map.64), channel_id=1, source_target_pairs={{0,12},{4,8},{8,4},{12,0},{1,13},{5,9},{9,5},{13,1},{2,14},{6,10},... | collective-permute-start | bytes 221192 | tf_op jit(solution)/shard_map/ppermute | solution.py:192
  60.2 2.5 %collective-permute-start.16 = (f32[8,2304]{1,0:T(8,128)S(1)}, f32[8,2304]{1,0:T(8,128)S(1)}, u32[]{:S(2)}, u32[]{:S(2)}) collective-permute-start(f32[8,2304]{1,0:T(8,128)S(1)} %shard_map.64), channel_id=1, source_target_pairs={{0,8},{4,12},{8,0},{12,4},{1,9},{5,13},{9,1},{13,5},{2,10},{6,14},... | collective-permute-start | bytes 221192 | tf_op jit(solution)/shard_map/ppermute | solution.py:192
  70.2 3.0 %collective-permute-done.21.far_ref = f32[8,2304]{1,0:T(8,128)S(1)} collective-permute-done((f32[8,2304]{1,0:T(8,128)S(1)}, f32[8,2304]{1,0:T(8,128)S(1)}, u32[]{:S(2)}, u32[]{:S(2)}) %collective-permute-start.21) | collective-permute-done | bytes 73760 | tf_op jit(solution)/shard_map/ppermute | solution.py:192
  76.7 2.1 %collective-permute-start.25 = (f32[8,4352]{1,0:T(8,128)S(1)}, f32[8,4352]{1,0:T(8,128)S(1)}, u32[]{:S(2)}, u32[]{:S(2)}) collective-permute-start(f32[8,4352]{1,0:T(8,128)S(1)} %add.80.own_ref), channel_id=1, source_target_pairs={{0,64},{32,96},{64,0},{96,32},{1,65},{33,97},{65,1},{97,33},{2,66}... | collective-permute-start | bytes 417800 | tf_op jit(solution)/shard_map/ppermute | solution.py:192
  80.5 3.9 %collective-permute-done.25.far_ref = f32[8,4352]{1,0:T(8,128)S(1)} collective-permute-done((f32[8,4352]{1,0:T(8,128)S(1)}, f32[8,4352]{1,0:T(8,128)S(1)}, u32[]{:S(2)}, u32[]{:S(2)}) %collective-permute-start.25) | collective-permute-done | bytes 139296 | tf_op jit(solution)/shard_map/ppermute | solution.py:192
  84.3 2.7 %collective-permute-done.24.right_ref = f32[8,4352]{1,0:T(8,128)S(1)} collective-permute-done((f32[8,4352]{1,0:T(8,128)S(1)}, f32[8,4352]{1,0:T(8,128)S(1)}, u32[]{:S(2)}, u32[]{:S(2)}) %collective-permute-start.24) | collective-permute-done | bytes 139296 | tf_op jit(solution)/shard_map/ppermute | solution.py:192
  90.4 2.0 %collective-permute-start.29 = (f32[8,2304]{1,0:T(8,128)S(1)}, f32[8,2304]{1,0:T(8,128)S(1)}, u32[]{:S(2)}, u32[]{:S(2)}) collective-permute-start(f32[8,2304]{1,0:T(8,128)S(1)} %shard_map.67), channel_id=1, source_target_pairs={{0,12},{4,8},{8,4},{12,0},{1,13},{5,9},{9,5},{13,1},{2,14},{6,10},... | collective-permute-start | bytes 221192 | tf_op jit(solution)/shard_map/ppermute | solution.py:192
  92.4 2.7 %collective-permute-start.27 = (f32[8,2304]{1,0:T(8,128)S(1)}, f32[8,2304]{1,0:T(8,128)S(1)}, u32[]{:S(2)}, u32[]{:S(2)}) collective-permute-start(f32[8,2304]{1,0:T(8,128)S(1)} %shard_map.67), channel_id=1, source_target_pairs={{0,8},{4,12},{8,0},{12,4},{1,9},{5,13},{9,1},{13,5},{2,10},{6,14},... | collective-permute-start | bytes 221192 | tf_op jit(solution)/shard_map/ppermute | solution.py:192
  98.7 2.1 %collective-permute-start.32 = (f32[8,2304]{1,0:T(8,128)S(1)}, f32[8,2304]{1,0:T(8,128)S(1)}, u32[]{:S(2)}, u32[]{:S(2)}) collective-permute-start(f32[8,2304]{1,0:T(8,128)S(1)} %add_add_fusion.1.own_ref), channel_id=1, source_target_pairs={{0,2},{1,3},{2,0},{3,1},{4,6},{5,7},{6,4},{7,5},{8,10},{9,11},{10,... | collective-permute-start | bytes 221192 | tf_op jit(solution)/shard_map/ppermute | solution.py:192
  102.3 2.8 %collective-permute-done.32.far_ref = f32[8,2304]{1,0:T(8,128)S(1)} collective-permute-done((f32[8,2304]{1,0:T(8,128)S(1)}, f32[8,2304]{1,0:T(8,128)S(1)}, u32[]{:S(2)}, u32[]{:S(2)}) %collective-permute-start.32) | collective-permute-done | bytes 73760 | tf_op jit(solution)/shard_map/ppermute | solution.py:192
  109.3 2.1 %collective-permute-start.36 = (f32[8,4352]{1,0:T(8,128)S(1)}, f32[8,4352]{1,0:T(8,128)S(1)}, u32[]{:S(2)}, u32[]{:S(2)}) collective-permute-start(f32[8,4352]{1,0:T(8,128)S(1)} %add.84.own_ref), channel_id=1, source_target_pairs={{0,64},{32,96},{64,0},{96,32},{1,65},{33,97},{65,1},{97,33},{2,66}... | collective-permute-start | bytes 417800 | tf_op jit(solution)/shard_map/ppermute | solution.py:192
  113.0 3.9 %collective-permute-done.36.far_ref = f32[8,4352]{1,0:T(8,128)S(1)} collective-permute-done((f32[8,4352]{1,0:T(8,128)S(1)}, f32[8,4352]{1,0:T(8,128)S(1)}, u32[]{:S(2)}, u32[]{:S(2)}) %collective-permute-start.36) | collective-permute-done | bytes 139296 | tf_op jit(solution)/shard_map/ppermute | solution.py:192
  116.9 2.7 %collective-permute-done.35.right_ref = f32[8,4352]{1,0:T(8,128)S(1)} collective-permute-done((f32[8,4352]{1,0:T(8,128)S(1)}, f32[8,4352]{1,0:T(8,128)S(1)}, u32[]{:S(2)}, u32[]{:S(2)}) %collective-permute-start.35) | collective-permute-done | bytes 139296 | tf_op jit(solution)/shard_map/ppermute | solution.py:192
  121.2 1.7 %shard_map.70 = f32[8,2304]{1,0:T(8,128)S(1)} custom-call(s32[65]{0:T(128)S(1)} %pad_add_fusion.place_ref, f32[8,4096]{1,0:T(8,128)S(1)} %get-tuple-element.49.own_ref.rest_3_, f32[8,4096]{1,0:T(8,128)S(1)} %collective-permute-done.37.other_ref.rest_7_, bf16[8,4,256,256]{3,2,1,0:T(8,128)(2,1)S(1)} %get-tuple-element.32.tiles_ref), custom_call_target="tpu_custom_call" | custom-call | tf_op jit(solution)/shard_map/pallas_call | solution.py:163
  122.9 2.0 %collective-permute-start.40 = (f32[8,2304]{1,0:T(8,128)S(1)}, f32[8,2304]{1,0:T(8,128)S(1)}, u32[]{:S(2)}, u32[]{:S(2)}) collective-permute-start(f32[8,2304]{1,0:T(8,128)S(1)} %shard_map.70), channel_id=1, source_target_pairs={{0,12},{4,8},{8,4},{12,0},{1,13},{5,9},{9,5},{13,1},{2,14},{6,10},... | collective-permute-start | bytes 221192 | tf_op jit(solution)/shard_map/ppermute | solution.py:192
  125.2 2.5 %collective-permute-start.38 = (f32[8,2304]{1,0:T(8,128)S(1)}, f32[8,2304]{1,0:T(8,128)S(1)}, u32[]{:S(2)}, u32[]{:S(2)}) collective-permute-start(f32[8,2304]{1,0:T(8,128)S(1)} %shard_map.70), channel_id=1, source_target_pairs={{0,8},{4,12},{8,0},{12,4},{1,9},{5,13},{9,1},{13,5},{2,10},{6,14},... | collective-permute-start | bytes 221192 | tf_op jit(solution)/shard_map/ppermute | solution.py:192
  134.8 3.1 %collective-permute-done.43.far_ref = f32[8,2304]{1,0:T(8,128)S(1)} collective-permute-done((f32[8,2304]{1,0:T(8,128)S(1)}, f32[8,2304]{1,0:T(8,128)S(1)}, u32[]{:S(2)}, u32[]{:S(2)}) %collective-permute-start.43) | collective-permute-done | bytes 73760 | tf_op jit(solution)/shard_map/ppermute | solution.py:192
  140.0 2.0 %collective-permute-start.47 = (f32[8,128]{1,0:T(8,128)S(1)}, f32[8,128]{1,0:T(8,128)S(1)}, u32[]{:S(2)}, u32[]{:S(2)}) collective-permute-start(f32[8,128]{1,0:T(8,128)S(1)} %add.88.own_ref), channel_id=1, source_target_pairs={{0,64},{32,96},{64,0},{96,32},{1,65},{33,97},{65,1},{97,33},{2,66}... | collective-permute-start | bytes 12296 | tf_op jit(solution)/shard_map/ppermute | solution.py:192
  (100 shorter events, 65.1 us)
Async XLA Ops:
  8.7 8.1 %collective-permute-start.3 = (f32[8,4352]{1,0:T(8,128)S(1)}, f32[8,4352]{1,0:T(8,128)S(1)}, u32[]{:S(2)}, u32[]{:S(2)}) collective-permute-start(f32[8,4352]{1,0:T(8,128)S(1)} %add.72.own_ref), channel_id=1, source_target_pairs={{0,64},{32,96},{64,0},{96,32},{1,65},{33,97},{65,1},{97,33},{2,66}... | collective-permute-start | bytes 417800 | tf_op jit(solution)/shard_map/ppermute | solution.py:192
  12.8 7.0 %collective-permute-start.2 = (f32[8,4352]{1,0:T(8,128)S(1)}, f32[8,4352]{1,0:T(8,128)S(1)}, u32[]{:S(2)}, u32[]{:S(2)}) collective-permute-start(f32[8,4352]{1,0:T(8,128)S(1)} %add.72.own_ref), channel_id=1, source_target_pairs={{0,96},{32,64},{64,32},{96,0},{1,97},{33,65},{65,33},{97,1},{2,98}... | collective-permute-start | bytes 417800 | tf_op jit(solution)/shard_map/ppermute | solution.py:192
  13.5 7.0 %collective-permute-start.1 = (f32[8,4352]{1,0:T(8,128)S(1)}, f32[8,4352]{1,0:T(8,128)S(1)}, u32[]{:S(2)}, u32[]{:S(2)}) collective-permute-start(f32[8,4352]{1,0:T(8,128)S(1)} %add.72.own_ref), channel_id=1, source_target_pairs={{0,32},{32,0},{64,96},{96,64},{1,33},{33,1},{65,97},{97,65},{2,34}... | collective-permute-start | bytes 417800 | tf_op jit(solution)/shard_map/ppermute | solution.py:192
  23.8 5.6 %collective-permute-start.7 = (f32[8,2304]{1,0:T(8,128)S(1)}, f32[8,2304]{1,0:T(8,128)S(1)}, u32[]{:S(2)}, u32[]{:S(2)}) collective-permute-start(f32[8,2304]{1,0:T(8,128)S(1)} %shard_map.61), channel_id=1, source_target_pairs={{0,12},{4,8},{8,4},{12,0},{1,13},{5,9},{9,5},{13,1},{2,14},{6,10},... | collective-permute-start | bytes 221192 | tf_op jit(solution)/shard_map/ppermute | solution.py:192
  26.6 4.8 %collective-permute-start.6 = (f32[8,2304]{1,0:T(8,128)S(1)}, f32[8,2304]{1,0:T(8,128)S(1)}, u32[]{:S(2)}, u32[]{:S(2)}) collective-permute-start(f32[8,2304]{1,0:T(8,128)S(1)} %shard_map.61), channel_id=1, source_target_pairs={{0,4},{4,0},{8,12},{12,8},{1,5},{5,1},{9,13},{13,9},{2,6},{6,2},{1... | collective-permute-start | bytes 221192 | tf_op jit(solution)/shard_map/ppermute | solution.py:192
  26.8 5.9 %collective-permute-start.5 = (f32[8,2304]{1,0:T(8,128)S(1)}, f32[8,2304]{1,0:T(8,128)S(1)}, u32[]{:S(2)}, u32[]{:S(2)}) collective-permute-start(f32[8,2304]{1,0:T(8,128)S(1)} %shard_map.61), channel_id=1, source_target_pairs={{0,8},{4,12},{8,0},{12,4},{1,9},{5,13},{9,1},{13,5},{2,10},{6,14},... | collective-permute-start | bytes 221192 | tf_op jit(solution)/shard_map/ppermute | solution.py:192
  32.7 6.0 %collective-permute-start.10 = (f32[8,2304]{1,0:T(8,128)S(1)}, f32[8,2304]{1,0:T(8,128)S(1)}, u32[]{:S(2)}, u32[]{:S(2)}) collective-permute-start(f32[8,2304]{1,0:T(8,128)S(1)} %add_add_fusion.3.own_ref), channel_id=1, source_target_pairs={{0,2},{1,3},{2,0},{3,1},{4,6},{5,7},{6,4},{7,5},{8,10},{9,11},{10,... | collective-permute-start | bytes 221192 | tf_op jit(solution)/shard_map/ppermute | solution.py:192
  35.9 5.6 %collective-permute-start.9 = (f32[8,2304]{1,0:T(8,128)S(1)}, f32[8,2304]{1,0:T(8,128)S(1)}, u32[]{:S(2)}, u32[]{:S(2)}) collective-permute-start(f32[8,2304]{1,0:T(8,128)S(1)} %add_add_fusion.3.own_ref), channel_id=1, source_target_pairs={{0,3},{1,2},{2,1},{3,0},{4,7},{5,6},{6,5},{7,4},{8,11},{9,10},{10,... | collective-permute-start | bytes 221192 | tf_op jit(solution)/shard_map/ppermute | solution.py:192
  44.3 7.6 %collective-permute-start.14 = (f32[8,4352]{1,0:T(8,128)S(1)}, f32[8,4352]{1,0:T(8,128)S(1)}, u32[]{:S(2)}, u32[]{:S(2)}) collective-permute-start(f32[8,4352]{1,0:T(8,128)S(1)} %add.76.own_ref), channel_id=1, source_target_pairs={{0,64},{32,96},{64,0},{96,32},{1,65},{33,97},{65,1},{97,33},{2,66}... | collective-permute-start | bytes 417800 | tf_op jit(solution)/shard_map/ppermute | solution.py:192
  46.5 8.2 %collective-permute-start.13 = (f32[8,4352]{1,0:T(8,128)S(1)}, f32[8,4352]{1,0:T(8,128)S(1)}, u32[]{:S(2)}, u32[]{:S(2)}) collective-permute-start(f32[8,4352]{1,0:T(8,128)S(1)} %add.76.own_ref), channel_id=1, source_target_pairs={{0,96},{32,64},{64,32},{96,0},{1,97},{33,65},{65,33},{97,1},{2,98}... | collective-permute-start | bytes 417800 | tf_op jit(solution)/shard_map/ppermute | solution.py:192
  48.1 6.5 %collective-permute-start.12 = (f32[8,4352]{1,0:T(8,128)S(1)}, f32[8,4352]{1,0:T(8,128)S(1)}, u32[]{:S(2)}, u32[]{:S(2)}) collective-permute-start(f32[8,4352]{1,0:T(8,128)S(1)} %add.76.own_ref), channel_id=1, source_target_pairs={{0,32},{32,0},{64,96},{96,64},{1,33},{33,1},{65,97},{97,65},{2,34}... | collective-permute-start | bytes 417800 | tf_op jit(solution)/shard_map/ppermute | solution.py:192
  58.0 5.6 %collective-permute-start.18 = (f32[8,2304]{1,0:T(8,128)S(1)}, f32[8,2304]{1,0:T(8,128)S(1)}, u32[]{:S(2)}, u32[]{:S(2)}) collective-permute-start(f32[8,2304]{1,0:T(8,128)S(1)} %shard_map.64), channel_id=1, source_target_pairs={{0,12},{4,8},{8,4},{12,0},{1,13},{5,9},{9,5},{13,1},{2,14},{6,10},... | collective-permute-start | bytes 221192 | tf_op jit(solution)/shard_map/ppermute | solution.py:192
  60.2 4.8 %collective-permute-start.17 = (f32[8,2304]{1,0:T(8,128)S(1)}, f32[8,2304]{1,0:T(8,128)S(1)}, u32[]{:S(2)}, u32[]{:S(2)}) collective-permute-start(f32[8,2304]{1,0:T(8,128)S(1)} %shard_map.64), channel_id=1, source_target_pairs={{0,4},{4,0},{8,12},{12,8},{1,5},{5,1},{9,13},{13,9},{2,6},{6,2},{1... | collective-permute-start | bytes 221192 | tf_op jit(solution)/shard_map/ppermute | solution.py:192
  60.2 6.3 %collective-permute-start.16 = (f32[8,2304]{1,0:T(8,128)S(1)}, f32[8,2304]{1,0:T(8,128)S(1)}, u32[]{:S(2)}, u32[]{:S(2)}) collective-permute-start(f32[8,2304]{1,0:T(8,128)S(1)} %shard_map.64), channel_id=1, source_target_pairs={{0,8},{4,12},{8,0},{12,4},{1,9},{5,13},{9,1},{13,5},{2,10},{6,14},... | collective-permute-start | bytes 221192 | tf_op jit(solution)/shard_map/ppermute | solution.py:192
  66.6 6.6 %collective-permute-start.21 = (f32[8,2304]{1,0:T(8,128)S(1)}, f32[8,2304]{1,0:T(8,128)S(1)}, u32[]{:S(2)}, u32[]{:S(2)}) collective-permute-start(f32[8,2304]{1,0:T(8,128)S(1)} %add_add_fusion.2.own_ref), channel_id=1, source_target_pairs={{0,2},{1,3},{2,0},{3,1},{4,6},{5,7},{6,4},{7,5},{8,10},{9,11},{10,... | collective-permute-start | bytes 221192 | tf_op jit(solution)/shard_map/ppermute | solution.py:192
  68.2 5.7 %collective-permute-start.20 = (f32[8,2304]{1,0:T(8,128)S(1)}, f32[8,2304]{1,0:T(8,128)S(1)}, u32[]{:S(2)}, u32[]{:S(2)}) collective-permute-start(f32[8,2304]{1,0:T(8,128)S(1)} %add_add_fusion.2.own_ref), channel_id=1, source_target_pairs={{0,3},{1,2},{2,1},{3,0},{4,7},{5,6},{6,5},{7,4},{8,11},{9,10},{10,... | collective-permute-start | bytes 221192 | tf_op jit(solution)/shard_map/ppermute | solution.py:192
  76.7 7.6 %collective-permute-start.25 = (f32[8,4352]{1,0:T(8,128)S(1)}, f32[8,4352]{1,0:T(8,128)S(1)}, u32[]{:S(2)}, u32[]{:S(2)}) collective-permute-start(f32[8,4352]{1,0:T(8,128)S(1)} %add.80.own_ref), channel_id=1, source_target_pairs={{0,64},{32,96},{64,0},{96,32},{1,65},{33,97},{65,1},{97,33},{2,66}... | collective-permute-start | bytes 417800 | tf_op jit(solution)/shard_map/ppermute | solution.py:192
  78.8 8.2 %collective-permute-start.24 = (f32[8,4352]{1,0:T(8,128)S(1)}, f32[8,4352]{1,0:T(8,128)S(1)}, u32[]{:S(2)}, u32[]{:S(2)}) collective-permute-start(f32[8,4352]{1,0:T(8,128)S(1)} %add.80.own_ref), channel_id=1, source_target_pairs={{0,96},{32,64},{64,32},{96,0},{1,97},{33,65},{65,33},{97,1},{2,98}... | collective-permute-start | bytes 417800 | tf_op jit(solution)/shard_map/ppermute | solution.py:192
  80.5 6.6 %collective-permute-start.23 = (f32[8,4352]{1,0:T(8,128)S(1)}, f32[8,4352]{1,0:T(8,128)S(1)}, u32[]{:S(2)}, u32[]{:S(2)}) collective-permute-start(f32[8,4352]{1,0:T(8,128)S(1)} %add.80.own_ref), channel_id=1, source_target_pairs={{0,32},{32,0},{64,96},{96,64},{1,33},{33,1},{65,97},{97,65},{2,34}... | collective-permute-start | bytes 417800 | tf_op jit(solution)/shard_map/ppermute | solution.py:192
  90.4 5.6 %collective-permute-start.29 = (f32[8,2304]{1,0:T(8,128)S(1)}, f32[8,2304]{1,0:T(8,128)S(1)}, u32[]{:S(2)}, u32[]{:S(2)}) collective-permute-start(f32[8,2304]{1,0:T(8,128)S(1)} %shard_map.67), channel_id=1, source_target_pairs={{0,12},{4,8},{8,4},{12,0},{1,13},{5,9},{9,5},{13,1},{2,14},{6,10},... | collective-permute-start | bytes 221192 | tf_op jit(solution)/shard_map/ppermute | solution.py:192
  92.4 4.8 %collective-permute-start.28 = (f32[8,2304]{1,0:T(8,128)S(1)}, f32[8,2304]{1,0:T(8,128)S(1)}, u32[]{:S(2)}, u32[]{:S(2)}) collective-permute-start(f32[8,2304]{1,0:T(8,128)S(1)} %shard_map.67), channel_id=1, source_target_pairs={{0,4},{4,0},{8,12},{12,8},{1,5},{5,1},{9,13},{13,9},{2,6},{6,2},{1... | collective-permute-start | bytes 221192 | tf_op jit(solution)/shard_map/ppermute | solution.py:192
  92.4 6.3 %collective-permute-start.27 = (f32[8,2304]{1,0:T(8,128)S(1)}, f32[8,2304]{1,0:T(8,128)S(1)}, u32[]{:S(2)}, u32[]{:S(2)}) collective-permute-start(f32[8,2304]{1,0:T(8,128)S(1)} %shard_map.67), channel_id=1, source_target_pairs={{0,8},{4,12},{8,0},{12,4},{1,9},{5,13},{9,1},{13,5},{2,10},{6,14},... | collective-permute-start | bytes 221192 | tf_op jit(solution)/shard_map/ppermute | solution.py:192
  98.7 6.4 %collective-permute-start.32 = (f32[8,2304]{1,0:T(8,128)S(1)}, f32[8,2304]{1,0:T(8,128)S(1)}, u32[]{:S(2)}, u32[]{:S(2)}) collective-permute-start(f32[8,2304]{1,0:T(8,128)S(1)} %add_add_fusion.1.own_ref), channel_id=1, source_target_pairs={{0,2},{1,3},{2,0},{3,1},{4,6},{5,7},{6,4},{7,5},{8,10},{9,11},{10,... | collective-permute-start | bytes 221192 | tf_op jit(solution)/shard_map/ppermute | solution.py:192
  100.9 5.6 %collective-permute-start.31 = (f32[8,2304]{1,0:T(8,128)S(1)}, f32[8,2304]{1,0:T(8,128)S(1)}, u32[]{:S(2)}, u32[]{:S(2)}) collective-permute-start(f32[8,2304]{1,0:T(8,128)S(1)} %add_add_fusion.1.own_ref), channel_id=1, source_target_pairs={{0,3},{1,2},{2,1},{3,0},{4,7},{5,6},{6,5},{7,4},{8,11},{9,10},{10,... | collective-permute-start | bytes 221192 | tf_op jit(solution)/shard_map/ppermute | solution.py:192
  109.3 7.6 %collective-permute-start.36 = (f32[8,4352]{1,0:T(8,128)S(1)}, f32[8,4352]{1,0:T(8,128)S(1)}, u32[]{:S(2)}, u32[]{:S(2)}) collective-permute-start(f32[8,4352]{1,0:T(8,128)S(1)} %add.84.own_ref), channel_id=1, source_target_pairs={{0,64},{32,96},{64,0},{96,32},{1,65},{33,97},{65,1},{97,33},{2,66}... | collective-permute-start | bytes 417800 | tf_op jit(solution)/shard_map/ppermute | solution.py:192
  111.4 8.2 %collective-permute-start.35 = (f32[8,4352]{1,0:T(8,128)S(1)}, f32[8,4352]{1,0:T(8,128)S(1)}, u32[]{:S(2)}, u32[]{:S(2)}) collective-permute-start(f32[8,4352]{1,0:T(8,128)S(1)} %add.84.own_ref), channel_id=1, source_target_pairs={{0,96},{32,64},{64,32},{96,0},{1,97},{33,65},{65,33},{97,1},{2,98}... | collective-permute-start | bytes 417800 | tf_op jit(solution)/shard_map/ppermute | solution.py:192
  113.0 6.6 %collective-permute-start.34 = (f32[8,4352]{1,0:T(8,128)S(1)}, f32[8,4352]{1,0:T(8,128)S(1)}, u32[]{:S(2)}, u32[]{:S(2)}) collective-permute-start(f32[8,4352]{1,0:T(8,128)S(1)} %add.84.own_ref), channel_id=1, source_target_pairs={{0,32},{32,0},{64,96},{96,64},{1,33},{33,1},{65,97},{97,65},{2,34}... | collective-permute-start | bytes 417800 | tf_op jit(solution)/shard_map/ppermute | solution.py:192
  122.9 5.6 %collective-permute-start.40 = (f32[8,2304]{1,0:T(8,128)S(1)}, f32[8,2304]{1,0:T(8,128)S(1)}, u32[]{:S(2)}, u32[]{:S(2)}) collective-permute-start(f32[8,2304]{1,0:T(8,128)S(1)} %shard_map.70), channel_id=1, source_target_pairs={{0,12},{4,8},{8,4},{12,0},{1,13},{5,9},{9,5},{13,1},{2,14},{6,10},... | collective-permute-start | bytes 221192 | tf_op jit(solution)/shard_map/ppermute | solution.py:192
  125.2 6.1 %collective-permute-start.38 = (f32[8,2304]{1,0:T(8,128)S(1)}, f32[8,2304]{1,0:T(8,128)S(1)}, u32[]{:S(2)}, u32[]{:S(2)}) collective-permute-start(f32[8,2304]{1,0:T(8,128)S(1)} %shard_map.70), channel_id=1, source_target_pairs={{0,8},{4,12},{8,0},{12,4},{1,9},{5,13},{9,1},{13,5},{2,10},{6,14},... | collective-permute-start | bytes 221192 | tf_op jit(solution)/shard_map/ppermute | solution.py:192
  131.3 6.7 %collective-permute-start.43 = (f32[8,2304]{1,0:T(8,128)S(1)}, f32[8,2304]{1,0:T(8,128)S(1)}, u32[]{:S(2)}, u32[]{:S(2)}) collective-permute-start(f32[8,2304]{1,0:T(8,128)S(1)} %add_add_fusion.own_ref), channel_id=1, source_target_pairs={{0,2},{1,3},{2,0},{3,1},{4,6},{5,7},{6,4},{7,5},{8,10},{9,11},{10,... | collective-permute-start | bytes 221192 | tf_op jit(solution)/shard_map/ppermute | solution.py:192
  132.8 5.8 %collective-permute-start.42 = (f32[8,2304]{1,0:T(8,128)S(1)}, f32[8,2304]{1,0:T(8,128)S(1)}, u32[]{:S(2)}, u32[]{:S(2)}) collective-permute-start(f32[8,2304]{1,0:T(8,128)S(1)} %add_add_fusion.own_ref), channel_id=1, source_target_pairs={{0,3},{1,2},{2,1},{3,0},{4,7},{5,6},{6,5},{7,4},{8,11},{9,10},{10,... | collective-permute-start | bytes 221192 | tf_op jit(solution)/shard_map/ppermute | solution.py:192
  140.0 5.1 %collective-permute-start.47 = (f32[8,128]{1,0:T(8,128)S(1)}, f32[8,128]{1,0:T(8,128)S(1)}, u32[]{:S(2)}, u32[]{:S(2)}) collective-permute-start(f32[8,128]{1,0:T(8,128)S(1)} %add.88.own_ref), channel_id=1, source_target_pairs={{0,64},{32,96},{64,0},{96,32},{1,65},{33,97},{65,1},{97,33},{2,66}... | collective-permute-start | bytes 12296 | tf_op jit(solution)/shard_map/ppermute | solution.py:192
  (19 other events, 62.6 us)

commit v3 on v2

--- a/solution.py
+++ b/solution.py
@@ -10,6 +10,9 @@
 BLK_DEV = 32
 ITERS = 4
 EPS = 1e-06
+TINY = 1e-30
+DIGITS = 8192.0
+CODES = 32000.0
 F32 = jnp.float32
 BF16 = jnp.bfloat16
 
@@ -34,9 +37,9 @@
     return jnp.broadcast_to(x, (x.shape[0], 128))
 
 
-def scatter_products(u, place_ref, tiles_ref, keep_ref, send_ref, acc_ref, copies=None):
+def scatter_products(u, block_of, tiles_ref, keep_ref, send_ref, acc_ref, copies=None):
     bundles, slots, rays, cells = tiles_ref.shape
-    half = keep_ref.shape[1]
+    half = keep_ref.shape[1] - 128
     acc_ref[...] = jnp.zeros_like(acc_ref)
     low = u.astype(BF16)
     for b in range(bundles):
@@ -45,24 +48,37 @@
         rows = low[:, b * rays : (b + 1) * rays]
         for s in range(slots):
             part = jnp.dot(rows, tiles_ref[b, s], preferred_element_type=F32)
-            at = pl.multiple_of(place_ref[b * slots + s] * cells, cells)
+            at = pl.multiple_of(block_of(b, s) * cells, cells)
             acc_ref[:, pl.ds(at, cells)] += part
-    squares = fold_sq(u, cells)
-    for out_ref, at in ((keep_ref, 0), (send_ref, half)):
-        out_ref[:, : half - cells] = acc_ref[:, at : at + half - cells]
-        out_ref[:, half - cells :] = squares
+    squares = fold_sq(u, 128)
+    for out_ref, at in ((keep_ref, 0), (send_ref, half + cells)):
+        out_ref[:, :half] = acc_ref[:, at : at + half]
+        out_ref[:, half:] = squares
 
 
 def first_adjoint(
-    place_ref, right_ref, source_ref, keep_ref, send_ref, tiles_ref, acc_ref, sem
-):
-    copies = [
+    pattern_ref, counts_ref, source_u_ref, source_ref, keep_ref, send_ref, tiles_ref, acc_ref,
+    u_ref, sem,
+):
+    bundles = source_ref.shape[0]
+    copies = [pltpu.make_async_copy(source_u_ref, u_ref, sem.at[bundles])] + [
         pltpu.make_async_copy(source_ref.at[b], tiles_ref.at[b], sem.at[b])
-        for b in range(source_ref.shape[0])
+        for b in range(bundles)
     ]
     for copy in copies:
         copy.start()
-    scatter_products(right_ref[...], place_ref, tiles_ref, keep_ref, send_ref, acc_ref, copies)
+    core = lax.axis_index("core")
+    blocks = BLK_DEV // 2
+
+    def block_of(b, s):
+        found = pattern_ref[b, s]
+        upper = (found >= blocks).astype(jnp.int32)
+        within = found - blocks * upper
+        at = jnp.where(upper == core, within, within + blocks + 1)
+        return jnp.where(s < counts_ref[b, 0], at, blocks)
+
+    copies[0].wait()
+    scatter_products(u_ref[...], block_of, tiles_ref, keep_ref, send_ref, acc_ref, copies[1:])
 
 
 def ray_vector(own_ref, left_ref, right_ref, far_ref, prev_ref, beta_ref):
@@ -80,7 +96,10 @@
     u, alpha = ray_vector(own_ref, left_ref, right_ref, far_ref, prev_ref, beta_ref)
     u_ref[...] = u
     alpha_ref[...] = wide(alpha)
-    scatter_products(u, place_ref, tiles_ref, keep_ref, send_ref, acc_ref)
+    slots = tiles_ref.shape[1]
+    scatter_products(
+        u, lambda b, s: place_ref[b * slots + s], tiles_ref, keep_ref, send_ref, acc_ref
+    )
 
 
 def last_norm(
@@ -91,13 +110,49 @@
     out_ref[...] = fold_sq(u, 128)
 
 
+def split(value, digits):
+    power = jnp.floor(jnp.log2(value))
+    return power, value * jnp.exp2(-power) * digits
+
+
+def pack(keep_ref, other_ref, out_ref):
+    total = keep_ref[...] + other_ref[...]
+    width = out_ref.shape[1] - 128
+    body = total[:, :width]
+    peak = jnp.maximum(jnp.max(jnp.abs(body), axis=1, keepdims=True), TINY)
+    power, mantissa = split(peak, DIGITS)
+    mantissa = jnp.floor(mantissa) + 1.0
+    scale = mantissa * jnp.exp2(power) * (1.0 / DIGITS)
+    norm_power, norm = split(jnp.maximum(lane_sum(total[:, width:]), TINY), DIGITS)
+    high = jnp.floor(norm)
+    low = (norm - high) * DIGITS
+    lane = lax.broadcasted_iota(jnp.int32, (total.shape[0], 128), 1)
+    fields = jnp.zeros_like(lane).astype(F32)
+    for at, field in enumerate((power, mantissa, norm_power, high, low)):
+        fields = jnp.where(lane == at, field, fields)
+
+    def code(x):
+        return jnp.round(x).astype(jnp.int32).astype(jnp.int16)
+
+    out_ref[:, :width] = code(body * (CODES / scale))
+    out_ref[:, width:] = code(fields)
+
+
+def unpack(ref):
+    width = ref.shape[1] - 128
+    codes = ref[...].astype(jnp.int32).astype(F32)
+    power, mantissa, norm_power, high, low = [codes[:, width + at : width + at + 1] for at in range(5)]
+    scale = mantissa * jnp.exp2(power) * (1.0 / DIGITS)
+    norm = (high + low * (1.0 / DIGITS)) * jnp.exp2(norm_power) * (1.0 / DIGITS)
+    return codes[:, :width] * (scale * (1.0 / CODES)), norm
+
+
 def cell_vector(
     first, own_ref, left_ref, right_ref, far_ref, prev_ref, alpha_ref, v_ref, beta_ref
 ):
-    total = (own_ref[...] + far_ref[...]) + (left_ref[...] + right_ref[...])
-    width = v_ref.shape[1]
-    beta = jnp.sqrt(lane_sum(total[:, width:]) + EPS)
-    v = total[:, :width] / beta
+    own, left, right, far = [unpack(ref) for ref in (own_ref, left_ref, right_ref, far_ref)]
+    beta = jnp.sqrt((own[1] + far[1]) + (left[1] + right[1]) + EPS)
+    v = ((own[0] + far[0]) + (left[0] + right[0])) / beta
     if not first:
         v = v - (beta / alpha_ref[:, :1]) * prev_ref[...]
     v_ref[...] = v
@@ -122,41 +177,58 @@
             )
             acc = part if acc is None else acc + part
         out_ref[:, b * rays : (b + 1) * rays] = acc
-    out_ref[:, bundles * rays :] = fold_sq(own, cells) + fold_sq(other, cells)
-
-
-def finish(place_ref, own_ref, left_ref, right_ref, far_ref, *rest):
+    out_ref[:, bundles * rays :] = fold_sq(own, 128) + fold_sq(other, 128)
+
+
+def gather_up(*refs):
     count = ITERS
-    own_refs, other_refs = rest[:count], rest[count : 2 * count]
-    alpha_refs, beta_refs = rest[2 * count : 3 * count], rest[3 * count : 4 * count]
-    x_ref, misfit_ref = rest[4 * count :]
-    width = own_refs[0].shape[1]
-    total = (own_ref[...] + far_ref[...]) + (left_ref[...] + right_ref[...])
-    last_beta = jnp.sqrt(lane_sum(total) + EPS)
+    own_refs, other_refs = refs[:count], refs[count : 2 * count]
+    alpha_refs, beta_refs = refs[2 * count : 3 * count], refs[3 * count : 4 * count]
+    x_refs, w_refs, phibar_ref, rhobar_ref = refs[4 * count : 4 * count + 2], refs[
+        4 * count + 2 : 4 * count + 4], refs[-2], refs[-1]
     alphas = [ref[:, :1] for ref in alpha_refs]
-    betas = [ref[:, :1] for ref in beta_refs] + [last_beta]
+    betas = [ref[:, :1] for ref in beta_refs]
     phibar, rhobar = betas[0], alphas[0]
     steps, turns = [], []
-    for k in range(count):
+    for k in range(count - 1):
         beta = betas[k + 1]
         rho = jnp.sqrt(rhobar * rhobar + beta * beta)
         cosine, sine = rhobar / rho, beta / rho
-        phi = cosine * phibar
+        steps.append(cosine * phibar / rho)
         phibar = sine * phibar
-        steps.append(phi / rho)
-        if k + 1 < count:
-            theta = sine * alphas[k + 1]
-            rhobar = -cosine * alphas[k + 1]
-            turns.append(theta / rho)
-    core = place_ref[place_ref.shape[0] - 1]
-    for refs, half in ((own_refs, core), (other_refs, 1 - core)):
+        turns.append(sine * alphas[k + 1] / rho)
+        rhobar = -cosine * alphas[k + 1]
+    for refs, x_ref, w_ref in zip((own_refs, other_refs), x_refs, w_refs):
         w = refs[0][...] / alphas[0]
         x = steps[0] * w
         for k in range(1, count):
             w = refs[k][...] / alphas[k] - turns[k - 1] * w
-            x = x + steps[k] * w
-        x_ref[:, pl.ds(pl.multiple_of(half * width, width), width)] = x
-    misfit_ref[...] = wide(phibar)
+            if k + 1 < count:
+                x = x + steps[k] * w
+        x_ref[...] = x
+        w_ref[...] = w
+    phibar_ref[...] = wide(phibar)
+    rhobar_ref[...] = wide(rhobar)
+
+
+def finish(
+    place_ref, own_ref, left_ref, right_ref, far_ref, own_x_ref, other_x_ref, own_w_ref,
+    other_w_ref, phibar_ref, rhobar_ref, x_ref, misfit_ref,
+):
+    width = own_x_ref.shape[1]
+    total = (own_ref[...] + far_ref[...]) + (left_ref[...] + right_ref[...])
+    beta = jnp.sqrt(lane_sum(total) + EPS)
+    phibar, rhobar = phibar_ref[:, :1], rhobar_ref[:, :1]
+    rho = jnp.sqrt(rhobar * rhobar + beta * beta)
+    step = (rhobar / rho) * phibar / rho
+    core = place_ref[place_ref.shape[0] - 1]
+    for half, xs_ref, w_ref in ((core, own_x_ref, own_w_ref), (1 - core, other_x_ref, other_w_ref)):
+        at = pl.multiple_of(half * width, width)
+        x_ref[:, pl.ds(at, width)] = xs_ref[...] + step * w_ref[...]
+    last = wide((beta / rho) * phibar)
+    row = lax.broadcasted_iota(jnp.int32, last.shape, 0)
+    lane = lax.broadcasted_iota(jnp.int32, last.shape, 1)
+    misfit_ref[...] = jnp.sum(jnp.where(row == lane, last, 0.0), axis=0, keepdims=True)
 
 
 def call(body, outs, specs, args, scratch=()):
@@ -200,27 +272,33 @@
         own, left, right, far = spread(partial, "x")
         return spread((own + far) + (left + right), "y")
 
-    halves = [shape(half + cells)] * 2
+    halves = [shape(half + 128)] * 2
     store = [pltpu.VMEM((nrhs, 2 * (half + cells)), F32)]
     keep, send, tiles = call(
         first_adjoint, halves + [jax.ShapeDtypeStruct(tiles.shape, tiles.dtype)],
-        [SMEM, VMEM, HBM], (place, right_side, tiles),
-        store + [pltpu.SemaphoreType.DMA((bundles,))],
+        [SMEM, SMEM, HBM, HBM], (
+            pattern, counts, pltpu.with_memory_space_constraint(right_side, pltpu.HBM),
+            pltpu.with_memory_space_constraint(tiles, pltpu.HBM),
+        ),
+        store + [pltpu.VMEM(right_side.shape, F32), pltpu.SemaphoreType.DMA((bundles + 1,))],
     )
     u = right_side
     owns, others, alphas, betas = [], [], [], []
     for step in range(ITERS):
         prev = (owns[-1], alphas[-1]) if step else (right_side, right_side)
+        packed, = call(
+            pack, [shape(half + 128, jnp.int16)], [VMEM] * 2, (keep, swap(send))
+        )
         v, beta = call(
             functools.partial(cell_vector, step == 0), [shape(half), shape(128)], [VMEM] * 6,
-            (*spread(keep + swap(send), "z"), *prev),
+            (*spread(packed, "z"), *prev),
         )
         other = swap(v)
         owns.append(v)
         others.append(other)
         betas.append(beta)
         products, = call(
-            forward, [shape(rows + cells)], [SMEM] + [VMEM] * 3, (place, v, other, tiles),
+            forward, [shape(rows + 128)], [SMEM] + [VMEM] * 3, (place, v, other, tiles),
             [pltpu.VMEM((nrhs, 2 * half + cells), BF16)],
         )
         rows_in = over_cell(products)
@@ -234,11 +312,15 @@
                 last_norm, [shape(128), shape(128)], [VMEM] * 6, (*rows_in, u, beta)
             )
         alphas.append(alpha)
+    so_far = call(
+        gather_up, [shape(half)] * 4 + [shape(128)] * 2, [VMEM] * (4 * ITERS),
+        (*owns, *others, *alphas, *betas),
+    )
     x, misfit = call(
-        finish, [shape(2 * half), shape(128)], [SMEM] + [VMEM] * (4 + 4 * ITERS),
-        (place, *spread(squares + swap(squares), "z"), *owns, *others, *alphas, *betas),
+        finish, [shape(2 * half), jax.ShapeDtypeStruct((1, 128), F32)], [SMEM] + [VMEM] * 10,
+        (place, *spread(squares + swap(squares), "z"), *so_far),
     )
-    return x, misfit[:, 0]
+    return x, misfit[0, :nrhs]
 
 
 def solution(mesh):

time: 150 us -> 141 us (0.940)
  waiting for transfers between devices: 73.1 us -> 61 us
  local copies, waits for them, and re-layouts: 3.99 us -> 6.55 us
  Pallas kernels: 15.9 us -> 17.6 us
    ppermute x39, waiting for transfers between devices: 61.3 us -> 49.6 us  [spread(): lax.ppermute(value, axis, [(i, i ^ by) for i in range(n)])]
    unnamed x6 -> x14, local copies, waits for them, and re-layouts: 3.04 us -> 5.72 us
    pallas_call x14 -> x19, Pallas kernels: 15.9 us -> 17.6 us  [call(): pl.pallas_call(body, out_shape=outs, in_specs=specs, out_specs=[VMEM] * l...]
  transfers between devices with their start and end apart: 48 -> 48, of which waited for: 41 -> 39; matrix products, arithmetic and copies ran while one was open for 0% -> 0% of each run, Pallas kernels for 0% -> 0%
where the time goes in v3:
time: 141 us; the launch traced here: 140 us
  waiting for transfers between devices  61 us (43%)
  starting transfers between devices  54 us (38%)
  Pallas kernels  17.6 us (12%)
  local copies, waits for them, and re-layouts  6.55 us (5%)
    ppermute x39, starting transfers between devices, spread(): lax.ppermute(value, axis, [(i, i ^ by) for i in range(n)])  53.3 us
    ppermute x39, waiting for transfers between devices, spread(): lax.ppermute(value, axis, [(i, i ^ by) for i in range(n)])  49.6 us
    pallas_call x19, Pallas kernels, call(): pl.pallas_call(body, out_shape=outs, in_specs=specs, out_specs=[VMEM] * l...  17.6 us
    ppermute x9, waiting for transfers between devices, swap(): return lax.ppermute(value, 'core', [(0, 1), (1, 0)])  11.4 us
    unnamed x14, local copies, waits for them, and re-layouts  5.72 us
  transfers between devices with their start and end apart: 48, of which 39 were waited for; matrix products, arithmetic and copies ran while one was open for 0% of the time, Pallas kernels for 0%

profile of v3, /device:TPU:0, one launch (start us, length us, event | category | flops | bytes accessed | tf_op | source)
XLA Modules:
  0.0 140.3 jit_solution(5492358153464515050)
XLA Ops:
  2.2 3.3 %shard_map.59 = (f32[8,4224]{1,0:T(8,128)S(1)}, f32[8,4224]{1,0:T(8,128)S(1)}, bf16[8,4,256,256]{3,2,1,0:T(8,128)(2,1)S(1)}) custom-call(s32[8,4]{1,0:T(8,128)S(1)} %copy.12.pattern_ref, s32[8,1]{1,0:T(8,128)S(1)} %copy.13.counts_ref, f32[8,2048]{1,0:T(8,128)} %prev_ref.3, bf16[8,4,256,256]{3,2,1,0:T(8,128)(2,1)} %source_ref.1), custom_call_target="tpu_custom_call" | custom-call | tf_op jit(solution)/shard_map/pallas_call | solution.py:235
  5.6 2.0 %copy-done = bf16[8,4,256,256]{3,2,1,0:T(8,128)(2,1)} copy-done((bf16[8,4,256,256]{3,2,1,0:T(8,128)(2,1)}, bf16[8,4,256,256]{3,2,1,0:T(8,128)(2,1)S(1)}, u32[]{:S(2)}) %copy-start) | copy-done | bytes 4194328
  9.0 4.0 %collective-permute-start.3 = (s16[8,4224]{1,0:T(8,128)(2,1)S(1)}, s16[8,4224]{1,0:T(8,128)(2,1)S(1)}, u32[]{:S(2)}, u32[]{:S(2)}) collective-permute-start(s16[8,4224]{1,0:T(8,128)(2,1)S(1)} %shard_map.60.own_ref), channel_id=1, source_target_pairs={{0,64},{32,96},{64,0},{96,32},{1,65},{33,97},{65,1},{97,33},{2,66}... | collective-permute-start | bytes 202760 | tf_op jit(solution)/shard_map/ppermute | solution.py:264
  15.5 3.0 %collective-permute-done.2.right_ref = s16[8,4224]{1,0:T(8,128)(2,1)S(1)} collective-permute-done((s16[8,4224]{1,0:T(8,128)(2,1)S(1)}, s16[8,4224]{1,0:T(8,128)(2,1)S(1)}, u32[]{:S(2)}, u32[]{:S(2)}) %collective-permute-start.2) | collective-permute-done | bytes 67616 | tf_op jit(solution)/shard_map/ppermute | solution.py:264
  20.2 2.2 %copy-done.1 = bf16[8,4,256,256]{3,2,1,0:T(8,128)(2,1)S(1)} copy-done((bf16[8,4,256,256]{3,2,1,0:T(8,128)(2,1)S(1)}, bf16[8,4,256,256]{3,2,1,0:T(8,128)(2,1)}, u32[]{:S(2)}) %copy-start.1) | copy-done | bytes 4194328
  22.4 1.7 %shard_map.62 = f32[8,2176]{1,0:T(8,128)S(1)} custom-call(s32[65]{0:T(128)S(1)} %pad_add_fusion.place_ref, f32[8,4096]{1,0:T(8,128)S(1)} %get-tuple-element.37.own_ref.prev_ref.refs_0_, f32[8,4096]{1,0:T(8,128)S(1)} %collective-permute-done.4.other_ref.refs_4_, bf16[8,4,256,256]{3,2,1,0:T(8,128)(2,1)S(1)} %copy-done.1), custom_call_target="tpu_custom_call" | custom-call | tf_op jit(solution)/shard_map/pallas_call | solution.py:235
  24.1 2.8 %collective-permute-start.7 = (f32[8,2176]{1,0:T(8,128)S(1)}, f32[8,2176]{1,0:T(8,128)S(1)}, u32[]{:S(2)}, u32[]{:S(2)}) collective-permute-start(f32[8,2176]{1,0:T(8,128)S(1)} %shard_map.62), channel_id=1, source_target_pairs={{0,12},{4,8},{8,4},{12,0},{1,13},{5,9},{9,5},{13,1},{2,14},{6,10},... | collective-permute-start | bytes 208904 | tf_op jit(solution)/shard_map/ppermute | solution.py:264
  27.1 1.7 %collective-permute-start.5 = (f32[8,2176]{1,0:T(8,128)S(1)}, f32[8,2176]{1,0:T(8,128)S(1)}, u32[]{:S(2)}, u32[]{:S(2)}) collective-permute-start(f32[8,2176]{1,0:T(8,128)S(1)} %shard_map.62), channel_id=1, source_target_pairs={{0,8},{4,12},{8,0},{12,4},{1,9},{5,13},{9,1},{13,5},{2,10},{6,14},... | collective-permute-start | bytes 208904 | tf_op jit(solution)/shard_map/ppermute | solution.py:264
  29.7 1.9 %collective-permute-done.6 = f32[8,2176]{1,0:T(8,128)S(1)} collective-permute-done((f32[8,2176]{1,0:T(8,128)S(1)}, f32[8,2176]{1,0:T(8,128)S(1)}, u32[]{:S(2)}, u32[]{:S(2)}) %collective-permute-start.6) | collective-permute-done | bytes 69664 | tf_op jit(solution)/shard_map/ppermute | solution.py:264
  32.9 3.3 %collective-permute-start.10 = (f32[8,2176]{1,0:T(8,128)S(1)}, f32[8,2176]{1,0:T(8,128)S(1)}, u32[]{:S(2)}, u32[]{:S(2)}) collective-permute-start(f32[8,2176]{1,0:T(8,128)S(1)} %add_add_fusion.3.own_ref), channel_id=1, source_target_pairs={{0,2},{1,3},{2,0},{3,1},{4,6},{5,7},{6,4},{7,5},{8,10},{9,11},{10,... | collective-permute-start | bytes 208904 | tf_op jit(solution)/shard_map/ppermute | solution.py:264
  38.9 2.9 %collective-permute-done.9.right_ref = f32[8,2176]{1,0:T(8,128)S(1)} collective-permute-done((f32[8,2176]{1,0:T(8,128)S(1)}, f32[8,2176]{1,0:T(8,128)S(1)}, u32[]{:S(2)}, u32[]{:S(2)}) %collective-permute-start.9) | collective-permute-done | bytes 69664 | tf_op jit(solution)/shard_map/ppermute | solution.py:264
  44.7 2.0 %collective-permute-start.14 = (s16[8,4224]{1,0:T(8,128)(2,1)S(1)}, s16[8,4224]{1,0:T(8,128)(2,1)S(1)}, u32[]{:S(2)}, u32[]{:S(2)}) collective-permute-start(s16[8,4224]{1,0:T(8,128)(2,1)S(1)} %shard_map.64.own_ref), channel_id=1, source_target_pairs={{0,64},{32,96},{64,0},{96,32},{1,65},{33,97},{65,1},{97,33},{2,66}... | collective-permute-start | bytes 202760 | tf_op jit(solution)/shard_map/ppermute | solution.py:264
  48.3 2.3 %collective-permute-done.14.far_ref = s16[8,4224]{1,0:T(8,128)(2,1)S(1)} collective-permute-done((s16[8,4224]{1,0:T(8,128)(2,1)S(1)}, s16[8,4224]{1,0:T(8,128)(2,1)S(1)}, u32[]{:S(2)}, u32[]{:S(2)}) %collective-permute-start.14) | collective-permute-done | bytes 67616 | tf_op jit(solution)/shard_map/ppermute | solution.py:264
  53.8 1.7 %shard_map.66 = f32[8,2176]{1,0:T(8,128)S(1)} custom-call(s32[65]{0:T(128)S(1)} %pad_add_fusion.place_ref, f32[8,4096]{1,0:T(8,128)S(1)} %get-tuple-element.43.own_ref.prev_ref.refs_1_, f32[8,4096]{1,0:T(8,128)S(1)} %collective-permute-done.15.other_ref.refs_5_, bf16[8,4,256,256]{3,2,1,0:T(8,128)(2,1)S(1)} %copy-done.2), custom_call_target="tpu_custom_call" | custom-call | tf_op jit(solution)/shard_map/pallas_call | solution.py:235
  55.5 2.1 %collective-permute-start.18 = (f32[8,2176]{1,0:T(8,128)S(1)}, f32[8,2176]{1,0:T(8,128)S(1)}, u32[]{:S(2)}, u32[]{:S(2)}) collective-permute-start(f32[8,2176]{1,0:T(8,128)S(1)} %shard_map.66), channel_id=1, source_target_pairs={{0,12},{4,8},{8,4},{12,0},{1,13},{5,9},{9,5},{13,1},{2,14},{6,10},... | collective-permute-start | bytes 208904 | tf_op jit(solution)/shard_map/ppermute | solution.py:264
  57.6 2.6 %collective-permute-start.16 = (f32[8,2176]{1,0:T(8,128)S(1)}, f32[8,2176]{1,0:T(8,128)S(1)}, u32[]{:S(2)}, u32[]{:S(2)}) collective-permute-start(f32[8,2176]{1,0:T(8,128)S(1)} %shard_map.66), channel_id=1, source_target_pairs={{0,8},{4,12},{8,0},{12,4},{1,9},{5,13},{9,1},{13,5},{2,10},{6,14},... | collective-permute-start | bytes 208904 | tf_op jit(solution)/shard_map/ppermute | solution.py:264
  63.9 1.6 %collective-permute-start.21 = (f32[8,2176]{1,0:T(8,128)S(1)}, f32[8,2176]{1,0:T(8,128)S(1)}, u32[]{:S(2)}, u32[]{:S(2)}) collective-permute-start(f32[8,2176]{1,0:T(8,128)S(1)} %add_add_fusion.2.own_ref), channel_id=1, source_target_pairs={{0,2},{1,3},{2,0},{3,1},{4,6},{5,7},{6,4},{7,5},{8,10},{9,11},{10,... | collective-permute-start | bytes 208904 | tf_op jit(solution)/shard_map/ppermute | solution.py:264
  67.4 3.0 %collective-permute-done.21.far_ref = f32[8,2176]{1,0:T(8,128)S(1)} collective-permute-done((f32[8,2176]{1,0:T(8,128)S(1)}, f32[8,2176]{1,0:T(8,128)S(1)}, u32[]{:S(2)}, u32[]{:S(2)}) %collective-permute-start.21) | collective-permute-done | bytes 69664 | tf_op jit(solution)/shard_map/ppermute | solution.py:264
  74.0 1.9 %collective-permute-start.25 = (s16[8,4224]{1,0:T(8,128)(2,1)S(1)}, s16[8,4224]{1,0:T(8,128)(2,1)S(1)}, u32[]{:S(2)}, u32[]{:S(2)}) collective-permute-start(s16[8,4224]{1,0:T(8,128)(2,1)S(1)} %shard_map.68.own_ref), channel_id=1, source_target_pairs={{0,64},{32,96},{64,0},{96,32},{1,65},{33,97},{65,1},{97,33},{2,66}... | collective-permute-start | bytes 202760 | tf_op jit(solution)/shard_map/ppermute | solution.py:264
  77.6 2.3 %collective-permute-done.25.far_ref = s16[8,4224]{1,0:T(8,128)(2,1)S(1)} collective-permute-done((s16[8,4224]{1,0:T(8,128)(2,1)S(1)}, s16[8,4224]{1,0:T(8,128)(2,1)S(1)}, u32[]{:S(2)}, u32[]{:S(2)}) %collective-permute-start.25) | collective-permute-done | bytes 67616 | tf_op jit(solution)/shard_map/ppermute | solution.py:264
  83.1 1.7 %shard_map.70 = f32[8,2176]{1,0:T(8,128)S(1)} custom-call(s32[65]{0:T(128)S(1)} %pad_add_fusion.place_ref, f32[8,4096]{1,0:T(8,128)S(1)} %get-tuple-element.49.own_ref.prev_ref.refs_2_, f32[8,4096]{1,0:T(8,128)S(1)} %collective-permute-done.26.other_ref.refs_6_, bf16[8,4,256,256]{3,2,1,0:T(8,128)(2,1)S(1)} %copy-done.2), custom_call_target="tpu_custom_call" | custom-call | tf_op jit(solution)/shard_map/pallas_call | solution.py:235
  84.9 2.2 %collective-permute-start.29 = (f32[8,2176]{1,0:T(8,128)S(1)}, f32[8,2176]{1,0:T(8,128)S(1)}, u32[]{:S(2)}, u32[]{:S(2)}) collective-permute-start(f32[8,2176]{1,0:T(8,128)S(1)} %shard_map.70), channel_id=1, source_target_pairs={{0,12},{4,8},{8,4},{12,0},{1,13},{5,9},{9,5},{13,1},{2,14},{6,10},... | collective-permute-start | bytes 208904 | tf_op jit(solution)/shard_map/ppermute | solution.py:264
  87.1 2.6 %collective-permute-start.27 = (f32[8,2176]{1,0:T(8,128)S(1)}, f32[8,2176]{1,0:T(8,128)S(1)}, u32[]{:S(2)}, u32[]{:S(2)}) collective-permute-start(f32[8,2176]{1,0:T(8,128)S(1)} %shard_map.70), channel_id=1, source_target_pairs={{0,8},{4,12},{8,0},{12,4},{1,9},{5,13},{9,1},{13,5},{2,10},{6,14},... | collective-permute-start | bytes 208904 | tf_op jit(solution)/shard_map/ppermute | solution.py:264
  93.3 2.2 %collective-permute-start.32 = (f32[8,2176]{1,0:T(8,128)S(1)}, f32[8,2176]{1,0:T(8,128)S(1)}, u32[]{:S(2)}, u32[]{:S(2)}) collective-permute-start(f32[8,2176]{1,0:T(8,128)S(1)} %add_add_fusion.1.own_ref), channel_id=1, source_target_pairs={{0,2},{1,3},{2,0},{3,1},{4,6},{5,7},{6,4},{7,5},{8,10},{9,11},{10,... | collective-permute-start | bytes 208904 | tf_op jit(solution)/shard_map/ppermute | solution.py:264
  96.9 2.5 %collective-permute-done.32.far_ref = f32[8,2176]{1,0:T(8,128)S(1)} collective-permute-done((f32[8,2176]{1,0:T(8,128)S(1)}, f32[8,2176]{1,0:T(8,128)S(1)}, u32[]{:S(2)}, u32[]{:S(2)}) %collective-permute-start.32) | collective-permute-done | bytes 69664 | tf_op jit(solution)/shard_map/ppermute | solution.py:264
  104.0 2.0 %collective-permute-start.36 = (s16[8,4224]{1,0:T(8,128)(2,1)S(1)}, s16[8,4224]{1,0:T(8,128)(2,1)S(1)}, u32[]{:S(2)}, u32[]{:S(2)}) collective-permute-start(s16[8,4224]{1,0:T(8,128)(2,1)S(1)} %shard_map.72.own_ref), channel_id=1, source_target_pairs={{0,64},{32,96},{64,0},{96,32},{1,65},{33,97},{65,1},{97,33},{2,66}... | collective-permute-start | bytes 202760 | tf_op jit(solution)/shard_map/ppermute | solution.py:264
  107.5 2.3 %collective-permute-done.36.far_ref = s16[8,4224]{1,0:T(8,128)(2,1)S(1)} collective-permute-done((s16[8,4224]{1,0:T(8,128)(2,1)S(1)}, s16[8,4224]{1,0:T(8,128)(2,1)S(1)}, u32[]{:S(2)}, u32[]{:S(2)}) %collective-permute-start.36) | collective-permute-done | bytes 67616 | tf_op jit(solution)/shard_map/ppermute | solution.py:264
  113.1 1.7 %shard_map.74 = f32[8,2176]{1,0:T(8,128)S(1)} custom-call(s32[65]{0:T(128)S(1)} %pad_add_fusion.place_ref, f32[8,4096]{1,0:T(8,128)S(1)} %get-tuple-element.55.own_ref.refs_3_, f32[8,4096]{1,0:T(8,128)S(1)} %collective-permute-done.37.other_ref.refs_7_, bf16[8,4,256,256]{3,2,1,0:T(8,128)(2,1)S(1)} %copy-done.2), custom_call_target="tpu_custom_call" | custom-call | tf_op jit(solution)/shard_map/pallas_call | solution.py:235
  114.8 1.9 %collective-permute-start.40 = (f32[8,2176]{1,0:T(8,128)S(1)}, f32[8,2176]{1,0:T(8,128)S(1)}, u32[]{:S(2)}, u32[]{:S(2)}) collective-permute-start(f32[8,2176]{1,0:T(8,128)S(1)} %shard_map.74), channel_id=1, source_target_pairs={{0,12},{4,8},{8,4},{12,0},{1,13},{5,9},{9,5},{13,1},{2,14},{6,10},... | collective-permute-start | bytes 208904 | tf_op jit(solution)/shard_map/ppermute | solution.py:264
  117.0 2.5 %collective-permute-start.38 = (f32[8,2176]{1,0:T(8,128)S(1)}, f32[8,2176]{1,0:T(8,128)S(1)}, u32[]{:S(2)}, u32[]{:S(2)}) collective-permute-start(f32[8,2176]{1,0:T(8,128)S(1)} %shard_map.74), channel_id=1, source_target_pairs={{0,8},{4,12},{8,0},{12,4},{1,9},{5,13},{9,1},{13,5},{2,10},{6,14},... | collective-permute-start | bytes 208904 | tf_op jit(solution)/shard_map/ppermute | solution.py:264
  126.5 3.1 %collective-permute-done.43.far_ref = f32[8,2176]{1,0:T(8,128)S(1)} collective-permute-done((f32[8,2176]{1,0:T(8,128)S(1)}, f32[8,2176]{1,0:T(8,128)S(1)}, u32[]{:S(2)}, u32[]{:S(2)}) %collective-permute-start.43) | collective-permute-done | bytes 69664 | tf_op jit(solution)/shard_map/ppermute | solution.py:264
  131.7 1.9 %collective-permute-start.47 = (f32[8,128]{1,0:T(8,128)S(1)}, f32[8,128]{1,0:T(8,128)S(1)}, u32[]{:S(2)}, u32[]{:S(2)}) collective-permute-start(f32[8,128]{1,0:T(8,128)S(1)} %add.72.own_ref), channel_id=1, source_target_pairs={{0,64},{32,96},{64,0},{96,32},{1,65},{33,97},{65,1},{97,33},{2,66}... | collective-permute-start | bytes 12296 | tf_op jit(solution)/shard_map/ppermute | solution.py:264
  (109 shorter events, 64.2 us)
Async XLA Ops:
  9.0 6.5 %collective-permute-start.3 = (s16[8,4224]{1,0:T(8,128)(2,1)S(1)}, s16[8,4224]{1,0:T(8,128)(2,1)S(1)}, u32[]{:S(2)}, u32[]{:S(2)}) collective-permute-start(s16[8,4224]{1,0:T(8,128)(2,1)S(1)} %shard_map.60.own_ref), channel_id=1, source_target_pairs={{0,64},{32,96},{64,0},{96,32},{1,65},{33,97},{65,1},{97,33},{2,66}... | collective-permute-start | bytes 202760 | tf_op jit(solution)/shard_map/ppermute | solution.py:264
  13.1 5.5 %collective-permute-start.2 = (s16[8,4224]{1,0:T(8,128)(2,1)S(1)}, s16[8,4224]{1,0:T(8,128)(2,1)S(1)}, u32[]{:S(2)}, u32[]{:S(2)}) collective-permute-start(s16[8,4224]{1,0:T(8,128)(2,1)S(1)} %shard_map.60.own_ref), channel_id=1, source_target_pairs={{0,96},{32,64},{64,32},{96,0},{1,97},{33,65},{65,33},{97,1},{2,98}... | collective-permute-start | bytes 202760 | tf_op jit(solution)/shard_map/ppermute | solution.py:264
  13.8 4.8 %collective-permute-start.1 = (s16[8,4224]{1,0:T(8,128)(2,1)S(1)}, s16[8,4224]{1,0:T(8,128)(2,1)S(1)}, u32[]{:S(2)}, u32[]{:S(2)}) collective-permute-start(s16[8,4224]{1,0:T(8,128)(2,1)S(1)} %shard_map.60.own_ref), channel_id=1, source_target_pairs={{0,32},{32,0},{64,96},{96,64},{1,33},{33,1},{65,97},{97,65},{2,34}... | collective-permute-start | bytes 202760 | tf_op jit(solution)/shard_map/ppermute | solution.py:264
  24.1 5.5 %collective-permute-start.7 = (f32[8,2176]{1,0:T(8,128)S(1)}, f32[8,2176]{1,0:T(8,128)S(1)}, u32[]{:S(2)}, u32[]{:S(2)}) collective-permute-start(f32[8,2176]{1,0:T(8,128)S(1)} %shard_map.62), channel_id=1, source_target_pairs={{0,12},{4,8},{8,4},{12,0},{1,13},{5,9},{9,5},{13,1},{2,14},{6,10},... | collective-permute-start | bytes 208904 | tf_op jit(solution)/shard_map/ppermute | solution.py:264
  26.9 4.7 %collective-permute-start.6 = (f32[8,2176]{1,0:T(8,128)S(1)}, f32[8,2176]{1,0:T(8,128)S(1)}, u32[]{:S(2)}, u32[]{:S(2)}) collective-permute-start(f32[8,2176]{1,0:T(8,128)S(1)} %shard_map.62), channel_id=1, source_target_pairs={{0,4},{4,0},{8,12},{12,8},{1,5},{5,1},{9,13},{13,9},{2,6},{6,2},{1... | collective-permute-start | bytes 208904 | tf_op jit(solution)/shard_map/ppermute | solution.py:264
  27.1 5.8 %collective-permute-start.5 = (f32[8,2176]{1,0:T(8,128)S(1)}, f32[8,2176]{1,0:T(8,128)S(1)}, u32[]{:S(2)}, u32[]{:S(2)}) collective-permute-start(f32[8,2176]{1,0:T(8,128)S(1)} %shard_map.62), channel_id=1, source_target_pairs={{0,8},{4,12},{8,0},{12,4},{1,9},{5,13},{9,1},{13,5},{2,10},{6,14},... | collective-permute-start | bytes 208904 | tf_op jit(solution)/shard_map/ppermute | solution.py:264
  32.9 5.9 %collective-permute-start.10 = (f32[8,2176]{1,0:T(8,128)S(1)}, f32[8,2176]{1,0:T(8,128)S(1)}, u32[]{:S(2)}, u32[]{:S(2)}) collective-permute-start(f32[8,2176]{1,0:T(8,128)S(1)} %add_add_fusion.3.own_ref), channel_id=1, source_target_pairs={{0,2},{1,3},{2,0},{3,1},{4,6},{5,7},{6,4},{7,5},{8,10},{9,11},{10,... | collective-permute-start | bytes 208904 | tf_op jit(solution)/shard_map/ppermute | solution.py:264
  36.2 5.5 %collective-permute-start.9 = (f32[8,2176]{1,0:T(8,128)S(1)}, f32[8,2176]{1,0:T(8,128)S(1)}, u32[]{:S(2)}, u32[]{:S(2)}) collective-permute-start(f32[8,2176]{1,0:T(8,128)S(1)} %add_add_fusion.3.own_ref), channel_id=1, source_target_pairs={{0,3},{1,2},{2,1},{3,0},{4,7},{5,6},{6,5},{7,4},{8,11},{9,10},{10,... | collective-permute-start | bytes 208904 | tf_op jit(solution)/shard_map/ppermute | solution.py:264
  44.7 5.9 %collective-permute-start.14 = (s16[8,4224]{1,0:T(8,128)(2,1)S(1)}, s16[8,4224]{1,0:T(8,128)(2,1)S(1)}, u32[]{:S(2)}, u32[]{:S(2)}) collective-permute-start(s16[8,4224]{1,0:T(8,128)(2,1)S(1)} %shard_map.64.own_ref), channel_id=1, source_target_pairs={{0,64},{32,96},{64,0},{96,32},{1,65},{33,97},{65,1},{97,33},{2,66}... | collective-permute-start | bytes 202760 | tf_op jit(solution)/shard_map/ppermute | solution.py:264
  46.6 5.5 %collective-permute-start.13 = (s16[8,4224]{1,0:T(8,128)(2,1)S(1)}, s16[8,4224]{1,0:T(8,128)(2,1)S(1)}, u32[]{:S(2)}, u32[]{:S(2)}) collective-permute-start(s16[8,4224]{1,0:T(8,128)(2,1)S(1)} %shard_map.64.own_ref), channel_id=1, source_target_pairs={{0,96},{32,64},{64,32},{96,0},{1,97},{33,65},{65,33},{97,1},{2,98}... | collective-permute-start | bytes 202760 | tf_op jit(solution)/shard_map/ppermute | solution.py:264
  55.5 5.5 %collective-permute-start.18 = (f32[8,2176]{1,0:T(8,128)S(1)}, f32[8,2176]{1,0:T(8,128)S(1)}, u32[]{:S(2)}, u32[]{:S(2)}) collective-permute-start(f32[8,2176]{1,0:T(8,128)S(1)} %shard_map.66), channel_id=1, source_target_pairs={{0,12},{4,8},{8,4},{12,0},{1,13},{5,9},{9,5},{13,1},{2,14},{6,10},... | collective-permute-start | bytes 208904 | tf_op jit(solution)/shard_map/ppermute | solution.py:264
  57.6 4.9 %collective-permute-start.17 = (f32[8,2176]{1,0:T(8,128)S(1)}, f32[8,2176]{1,0:T(8,128)S(1)}, u32[]{:S(2)}, u32[]{:S(2)}) collective-permute-start(f32[8,2176]{1,0:T(8,128)S(1)} %shard_map.66), channel_id=1, source_target_pairs={{0,4},{4,0},{8,12},{12,8},{1,5},{5,1},{9,13},{13,9},{2,6},{6,2},{1... | collective-permute-start | bytes 208904 | tf_op jit(solution)/shard_map/ppermute | solution.py:264
  57.6 6.2 %collective-permute-start.16 = (f32[8,2176]{1,0:T(8,128)S(1)}, f32[8,2176]{1,0:T(8,128)S(1)}, u32[]{:S(2)}, u32[]{:S(2)}) collective-permute-start(f32[8,2176]{1,0:T(8,128)S(1)} %shard_map.66), channel_id=1, source_target_pairs={{0,8},{4,12},{8,0},{12,4},{1,9},{5,13},{9,1},{13,5},{2,10},{6,14},... | collective-permute-start | bytes 208904 | tf_op jit(solution)/shard_map/ppermute | solution.py:264
  63.9 6.6 %collective-permute-start.21 = (f32[8,2176]{1,0:T(8,128)S(1)}, f32[8,2176]{1,0:T(8,128)S(1)}, u32[]{:S(2)}, u32[]{:S(2)}) collective-permute-start(f32[8,2176]{1,0:T(8,128)S(1)} %add_add_fusion.2.own_ref), channel_id=1, source_target_pairs={{0,2},{1,3},{2,0},{3,1},{4,6},{5,7},{6,4},{7,5},{8,10},{9,11},{10,... | collective-permute-start | bytes 208904 | tf_op jit(solution)/shard_map/ppermute | solution.py:264
  65.5 5.6 %collective-permute-start.20 = (f32[8,2176]{1,0:T(8,128)S(1)}, f32[8,2176]{1,0:T(8,128)S(1)}, u32[]{:S(2)}, u32[]{:S(2)}) collective-permute-start(f32[8,2176]{1,0:T(8,128)S(1)} %add_add_fusion.2.own_ref), channel_id=1, source_target_pairs={{0,3},{1,2},{2,1},{3,0},{4,7},{5,6},{6,5},{7,4},{8,11},{9,10},{10,... | collective-permute-start | bytes 208904 | tf_op jit(solution)/shard_map/ppermute | solution.py:264
  66.4 4.7 %collective-permute-start.19 = (f32[8,2176]{1,0:T(8,128)S(1)}, f32[8,2176]{1,0:T(8,128)S(1)}, u32[]{:S(2)}, u32[]{:S(2)}) collective-permute-start(f32[8,2176]{1,0:T(8,128)S(1)} %add_add_fusion.2.own_ref), channel_id=1, source_target_pairs={{0,1},{1,0},{2,3},{3,2},{4,5},{5,4},{6,7},{7,6},{8,9},{9,8},{10,11... | collective-permute-start | bytes 208904 | tf_op jit(solution)/shard_map/ppermute | solution.py:264
  74.0 5.9 %collective-permute-start.25 = (s16[8,4224]{1,0:T(8,128)(2,1)S(1)}, s16[8,4224]{1,0:T(8,128)(2,1)S(1)}, u32[]{:S(2)}, u32[]{:S(2)}) collective-permute-start(s16[8,4224]{1,0:T(8,128)(2,1)S(1)} %shard_map.68.own_ref), channel_id=1, source_target_pairs={{0,64},{32,96},{64,0},{96,32},{1,65},{33,97},{65,1},{97,33},{2,66}... | collective-permute-start | bytes 202760 | tf_op jit(solution)/shard_map/ppermute | solution.py:264
  76.0 5.5 %collective-permute-start.24 = (s16[8,4224]{1,0:T(8,128)(2,1)S(1)}, s16[8,4224]{1,0:T(8,128)(2,1)S(1)}, u32[]{:S(2)}, u32[]{:S(2)}) collective-permute-start(s16[8,4224]{1,0:T(8,128)(2,1)S(1)} %shard_map.68.own_ref), channel_id=1, source_target_pairs={{0,96},{32,64},{64,32},{96,0},{1,97},{33,65},{65,33},{97,1},{2,98}... | collective-permute-start | bytes 202760 | tf_op jit(solution)/shard_map/ppermute | solution.py:264
  84.9 5.7 %collective-permute-start.29 = (f32[8,2176]{1,0:T(8,128)S(1)}, f32[8,2176]{1,0:T(8,128)S(1)}, u32[]{:S(2)}, u32[]{:S(2)}) collective-permute-start(f32[8,2176]{1,0:T(8,128)S(1)} %shard_map.70), channel_id=1, source_target_pairs={{0,12},{4,8},{8,4},{12,0},{1,13},{5,9},{9,5},{13,1},{2,14},{6,10},... | collective-permute-start | bytes 208904 | tf_op jit(solution)/shard_map/ppermute | solution.py:264
  87.1 4.7 %collective-permute-start.28 = (f32[8,2176]{1,0:T(8,128)S(1)}, f32[8,2176]{1,0:T(8,128)S(1)}, u32[]{:S(2)}, u32[]{:S(2)}) collective-permute-start(f32[8,2176]{1,0:T(8,128)S(1)} %shard_map.70), channel_id=1, source_target_pairs={{0,4},{4,0},{8,12},{12,8},{1,5},{5,1},{9,13},{13,9},{2,6},{6,2},{1... | collective-permute-start | bytes 208904 | tf_op jit(solution)/shard_map/ppermute | solution.py:264
  87.1 6.2 %collective-permute-start.27 = (f32[8,2176]{1,0:T(8,128)S(1)}, f32[8,2176]{1,0:T(8,128)S(1)}, u32[]{:S(2)}, u32[]{:S(2)}) collective-permute-start(f32[8,2176]{1,0:T(8,128)S(1)} %shard_map.70), channel_id=1, source_target_pairs={{0,8},{4,12},{8,0},{12,4},{1,9},{5,13},{9,1},{13,5},{2,10},{6,14},... | collective-permute-start | bytes 208904 | tf_op jit(solution)/shard_map/ppermute | solution.py:264
  93.3 6.1 %collective-permute-start.32 = (f32[8,2176]{1,0:T(8,128)S(1)}, f32[8,2176]{1,0:T(8,128)S(1)}, u32[]{:S(2)}, u32[]{:S(2)}) collective-permute-start(f32[8,2176]{1,0:T(8,128)S(1)} %add_add_fusion.1.own_ref), channel_id=1, source_target_pairs={{0,2},{1,3},{2,0},{3,1},{4,6},{5,7},{6,4},{7,5},{8,10},{9,11},{10,... | collective-permute-start | bytes 208904 | tf_op jit(solution)/shard_map/ppermute | solution.py:264
  95.5 5.5 %collective-permute-start.31 = (f32[8,2176]{1,0:T(8,128)S(1)}, f32[8,2176]{1,0:T(8,128)S(1)}, u32[]{:S(2)}, u32[]{:S(2)}) collective-permute-start(f32[8,2176]{1,0:T(8,128)S(1)} %add_add_fusion.1.own_ref), channel_id=1, source_target_pairs={{0,3},{1,2},{2,1},{3,0},{4,7},{5,6},{6,5},{7,4},{8,11},{9,10},{10,... | collective-permute-start | bytes 208904 | tf_op jit(solution)/shard_map/ppermute | solution.py:264
  104.0 5.9 %collective-permute-start.36 = (s16[8,4224]{1,0:T(8,128)(2,1)S(1)}, s16[8,4224]{1,0:T(8,128)(2,1)S(1)}, u32[]{:S(2)}, u32[]{:S(2)}) collective-permute-start(s16[8,4224]{1,0:T(8,128)(2,1)S(1)} %shard_map.72.own_ref), channel_id=1, source_target_pairs={{0,64},{32,96},{64,0},{96,32},{1,65},{33,97},{65,1},{97,33},{2,66}... | collective-permute-start | bytes 202760 | tf_op jit(solution)/shard_map/ppermute | solution.py:264
  105.9 5.5 %collective-permute-start.35 = (s16[8,4224]{1,0:T(8,128)(2,1)S(1)}, s16[8,4224]{1,0:T(8,128)(2,1)S(1)}, u32[]{:S(2)}, u32[]{:S(2)}) collective-permute-start(s16[8,4224]{1,0:T(8,128)(2,1)S(1)} %shard_map.72.own_ref), channel_id=1, source_target_pairs={{0,96},{32,64},{64,32},{96,0},{1,97},{33,65},{65,33},{97,1},{2,98}... | collective-permute-start | bytes 202760 | tf_op jit(solution)/shard_map/ppermute | solution.py:264
  114.8 5.5 %collective-permute-start.40 = (f32[8,2176]{1,0:T(8,128)S(1)}, f32[8,2176]{1,0:T(8,128)S(1)}, u32[]{:S(2)}, u32[]{:S(2)}) collective-permute-start(f32[8,2176]{1,0:T(8,128)S(1)} %shard_map.74), channel_id=1, source_target_pairs={{0,12},{4,8},{8,4},{12,0},{1,13},{5,9},{9,5},{13,1},{2,14},{6,10},... | collective-permute-start | bytes 208904 | tf_op jit(solution)/shard_map/ppermute | solution.py:264
  116.7 4.9 %collective-permute-start.39 = (f32[8,2176]{1,0:T(8,128)S(1)}, f32[8,2176]{1,0:T(8,128)S(1)}, u32[]{:S(2)}, u32[]{:S(2)}) collective-permute-start(f32[8,2176]{1,0:T(8,128)S(1)} %shard_map.74), channel_id=1, source_target_pairs={{0,4},{4,0},{8,12},{12,8},{1,5},{5,1},{9,13},{13,9},{2,6},{6,2},{1... | collective-permute-start | bytes 208904 | tf_op jit(solution)/shard_map/ppermute | solution.py:264
  117.0 5.9 %collective-permute-start.38 = (f32[8,2176]{1,0:T(8,128)S(1)}, f32[8,2176]{1,0:T(8,128)S(1)}, u32[]{:S(2)}, u32[]{:S(2)}) collective-permute-start(f32[8,2176]{1,0:T(8,128)S(1)} %shard_map.74), channel_id=1, source_target_pairs={{0,8},{4,12},{8,0},{12,4},{1,9},{5,13},{9,1},{13,5},{2,10},{6,14},... | collective-permute-start | bytes 208904 | tf_op jit(solution)/shard_map/ppermute | solution.py:264
  123.0 6.7 %collective-permute-start.43 = (f32[8,2176]{1,0:T(8,128)S(1)}, f32[8,2176]{1,0:T(8,128)S(1)}, u32[]{:S(2)}, u32[]{:S(2)}) collective-permute-start(f32[8,2176]{1,0:T(8,128)S(1)} %add_add_fusion.own_ref), channel_id=1, source_target_pairs={{0,2},{1,3},{2,0},{3,1},{4,6},{5,7},{6,4},{7,5},{8,10},{9,11},{10,... | collective-permute-start | bytes 208904 | tf_op jit(solution)/shard_map/ppermute | solution.py:264
  124.6 5.7 %collective-permute-start.42 = (f32[8,2176]{1,0:T(8,128)S(1)}, f32[8,2176]{1,0:T(8,128)S(1)}, u32[]{:S(2)}, u32[]{:S(2)}) collective-permute-start(f32[8,2176]{1,0:T(8,128)S(1)} %add_add_fusion.own_ref), channel_id=1, source_target_pairs={{0,3},{1,2},{2,1},{3,0},{4,7},{5,6},{6,5},{7,4},{8,11},{9,10},{10,... | collective-permute-start | bytes 208904 | tf_op jit(solution)/shard_map/ppermute | solution.py:264
  131.7 5.1 %collective-permute-start.47 = (f32[8,128]{1,0:T(8,128)S(1)}, f32[8,128]{1,0:T(8,128)S(1)}, u32[]{:S(2)}, u32[]{:S(2)}) collective-permute-start(f32[8,128]{1,0:T(8,128)S(1)} %add.72.own_ref), channel_id=1, source_target_pairs={{0,64},{32,96},{64,0},{96,32},{1,65},{33,97},{65,1},{97,33},{2,66}... | collective-permute-start | bytes 12296 | tf_op jit(solution)/shard_map/ppermute | solution.py:264
  133.5 4.8 %collective-permute-start.46 = (f32[8,128]{1,0:T(8,128)S(1)}, f32[8,128]{1,0:T(8,128)S(1)}, u32[]{:S(2)}, u32[]{:S(2)}) collective-permute-start(f32[8,128]{1,0:T(8,128)S(1)} %add.72.own_ref), channel_id=1, source_target_pairs={{0,96},{32,64},{64,32},{96,0},{1,97},{33,65},{65,33},{97,1},{2,98}... | collective-permute-start | bytes 12296 | tf_op jit(solution)/shard_map/ppermute | solution.py:264
  (22 other events, 120.4 us)

commit v4 on v3

--- a/solution.py
+++ b/solution.py
@@ -35,6 +35,19 @@
 
 def wide(x):
     return jnp.broadcast_to(x, (x.shape[0], 128))
+
+
+def slots_of(pattern_ref, counts_ref, second, dead):
+    blocks = BLK_DEV // 2
+    core = lax.axis_index("core")
+
+    def block_of(b, s):
+        found = pattern_ref[s, b]
+        within = found % blocks
+        at = jnp.where(found // blocks == core, within, within + second)
+        return jnp.where(s < counts_ref[0, b], at, dead)
+
+    return block_of
 
 
 def scatter_products(u, block_of, tiles_ref, keep_ref, send_ref, acc_ref, copies=None):
@@ -57,28 +70,25 @@
 
 
 def first_adjoint(
-    pattern_ref, counts_ref, source_u_ref, source_ref, keep_ref, send_ref, tiles_ref, acc_ref,
-    u_ref, sem,
+    source_p_ref, source_c_ref, source_u_ref, source_ref, keep_ref, send_ref, tiles_ref, acc_ref,
+    pattern_ref, counts_ref, u_ref, sem,
 ):
     bundles = source_ref.shape[0]
-    copies = [pltpu.make_async_copy(source_u_ref, u_ref, sem.at[bundles])] + [
+    small = ((source_p_ref, pattern_ref), (source_c_ref, counts_ref), (source_u_ref, u_ref))
+    first = [
+        pltpu.make_async_copy(source, target, sem.at[bundles + at])
+        for at, (source, target) in enumerate(small)
+    ]
+    copies = [
         pltpu.make_async_copy(source_ref.at[b], tiles_ref.at[b], sem.at[b])
         for b in range(bundles)
     ]
-    for copy in copies:
+    for copy in first + copies:
         copy.start()
-    core = lax.axis_index("core")
-    blocks = BLK_DEV // 2
-
-    def block_of(b, s):
-        found = pattern_ref[b, s]
-        upper = (found >= blocks).astype(jnp.int32)
-        within = found - blocks * upper
-        at = jnp.where(upper == core, within, within + blocks + 1)
-        return jnp.where(s < counts_ref[b, 0], at, blocks)
-
-    copies[0].wait()
-    scatter_products(u_ref[...], block_of, tiles_ref, keep_ref, send_ref, acc_ref, copies[1:])
+    for copy in first:
+        copy.wait()
+    put = slots_of(pattern_ref, counts_ref, BLK_DEV // 2 + 1, BLK_DEV // 2)
+    scatter_products(u_ref[...], put, tiles_ref, keep_ref, send_ref, acc_ref, copies)
 
 
 def ray_vector(own_ref, left_ref, right_ref, far_ref, prev_ref, beta_ref):
@@ -90,16 +100,14 @@
 
 
 def next_adjoint(
-    place_ref, own_ref, left_ref, right_ref, far_ref, prev_ref, beta_ref, tiles_ref,
+    pattern_ref, counts_ref, own_ref, left_ref, right_ref, far_ref, prev_ref, beta_ref, tiles_ref,
     keep_ref, send_ref, u_ref, alpha_ref, acc_ref,
 ):
     u, alpha = ray_vector(own_ref, left_ref, right_ref, far_ref, prev_ref, beta_ref)
     u_ref[...] = u
     alpha_ref[...] = wide(alpha)
-    slots = tiles_ref.shape[1]
-    scatter_products(
-        u, lambda b, s: place_ref[b * slots + s], tiles_ref, keep_ref, send_ref, acc_ref
-    )
+    put = slots_of(pattern_ref, counts_ref, BLK_DEV // 2 + 1, BLK_DEV // 2)
+    scatter_products(u, put, tiles_ref, keep_ref, send_ref, acc_ref)
 
 
 def last_norm(
@@ -159,18 +167,18 @@
     beta_ref[...] = wide(beta)
 
 
-def forward(place_ref, own_ref, other_ref, tiles_ref, out_ref, low_ref):
+def forward(pattern_ref, counts_ref, own_ref, other_ref, tiles_ref, out_ref, low_ref):
     bundles, slots, rays, cells = tiles_ref.shape
     width = own_ref.shape[1]
     own, other = own_ref[...], other_ref[...]
     low_ref[:, :width] = own.astype(BF16)
     low_ref[:, width : 2 * width] = other.astype(BF16)
     low_ref[:, 2 * width :] = jnp.zeros((own.shape[0], cells), BF16)
-    base = bundles * slots
+    get = slots_of(pattern_ref, counts_ref, BLK_DEV // 2, BLK_DEV)
     for b in range(bundles):
         acc = None
         for s in range(slots):
-            at = pl.multiple_of(place_ref[base + b * slots + s] * cells, cells)
+            at = pl.multiple_of(get(b, s) * cells, cells)
             part = lax.dot_general(
                 low_ref[:, pl.ds(at, cells)], tiles_ref[b, s],
                 (((1,), (1,)), ((), ())), preferred_element_type=F32,
@@ -212,7 +220,7 @@
 
 
 def finish(
-    place_ref, own_ref, left_ref, right_ref, far_ref, own_x_ref, other_x_ref, own_w_ref,
+    own_ref, left_ref, right_ref, far_ref, own_x_ref, other_x_ref, own_w_ref,
     other_w_ref, phibar_ref, rhobar_ref, x_ref, misfit_ref,
 ):
     width = own_x_ref.shape[1]
@@ -221,14 +229,15 @@
     phibar, rhobar = phibar_ref[:, :1], rhobar_ref[:, :1]
     rho = jnp.sqrt(rhobar * rhobar + beta * beta)
     step = (rhobar / rho) * phibar / rho
-    core = place_ref[place_ref.shape[0] - 1]
+    core = lax.axis_index("core")
     for half, xs_ref, w_ref in ((core, own_x_ref, own_w_ref), (1 - core, other_x_ref, other_w_ref)):
         at = pl.multiple_of(half * width, width)
         x_ref[:, pl.ds(at, width)] = xs_ref[...] + step * w_ref[...]
     last = wide((beta / rho) * phibar)
     row = lax.broadcasted_iota(jnp.int32, last.shape, 0)
     lane = lax.broadcasted_iota(jnp.int32, last.shape, 1)
-    misfit_ref[...] = jnp.sum(jnp.where(row == lane, last, 0.0), axis=0, keepdims=True)
+    across = jnp.sum(jnp.where(row == lane, last, 0.0), axis=0, keepdims=True)
+    misfit_ref[...] = across[:, : misfit_ref.shape[1]]
 
 
 def call(body, outs, specs, args, scratch=()):
@@ -247,13 +256,7 @@
     bundles, slots, rays, cells = tiles.shape
     blocks = BLK_DEV // 2
     half = blocks * cells
-    core = lax.axis_index("core")
-    live = lax.broadcasted_iota(jnp.int32, pattern.shape, 1) < counts
-    mine = pattern // blocks == core
-    within = pattern % blocks
-    put = jnp.where(live, jnp.where(mine, within, blocks + 1 + within), blocks)
-    get = jnp.where(live, jnp.where(mine, within, blocks + within), BLK_DEV)
-    place = jnp.concatenate([put.reshape(-1), get.reshape(-1), core.astype(jnp.int32).reshape(1)])
+    slots_in = (pattern.T, counts.T)
 
     def shape(columns, dtype=F32):
         return jax.ShapeDtypeStruct((nrhs, columns), dtype)
@@ -276,11 +279,12 @@
     store = [pltpu.VMEM((nrhs, 2 * (half + cells)), F32)]
     keep, send, tiles = call(
         first_adjoint, halves + [jax.ShapeDtypeStruct(tiles.shape, tiles.dtype)],
-        [SMEM, SMEM, HBM, HBM], (
-            pattern, counts, pltpu.with_memory_space_constraint(right_side, pltpu.HBM),
-            pltpu.with_memory_space_constraint(tiles, pltpu.HBM),
-        ),
-        store + [pltpu.VMEM(right_side.shape, F32), pltpu.SemaphoreType.DMA((bundles + 1,))],
+        [HBM] * 4,
+        [pltpu.with_memory_space_constraint(z, pltpu.HBM) for z in (*slots_in, right_side, tiles)],
+        store + [
+            pltpu.SMEM((slots, bundles), jnp.int32), pltpu.SMEM((1, bundles), jnp.int32),
+            pltpu.VMEM(right_side.shape, F32), pltpu.SemaphoreType.DMA((bundles + 3,)),
+        ],
     )
     u = right_side
     owns, others, alphas, betas = [], [], [], []
@@ -298,14 +302,14 @@
         others.append(other)
         betas.append(beta)
         products, = call(
-            forward, [shape(rows + 128)], [SMEM] + [VMEM] * 3, (place, v, other, tiles),
+            forward, [shape(rows + 128)], [SMEM] * 2 + [VMEM] * 3, (*slots_in, v, other, tiles),
             [pltpu.VMEM((nrhs, 2 * half + cells), BF16)],
         )
         rows_in = over_cell(products)
         if step + 1 < ITERS:
             keep, send, u, alpha = call(
-                next_adjoint, halves + [shape(rows), shape(128)], [SMEM] + [VMEM] * 7,
-                (place, *rows_in, u, beta, tiles), store,
+                next_adjoint, halves + [shape(rows), shape(128)], [SMEM] * 2 + [VMEM] * 7,
+                (*slots_in, *rows_in, u, beta, tiles), store,
             )
         else:
             squares, alpha = call(
@@ -317,10 +321,10 @@
         (*owns, *others, *alphas, *betas),
     )
     x, misfit = call(
-        finish, [shape(2 * half), jax.ShapeDtypeStruct((1, 128), F32)], [SMEM] + [VMEM] * 10,
-        (place, *spread(squares + swap(squares), "z"), *so_far),
+        finish, [shape(2 * half), jax.ShapeDtypeStruct((1, nrhs), F32)], [VMEM] * 10,
+        (*spread(squares + swap(squares), "z"), *so_far),
     )
-    return x, misfit[0, :nrhs]
+    return x, misfit.reshape(nrhs)
 
 
 def solution(mesh):

time: 141 us -> 133 us (0.943)
  local copies, waits for them, and re-layouts: 6.55 us -> 0.01 us
    unnamed x14 -> x6, local copies, waits for them, and re-layouts: 5.72 us -> 0.01 us
where the time goes in v4:
time: 133 us
  waiting for transfers between devices  61.5 us (46%)
  starting transfers between devices  54.1 us (41%)
  Pallas kernels  16.7 us (13%)
    ppermute x39, starting transfers between devices, spread(): lax.ppermute(value, axis, [(i, i ^ by) for i in range(n)])  53.2 us
    ppermute x39, waiting for transfers between devices, spread(): lax.ppermute(value, axis, [(i, i ^ by) for i in range(n)])  49.7 us
    pallas_call x19, Pallas kernels, call(): pl.pallas_call(body, out_shape=outs, in_specs=specs, out_specs=[VMEM] * l...  16.7 us
    ppermute x9, waiting for transfers between devices, swap(): return lax.ppermute(value, 'core', [(0, 1), (1, 0)])  11.9 us
  transfers between devices with their start and end apart: 48, of which 39 were waited for; matrix products, arithmetic and copies ran while one was open for 0% of the time, Pallas kernels for 0%

profile of v4, /device:TPU:0, one launch (start us, length us, event | category | flops | bytes accessed | tf_op | source)
XLA Modules:
  0.0 133.3 jit_solution(1601863870920232067)
XLA Ops:
  0.7 2.7 %shard_map.59 = (f32[8,4224]{1,0:T(8,128)S(1)}, f32[8,4224]{1,0:T(8,128)S(1)}, bf16[8,4,256,256]{3,2,1,0:T(8,128)(2,1)S(1)}) custom-call(s32[4,8]{1,0:T(4,128)} %bitcast.3, s32[1,8]{1,0:T(1,128)} %bitcast.11, f32[8,2048]{1,0:T(8,128)} %prev_ref.3, bf16[8,4,256,256]{3,2,1,0:T(8,128)(2,1)} %source_ref.1), custom_call_target="tpu_custom_call" | custom-call | tf_op jit(solution)/shard_map/pallas_call | solution.py:244
  5.0 4.0 %collective-permute-start.3 = (s16[8,4224]{1,0:T(8,128)(2,1)S(1)}, s16[8,4224]{1,0:T(8,128)(2,1)S(1)}, u32[]{:S(2)}, u32[]{:S(2)}) collective-permute-start(s16[8,4224]{1,0:T(8,128)(2,1)S(1)} %shard_map.60.own_ref), channel_id=1, source_target_pairs={{0,64},{32,96},{64,0},{96,32},{1,65},{33,97},{65,1},{97,33},{2,66}... | collective-permute-start | bytes 202760 | tf_op jit(solution)/shard_map/ppermute | solution.py:267
  11.5 3.0 %collective-permute-done.2.right_ref = s16[8,4224]{1,0:T(8,128)(2,1)S(1)} collective-permute-done((s16[8,4224]{1,0:T(8,128)(2,1)S(1)}, s16[8,4224]{1,0:T(8,128)(2,1)S(1)}, u32[]{:S(2)}, u32[]{:S(2)}) %collective-permute-start.2) | collective-permute-done | bytes 67616 | tf_op jit(solution)/shard_map/ppermute | solution.py:267
  16.2 1.8 %shard_map.62 = f32[8,2176]{1,0:T(8,128)S(1)} custom-call(s32[4,8]{1,0:T(4,128)S(1)} %bitcast.4, s32[1,8]{1,0:T(1,128)S(1)} %bitcast.12, f32[8,4096]{1,0:T(8,128)S(1)} %get-tuple-element.37.own_ref.prev_ref.refs_0_, f32[8,4096]{1,0:T(8,128)S(1)} %collective-permute-done.4.other_ref.refs_4_, bf16[8,4,256,256]{3,2,1,0:T(8,128)(2,1)S(1)} %get-tuple-element.38.tiles_ref), custom_call_target="tpu_custom_call" | custom-call | tf_op jit(solution)/shard_map/pallas_call | solution.py:244
  17.9 2.8 %collective-permute-start.7 = (f32[8,2176]{1,0:T(8,128)S(1)}, f32[8,2176]{1,0:T(8,128)S(1)}, u32[]{:S(2)}, u32[]{:S(2)}) collective-permute-start(f32[8,2176]{1,0:T(8,128)S(1)} %shard_map.62), channel_id=1, source_target_pairs={{0,12},{4,8},{8,4},{12,0},{1,13},{5,9},{9,5},{13,1},{2,14},{6,10},... | collective-permute-start | bytes 208904 | tf_op jit(solution)/shard_map/ppermute | solution.py:267
  20.9 1.7 %collective-permute-start.5 = (f32[8,2176]{1,0:T(8,128)S(1)}, f32[8,2176]{1,0:T(8,128)S(1)}, u32[]{:S(2)}, u32[]{:S(2)}) collective-permute-start(f32[8,2176]{1,0:T(8,128)S(1)} %shard_map.62), channel_id=1, source_target_pairs={{0,8},{4,12},{8,0},{12,4},{1,9},{5,13},{9,1},{13,5},{2,10},{6,14},... | collective-permute-start | bytes 208904 | tf_op jit(solution)/shard_map/ppermute | solution.py:267
  23.5 1.9 %collective-permute-done.6 = f32[8,2176]{1,0:T(8,128)S(1)} collective-permute-done((f32[8,2176]{1,0:T(8,128)S(1)}, f32[8,2176]{1,0:T(8,128)S(1)}, u32[]{:S(2)}, u32[]{:S(2)}) %collective-permute-start.6) | collective-permute-done | bytes 69664 | tf_op jit(solution)/shard_map/ppermute | solution.py:267
  26.7 3.3 %collective-permute-start.10 = (f32[8,2176]{1,0:T(8,128)S(1)}, f32[8,2176]{1,0:T(8,128)S(1)}, u32[]{:S(2)}, u32[]{:S(2)}) collective-permute-start(f32[8,2176]{1,0:T(8,128)S(1)} %add_add_fusion.3.own_ref), channel_id=1, source_target_pairs={{0,2},{1,3},{2,0},{3,1},{4,6},{5,7},{6,4},{7,5},{8,10},{9,11},{10,... | collective-permute-start | bytes 208904 | tf_op jit(solution)/shard_map/ppermute | solution.py:267
  32.7 2.9 %collective-permute-done.9.right_ref = f32[8,2176]{1,0:T(8,128)S(1)} collective-permute-done((f32[8,2176]{1,0:T(8,128)S(1)}, f32[8,2176]{1,0:T(8,128)S(1)}, u32[]{:S(2)}, u32[]{:S(2)}) %collective-permute-start.9) | collective-permute-done | bytes 69664 | tf_op jit(solution)/shard_map/ppermute | solution.py:267
  38.5 2.0 %collective-permute-start.14 = (s16[8,4224]{1,0:T(8,128)(2,1)S(1)}, s16[8,4224]{1,0:T(8,128)(2,1)S(1)}, u32[]{:S(2)}, u32[]{:S(2)}) collective-permute-start(s16[8,4224]{1,0:T(8,128)(2,1)S(1)} %shard_map.64.own_ref), channel_id=1, source_target_pairs={{0,64},{32,96},{64,0},{96,32},{1,65},{33,97},{65,1},{97,33},{2,66}... | collective-permute-start | bytes 202760 | tf_op jit(solution)/shard_map/ppermute | solution.py:267
  42.1 2.3 %collective-permute-done.14.far_ref = s16[8,4224]{1,0:T(8,128)(2,1)S(1)} collective-permute-done((s16[8,4224]{1,0:T(8,128)(2,1)S(1)}, s16[8,4224]{1,0:T(8,128)(2,1)S(1)}, u32[]{:S(2)}, u32[]{:S(2)}) %collective-permute-start.14) | collective-permute-done | bytes 67616 | tf_op jit(solution)/shard_map/ppermute | solution.py:267
  47.6 1.7 %shard_map.66 = f32[8,2176]{1,0:T(8,128)S(1)} custom-call(s32[4,8]{1,0:T(4,128)S(1)} %bitcast.6, s32[1,8]{1,0:T(1,128)S(1)} %bitcast.14, f32[8,4096]{1,0:T(8,128)S(1)} %get-tuple-element.43.own_ref.prev_ref.refs_1_, f32[8,4096]{1,0:T(8,128)S(1)} %collective-permute-done.15.other_ref.refs_5_, bf16[8,4,256,256]{3,2,1,0:T(8,128)(2,1)S(1)} %get-tuple-element.38.tiles_ref), custom_call_target="tpu_custom_call" | custom-call | tf_op jit(solution)/shard_map/pallas_call | solution.py:244
  49.4 2.1 %collective-permute-start.18 = (f32[8,2176]{1,0:T(8,128)S(1)}, f32[8,2176]{1,0:T(8,128)S(1)}, u32[]{:S(2)}, u32[]{:S(2)}) collective-permute-start(f32[8,2176]{1,0:T(8,128)S(1)} %shard_map.66), channel_id=1, source_target_pairs={{0,12},{4,8},{8,4},{12,0},{1,13},{5,9},{9,5},{13,1},{2,14},{6,10},... | collective-permute-start | bytes 208904 | tf_op jit(solution)/shard_map/ppermute | solution.py:267
  51.5 2.6 %collective-permute-start.16 = (f32[8,2176]{1,0:T(8,128)S(1)}, f32[8,2176]{1,0:T(8,128)S(1)}, u32[]{:S(2)}, u32[]{:S(2)}) collective-permute-start(f32[8,2176]{1,0:T(8,128)S(1)} %shard_map.66), channel_id=1, source_target_pairs={{0,8},{4,12},{8,0},{12,4},{1,9},{5,13},{9,1},{13,5},{2,10},{6,14},... | collective-permute-start | bytes 208904 | tf_op jit(solution)/shard_map/ppermute | solution.py:267
  57.7 1.6 %collective-permute-start.21 = (f32[8,2176]{1,0:T(8,128)S(1)}, f32[8,2176]{1,0:T(8,128)S(1)}, u32[]{:S(2)}, u32[]{:S(2)}) collective-permute-start(f32[8,2176]{1,0:T(8,128)S(1)} %add_add_fusion.2.own_ref), channel_id=1, source_target_pairs={{0,2},{1,3},{2,0},{3,1},{4,6},{5,7},{6,4},{7,5},{8,10},{9,11},{10,... | collective-permute-start | bytes 208904 | tf_op jit(solution)/shard_map/ppermute | solution.py:267
  61.3 3.0 %collective-permute-done.21.far_ref = f32[8,2176]{1,0:T(8,128)S(1)} collective-permute-done((f32[8,2176]{1,0:T(8,128)S(1)}, f32[8,2176]{1,0:T(8,128)S(1)}, u32[]{:S(2)}, u32[]{:S(2)}) %collective-permute-start.21) | collective-permute-done | bytes 69664 | tf_op jit(solution)/shard_map/ppermute | solution.py:267
  67.9 1.9 %collective-permute-start.25 = (s16[8,4224]{1,0:T(8,128)(2,1)S(1)}, s16[8,4224]{1,0:T(8,128)(2,1)S(1)}, u32[]{:S(2)}, u32[]{:S(2)}) collective-permute-start(s16[8,4224]{1,0:T(8,128)(2,1)S(1)} %shard_map.68.own_ref), channel_id=1, source_target_pairs={{0,64},{32,96},{64,0},{96,32},{1,65},{33,97},{65,1},{97,33},{2,66}... | collective-permute-start | bytes 202760 | tf_op jit(solution)/shard_map/ppermute | solution.py:267
  71.5 2.3 %collective-permute-done.25.far_ref = s16[8,4224]{1,0:T(8,128)(2,1)S(1)} collective-permute-done((s16[8,4224]{1,0:T(8,128)(2,1)S(1)}, s16[8,4224]{1,0:T(8,128)(2,1)S(1)}, u32[]{:S(2)}, u32[]{:S(2)}) %collective-permute-start.25) | collective-permute-done | bytes 67616 | tf_op jit(solution)/shard_map/ppermute | solution.py:267
  77.2 1.7 %shard_map.70 = f32[8,2176]{1,0:T(8,128)S(1)} custom-call(s32[4,8]{1,0:T(4,128)S(1)} %bitcast.8, s32[1,8]{1,0:T(1,128)S(1)} %bitcast.16, f32[8,4096]{1,0:T(8,128)S(1)} %get-tuple-element.49.own_ref.prev_ref.refs_2_, f32[8,4096]{1,0:T(8,128)S(1)} %collective-permute-done.26.other_ref.refs_6_, bf16[8,4,256,256]{3,2,1,0:T(8,128)(2,1)S(1)} %get-tuple-element.38.tiles_ref), custom_call_target="tpu_custom_call" | custom-call | tf_op jit(solution)/shard_map/pallas_call | solution.py:244
  78.9 2.1 %collective-permute-start.29 = (f32[8,2176]{1,0:T(8,128)S(1)}, f32[8,2176]{1,0:T(8,128)S(1)}, u32[]{:S(2)}, u32[]{:S(2)}) collective-permute-start(f32[8,2176]{1,0:T(8,128)S(1)} %shard_map.70), channel_id=1, source_target_pairs={{0,12},{4,8},{8,4},{12,0},{1,13},{5,9},{9,5},{13,1},{2,14},{6,10},... | collective-permute-start | bytes 208904 | tf_op jit(solution)/shard_map/ppermute | solution.py:267
  81.0 2.6 %collective-permute-start.27 = (f32[8,2176]{1,0:T(8,128)S(1)}, f32[8,2176]{1,0:T(8,128)S(1)}, u32[]{:S(2)}, u32[]{:S(2)}) collective-permute-start(f32[8,2176]{1,0:T(8,128)S(1)} %shard_map.70), channel_id=1, source_target_pairs={{0,8},{4,12},{8,0},{12,4},{1,9},{5,13},{9,1},{13,5},{2,10},{6,14},... | collective-permute-start | bytes 208904 | tf_op jit(solution)/shard_map/ppermute | solution.py:267
  87.3 2.2 %collective-permute-start.32 = (f32[8,2176]{1,0:T(8,128)S(1)}, f32[8,2176]{1,0:T(8,128)S(1)}, u32[]{:S(2)}, u32[]{:S(2)}) collective-permute-start(f32[8,2176]{1,0:T(8,128)S(1)} %add_add_fusion.1.own_ref), channel_id=1, source_target_pairs={{0,2},{1,3},{2,0},{3,1},{4,6},{5,7},{6,4},{7,5},{8,10},{9,11},{10,... | collective-permute-start | bytes 208904 | tf_op jit(solution)/shard_map/ppermute | solution.py:267
  90.8 2.5 %collective-permute-done.32.far_ref = f32[8,2176]{1,0:T(8,128)S(1)} collective-permute-done((f32[8,2176]{1,0:T(8,128)S(1)}, f32[8,2176]{1,0:T(8,128)S(1)}, u32[]{:S(2)}, u32[]{:S(2)}) %collective-permute-start.32) | collective-permute-done | bytes 69664 | tf_op jit(solution)/shard_map/ppermute | solution.py:267
  93.4 1.6 %collective-permute-done.31.right_ref = f32[8,2176]{1,0:T(8,128)S(1)} collective-permute-done((f32[8,2176]{1,0:T(8,128)S(1)}, f32[8,2176]{1,0:T(8,128)S(1)}, u32[]{:S(2)}, u32[]{:S(2)}) %collective-permute-start.31) | collective-permute-done | bytes 69664 | tf_op jit(solution)/shard_map/ppermute | solution.py:267
  97.9 1.9 %collective-permute-start.36 = (s16[8,4224]{1,0:T(8,128)(2,1)S(1)}, s16[8,4224]{1,0:T(8,128)(2,1)S(1)}, u32[]{:S(2)}, u32[]{:S(2)}) collective-permute-start(s16[8,4224]{1,0:T(8,128)(2,1)S(1)} %shard_map.72.own_ref), channel_id=1, source_target_pairs={{0,64},{32,96},{64,0},{96,32},{1,65},{33,97},{65,1},{97,33},{2,66}... | collective-permute-start | bytes 202760 | tf_op jit(solution)/shard_map/ppermute | solution.py:267
  101.5 2.3 %collective-permute-done.36.far_ref = s16[8,4224]{1,0:T(8,128)(2,1)S(1)} collective-permute-done((s16[8,4224]{1,0:T(8,128)(2,1)S(1)}, s16[8,4224]{1,0:T(8,128)(2,1)S(1)}, u32[]{:S(2)}, u32[]{:S(2)}) %collective-permute-start.36) | collective-permute-done | bytes 67616 | tf_op jit(solution)/shard_map/ppermute | solution.py:267
  107.0 1.8 %shard_map.74 = f32[8,2176]{1,0:T(8,128)S(1)} custom-call(s32[4,8]{1,0:T(4,128)S(1)} %bitcast.10, s32[1,8]{1,0:T(1,128)S(1)} %bitcast.18, f32[8,4096]{1,0:T(8,128)S(1)} %get-tuple-element.55.own_ref.refs_3_, f32[8,4096]{1,0:T(8,128)S(1)} %collective-permute-done.37.other_ref.refs_7_, bf16[8,4,256,256]{3,2,1,0:T(8,128)(2,1)S(1)} %get-tuple-element.38.tiles_ref), custom_call_target="tpu_custom_call" | custom-call | tf_op jit(solution)/shard_map/pallas_call | solution.py:244
  108.8 1.9 %collective-permute-start.40 = (f32[8,2176]{1,0:T(8,128)S(1)}, f32[8,2176]{1,0:T(8,128)S(1)}, u32[]{:S(2)}, u32[]{:S(2)}) collective-permute-start(f32[8,2176]{1,0:T(8,128)S(1)} %shard_map.74), channel_id=1, source_target_pairs={{0,12},{4,8},{8,4},{12,0},{1,13},{5,9},{9,5},{13,1},{2,14},{6,10},... | collective-permute-start | bytes 208904 | tf_op jit(solution)/shard_map/ppermute | solution.py:267
  111.0 2.5 %collective-permute-start.38 = (f32[8,2176]{1,0:T(8,128)S(1)}, f32[8,2176]{1,0:T(8,128)S(1)}, u32[]{:S(2)}, u32[]{:S(2)}) collective-permute-start(f32[8,2176]{1,0:T(8,128)S(1)} %shard_map.74), channel_id=1, source_target_pairs={{0,8},{4,12},{8,0},{12,4},{1,9},{5,13},{9,1},{13,5},{2,10},{6,14},... | collective-permute-start | bytes 208904 | tf_op jit(solution)/shard_map/ppermute | solution.py:267
  117.0 1.6 %collective-permute-start.43 = (f32[8,2176]{1,0:T(8,128)S(1)}, f32[8,2176]{1,0:T(8,128)S(1)}, u32[]{:S(2)}, u32[]{:S(2)}) collective-permute-start(f32[8,2176]{1,0:T(8,128)S(1)} %add_add_fusion.own_ref), channel_id=1, source_target_pairs={{0,2},{1,3},{2,0},{3,1},{4,6},{5,7},{6,4},{7,5},{8,10},{9,11},{10,... | collective-permute-start | bytes 208904 | tf_op jit(solution)/shard_map/ppermute | solution.py:267
  120.5 3.0 %collective-permute-done.43.far_ref = f32[8,2176]{1,0:T(8,128)S(1)} collective-permute-done((f32[8,2176]{1,0:T(8,128)S(1)}, f32[8,2176]{1,0:T(8,128)S(1)}, u32[]{:S(2)}, u32[]{:S(2)}) %collective-permute-start.43) | collective-permute-done | bytes 69664 | tf_op jit(solution)/shard_map/ppermute | solution.py:267
  125.6 1.9 %collective-permute-start.47 = (f32[8,128]{1,0:T(8,128)S(1)}, f32[8,128]{1,0:T(8,128)S(1)}, u32[]{:S(2)}, u32[]{:S(2)}) collective-permute-start(f32[8,128]{1,0:T(8,128)S(1)} %add.51.own_ref), channel_id=1, source_target_pairs={{0,64},{32,96},{64,0},{96,32},{1,65},{33,97},{65,1},{97,33},{2,66}... | collective-permute-start | bytes 12296 | tf_op jit(solution)/shard_map/ppermute | solution.py:267
  (94 shorter events, 58.9 us)
Async XLA Ops:
  5.0 6.5 %collective-permute-start.3 = (s16[8,4224]{1,0:T(8,128)(2,1)S(1)}, s16[8,4224]{1,0:T(8,128)(2,1)S(1)}, u32[]{:S(2)}, u32[]{:S(2)}) collective-permute-start(s16[8,4224]{1,0:T(8,128)(2,1)S(1)} %shard_map.60.own_ref), channel_id=1, source_target_pairs={{0,64},{32,96},{64,0},{96,32},{1,65},{33,97},{65,1},{97,33},{2,66}... | collective-permute-start | bytes 202760 | tf_op jit(solution)/shard_map/ppermute | solution.py:267
  9.0 5.5 %collective-permute-start.2 = (s16[8,4224]{1,0:T(8,128)(2,1)S(1)}, s16[8,4224]{1,0:T(8,128)(2,1)S(1)}, u32[]{:S(2)}, u32[]{:S(2)}) collective-permute-start(s16[8,4224]{1,0:T(8,128)(2,1)S(1)} %shard_map.60.own_ref), channel_id=1, source_target_pairs={{0,96},{32,64},{64,32},{96,0},{1,97},{33,65},{65,33},{97,1},{2,98}... | collective-permute-start | bytes 202760 | tf_op jit(solution)/shard_map/ppermute | solution.py:267
  9.7 4.8 %collective-permute-start.1 = (s16[8,4224]{1,0:T(8,128)(2,1)S(1)}, s16[8,4224]{1,0:T(8,128)(2,1)S(1)}, u32[]{:S(2)}, u32[]{:S(2)}) collective-permute-start(s16[8,4224]{1,0:T(8,128)(2,1)S(1)} %shard_map.60.own_ref), channel_id=1, source_target_pairs={{0,32},{32,0},{64,96},{96,64},{1,33},{33,1},{65,97},{97,65},{2,34}... | collective-permute-start | bytes 202760 | tf_op jit(solution)/shard_map/ppermute | solution.py:267
  17.9 5.5 %collective-permute-start.7 = (f32[8,2176]{1,0:T(8,128)S(1)}, f32[8,2176]{1,0:T(8,128)S(1)}, u32[]{:S(2)}, u32[]{:S(2)}) collective-permute-start(f32[8,2176]{1,0:T(8,128)S(1)} %shard_map.62), channel_id=1, source_target_pairs={{0,12},{4,8},{8,4},{12,0},{1,13},{5,9},{9,5},{13,1},{2,14},{6,10},... | collective-permute-start | bytes 208904 | tf_op jit(solution)/shard_map/ppermute | solution.py:267
  20.7 4.7 %collective-permute-start.6 = (f32[8,2176]{1,0:T(8,128)S(1)}, f32[8,2176]{1,0:T(8,128)S(1)}, u32[]{:S(2)}, u32[]{:S(2)}) collective-permute-start(f32[8,2176]{1,0:T(8,128)S(1)} %shard_map.62), channel_id=1, source_target_pairs={{0,4},{4,0},{8,12},{12,8},{1,5},{5,1},{9,13},{13,9},{2,6},{6,2},{1... | collective-permute-start | bytes 208904 | tf_op jit(solution)/shard_map/ppermute | solution.py:267
  20.9 5.8 %collective-permute-start.5 = (f32[8,2176]{1,0:T(8,128)S(1)}, f32[8,2176]{1,0:T(8,128)S(1)}, u32[]{:S(2)}, u32[]{:S(2)}) collective-permute-start(f32[8,2176]{1,0:T(8,128)S(1)} %shard_map.62), channel_id=1, source_target_pairs={{0,8},{4,12},{8,0},{12,4},{1,9},{5,13},{9,1},{13,5},{2,10},{6,14},... | collective-permute-start | bytes 208904 | tf_op jit(solution)/shard_map/ppermute | solution.py:267
  26.7 5.9 %collective-permute-start.10 = (f32[8,2176]{1,0:T(8,128)S(1)}, f32[8,2176]{1,0:T(8,128)S(1)}, u32[]{:S(2)}, u32[]{:S(2)}) collective-permute-start(f32[8,2176]{1,0:T(8,128)S(1)} %add_add_fusion.3.own_ref), channel_id=1, source_target_pairs={{0,2},{1,3},{2,0},{3,1},{4,6},{5,7},{6,4},{7,5},{8,10},{9,11},{10,... | collective-permute-start | bytes 208904 | tf_op jit(solution)/shard_map/ppermute | solution.py:267
  30.0 5.5 %collective-permute-start.9 = (f32[8,2176]{1,0:T(8,128)S(1)}, f32[8,2176]{1,0:T(8,128)S(1)}, u32[]{:S(2)}, u32[]{:S(2)}) collective-permute-start(f32[8,2176]{1,0:T(8,128)S(1)} %add_add_fusion.3.own_ref), channel_id=1, source_target_pairs={{0,3},{1,2},{2,1},{3,0},{4,7},{5,6},{6,5},{7,4},{8,11},{9,10},{10,... | collective-permute-start | bytes 208904 | tf_op jit(solution)/shard_map/ppermute | solution.py:267
  38.5 5.9 %collective-permute-start.14 = (s16[8,4224]{1,0:T(8,128)(2,1)S(1)}, s16[8,4224]{1,0:T(8,128)(2,1)S(1)}, u32[]{:S(2)}, u32[]{:S(2)}) collective-permute-start(s16[8,4224]{1,0:T(8,128)(2,1)S(1)} %shard_map.64.own_ref), channel_id=1, source_target_pairs={{0,64},{32,96},{64,0},{96,32},{1,65},{33,97},{65,1},{97,33},{2,66}... | collective-permute-start | bytes 202760 | tf_op jit(solution)/shard_map/ppermute | solution.py:267
  40.5 5.5 %collective-permute-start.13 = (s16[8,4224]{1,0:T(8,128)(2,1)S(1)}, s16[8,4224]{1,0:T(8,128)(2,1)S(1)}, u32[]{:S(2)}, u32[]{:S(2)}) collective-permute-start(s16[8,4224]{1,0:T(8,128)(2,1)S(1)} %shard_map.64.own_ref), channel_id=1, source_target_pairs={{0,96},{32,64},{64,32},{96,0},{1,97},{33,65},{65,33},{97,1},{2,98}... | collective-permute-start | bytes 202760 | tf_op jit(solution)/shard_map/ppermute | solution.py:267
  49.4 5.5 %collective-permute-start.18 = (f32[8,2176]{1,0:T(8,128)S(1)}, f32[8,2176]{1,0:T(8,128)S(1)}, u32[]{:S(2)}, u32[]{:S(2)}) collective-permute-start(f32[8,2176]{1,0:T(8,128)S(1)} %shard_map.66), channel_id=1, source_target_pairs={{0,12},{4,8},{8,4},{12,0},{1,13},{5,9},{9,5},{13,1},{2,14},{6,10},... | collective-permute-start | bytes 208904 | tf_op jit(solution)/shard_map/ppermute | solution.py:267
  51.5 4.9 %collective-permute-start.17 = (f32[8,2176]{1,0:T(8,128)S(1)}, f32[8,2176]{1,0:T(8,128)S(1)}, u32[]{:S(2)}, u32[]{:S(2)}) collective-permute-start(f32[8,2176]{1,0:T(8,128)S(1)} %shard_map.66), channel_id=1, source_target_pairs={{0,4},{4,0},{8,12},{12,8},{1,5},{5,1},{9,13},{13,9},{2,6},{6,2},{1... | collective-permute-start | bytes 208904 | tf_op jit(solution)/shard_map/ppermute | solution.py:267
  51.5 6.2 %collective-permute-start.16 = (f32[8,2176]{1,0:T(8,128)S(1)}, f32[8,2176]{1,0:T(8,128)S(1)}, u32[]{:S(2)}, u32[]{:S(2)}) collective-permute-start(f32[8,2176]{1,0:T(8,128)S(1)} %shard_map.66), channel_id=1, source_target_pairs={{0,8},{4,12},{8,0},{12,4},{1,9},{5,13},{9,1},{13,5},{2,10},{6,14},... | collective-permute-start | bytes 208904 | tf_op jit(solution)/shard_map/ppermute | solution.py:267
  57.7 6.6 %collective-permute-start.21 = (f32[8,2176]{1,0:T(8,128)S(1)}, f32[8,2176]{1,0:T(8,128)S(1)}, u32[]{:S(2)}, u32[]{:S(2)}) collective-permute-start(f32[8,2176]{1,0:T(8,128)S(1)} %add_add_fusion.2.own_ref), channel_id=1, source_target_pairs={{0,2},{1,3},{2,0},{3,1},{4,6},{5,7},{6,4},{7,5},{8,10},{9,11},{10,... | collective-permute-start | bytes 208904 | tf_op jit(solution)/shard_map/ppermute | solution.py:267
  59.3 5.6 %collective-permute-start.20 = (f32[8,2176]{1,0:T(8,128)S(1)}, f32[8,2176]{1,0:T(8,128)S(1)}, u32[]{:S(2)}, u32[]{:S(2)}) collective-permute-start(f32[8,2176]{1,0:T(8,128)S(1)} %add_add_fusion.2.own_ref), channel_id=1, source_target_pairs={{0,3},{1,2},{2,1},{3,0},{4,7},{5,6},{6,5},{7,4},{8,11},{9,10},{10,... | collective-permute-start | bytes 208904 | tf_op jit(solution)/shard_map/ppermute | solution.py:267
  60.3 4.6 %collective-permute-start.19 = (f32[8,2176]{1,0:T(8,128)S(1)}, f32[8,2176]{1,0:T(8,128)S(1)}, u32[]{:S(2)}, u32[]{:S(2)}) collective-permute-start(f32[8,2176]{1,0:T(8,128)S(1)} %add_add_fusion.2.own_ref), channel_id=1, source_target_pairs={{0,1},{1,0},{2,3},{3,2},{4,5},{5,4},{6,7},{7,6},{8,9},{9,8},{10,11... | collective-permute-start | bytes 208904 | tf_op jit(solution)/shard_map/ppermute | solution.py:267
  67.9 5.9 %collective-permute-start.25 = (s16[8,4224]{1,0:T(8,128)(2,1)S(1)}, s16[8,4224]{1,0:T(8,128)(2,1)S(1)}, u32[]{:S(2)}, u32[]{:S(2)}) collective-permute-start(s16[8,4224]{1,0:T(8,128)(2,1)S(1)} %shard_map.68.own_ref), channel_id=1, source_target_pairs={{0,64},{32,96},{64,0},{96,32},{1,65},{33,97},{65,1},{97,33},{2,66}... | collective-permute-start | bytes 202760 | tf_op jit(solution)/shard_map/ppermute | solution.py:267
  69.9 5.5 %collective-permute-start.24 = (s16[8,4224]{1,0:T(8,128)(2,1)S(1)}, s16[8,4224]{1,0:T(8,128)(2,1)S(1)}, u32[]{:S(2)}, u32[]{:S(2)}) collective-permute-start(s16[8,4224]{1,0:T(8,128)(2,1)S(1)} %shard_map.68.own_ref), channel_id=1, source_target_pairs={{0,96},{32,64},{64,32},{96,0},{1,97},{33,65},{65,33},{97,1},{2,98}... | collective-permute-start | bytes 202760 | tf_op jit(solution)/shard_map/ppermute | solution.py:267
  78.9 5.5 %collective-permute-start.29 = (f32[8,2176]{1,0:T(8,128)S(1)}, f32[8,2176]{1,0:T(8,128)S(1)}, u32[]{:S(2)}, u32[]{:S(2)}) collective-permute-start(f32[8,2176]{1,0:T(8,128)S(1)} %shard_map.70), channel_id=1, source_target_pairs={{0,12},{4,8},{8,4},{12,0},{1,13},{5,9},{9,5},{13,1},{2,14},{6,10},... | collective-permute-start | bytes 208904 | tf_op jit(solution)/shard_map/ppermute | solution.py:267
  81.0 4.7 %collective-permute-start.28 = (f32[8,2176]{1,0:T(8,128)S(1)}, f32[8,2176]{1,0:T(8,128)S(1)}, u32[]{:S(2)}, u32[]{:S(2)}) collective-permute-start(f32[8,2176]{1,0:T(8,128)S(1)} %shard_map.70), channel_id=1, source_target_pairs={{0,4},{4,0},{8,12},{12,8},{1,5},{5,1},{9,13},{13,9},{2,6},{6,2},{1... | collective-permute-start | bytes 208904 | tf_op jit(solution)/shard_map/ppermute | solution.py:267
  81.0 6.2 %collective-permute-start.27 = (f32[8,2176]{1,0:T(8,128)S(1)}, f32[8,2176]{1,0:T(8,128)S(1)}, u32[]{:S(2)}, u32[]{:S(2)}) collective-permute-start(f32[8,2176]{1,0:T(8,128)S(1)} %shard_map.70), channel_id=1, source_target_pairs={{0,8},{4,12},{8,0},{12,4},{1,9},{5,13},{9,1},{13,5},{2,10},{6,14},... | collective-permute-start | bytes 208904 | tf_op jit(solution)/shard_map/ppermute | solution.py:267
  87.3 6.1 %collective-permute-start.32 = (f32[8,2176]{1,0:T(8,128)S(1)}, f32[8,2176]{1,0:T(8,128)S(1)}, u32[]{:S(2)}, u32[]{:S(2)}) collective-permute-start(f32[8,2176]{1,0:T(8,128)S(1)} %add_add_fusion.1.own_ref), channel_id=1, source_target_pairs={{0,2},{1,3},{2,0},{3,1},{4,6},{5,7},{6,4},{7,5},{8,10},{9,11},{10,... | collective-permute-start | bytes 208904 | tf_op jit(solution)/shard_map/ppermute | solution.py:267
  89.4 5.5 %collective-permute-start.31 = (f32[8,2176]{1,0:T(8,128)S(1)}, f32[8,2176]{1,0:T(8,128)S(1)}, u32[]{:S(2)}, u32[]{:S(2)}) collective-permute-start(f32[8,2176]{1,0:T(8,128)S(1)} %add_add_fusion.1.own_ref), channel_id=1, source_target_pairs={{0,3},{1,2},{2,1},{3,0},{4,7},{5,6},{6,5},{7,4},{8,11},{9,10},{10,... | collective-permute-start | bytes 208904 | tf_op jit(solution)/shard_map/ppermute | solution.py:267
  97.9 5.9 %collective-permute-start.36 = (s16[8,4224]{1,0:T(8,128)(2,1)S(1)}, s16[8,4224]{1,0:T(8,128)(2,1)S(1)}, u32[]{:S(2)}, u32[]{:S(2)}) collective-permute-start(s16[8,4224]{1,0:T(8,128)(2,1)S(1)} %shard_map.72.own_ref), channel_id=1, source_target_pairs={{0,64},{32,96},{64,0},{96,32},{1,65},{33,97},{65,1},{97,33},{2,66}... | collective-permute-start | bytes 202760 | tf_op jit(solution)/shard_map/ppermute | solution.py:267
  99.9 5.5 %collective-permute-start.35 = (s16[8,4224]{1,0:T(8,128)(2,1)S(1)}, s16[8,4224]{1,0:T(8,128)(2,1)S(1)}, u32[]{:S(2)}, u32[]{:S(2)}) collective-permute-start(s16[8,4224]{1,0:T(8,128)(2,1)S(1)} %shard_map.72.own_ref), channel_id=1, source_target_pairs={{0,96},{32,64},{64,32},{96,0},{1,97},{33,65},{65,33},{97,1},{2,98}... | collective-permute-start | bytes 202760 | tf_op jit(solution)/shard_map/ppermute | solution.py:267
  108.8 5.5 %collective-permute-start.40 = (f32[8,2176]{1,0:T(8,128)S(1)}, f32[8,2176]{1,0:T(8,128)S(1)}, u32[]{:S(2)}, u32[]{:S(2)}) collective-permute-start(f32[8,2176]{1,0:T(8,128)S(1)} %shard_map.74), channel_id=1, source_target_pairs={{0,12},{4,8},{8,4},{12,0},{1,13},{5,9},{9,5},{13,1},{2,14},{6,10},... | collective-permute-start | bytes 208904 | tf_op jit(solution)/shard_map/ppermute | solution.py:267
  110.7 4.8 %collective-permute-start.39 = (f32[8,2176]{1,0:T(8,128)S(1)}, f32[8,2176]{1,0:T(8,128)S(1)}, u32[]{:S(2)}, u32[]{:S(2)}) collective-permute-start(f32[8,2176]{1,0:T(8,128)S(1)} %shard_map.74), channel_id=1, source_target_pairs={{0,4},{4,0},{8,12},{12,8},{1,5},{5,1},{9,13},{13,9},{2,6},{6,2},{1... | collective-permute-start | bytes 208904 | tf_op jit(solution)/shard_map/ppermute | solution.py:267
  111.0 5.9 %collective-permute-start.38 = (f32[8,2176]{1,0:T(8,128)S(1)}, f32[8,2176]{1,0:T(8,128)S(1)}, u32[]{:S(2)}, u32[]{:S(2)}) collective-permute-start(f32[8,2176]{1,0:T(8,128)S(1)} %shard_map.74), channel_id=1, source_target_pairs={{0,8},{4,12},{8,0},{12,4},{1,9},{5,13},{9,1},{13,5},{2,10},{6,14},... | collective-permute-start | bytes 208904 | tf_op jit(solution)/shard_map/ppermute | solution.py:267
  117.0 6.6 %collective-permute-start.43 = (f32[8,2176]{1,0:T(8,128)S(1)}, f32[8,2176]{1,0:T(8,128)S(1)}, u32[]{:S(2)}, u32[]{:S(2)}) collective-permute-start(f32[8,2176]{1,0:T(8,128)S(1)} %add_add_fusion.own_ref), channel_id=1, source_target_pairs={{0,2},{1,3},{2,0},{3,1},{4,6},{5,7},{6,4},{7,5},{8,10},{9,11},{10,... | collective-permute-start | bytes 208904 | tf_op jit(solution)/shard_map/ppermute | solution.py:267
  118.6 5.7 %collective-permute-start.42 = (f32[8,2176]{1,0:T(8,128)S(1)}, f32[8,2176]{1,0:T(8,128)S(1)}, u32[]{:S(2)}, u32[]{:S(2)}) collective-permute-start(f32[8,2176]{1,0:T(8,128)S(1)} %add_add_fusion.own_ref), channel_id=1, source_target_pairs={{0,3},{1,2},{2,1},{3,0},{4,7},{5,6},{6,5},{7,4},{8,11},{9,10},{10,... | collective-permute-start | bytes 208904 | tf_op jit(solution)/shard_map/ppermute | solution.py:267
  125.6 5.1 %collective-permute-start.47 = (f32[8,128]{1,0:T(8,128)S(1)}, f32[8,128]{1,0:T(8,128)S(1)}, u32[]{:S(2)}, u32[]{:S(2)}) collective-permute-start(f32[8,128]{1,0:T(8,128)S(1)} %add.51.own_ref), channel_id=1, source_target_pairs={{0,64},{32,96},{64,0},{96,32},{1,65},{33,97},{65,1},{97,33},{2,66}... | collective-permute-start | bytes 12296 | tf_op jit(solution)/shard_map/ppermute | solution.py:267
  127.5 4.8 %collective-permute-start.46 = (f32[8,128]{1,0:T(8,128)S(1)}, f32[8,128]{1,0:T(8,128)S(1)}, u32[]{:S(2)}, u32[]{:S(2)}) collective-permute-start(f32[8,128]{1,0:T(8,128)S(1)} %add.51.own_ref), channel_id=1, source_target_pairs={{0,96},{32,64},{64,32},{96,0},{1,97},{33,65},{65,33},{97,1},{2,98}... | collective-permute-start | bytes 12296 | tf_op jit(solution)/shard_map/ppermute | solution.py:267
  (19 other events, 87.6 us)

commit v5 on v4

--- a/solution.py
+++ b/solution.py
@@ -167,8 +167,14 @@
     beta_ref[...] = wide(beta)
 
 
+def turn(tiles_ref, out_ref):
+    for b in range(tiles_ref.shape[0]):
+        for s in range(tiles_ref.shape[1]):
+            out_ref[b, s] = tiles_ref[b, s].T
+
+
 def forward(pattern_ref, counts_ref, own_ref, other_ref, tiles_ref, out_ref, low_ref):
-    bundles, slots, rays, cells = tiles_ref.shape
+    bundles, slots, cells, rays = tiles_ref.shape
     width = own_ref.shape[1]
     own, other = own_ref[...], other_ref[...]
     low_ref[:, :width] = own.astype(BF16)
@@ -179,9 +185,8 @@
         acc = None
         for s in range(slots):
             at = pl.multiple_of(get(b, s) * cells, cells)
-            part = lax.dot_general(
-                low_ref[:, pl.ds(at, cells)], tiles_ref[b, s],
-                (((1,), (1,)), ((), ())), preferred_element_type=F32,
+            part = jnp.dot(
+                low_ref[:, pl.ds(at, cells)], tiles_ref[b, s], preferred_element_type=F32
             )
             acc = part if acc is None else acc + part
         out_ref[:, b * rays : (b + 1) * rays] = acc
@@ -286,6 +291,9 @@
             pltpu.VMEM(right_side.shape, F32), pltpu.SemaphoreType.DMA((bundles + 3,)),
         ],
     )
+    turned, = call(
+        turn, [jax.ShapeDtypeStruct((bundles, slots, cells, rays), tiles.dtype)], [VMEM], (tiles,)
+    )
     u = right_side
     owns, others, alphas, betas = [], [], [], []
     for step in range(ITERS):
@@ -302,7 +310,7 @@
         others.append(other)
         betas.append(beta)
         products, = call(
-            forward, [shape(rows + 128)], [SMEM] * 2 + [VMEM] * 3, (*slots_in, v, other, tiles),
+            forward, [shape(rows + 128)], [SMEM] * 2 + [VMEM] * 3, (*slots_in, v, other, turned),
             [pltpu.VMEM((nrhs, 2 * half + cells), BF16)],
         )
         rows_in = over_cell(products)

time: 133 us -> 131 us (0.985)
    pallas_call x19 -> x20, Pallas kernels: 16.7 us -> 15.7 us  [call(): pl.pallas_call(body, out_shape=outs, in_specs=specs, out_specs=[VMEM] * l...]
  transfers between devices with their start and end apart: 48 -> 48, of which waited for: 39 -> 39; matrix products, arithmetic and copies ran while one was open for 0% -> 0% of each run, Pallas kernels for 0% -> 1%
where the time goes in v5:
time: 131 us
  waiting for transfers between devices  60.5 us (46%)
  starting transfers between devices  53.9 us (41%)
  Pallas kernels  15.7 us (12%)
    ppermute x39, starting transfers between devices, spread(): lax.ppermute(value, axis, [(i, i ^ by) for i in range(n)])  53.1 us
    ppermute x39, waiting for transfers between devices, spread(): lax.ppermute(value, axis, [(i, i ^ by) for i in range(n)])  49.8 us
    pallas_call x20, Pallas kernels, call(): pl.pallas_call(body, out_shape=outs, in_specs=specs, out_specs=[VMEM] * l...  15.7 us
    ppermute x9, waiting for transfers between devices, swap(): return lax.ppermute(value, 'core', [(0, 1), (1, 0)])  10.7 us
  transfers between devices with their start and end apart: 48, of which 39 were waited for; matrix products, arithmetic and copies ran while one was open for 0% of the time, Pallas kernels for 1%

profile of v5, /device:TPU:0, one launch (start us, length us, event | category | flops | bytes accessed | tf_op | source)
XLA Modules:
  0.0 131.1 jit_solution(5581337592105882235)
XLA Ops:
  0.6 2.7 %shard_map.59 = (f32[8,4224]{1,0:T(8,128)S(1)}, f32[8,4224]{1,0:T(8,128)S(1)}, bf16[8,4,256,256]{3,2,1,0:T(8,128)(2,1)S(1)}) custom-call(s32[4,8]{1,0:T(4,128)} %bitcast.3, s32[1,8]{1,0:T(1,128)} %bitcast.11, f32[8,2048]{1,0:T(8,128)} %prev_ref.3, bf16[8,4,256,256]{3,2,1,0:T(8,128)(2,1)} %source_ref.1), custom_call_target="tpu_custom_call" | custom-call | tf_op jit(solution)/shard_map/pallas_call | solution.py:249
  5.0 4.0 %collective-permute-start.3 = (s16[8,4224]{1,0:T(8,128)(2,1)S(1)}, s16[8,4224]{1,0:T(8,128)(2,1)S(1)}, u32[]{:S(2)}, u32[]{:S(2)}) collective-permute-start(s16[8,4224]{1,0:T(8,128)(2,1)S(1)} %shard_map.60.own_ref), channel_id=1, source_target_pairs={{0,64},{32,96},{64,0},{96,32},{1,65},{33,97},{65,1},{97,33},{2,66}... | collective-permute-start | bytes 202760 | tf_op jit(solution)/shard_map/ppermute | solution.py:272
  11.4 3.0 %collective-permute-done.2.right_ref = s16[8,4224]{1,0:T(8,128)(2,1)S(1)} collective-permute-done((s16[8,4224]{1,0:T(8,128)(2,1)S(1)}, s16[8,4224]{1,0:T(8,128)(2,1)S(1)}, u32[]{:S(2)}, u32[]{:S(2)}) %collective-permute-start.2) | collective-permute-done | bytes 67616 | tf_op jit(solution)/shard_map/ppermute | solution.py:272
  17.4 2.8 %collective-permute-start.7 = (f32[8,2176]{1,0:T(8,128)S(1)}, f32[8,2176]{1,0:T(8,128)S(1)}, u32[]{:S(2)}, u32[]{:S(2)}) collective-permute-start(f32[8,2176]{1,0:T(8,128)S(1)} %shard_map.63), channel_id=1, source_target_pairs={{0,12},{4,8},{8,4},{12,0},{1,13},{5,9},{9,5},{13,1},{2,14},{6,10},... | collective-permute-start | bytes 208904 | tf_op jit(solution)/shard_map/ppermute | solution.py:272
  20.4 1.7 %collective-permute-start.5 = (f32[8,2176]{1,0:T(8,128)S(1)}, f32[8,2176]{1,0:T(8,128)S(1)}, u32[]{:S(2)}, u32[]{:S(2)}) collective-permute-start(f32[8,2176]{1,0:T(8,128)S(1)} %shard_map.63), channel_id=1, source_target_pairs={{0,8},{4,12},{8,0},{12,4},{1,9},{5,13},{9,1},{13,5},{2,10},{6,14},... | collective-permute-start | bytes 208904 | tf_op jit(solution)/shard_map/ppermute | solution.py:272
  23.0 2.0 %collective-permute-done.6 = f32[8,2176]{1,0:T(8,128)S(1)} collective-permute-done((f32[8,2176]{1,0:T(8,128)S(1)}, f32[8,2176]{1,0:T(8,128)S(1)}, u32[]{:S(2)}, u32[]{:S(2)}) %collective-permute-start.6) | collective-permute-done | bytes 69664 | tf_op jit(solution)/shard_map/ppermute | solution.py:272
  26.2 3.3 %collective-permute-start.10 = (f32[8,2176]{1,0:T(8,128)S(1)}, f32[8,2176]{1,0:T(8,128)S(1)}, u32[]{:S(2)}, u32[]{:S(2)}) collective-permute-start(f32[8,2176]{1,0:T(8,128)S(1)} %add_add_fusion.3.own_ref), channel_id=1, source_target_pairs={{0,2},{1,3},{2,0},{3,1},{4,6},{5,7},{6,4},{7,5},{8,10},{9,11},{10,... | collective-permute-start | bytes 208904 | tf_op jit(solution)/shard_map/ppermute | solution.py:272
  30.5 1.6 %collective-permute-done.10.far_ref = f32[8,2176]{1,0:T(8,128)S(1)} collective-permute-done((f32[8,2176]{1,0:T(8,128)S(1)}, f32[8,2176]{1,0:T(8,128)S(1)}, u32[]{:S(2)}, u32[]{:S(2)}) %collective-permute-start.10) | collective-permute-done | bytes 69664 | tf_op jit(solution)/shard_map/ppermute | solution.py:272
  32.1 2.9 %collective-permute-done.9.right_ref = f32[8,2176]{1,0:T(8,128)S(1)} collective-permute-done((f32[8,2176]{1,0:T(8,128)S(1)}, f32[8,2176]{1,0:T(8,128)S(1)}, u32[]{:S(2)}, u32[]{:S(2)}) %collective-permute-start.9) | collective-permute-done | bytes 69664 | tf_op jit(solution)/shard_map/ppermute | solution.py:272
  38.0 1.9 %collective-permute-start.14 = (s16[8,4224]{1,0:T(8,128)(2,1)S(1)}, s16[8,4224]{1,0:T(8,128)(2,1)S(1)}, u32[]{:S(2)}, u32[]{:S(2)}) collective-permute-start(s16[8,4224]{1,0:T(8,128)(2,1)S(1)} %shard_map.65.own_ref), channel_id=1, source_target_pairs={{0,64},{32,96},{64,0},{96,32},{1,65},{33,97},{65,1},{97,33},{2,66}... | collective-permute-start | bytes 202760 | tf_op jit(solution)/shard_map/ppermute | solution.py:272
  41.5 2.3 %collective-permute-done.14.far_ref = s16[8,4224]{1,0:T(8,128)(2,1)S(1)} collective-permute-done((s16[8,4224]{1,0:T(8,128)(2,1)S(1)}, s16[8,4224]{1,0:T(8,128)(2,1)S(1)}, u32[]{:S(2)}, u32[]{:S(2)}) %collective-permute-start.14) | collective-permute-done | bytes 67616 | tf_op jit(solution)/shard_map/ppermute | solution.py:272
  43.9 1.5 %collective-permute-done.13.right_ref = s16[8,4224]{1,0:T(8,128)(2,1)S(1)} collective-permute-done((s16[8,4224]{1,0:T(8,128)(2,1)S(1)}, s16[8,4224]{1,0:T(8,128)(2,1)S(1)}, u32[]{:S(2)}, u32[]{:S(2)}) %collective-permute-start.13) | collective-permute-done | bytes 67616 | tf_op jit(solution)/shard_map/ppermute | solution.py:272
  48.3 2.3 %collective-permute-start.18 = (f32[8,2176]{1,0:T(8,128)S(1)}, f32[8,2176]{1,0:T(8,128)S(1)}, u32[]{:S(2)}, u32[]{:S(2)}) collective-permute-start(f32[8,2176]{1,0:T(8,128)S(1)} %shard_map.67), channel_id=1, source_target_pairs={{0,12},{4,8},{8,4},{12,0},{1,13},{5,9},{9,5},{13,1},{2,14},{6,10},... | collective-permute-start | bytes 208904 | tf_op jit(solution)/shard_map/ppermute | solution.py:272
  50.6 2.4 %collective-permute-start.16 = (f32[8,2176]{1,0:T(8,128)S(1)}, f32[8,2176]{1,0:T(8,128)S(1)}, u32[]{:S(2)}, u32[]{:S(2)}) collective-permute-start(f32[8,2176]{1,0:T(8,128)S(1)} %shard_map.67), channel_id=1, source_target_pairs={{0,8},{4,12},{8,0},{12,4},{1,9},{5,13},{9,1},{13,5},{2,10},{6,14},... | collective-permute-start | bytes 208904 | tf_op jit(solution)/shard_map/ppermute | solution.py:272
  56.8 1.6 %collective-permute-start.21 = (f32[8,2176]{1,0:T(8,128)S(1)}, f32[8,2176]{1,0:T(8,128)S(1)}, u32[]{:S(2)}, u32[]{:S(2)}) collective-permute-start(f32[8,2176]{1,0:T(8,128)S(1)} %add_add_fusion.2.own_ref), channel_id=1, source_target_pairs={{0,2},{1,3},{2,0},{3,1},{4,6},{5,7},{6,4},{7,5},{8,10},{9,11},{10,... | collective-permute-start | bytes 208904 | tf_op jit(solution)/shard_map/ppermute | solution.py:272
  60.4 2.8 %collective-permute-done.21.far_ref = f32[8,2176]{1,0:T(8,128)S(1)} collective-permute-done((f32[8,2176]{1,0:T(8,128)S(1)}, f32[8,2176]{1,0:T(8,128)S(1)}, u32[]{:S(2)}, u32[]{:S(2)}) %collective-permute-start.21) | collective-permute-done | bytes 69664 | tf_op jit(solution)/shard_map/ppermute | solution.py:272
  66.9 1.9 %collective-permute-start.25 = (s16[8,4224]{1,0:T(8,128)(2,1)S(1)}, s16[8,4224]{1,0:T(8,128)(2,1)S(1)}, u32[]{:S(2)}, u32[]{:S(2)}) collective-permute-start(s16[8,4224]{1,0:T(8,128)(2,1)S(1)} %shard_map.69.own_ref), channel_id=1, source_target_pairs={{0,64},{32,96},{64,0},{96,32},{1,65},{33,97},{65,1},{97,33},{2,66}... | collective-permute-start | bytes 202760 | tf_op jit(solution)/shard_map/ppermute | solution.py:272
  70.5 2.3 %collective-permute-done.25.far_ref = s16[8,4224]{1,0:T(8,128)(2,1)S(1)} collective-permute-done((s16[8,4224]{1,0:T(8,128)(2,1)S(1)}, s16[8,4224]{1,0:T(8,128)(2,1)S(1)}, u32[]{:S(2)}, u32[]{:S(2)}) %collective-permute-start.25) | collective-permute-done | bytes 67616 | tf_op jit(solution)/shard_map/ppermute | solution.py:272
  72.8 1.5 %collective-permute-done.24.right_ref = s16[8,4224]{1,0:T(8,128)(2,1)S(1)} collective-permute-done((s16[8,4224]{1,0:T(8,128)(2,1)S(1)}, s16[8,4224]{1,0:T(8,128)(2,1)S(1)}, u32[]{:S(2)}, u32[]{:S(2)}) %collective-permute-start.24) | collective-permute-done | bytes 67616 | tf_op jit(solution)/shard_map/ppermute | solution.py:272
  77.2 2.0 %collective-permute-start.29 = (f32[8,2176]{1,0:T(8,128)S(1)}, f32[8,2176]{1,0:T(8,128)S(1)}, u32[]{:S(2)}, u32[]{:S(2)}) collective-permute-start(f32[8,2176]{1,0:T(8,128)S(1)} %shard_map.71), channel_id=1, source_target_pairs={{0,12},{4,8},{8,4},{12,0},{1,13},{5,9},{9,5},{13,1},{2,14},{6,10},... | collective-permute-start | bytes 208904 | tf_op jit(solution)/shard_map/ppermute | solution.py:272
  79.3 2.7 %collective-permute-start.27 = (f32[8,2176]{1,0:T(8,128)S(1)}, f32[8,2176]{1,0:T(8,128)S(1)}, u32[]{:S(2)}, u32[]{:S(2)}) collective-permute-start(f32[8,2176]{1,0:T(8,128)S(1)} %shard_map.71), channel_id=1, source_target_pairs={{0,8},{4,12},{8,0},{12,4},{1,9},{5,13},{9,1},{13,5},{2,10},{6,14},... | collective-permute-start | bytes 208904 | tf_op jit(solution)/shard_map/ppermute | solution.py:272
  85.5 2.2 %collective-permute-start.32 = (f32[8,2176]{1,0:T(8,128)S(1)}, f32[8,2176]{1,0:T(8,128)S(1)}, u32[]{:S(2)}, u32[]{:S(2)}) collective-permute-start(f32[8,2176]{1,0:T(8,128)S(1)} %add_add_fusion.1.own_ref), channel_id=1, source_target_pairs={{0,2},{1,3},{2,0},{3,1},{4,6},{5,7},{6,4},{7,5},{8,10},{9,11},{10,... | collective-permute-start | bytes 208904 | tf_op jit(solution)/shard_map/ppermute | solution.py:272
  89.1 2.7 %collective-permute-done.32.far_ref = f32[8,2176]{1,0:T(8,128)S(1)} collective-permute-done((f32[8,2176]{1,0:T(8,128)S(1)}, f32[8,2176]{1,0:T(8,128)S(1)}, u32[]{:S(2)}, u32[]{:S(2)}) %collective-permute-start.32) | collective-permute-done | bytes 69664 | tf_op jit(solution)/shard_map/ppermute | solution.py:272
  96.2 1.9 %collective-permute-start.36 = (s16[8,4224]{1,0:T(8,128)(2,1)S(1)}, s16[8,4224]{1,0:T(8,128)(2,1)S(1)}, u32[]{:S(2)}, u32[]{:S(2)}) collective-permute-start(s16[8,4224]{1,0:T(8,128)(2,1)S(1)} %shard_map.73.own_ref), channel_id=1, source_target_pairs={{0,64},{32,96},{64,0},{96,32},{1,65},{33,97},{65,1},{97,33},{2,66}... | collective-permute-start | bytes 202760 | tf_op jit(solution)/shard_map/ppermute | solution.py:272
  99.7 2.3 %collective-permute-done.36.far_ref = s16[8,4224]{1,0:T(8,128)(2,1)S(1)} collective-permute-done((s16[8,4224]{1,0:T(8,128)(2,1)S(1)}, s16[8,4224]{1,0:T(8,128)(2,1)S(1)}, u32[]{:S(2)}, u32[]{:S(2)}) %collective-permute-start.36) | collective-permute-done | bytes 67616 | tf_op jit(solution)/shard_map/ppermute | solution.py:272
  102.1 1.5 %collective-permute-done.35.right_ref = s16[8,4224]{1,0:T(8,128)(2,1)S(1)} collective-permute-done((s16[8,4224]{1,0:T(8,128)(2,1)S(1)}, s16[8,4224]{1,0:T(8,128)(2,1)S(1)}, u32[]{:S(2)}, u32[]{:S(2)}) %collective-permute-start.35) | collective-permute-done | bytes 67616 | tf_op jit(solution)/shard_map/ppermute | solution.py:272
  106.5 2.1 %collective-permute-start.40 = (f32[8,2176]{1,0:T(8,128)S(1)}, f32[8,2176]{1,0:T(8,128)S(1)}, u32[]{:S(2)}, u32[]{:S(2)}) collective-permute-start(f32[8,2176]{1,0:T(8,128)S(1)} %shard_map.75), channel_id=1, source_target_pairs={{0,12},{4,8},{8,4},{12,0},{1,13},{5,9},{9,5},{13,1},{2,14},{6,10},... | collective-permute-start | bytes 208904 | tf_op jit(solution)/shard_map/ppermute | solution.py:272
  108.9 2.3 %collective-permute-start.38 = (f32[8,2176]{1,0:T(8,128)S(1)}, f32[8,2176]{1,0:T(8,128)S(1)}, u32[]{:S(2)}, u32[]{:S(2)}) collective-permute-start(f32[8,2176]{1,0:T(8,128)S(1)} %shard_map.75), channel_id=1, source_target_pairs={{0,8},{4,12},{8,0},{12,4},{1,9},{5,13},{9,1},{13,5},{2,10},{6,14},... | collective-permute-start | bytes 208904 | tf_op jit(solution)/shard_map/ppermute | solution.py:272
  114.8 1.6 %collective-permute-start.43 = (f32[8,2176]{1,0:T(8,128)S(1)}, f32[8,2176]{1,0:T(8,128)S(1)}, u32[]{:S(2)}, u32[]{:S(2)}) collective-permute-start(f32[8,2176]{1,0:T(8,128)S(1)} %add_add_fusion.own_ref), channel_id=1, source_target_pairs={{0,2},{1,3},{2,0},{3,1},{4,6},{5,7},{6,4},{7,5},{8,10},{9,11},{10,... | collective-permute-start | bytes 208904 | tf_op jit(solution)/shard_map/ppermute | solution.py:272
  118.4 3.0 %collective-permute-done.43.far_ref = f32[8,2176]{1,0:T(8,128)S(1)} collective-permute-done((f32[8,2176]{1,0:T(8,128)S(1)}, f32[8,2176]{1,0:T(8,128)S(1)}, u32[]{:S(2)}, u32[]{:S(2)}) %collective-permute-start.43) | collective-permute-done | bytes 69664 | tf_op jit(solution)/shard_map/ppermute | solution.py:272
  123.5 1.9 %collective-permute-start.47 = (f32[8,128]{1,0:T(8,128)S(1)}, f32[8,128]{1,0:T(8,128)S(1)}, u32[]{:S(2)}, u32[]{:S(2)}) collective-permute-start(f32[8,128]{1,0:T(8,128)S(1)} %add.51.own_ref), channel_id=1, source_target_pairs={{0,64},{32,96},{64,0},{96,32},{1,65},{33,97},{65,1},{97,33},{2,66}... | collective-permute-start | bytes 12296 | tf_op jit(solution)/shard_map/ppermute | solution.py:272
  128.6 1.6 %collective-permute-done.46.right_ref = f32[8,128]{1,0:T(8,128)S(1)} collective-permute-done((f32[8,128]{1,0:T(8,128)S(1)}, f32[8,128]{1,0:T(8,128)S(1)}, u32[]{:S(2)}, u32[]{:S(2)}) %collective-permute-start.46) | collective-permute-done | bytes 4128 | tf_op jit(solution)/shard_map/ppermute | solution.py:272
  (95 shorter events, 57.5 us)
Async XLA Ops:
  5.0 6.5 %collective-permute-start.3 = (s16[8,4224]{1,0:T(8,128)(2,1)S(1)}, s16[8,4224]{1,0:T(8,128)(2,1)S(1)}, u32[]{:S(2)}, u32[]{:S(2)}) collective-permute-start(s16[8,4224]{1,0:T(8,128)(2,1)S(1)} %shard_map.60.own_ref), channel_id=1, source_target_pairs={{0,64},{32,96},{64,0},{96,32},{1,65},{33,97},{65,1},{97,33},{2,66}... | collective-permute-start | bytes 202760 | tf_op jit(solution)/shard_map/ppermute | solution.py:272
  9.0 5.5 %collective-permute-start.2 = (s16[8,4224]{1,0:T(8,128)(2,1)S(1)}, s16[8,4224]{1,0:T(8,128)(2,1)S(1)}, u32[]{:S(2)}, u32[]{:S(2)}) collective-permute-start(s16[8,4224]{1,0:T(8,128)(2,1)S(1)} %shard_map.60.own_ref), channel_id=1, source_target_pairs={{0,96},{32,64},{64,32},{96,0},{1,97},{33,65},{65,33},{97,1},{2,98}... | collective-permute-start | bytes 202760 | tf_op jit(solution)/shard_map/ppermute | solution.py:272
  9.7 4.8 %collective-permute-start.1 = (s16[8,4224]{1,0:T(8,128)(2,1)S(1)}, s16[8,4224]{1,0:T(8,128)(2,1)S(1)}, u32[]{:S(2)}, u32[]{:S(2)}) collective-permute-start(s16[8,4224]{1,0:T(8,128)(2,1)S(1)} %shard_map.60.own_ref), channel_id=1, source_target_pairs={{0,32},{32,0},{64,96},{96,64},{1,33},{33,1},{65,97},{97,65},{2,34}... | collective-permute-start | bytes 202760 | tf_op jit(solution)/shard_map/ppermute | solution.py:272
  17.4 5.6 %collective-permute-start.7 = (f32[8,2176]{1,0:T(8,128)S(1)}, f32[8,2176]{1,0:T(8,128)S(1)}, u32[]{:S(2)}, u32[]{:S(2)}) collective-permute-start(f32[8,2176]{1,0:T(8,128)S(1)} %shard_map.63), channel_id=1, source_target_pairs={{0,12},{4,8},{8,4},{12,0},{1,13},{5,9},{9,5},{13,1},{2,14},{6,10},... | collective-permute-start | bytes 208904 | tf_op jit(solution)/shard_map/ppermute | solution.py:272
  20.1 4.9 %collective-permute-start.6 = (f32[8,2176]{1,0:T(8,128)S(1)}, f32[8,2176]{1,0:T(8,128)S(1)}, u32[]{:S(2)}, u32[]{:S(2)}) collective-permute-start(f32[8,2176]{1,0:T(8,128)S(1)} %shard_map.63), channel_id=1, source_target_pairs={{0,4},{4,0},{8,12},{12,8},{1,5},{5,1},{9,13},{13,9},{2,6},{6,2},{1... | collective-permute-start | bytes 208904 | tf_op jit(solution)/shard_map/ppermute | solution.py:272
  20.4 5.8 %collective-permute-start.5 = (f32[8,2176]{1,0:T(8,128)S(1)}, f32[8,2176]{1,0:T(8,128)S(1)}, u32[]{:S(2)}, u32[]{:S(2)}) collective-permute-start(f32[8,2176]{1,0:T(8,128)S(1)} %shard_map.63), channel_id=1, source_target_pairs={{0,8},{4,12},{8,0},{12,4},{1,9},{5,13},{9,1},{13,5},{2,10},{6,14},... | collective-permute-start | bytes 208904 | tf_op jit(solution)/shard_map/ppermute | solution.py:272
  26.2 5.9 %collective-permute-start.10 = (f32[8,2176]{1,0:T(8,128)S(1)}, f32[8,2176]{1,0:T(8,128)S(1)}, u32[]{:S(2)}, u32[]{:S(2)}) collective-permute-start(f32[8,2176]{1,0:T(8,128)S(1)} %add_add_fusion.3.own_ref), channel_id=1, source_target_pairs={{0,2},{1,3},{2,0},{3,1},{4,6},{5,7},{6,4},{7,5},{8,10},{9,11},{10,... | collective-permute-start | bytes 208904 | tf_op jit(solution)/shard_map/ppermute | solution.py:272
  29.5 5.5 %collective-permute-start.9 = (f32[8,2176]{1,0:T(8,128)S(1)}, f32[8,2176]{1,0:T(8,128)S(1)}, u32[]{:S(2)}, u32[]{:S(2)}) collective-permute-start(f32[8,2176]{1,0:T(8,128)S(1)} %add_add_fusion.3.own_ref), channel_id=1, source_target_pairs={{0,3},{1,2},{2,1},{3,0},{4,7},{5,6},{6,5},{7,4},{8,11},{9,10},{10,... | collective-permute-start | bytes 208904 | tf_op jit(solution)/shard_map/ppermute | solution.py:272
  38.0 5.9 %collective-permute-start.14 = (s16[8,4224]{1,0:T(8,128)(2,1)S(1)}, s16[8,4224]{1,0:T(8,128)(2,1)S(1)}, u32[]{:S(2)}, u32[]{:S(2)}) collective-permute-start(s16[8,4224]{1,0:T(8,128)(2,1)S(1)} %shard_map.65.own_ref), channel_id=1, source_target_pairs={{0,64},{32,96},{64,0},{96,32},{1,65},{33,97},{65,1},{97,33},{2,66}... | collective-permute-start | bytes 202760 | tf_op jit(solution)/shard_map/ppermute | solution.py:272
  39.9 5.5 %collective-permute-start.13 = (s16[8,4224]{1,0:T(8,128)(2,1)S(1)}, s16[8,4224]{1,0:T(8,128)(2,1)S(1)}, u32[]{:S(2)}, u32[]{:S(2)}) collective-permute-start(s16[8,4224]{1,0:T(8,128)(2,1)S(1)} %shard_map.65.own_ref), channel_id=1, source_target_pairs={{0,96},{32,64},{64,32},{96,0},{1,97},{33,65},{65,33},{97,1},{2,98}... | collective-permute-start | bytes 202760 | tf_op jit(solution)/shard_map/ppermute | solution.py:272
  48.3 5.5 %collective-permute-start.18 = (f32[8,2176]{1,0:T(8,128)S(1)}, f32[8,2176]{1,0:T(8,128)S(1)}, u32[]{:S(2)}, u32[]{:S(2)}) collective-permute-start(f32[8,2176]{1,0:T(8,128)S(1)} %shard_map.67), channel_id=1, source_target_pairs={{0,12},{4,8},{8,4},{12,0},{1,13},{5,9},{9,5},{13,1},{2,14},{6,10},... | collective-permute-start | bytes 208904 | tf_op jit(solution)/shard_map/ppermute | solution.py:272
  50.6 4.7 %collective-permute-start.17 = (f32[8,2176]{1,0:T(8,128)S(1)}, f32[8,2176]{1,0:T(8,128)S(1)}, u32[]{:S(2)}, u32[]{:S(2)}) collective-permute-start(f32[8,2176]{1,0:T(8,128)S(1)} %shard_map.67), channel_id=1, source_target_pairs={{0,4},{4,0},{8,12},{12,8},{1,5},{5,1},{9,13},{13,9},{2,6},{6,2},{1... | collective-permute-start | bytes 208904 | tf_op jit(solution)/shard_map/ppermute | solution.py:272
  50.6 6.2 %collective-permute-start.16 = (f32[8,2176]{1,0:T(8,128)S(1)}, f32[8,2176]{1,0:T(8,128)S(1)}, u32[]{:S(2)}, u32[]{:S(2)}) collective-permute-start(f32[8,2176]{1,0:T(8,128)S(1)} %shard_map.67), channel_id=1, source_target_pairs={{0,8},{4,12},{8,0},{12,4},{1,9},{5,13},{9,1},{13,5},{2,10},{6,14},... | collective-permute-start | bytes 208904 | tf_op jit(solution)/shard_map/ppermute | solution.py:272
  56.8 6.4 %collective-permute-start.21 = (f32[8,2176]{1,0:T(8,128)S(1)}, f32[8,2176]{1,0:T(8,128)S(1)}, u32[]{:S(2)}, u32[]{:S(2)}) collective-permute-start(f32[8,2176]{1,0:T(8,128)S(1)} %add_add_fusion.2.own_ref), channel_id=1, source_target_pairs={{0,2},{1,3},{2,0},{3,1},{4,6},{5,7},{6,4},{7,5},{8,10},{9,11},{10,... | collective-permute-start | bytes 208904 | tf_op jit(solution)/shard_map/ppermute | solution.py:272
  58.4 5.5 %collective-permute-start.20 = (f32[8,2176]{1,0:T(8,128)S(1)}, f32[8,2176]{1,0:T(8,128)S(1)}, u32[]{:S(2)}, u32[]{:S(2)}) collective-permute-start(f32[8,2176]{1,0:T(8,128)S(1)} %add_add_fusion.2.own_ref), channel_id=1, source_target_pairs={{0,3},{1,2},{2,1},{3,0},{4,7},{5,6},{6,5},{7,4},{8,11},{9,10},{10,... | collective-permute-start | bytes 208904 | tf_op jit(solution)/shard_map/ppermute | solution.py:272
  59.4 4.5 %collective-permute-start.19 = (f32[8,2176]{1,0:T(8,128)S(1)}, f32[8,2176]{1,0:T(8,128)S(1)}, u32[]{:S(2)}, u32[]{:S(2)}) collective-permute-start(f32[8,2176]{1,0:T(8,128)S(1)} %add_add_fusion.2.own_ref), channel_id=1, source_target_pairs={{0,1},{1,0},{2,3},{3,2},{4,5},{5,4},{6,7},{7,6},{8,9},{9,8},{10,11... | collective-permute-start | bytes 208904 | tf_op jit(solution)/shard_map/ppermute | solution.py:272
  66.9 5.9 %collective-permute-start.25 = (s16[8,4224]{1,0:T(8,128)(2,1)S(1)}, s16[8,4224]{1,0:T(8,128)(2,1)S(1)}, u32[]{:S(2)}, u32[]{:S(2)}) collective-permute-start(s16[8,4224]{1,0:T(8,128)(2,1)S(1)} %shard_map.69.own_ref), channel_id=1, source_target_pairs={{0,64},{32,96},{64,0},{96,32},{1,65},{33,97},{65,1},{97,33},{2,66}... | collective-permute-start | bytes 202760 | tf_op jit(solution)/shard_map/ppermute | solution.py:272
  68.8 5.5 %collective-permute-start.24 = (s16[8,4224]{1,0:T(8,128)(2,1)S(1)}, s16[8,4224]{1,0:T(8,128)(2,1)S(1)}, u32[]{:S(2)}, u32[]{:S(2)}) collective-permute-start(s16[8,4224]{1,0:T(8,128)(2,1)S(1)} %shard_map.69.own_ref), channel_id=1, source_target_pairs={{0,96},{32,64},{64,32},{96,0},{1,97},{33,65},{65,33},{97,1},{2,98}... | collective-permute-start | bytes 202760 | tf_op jit(solution)/shard_map/ppermute | solution.py:272
  77.2 5.5 %collective-permute-start.29 = (f32[8,2176]{1,0:T(8,128)S(1)}, f32[8,2176]{1,0:T(8,128)S(1)}, u32[]{:S(2)}, u32[]{:S(2)}) collective-permute-start(f32[8,2176]{1,0:T(8,128)S(1)} %shard_map.71), channel_id=1, source_target_pairs={{0,12},{4,8},{8,4},{12,0},{1,13},{5,9},{9,5},{13,1},{2,14},{6,10},... | collective-permute-start | bytes 208904 | tf_op jit(solution)/shard_map/ppermute | solution.py:272
  79.3 4.7 %collective-permute-start.28 = (f32[8,2176]{1,0:T(8,128)S(1)}, f32[8,2176]{1,0:T(8,128)S(1)}, u32[]{:S(2)}, u32[]{:S(2)}) collective-permute-start(f32[8,2176]{1,0:T(8,128)S(1)} %shard_map.71), channel_id=1, source_target_pairs={{0,4},{4,0},{8,12},{12,8},{1,5},{5,1},{9,13},{13,9},{2,6},{6,2},{1... | collective-permute-start | bytes 208904 | tf_op jit(solution)/shard_map/ppermute | solution.py:272
  79.3 6.2 %collective-permute-start.27 = (f32[8,2176]{1,0:T(8,128)S(1)}, f32[8,2176]{1,0:T(8,128)S(1)}, u32[]{:S(2)}, u32[]{:S(2)}) collective-permute-start(f32[8,2176]{1,0:T(8,128)S(1)} %shard_map.71), channel_id=1, source_target_pairs={{0,8},{4,12},{8,0},{12,4},{1,9},{5,13},{9,1},{13,5},{2,10},{6,14},... | collective-permute-start | bytes 208904 | tf_op jit(solution)/shard_map/ppermute | solution.py:272
  85.5 6.3 %collective-permute-start.32 = (f32[8,2176]{1,0:T(8,128)S(1)}, f32[8,2176]{1,0:T(8,128)S(1)}, u32[]{:S(2)}, u32[]{:S(2)}) collective-permute-start(f32[8,2176]{1,0:T(8,128)S(1)} %add_add_fusion.1.own_ref), channel_id=1, source_target_pairs={{0,2},{1,3},{2,0},{3,1},{4,6},{5,7},{6,4},{7,5},{8,10},{9,11},{10,... | collective-permute-start | bytes 208904 | tf_op jit(solution)/shard_map/ppermute | solution.py:272
  87.7 5.5 %collective-permute-start.31 = (f32[8,2176]{1,0:T(8,128)S(1)}, f32[8,2176]{1,0:T(8,128)S(1)}, u32[]{:S(2)}, u32[]{:S(2)}) collective-permute-start(f32[8,2176]{1,0:T(8,128)S(1)} %add_add_fusion.1.own_ref), channel_id=1, source_target_pairs={{0,3},{1,2},{2,1},{3,0},{4,7},{5,6},{6,5},{7,4},{8,11},{9,10},{10,... | collective-permute-start | bytes 208904 | tf_op jit(solution)/shard_map/ppermute | solution.py:272
  96.2 5.9 %collective-permute-start.36 = (s16[8,4224]{1,0:T(8,128)(2,1)S(1)}, s16[8,4224]{1,0:T(8,128)(2,1)S(1)}, u32[]{:S(2)}, u32[]{:S(2)}) collective-permute-start(s16[8,4224]{1,0:T(8,128)(2,1)S(1)} %shard_map.73.own_ref), channel_id=1, source_target_pairs={{0,64},{32,96},{64,0},{96,32},{1,65},{33,97},{65,1},{97,33},{2,66}... | collective-permute-start | bytes 202760 | tf_op jit(solution)/shard_map/ppermute | solution.py:272
  98.1 5.5 %collective-permute-start.35 = (s16[8,4224]{1,0:T(8,128)(2,1)S(1)}, s16[8,4224]{1,0:T(8,128)(2,1)S(1)}, u32[]{:S(2)}, u32[]{:S(2)}) collective-permute-start(s16[8,4224]{1,0:T(8,128)(2,1)S(1)} %shard_map.73.own_ref), channel_id=1, source_target_pairs={{0,96},{32,64},{64,32},{96,0},{1,97},{33,65},{65,33},{97,1},{2,98}... | collective-permute-start | bytes 202760 | tf_op jit(solution)/shard_map/ppermute | solution.py:272
  106.5 5.5 %collective-permute-start.40 = (f32[8,2176]{1,0:T(8,128)S(1)}, f32[8,2176]{1,0:T(8,128)S(1)}, u32[]{:S(2)}, u32[]{:S(2)}) collective-permute-start(f32[8,2176]{1,0:T(8,128)S(1)} %shard_map.75), channel_id=1, source_target_pairs={{0,12},{4,8},{8,4},{12,0},{1,13},{5,9},{9,5},{13,1},{2,14},{6,10},... | collective-permute-start | bytes 208904 | tf_op jit(solution)/shard_map/ppermute | solution.py:272
  108.6 4.7 %collective-permute-start.39 = (f32[8,2176]{1,0:T(8,128)S(1)}, f32[8,2176]{1,0:T(8,128)S(1)}, u32[]{:S(2)}, u32[]{:S(2)}) collective-permute-start(f32[8,2176]{1,0:T(8,128)S(1)} %shard_map.75), channel_id=1, source_target_pairs={{0,4},{4,0},{8,12},{12,8},{1,5},{5,1},{9,13},{13,9},{2,6},{6,2},{1... | collective-permute-start | bytes 208904 | tf_op jit(solution)/shard_map/ppermute | solution.py:272
  108.9 5.9 %collective-permute-start.38 = (f32[8,2176]{1,0:T(8,128)S(1)}, f32[8,2176]{1,0:T(8,128)S(1)}, u32[]{:S(2)}, u32[]{:S(2)}) collective-permute-start(f32[8,2176]{1,0:T(8,128)S(1)} %shard_map.75), channel_id=1, source_target_pairs={{0,8},{4,12},{8,0},{12,4},{1,9},{5,13},{9,1},{13,5},{2,10},{6,14},... | collective-permute-start | bytes 208904 | tf_op jit(solution)/shard_map/ppermute | solution.py:272
  114.8 6.6 %collective-permute-start.43 = (f32[8,2176]{1,0:T(8,128)S(1)}, f32[8,2176]{1,0:T(8,128)S(1)}, u32[]{:S(2)}, u32[]{:S(2)}) collective-permute-start(f32[8,2176]{1,0:T(8,128)S(1)} %add_add_fusion.own_ref), channel_id=1, source_target_pairs={{0,2},{1,3},{2,0},{3,1},{4,6},{5,7},{6,4},{7,5},{8,10},{9,11},{10,... | collective-permute-start | bytes 208904 | tf_op jit(solution)/shard_map/ppermute | solution.py:272
  116.4 5.6 %collective-permute-start.42 = (f32[8,2176]{1,0:T(8,128)S(1)}, f32[8,2176]{1,0:T(8,128)S(1)}, u32[]{:S(2)}, u32[]{:S(2)}) collective-permute-start(f32[8,2176]{1,0:T(8,128)S(1)} %add_add_fusion.own_ref), channel_id=1, source_target_pairs={{0,3},{1,2},{2,1},{3,0},{4,7},{5,6},{6,5},{7,4},{8,11},{9,10},{10,... | collective-permute-start | bytes 208904 | tf_op jit(solution)/shard_map/ppermute | solution.py:272
  123.5 5.1 %collective-permute-start.47 = (f32[8,128]{1,0:T(8,128)S(1)}, f32[8,128]{1,0:T(8,128)S(1)}, u32[]{:S(2)}, u32[]{:S(2)}) collective-permute-start(f32[8,128]{1,0:T(8,128)S(1)} %add.51.own_ref), channel_id=1, source_target_pairs={{0,64},{32,96},{64,0},{96,32},{1,65},{33,97},{65,1},{97,33},{2,66}... | collective-permute-start | bytes 12296 | tf_op jit(solution)/shard_map/ppermute | solution.py:272
  125.3 4.8 %collective-permute-start.46 = (f32[8,128]{1,0:T(8,128)S(1)}, f32[8,128]{1,0:T(8,128)S(1)}, u32[]{:S(2)}, u32[]{:S(2)}) collective-permute-start(f32[8,128]{1,0:T(8,128)S(1)} %add.51.own_ref), channel_id=1, source_target_pairs={{0,96},{32,64},{64,32},{96,0},{1,97},{33,65},{65,33},{97,1},{2,98}... | collective-permute-start | bytes 12296 | tf_op jit(solution)/shard_map/ppermute | solution.py:272
  (19 other events, 59.1 us)

commit v6 on v5

--- a/solution.py
+++ b/solution.py
@@ -277,7 +277,7 @@
         return lax.ppermute(value, "core", [(0, 1), (1, 0)])
 
     def over_cell(partial):
-        own, left, right, far = spread(partial, "x")
+        own, left, right, far = lax.optimization_barrier(spread(partial, "x"))
         return spread((own + far) + (left + right), "y")
 
     halves = [shape(half + 128)] * 2

time: 131 us -> 128 us (0.977)
  starting transfers between devices: 53.9 us -> 49.7 us
    ppermute x39, starting transfers between devices: 53.1 us -> 48.9 us  [spread(): lax.ppermute(value, axis, [(i, i ^ by) for i in range(n)])]
  transfers between devices with their start and end apart: 48 -> 48, of which waited for: 39 -> 36; matrix products, arithmetic and copies ran while one was open for 0% -> 0% of each run, Pallas kernels for 1% -> 1%
where the time goes in v6:
time: 128 us
  waiting for transfers between devices  61.7 us (48%)
  starting transfers between devices  49.7 us (39%)
  Pallas kernels  15.7 us (12%)
    ppermute x39, waiting for transfers between devices, spread(): lax.ppermute(value, axis, [(i, i ^ by) for i in range(n)])  51 us
    ppermute x39, starting transfers between devices, spread(): lax.ppermute(value, axis, [(i, i ^ by) for i in range(n)])  48.9 us
    pallas_call x20, Pallas kernels, call(): pl.pallas_call(body, out_shape=outs, in_specs=specs, out_specs=[VMEM] * l...  15.7 us
    ppermute x9, waiting for transfers between devices, swap(): return lax.ppermute(value, 'core', [(0, 1), (1, 0)])  10.7 us
  transfers between devices with their start and end apart: 48, of which 36 were waited for; matrix products, arithmetic and copies ran while one was open for 0% of the time, Pallas kernels for 1%

profile of v6, /device:TPU:0, one launch (start us, length us, event | category | flops | bytes accessed | tf_op | source)
XLA Modules:
  0.0 128.1 jit_solution(16902844436113407405)
XLA Ops:
  0.6 2.7 %shard_map.59 = (f32[8,4224]{1,0:T(8,128)S(1)}, f32[8,4224]{1,0:T(8,128)S(1)}, bf16[8,4,256,256]{3,2,1,0:T(8,128)(2,1)S(1)}) custom-call(s32[4,8]{1,0:T(4,128)} %bitcast.3, s32[1,8]{1,0:T(1,128)} %bitcast.11, f32[8,2048]{1,0:T(8,128)} %prev_ref.3, bf16[8,4,256,256]{3,2,1,0:T(8,128)(2,1)} %source_ref.1), custom_call_target="tpu_custom_call" | custom-call | tf_op jit(solution)/shard_map/pallas_call | solution.py:249
  5.0 4.1 %collective-permute-start.3 = (s16[8,4224]{1,0:T(8,128)(2,1)S(1)}, s16[8,4224]{1,0:T(8,128)(2,1)S(1)}, u32[]{:S(2)}, u32[]{:S(2)}) collective-permute-start(s16[8,4224]{1,0:T(8,128)(2,1)S(1)} %shard_map.60.own_ref), channel_id=1, source_target_pairs={{0,64},{32,96},{64,0},{96,32},{1,65},{33,97},{65,1},{97,33},{2,66}... | collective-permute-start | bytes 202760 | tf_op jit(solution)/shard_map/ppermute | solution.py:272
  11.5 3.0 %collective-permute-done.2.right_ref = s16[8,4224]{1,0:T(8,128)(2,1)S(1)} collective-permute-done((s16[8,4224]{1,0:T(8,128)(2,1)S(1)}, s16[8,4224]{1,0:T(8,128)(2,1)S(1)}, u32[]{:S(2)}, u32[]{:S(2)}) %collective-permute-start.2) | collective-permute-done | bytes 67616 | tf_op jit(solution)/shard_map/ppermute | solution.py:272
  17.4 3.0 %collective-permute-start.7 = (f32[8,2176]{1,0:T(8,128)S(1)}, f32[8,2176]{1,0:T(8,128)S(1)}, u32[]{:S(2)}, u32[]{:S(2)}) collective-permute-start(f32[8,2176]{1,0:T(8,128)S(1)} %shard_map.63), channel_id=1, source_target_pairs={{0,8},{4,12},{8,0},{12,4},{1,9},{5,13},{9,1},{13,5},{2,10},{6,14},... | collective-permute-start | bytes 208904 | tf_op jit(solution)/shard_map/ppermute | solution.py:272
  21.5 1.8 %collective-permute-done.7 = f32[8,2176]{1,0:T(8,128)S(1)} collective-permute-done((f32[8,2176]{1,0:T(8,128)S(1)}, f32[8,2176]{1,0:T(8,128)S(1)}, u32[]{:S(2)}, u32[]{:S(2)}) %collective-permute-start.7) | collective-permute-done | bytes 69664 | tf_op jit(solution)/shard_map/ppermute | solution.py:272
  23.3 2.6 %collective-permute-done.6 = f32[8,2176]{1,0:T(8,128)S(1)} collective-permute-done((f32[8,2176]{1,0:T(8,128)S(1)}, f32[8,2176]{1,0:T(8,128)S(1)}, u32[]{:S(2)}, u32[]{:S(2)}) %collective-permute-start.6) | collective-permute-done | bytes 69664 | tf_op jit(solution)/shard_map/ppermute | solution.py:272
  25.9 3.3 %collective-permute-start.10 = (f32[8,2176]{1,0:T(8,128)S(1)}, f32[8,2176]{1,0:T(8,128)S(1)}, u32[]{:S(2)}, u32[]{:S(2)}) collective-permute-start(f32[8,2176]{1,0:T(8,128)S(1)} %add_add_fusion.3.own_ref), channel_id=1, source_target_pairs={{0,2},{1,3},{2,0},{3,1},{4,6},{5,7},{6,4},{7,5},{8,10},{9,11},{10,... | collective-permute-start | bytes 208904 | tf_op jit(solution)/shard_map/ppermute | solution.py:272
  30.3 1.6 %collective-permute-done.10.far_ref = f32[8,2176]{1,0:T(8,128)S(1)} collective-permute-done((f32[8,2176]{1,0:T(8,128)S(1)}, f32[8,2176]{1,0:T(8,128)S(1)}, u32[]{:S(2)}, u32[]{:S(2)}) %collective-permute-start.10) | collective-permute-done | bytes 69664 | tf_op jit(solution)/shard_map/ppermute | solution.py:272
  31.8 2.9 %collective-permute-done.9.right_ref = f32[8,2176]{1,0:T(8,128)S(1)} collective-permute-done((f32[8,2176]{1,0:T(8,128)S(1)}, f32[8,2176]{1,0:T(8,128)S(1)}, u32[]{:S(2)}, u32[]{:S(2)}) %collective-permute-start.9) | collective-permute-done | bytes 69664 | tf_op jit(solution)/shard_map/ppermute | solution.py:272
  37.7 1.9 %collective-permute-start.14 = (s16[8,4224]{1,0:T(8,128)(2,1)S(1)}, s16[8,4224]{1,0:T(8,128)(2,1)S(1)}, u32[]{:S(2)}, u32[]{:S(2)}) collective-permute-start(s16[8,4224]{1,0:T(8,128)(2,1)S(1)} %shard_map.65.own_ref), channel_id=1, source_target_pairs={{0,64},{32,96},{64,0},{96,32},{1,65},{33,97},{65,1},{97,33},{2,66}... | collective-permute-start | bytes 202760 | tf_op jit(solution)/shard_map/ppermute | solution.py:272
  41.3 2.3 %collective-permute-done.14.far_ref = s16[8,4224]{1,0:T(8,128)(2,1)S(1)} collective-permute-done((s16[8,4224]{1,0:T(8,128)(2,1)S(1)}, s16[8,4224]{1,0:T(8,128)(2,1)S(1)}, u32[]{:S(2)}, u32[]{:S(2)}) %collective-permute-start.14) | collective-permute-done | bytes 67616 | tf_op jit(solution)/shard_map/ppermute | solution.py:272
  43.6 1.6 %collective-permute-done.13.right_ref = s16[8,4224]{1,0:T(8,128)(2,1)S(1)} collective-permute-done((s16[8,4224]{1,0:T(8,128)(2,1)S(1)}, s16[8,4224]{1,0:T(8,128)(2,1)S(1)}, u32[]{:S(2)}, u32[]{:S(2)}) %collective-permute-start.13) | collective-permute-done | bytes 67616 | tf_op jit(solution)/shard_map/ppermute | solution.py:272
  49.5 1.6 %collective-permute-start.17 = (f32[8,2176]{1,0:T(8,128)S(1)}, f32[8,2176]{1,0:T(8,128)S(1)}, u32[]{:S(2)}, u32[]{:S(2)}) collective-permute-start(f32[8,2176]{1,0:T(8,128)S(1)} %shard_map.67), channel_id=1, source_target_pairs={{0,12},{4,8},{8,4},{12,0},{1,13},{5,9},{9,5},{13,1},{2,14},{6,10},... | collective-permute-start | bytes 208904 | tf_op jit(solution)/shard_map/ppermute | solution.py:272
  51.5 2.4 %collective-permute-done.18 = f32[8,2176]{1,0:T(8,128)S(1)} collective-permute-done((f32[8,2176]{1,0:T(8,128)S(1)}, f32[8,2176]{1,0:T(8,128)S(1)}, u32[]{:S(2)}, u32[]{:S(2)}) %collective-permute-start.18) | collective-permute-done | bytes 69664 | tf_op jit(solution)/shard_map/ppermute | solution.py:272
  55.4 1.6 %collective-permute-start.21 = (f32[8,2176]{1,0:T(8,128)S(1)}, f32[8,2176]{1,0:T(8,128)S(1)}, u32[]{:S(2)}, u32[]{:S(2)}) collective-permute-start(f32[8,2176]{1,0:T(8,128)S(1)} %add_add_fusion.2.own_ref), channel_id=1, source_target_pairs={{0,2},{1,3},{2,0},{3,1},{4,6},{5,7},{6,4},{7,5},{8,10},{9,11},{10,... | collective-permute-start | bytes 208904 | tf_op jit(solution)/shard_map/ppermute | solution.py:272
  59.0 2.4 %collective-permute-done.21.far_ref = f32[8,2176]{1,0:T(8,128)S(1)} collective-permute-done((f32[8,2176]{1,0:T(8,128)S(1)}, f32[8,2176]{1,0:T(8,128)S(1)}, u32[]{:S(2)}, u32[]{:S(2)}) %collective-permute-start.21) | collective-permute-done | bytes 69664 | tf_op jit(solution)/shard_map/ppermute | solution.py:272
  65.6 1.9 %collective-permute-start.25 = (s16[8,4224]{1,0:T(8,128)(2,1)S(1)}, s16[8,4224]{1,0:T(8,128)(2,1)S(1)}, u32[]{:S(2)}, u32[]{:S(2)}) collective-permute-start(s16[8,4224]{1,0:T(8,128)(2,1)S(1)} %shard_map.69.own_ref), channel_id=1, source_target_pairs={{0,64},{32,96},{64,0},{96,32},{1,65},{33,97},{65,1},{97,33},{2,66}... | collective-permute-start | bytes 202760 | tf_op jit(solution)/shard_map/ppermute | solution.py:272
  69.1 2.3 %collective-permute-done.25.far_ref = s16[8,4224]{1,0:T(8,128)(2,1)S(1)} collective-permute-done((s16[8,4224]{1,0:T(8,128)(2,1)S(1)}, s16[8,4224]{1,0:T(8,128)(2,1)S(1)}, u32[]{:S(2)}, u32[]{:S(2)}) %collective-permute-start.25) | collective-permute-done | bytes 67616 | tf_op jit(solution)/shard_map/ppermute | solution.py:272
  75.9 1.9 %collective-permute-start.29 = (f32[8,2176]{1,0:T(8,128)S(1)}, f32[8,2176]{1,0:T(8,128)S(1)}, u32[]{:S(2)}, u32[]{:S(2)}) collective-permute-start(f32[8,2176]{1,0:T(8,128)S(1)} %shard_map.71), channel_id=1, source_target_pairs={{0,8},{4,12},{8,0},{12,4},{1,9},{5,13},{9,1},{13,5},{2,10},{6,14},... | collective-permute-start | bytes 208904 | tf_op jit(solution)/shard_map/ppermute | solution.py:272
  79.4 2.3 %collective-permute-done.29 = f32[8,2176]{1,0:T(8,128)S(1)} collective-permute-done((f32[8,2176]{1,0:T(8,128)S(1)}, f32[8,2176]{1,0:T(8,128)S(1)}, u32[]{:S(2)}, u32[]{:S(2)}) %collective-permute-start.29) | collective-permute-done | bytes 69664 | tf_op jit(solution)/shard_map/ppermute | solution.py:272
  81.7 1.6 %collective-permute-done.28 = f32[8,2176]{1,0:T(8,128)S(1)} collective-permute-done((f32[8,2176]{1,0:T(8,128)S(1)}, f32[8,2176]{1,0:T(8,128)S(1)}, u32[]{:S(2)}, u32[]{:S(2)}) %collective-permute-start.28) | collective-permute-done | bytes 69664 | tf_op jit(solution)/shard_map/ppermute | solution.py:272
  83.3 2.3 %collective-permute-start.32 = (f32[8,2176]{1,0:T(8,128)S(1)}, f32[8,2176]{1,0:T(8,128)S(1)}, u32[]{:S(2)}, u32[]{:S(2)}) collective-permute-start(f32[8,2176]{1,0:T(8,128)S(1)} %add_add_fusion.1.own_ref), channel_id=1, source_target_pairs={{0,2},{1,3},{2,0},{3,1},{4,6},{5,7},{6,4},{7,5},{8,10},{9,11},{10,... | collective-permute-start | bytes 208904 | tf_op jit(solution)/shard_map/ppermute | solution.py:272
  86.9 2.4 %collective-permute-done.32.far_ref = f32[8,2176]{1,0:T(8,128)S(1)} collective-permute-done((f32[8,2176]{1,0:T(8,128)S(1)}, f32[8,2176]{1,0:T(8,128)S(1)}, u32[]{:S(2)}, u32[]{:S(2)}) %collective-permute-start.32) | collective-permute-done | bytes 69664 | tf_op jit(solution)/shard_map/ppermute | solution.py:272
  89.3 1.8 %collective-permute-done.31.right_ref = f32[8,2176]{1,0:T(8,128)S(1)} collective-permute-done((f32[8,2176]{1,0:T(8,128)S(1)}, f32[8,2176]{1,0:T(8,128)S(1)}, u32[]{:S(2)}, u32[]{:S(2)}) %collective-permute-start.31) | collective-permute-done | bytes 69664 | tf_op jit(solution)/shard_map/ppermute | solution.py:272
  94.1 1.9 %collective-permute-start.36 = (s16[8,4224]{1,0:T(8,128)(2,1)S(1)}, s16[8,4224]{1,0:T(8,128)(2,1)S(1)}, u32[]{:S(2)}, u32[]{:S(2)}) collective-permute-start(s16[8,4224]{1,0:T(8,128)(2,1)S(1)} %shard_map.73.own_ref), channel_id=1, source_target_pairs={{0,64},{32,96},{64,0},{96,32},{1,65},{33,97},{65,1},{97,33},{2,66}... | collective-permute-start | bytes 202760 | tf_op jit(solution)/shard_map/ppermute | solution.py:272
  97.7 2.3 %collective-permute-done.36.far_ref = s16[8,4224]{1,0:T(8,128)(2,1)S(1)} collective-permute-done((s16[8,4224]{1,0:T(8,128)(2,1)S(1)}, s16[8,4224]{1,0:T(8,128)(2,1)S(1)}, u32[]{:S(2)}, u32[]{:S(2)}) %collective-permute-start.36) | collective-permute-done | bytes 67616 | tf_op jit(solution)/shard_map/ppermute | solution.py:272
  104.4 1.7 %collective-permute-start.40 = (f32[8,2176]{1,0:T(8,128)S(1)}, f32[8,2176]{1,0:T(8,128)S(1)}, u32[]{:S(2)}, u32[]{:S(2)}) collective-permute-start(f32[8,2176]{1,0:T(8,128)S(1)} %shard_map.75), channel_id=1, source_target_pairs={{0,8},{4,12},{8,0},{12,4},{1,9},{5,13},{9,1},{13,5},{2,10},{6,14},... | collective-permute-start | bytes 208904 | tf_op jit(solution)/shard_map/ppermute | solution.py:272
  107.9 2.4 %collective-permute-done.40 = f32[8,2176]{1,0:T(8,128)S(1)} collective-permute-done((f32[8,2176]{1,0:T(8,128)S(1)}, f32[8,2176]{1,0:T(8,128)S(1)}, u32[]{:S(2)}, u32[]{:S(2)}) %collective-permute-start.40) | collective-permute-done | bytes 69664 | tf_op jit(solution)/shard_map/ppermute | solution.py:272
  111.8 1.6 %collective-permute-start.43 = (f32[8,2176]{1,0:T(8,128)S(1)}, f32[8,2176]{1,0:T(8,128)S(1)}, u32[]{:S(2)}, u32[]{:S(2)}) collective-permute-start(f32[8,2176]{1,0:T(8,128)S(1)} %add_add_fusion.own_ref), channel_id=1, source_target_pairs={{0,2},{1,3},{2,0},{3,1},{4,6},{5,7},{6,4},{7,5},{8,10},{9,11},{10,... | collective-permute-start | bytes 208904 | tf_op jit(solution)/shard_map/ppermute | solution.py:272
  115.4 2.6 %collective-permute-done.43.far_ref = f32[8,2176]{1,0:T(8,128)S(1)} collective-permute-done((f32[8,2176]{1,0:T(8,128)S(1)}, f32[8,2176]{1,0:T(8,128)S(1)}, u32[]{:S(2)}, u32[]{:S(2)}) %collective-permute-start.43) | collective-permute-done | bytes 69664 | tf_op jit(solution)/shard_map/ppermute | solution.py:272
  120.5 1.9 %collective-permute-start.47 = (f32[8,128]{1,0:T(8,128)S(1)}, f32[8,128]{1,0:T(8,128)S(1)}, u32[]{:S(2)}, u32[]{:S(2)}) collective-permute-start(f32[8,128]{1,0:T(8,128)S(1)} %add.51.own_ref), channel_id=1, source_target_pairs={{0,64},{32,96},{64,0},{96,32},{1,65},{33,97},{65,1},{97,33},{2,66}... | collective-permute-start | bytes 12296 | tf_op jit(solution)/shard_map/ppermute | solution.py:272
  125.6 1.6 %collective-permute-done.46.right_ref = f32[8,128]{1,0:T(8,128)S(1)} collective-permute-done((f32[8,128]{1,0:T(8,128)S(1)}, f32[8,128]{1,0:T(8,128)S(1)}, u32[]{:S(2)}, u32[]{:S(2)}) %collective-permute-start.46) | collective-permute-done | bytes 4128 | tf_op jit(solution)/shard_map/ppermute | solution.py:272
  (95 shorter events, 55.8 us)
Async XLA Ops:
  5.0 6.5 %collective-permute-start.3 = (s16[8,4224]{1,0:T(8,128)(2,1)S(1)}, s16[8,4224]{1,0:T(8,128)(2,1)S(1)}, u32[]{:S(2)}, u32[]{:S(2)}) collective-permute-start(s16[8,4224]{1,0:T(8,128)(2,1)S(1)} %shard_map.60.own_ref), channel_id=1, source_target_pairs={{0,64},{32,96},{64,0},{96,32},{1,65},{33,97},{65,1},{97,33},{2,66}... | collective-permute-start | bytes 202760 | tf_op jit(solution)/shard_map/ppermute | solution.py:272
  9.0 5.5 %collective-permute-start.2 = (s16[8,4224]{1,0:T(8,128)(2,1)S(1)}, s16[8,4224]{1,0:T(8,128)(2,1)S(1)}, u32[]{:S(2)}, u32[]{:S(2)}) collective-permute-start(s16[8,4224]{1,0:T(8,128)(2,1)S(1)} %shard_map.60.own_ref), channel_id=1, source_target_pairs={{0,96},{32,64},{64,32},{96,0},{1,97},{33,65},{65,33},{97,1},{2,98}... | collective-permute-start | bytes 202760 | tf_op jit(solution)/shard_map/ppermute | solution.py:272
  9.7 4.8 %collective-permute-start.1 = (s16[8,4224]{1,0:T(8,128)(2,1)S(1)}, s16[8,4224]{1,0:T(8,128)(2,1)S(1)}, u32[]{:S(2)}, u32[]{:S(2)}) collective-permute-start(s16[8,4224]{1,0:T(8,128)(2,1)S(1)} %shard_map.60.own_ref), channel_id=1, source_target_pairs={{0,32},{32,0},{64,96},{96,64},{1,33},{33,1},{65,97},{97,65},{2,34}... | collective-permute-start | bytes 202760 | tf_op jit(solution)/shard_map/ppermute | solution.py:272
  17.4 5.9 %collective-permute-start.7 = (f32[8,2176]{1,0:T(8,128)S(1)}, f32[8,2176]{1,0:T(8,128)S(1)}, u32[]{:S(2)}, u32[]{:S(2)}) collective-permute-start(f32[8,2176]{1,0:T(8,128)S(1)} %shard_map.63), channel_id=1, source_target_pairs={{0,8},{4,12},{8,0},{12,4},{1,9},{5,13},{9,1},{13,5},{2,10},{6,14},... | collective-permute-start | bytes 208904 | tf_op jit(solution)/shard_map/ppermute | solution.py:272
  20.4 5.5 %collective-permute-start.6 = (f32[8,2176]{1,0:T(8,128)S(1)}, f32[8,2176]{1,0:T(8,128)S(1)}, u32[]{:S(2)}, u32[]{:S(2)}) collective-permute-start(f32[8,2176]{1,0:T(8,128)S(1)} %shard_map.63), channel_id=1, source_target_pairs={{0,12},{4,8},{8,4},{12,0},{1,13},{5,9},{9,5},{13,1},{2,14},{6,10},... | collective-permute-start | bytes 208904 | tf_op jit(solution)/shard_map/ppermute | solution.py:272
  21.5 4.4 %collective-permute-start.5 = (f32[8,2176]{1,0:T(8,128)S(1)}, f32[8,2176]{1,0:T(8,128)S(1)}, u32[]{:S(2)}, u32[]{:S(2)}) collective-permute-start(f32[8,2176]{1,0:T(8,128)S(1)} %shard_map.63), channel_id=1, source_target_pairs={{0,4},{4,0},{8,12},{12,8},{1,5},{5,1},{9,13},{13,9},{2,6},{6,2},{1... | collective-permute-start | bytes 208904 | tf_op jit(solution)/shard_map/ppermute | solution.py:272
  25.9 5.9 %collective-permute-start.10 = (f32[8,2176]{1,0:T(8,128)S(1)}, f32[8,2176]{1,0:T(8,128)S(1)}, u32[]{:S(2)}, u32[]{:S(2)}) collective-permute-start(f32[8,2176]{1,0:T(8,128)S(1)} %add_add_fusion.3.own_ref), channel_id=1, source_target_pairs={{0,2},{1,3},{2,0},{3,1},{4,6},{5,7},{6,4},{7,5},{8,10},{9,11},{10,... | collective-permute-start | bytes 208904 | tf_op jit(solution)/shard_map/ppermute | solution.py:272
  29.2 5.5 %collective-permute-start.9 = (f32[8,2176]{1,0:T(8,128)S(1)}, f32[8,2176]{1,0:T(8,128)S(1)}, u32[]{:S(2)}, u32[]{:S(2)}) collective-permute-start(f32[8,2176]{1,0:T(8,128)S(1)} %add_add_fusion.3.own_ref), channel_id=1, source_target_pairs={{0,3},{1,2},{2,1},{3,0},{4,7},{5,6},{6,5},{7,4},{8,11},{9,10},{10,... | collective-permute-start | bytes 208904 | tf_op jit(solution)/shard_map/ppermute | solution.py:272
  30.3 4.5 %collective-permute-start.8 = (f32[8,2176]{1,0:T(8,128)S(1)}, f32[8,2176]{1,0:T(8,128)S(1)}, u32[]{:S(2)}, u32[]{:S(2)}) collective-permute-start(f32[8,2176]{1,0:T(8,128)S(1)} %add_add_fusion.3.own_ref), channel_id=1, source_target_pairs={{0,1},{1,0},{2,3},{3,2},{4,5},{5,4},{6,7},{7,6},{8,9},{9,8},{10,11... | collective-permute-start | bytes 208904 | tf_op jit(solution)/shard_map/ppermute | solution.py:272
  37.7 5.9 %collective-permute-start.14 = (s16[8,4224]{1,0:T(8,128)(2,1)S(1)}, s16[8,4224]{1,0:T(8,128)(2,1)S(1)}, u32[]{:S(2)}, u32[]{:S(2)}) collective-permute-start(s16[8,4224]{1,0:T(8,128)(2,1)S(1)} %shard_map.65.own_ref), channel_id=1, source_target_pairs={{0,64},{32,96},{64,0},{96,32},{1,65},{33,97},{65,1},{97,33},{2,66}... | collective-permute-start | bytes 202760 | tf_op jit(solution)/shard_map/ppermute | solution.py:272
  39.7 5.5 %collective-permute-start.13 = (s16[8,4224]{1,0:T(8,128)(2,1)S(1)}, s16[8,4224]{1,0:T(8,128)(2,1)S(1)}, u32[]{:S(2)}, u32[]{:S(2)}) collective-permute-start(s16[8,4224]{1,0:T(8,128)(2,1)S(1)} %shard_map.65.own_ref), channel_id=1, source_target_pairs={{0,96},{32,64},{64,32},{96,0},{1,97},{33,65},{65,33},{97,1},{2,98}... | collective-permute-start | bytes 202760 | tf_op jit(solution)/shard_map/ppermute | solution.py:272
  40.6 4.6 %collective-permute-start.12 = (s16[8,4224]{1,0:T(8,128)(2,1)S(1)}, s16[8,4224]{1,0:T(8,128)(2,1)S(1)}, u32[]{:S(2)}, u32[]{:S(2)}) collective-permute-start(s16[8,4224]{1,0:T(8,128)(2,1)S(1)} %shard_map.65.own_ref), channel_id=1, source_target_pairs={{0,32},{32,0},{64,96},{96,64},{1,33},{33,1},{65,97},{97,65},{2,34}... | collective-permute-start | bytes 202760 | tf_op jit(solution)/shard_map/ppermute | solution.py:272
  48.0 5.9 %collective-permute-start.18 = (f32[8,2176]{1,0:T(8,128)S(1)}, f32[8,2176]{1,0:T(8,128)S(1)}, u32[]{:S(2)}, u32[]{:S(2)}) collective-permute-start(f32[8,2176]{1,0:T(8,128)S(1)} %shard_map.67), channel_id=1, source_target_pairs={{0,8},{4,12},{8,0},{12,4},{1,9},{5,13},{9,1},{13,5},{2,10},{6,14},... | collective-permute-start | bytes 208904 | tf_op jit(solution)/shard_map/ppermute | solution.py:272
  49.5 5.9 %collective-permute-start.17 = (f32[8,2176]{1,0:T(8,128)S(1)}, f32[8,2176]{1,0:T(8,128)S(1)}, u32[]{:S(2)}, u32[]{:S(2)}) collective-permute-start(f32[8,2176]{1,0:T(8,128)S(1)} %shard_map.67), channel_id=1, source_target_pairs={{0,12},{4,8},{8,4},{12,0},{1,13},{5,9},{9,5},{13,1},{2,14},{6,10},... | collective-permute-start | bytes 208904 | tf_op jit(solution)/shard_map/ppermute | solution.py:272
  51.1 4.3 %collective-permute-start.16 = (f32[8,2176]{1,0:T(8,128)S(1)}, f32[8,2176]{1,0:T(8,128)S(1)}, u32[]{:S(2)}, u32[]{:S(2)}) collective-permute-start(f32[8,2176]{1,0:T(8,128)S(1)} %shard_map.67), channel_id=1, source_target_pairs={{0,4},{4,0},{8,12},{12,8},{1,5},{5,1},{9,13},{13,9},{2,6},{6,2},{1... | collective-permute-start | bytes 208904 | tf_op jit(solution)/shard_map/ppermute | solution.py:272
  55.4 6.0 %collective-permute-start.21 = (f32[8,2176]{1,0:T(8,128)S(1)}, f32[8,2176]{1,0:T(8,128)S(1)}, u32[]{:S(2)}, u32[]{:S(2)}) collective-permute-start(f32[8,2176]{1,0:T(8,128)S(1)} %add_add_fusion.2.own_ref), channel_id=1, source_target_pairs={{0,2},{1,3},{2,0},{3,1},{4,6},{5,7},{6,4},{7,5},{8,10},{9,11},{10,... | collective-permute-start | bytes 208904 | tf_op jit(solution)/shard_map/ppermute | solution.py:272
  57.0 5.5 %collective-permute-start.20 = (f32[8,2176]{1,0:T(8,128)S(1)}, f32[8,2176]{1,0:T(8,128)S(1)}, u32[]{:S(2)}, u32[]{:S(2)}) collective-permute-start(f32[8,2176]{1,0:T(8,128)S(1)} %add_add_fusion.2.own_ref), channel_id=1, source_target_pairs={{0,3},{1,2},{2,1},{3,0},{4,7},{5,6},{6,5},{7,4},{8,11},{9,10},{10,... | collective-permute-start | bytes 208904 | tf_op jit(solution)/shard_map/ppermute | solution.py:272
  65.6 5.9 %collective-permute-start.25 = (s16[8,4224]{1,0:T(8,128)(2,1)S(1)}, s16[8,4224]{1,0:T(8,128)(2,1)S(1)}, u32[]{:S(2)}, u32[]{:S(2)}) collective-permute-start(s16[8,4224]{1,0:T(8,128)(2,1)S(1)} %shard_map.69.own_ref), channel_id=1, source_target_pairs={{0,64},{32,96},{64,0},{96,32},{1,65},{33,97},{65,1},{97,33},{2,66}... | collective-permute-start | bytes 202760 | tf_op jit(solution)/shard_map/ppermute | solution.py:272
  67.5 5.5 %collective-permute-start.24 = (s16[8,4224]{1,0:T(8,128)(2,1)S(1)}, s16[8,4224]{1,0:T(8,128)(2,1)S(1)}, u32[]{:S(2)}, u32[]{:S(2)}) collective-permute-start(s16[8,4224]{1,0:T(8,128)(2,1)S(1)} %shard_map.69.own_ref), channel_id=1, source_target_pairs={{0,96},{32,64},{64,32},{96,0},{1,97},{33,65},{65,33},{97,1},{2,98}... | collective-permute-start | bytes 202760 | tf_op jit(solution)/shard_map/ppermute | solution.py:272
  75.9 5.8 %collective-permute-start.29 = (f32[8,2176]{1,0:T(8,128)S(1)}, f32[8,2176]{1,0:T(8,128)S(1)}, u32[]{:S(2)}, u32[]{:S(2)}) collective-permute-start(f32[8,2176]{1,0:T(8,128)S(1)} %shard_map.71), channel_id=1, source_target_pairs={{0,8},{4,12},{8,0},{12,4},{1,9},{5,13},{9,1},{13,5},{2,10},{6,14},... | collective-permute-start | bytes 208904 | tf_op jit(solution)/shard_map/ppermute | solution.py:272
  77.8 5.5 %collective-permute-start.28 = (f32[8,2176]{1,0:T(8,128)S(1)}, f32[8,2176]{1,0:T(8,128)S(1)}, u32[]{:S(2)}, u32[]{:S(2)}) collective-permute-start(f32[8,2176]{1,0:T(8,128)S(1)} %shard_map.71), channel_id=1, source_target_pairs={{0,12},{4,8},{8,4},{12,0},{1,13},{5,9},{9,5},{13,1},{2,14},{6,10},... | collective-permute-start | bytes 208904 | tf_op jit(solution)/shard_map/ppermute | solution.py:272
  83.3 6.0 %collective-permute-start.32 = (f32[8,2176]{1,0:T(8,128)S(1)}, f32[8,2176]{1,0:T(8,128)S(1)}, u32[]{:S(2)}, u32[]{:S(2)}) collective-permute-start(f32[8,2176]{1,0:T(8,128)S(1)} %add_add_fusion.1.own_ref), channel_id=1, source_target_pairs={{0,2},{1,3},{2,0},{3,1},{4,6},{5,7},{6,4},{7,5},{8,10},{9,11},{10,... | collective-permute-start | bytes 208904 | tf_op jit(solution)/shard_map/ppermute | solution.py:272
  85.6 5.5 %collective-permute-start.31 = (f32[8,2176]{1,0:T(8,128)S(1)}, f32[8,2176]{1,0:T(8,128)S(1)}, u32[]{:S(2)}, u32[]{:S(2)}) collective-permute-start(f32[8,2176]{1,0:T(8,128)S(1)} %add_add_fusion.1.own_ref), channel_id=1, source_target_pairs={{0,3},{1,2},{2,1},{3,0},{4,7},{5,6},{6,5},{7,4},{8,11},{9,10},{10,... | collective-permute-start | bytes 208904 | tf_op jit(solution)/shard_map/ppermute | solution.py:272
  86.8 4.3 %collective-permute-start.30 = (f32[8,2176]{1,0:T(8,128)S(1)}, f32[8,2176]{1,0:T(8,128)S(1)}, u32[]{:S(2)}, u32[]{:S(2)}) collective-permute-start(f32[8,2176]{1,0:T(8,128)S(1)} %add_add_fusion.1.own_ref), channel_id=1, source_target_pairs={{0,1},{1,0},{2,3},{3,2},{4,5},{5,4},{6,7},{7,6},{8,9},{9,8},{10,11... | collective-permute-start | bytes 208904 | tf_op jit(solution)/shard_map/ppermute | solution.py:272
  94.1 5.9 %collective-permute-start.36 = (s16[8,4224]{1,0:T(8,128)(2,1)S(1)}, s16[8,4224]{1,0:T(8,128)(2,1)S(1)}, u32[]{:S(2)}, u32[]{:S(2)}) collective-permute-start(s16[8,4224]{1,0:T(8,128)(2,1)S(1)} %shard_map.73.own_ref), channel_id=1, source_target_pairs={{0,64},{32,96},{64,0},{96,32},{1,65},{33,97},{65,1},{97,33},{2,66}... | collective-permute-start | bytes 202760 | tf_op jit(solution)/shard_map/ppermute | solution.py:272
  96.1 5.5 %collective-permute-start.35 = (s16[8,4224]{1,0:T(8,128)(2,1)S(1)}, s16[8,4224]{1,0:T(8,128)(2,1)S(1)}, u32[]{:S(2)}, u32[]{:S(2)}) collective-permute-start(s16[8,4224]{1,0:T(8,128)(2,1)S(1)} %shard_map.73.own_ref), channel_id=1, source_target_pairs={{0,96},{32,64},{64,32},{96,0},{1,97},{33,65},{65,33},{97,1},{2,98}... | collective-permute-start | bytes 202760 | tf_op jit(solution)/shard_map/ppermute | solution.py:272
  104.4 5.9 %collective-permute-start.40 = (f32[8,2176]{1,0:T(8,128)S(1)}, f32[8,2176]{1,0:T(8,128)S(1)}, u32[]{:S(2)}, u32[]{:S(2)}) collective-permute-start(f32[8,2176]{1,0:T(8,128)S(1)} %shard_map.75), channel_id=1, source_target_pairs={{0,8},{4,12},{8,0},{12,4},{1,9},{5,13},{9,1},{13,5},{2,10},{6,14},... | collective-permute-start | bytes 208904 | tf_op jit(solution)/shard_map/ppermute | solution.py:272
  106.2 5.6 %collective-permute-start.39 = (f32[8,2176]{1,0:T(8,128)S(1)}, f32[8,2176]{1,0:T(8,128)S(1)}, u32[]{:S(2)}, u32[]{:S(2)}) collective-permute-start(f32[8,2176]{1,0:T(8,128)S(1)} %shard_map.75), channel_id=1, source_target_pairs={{0,12},{4,8},{8,4},{12,0},{1,13},{5,9},{9,5},{13,1},{2,14},{6,10},... | collective-permute-start | bytes 208904 | tf_op jit(solution)/shard_map/ppermute | solution.py:272
  111.8 6.1 %collective-permute-start.43 = (f32[8,2176]{1,0:T(8,128)S(1)}, f32[8,2176]{1,0:T(8,128)S(1)}, u32[]{:S(2)}, u32[]{:S(2)}) collective-permute-start(f32[8,2176]{1,0:T(8,128)S(1)} %add_add_fusion.own_ref), channel_id=1, source_target_pairs={{0,2},{1,3},{2,0},{3,1},{4,6},{5,7},{6,4},{7,5},{8,10},{9,11},{10,... | collective-permute-start | bytes 208904 | tf_op jit(solution)/shard_map/ppermute | solution.py:272
  113.4 5.5 %collective-permute-start.42 = (f32[8,2176]{1,0:T(8,128)S(1)}, f32[8,2176]{1,0:T(8,128)S(1)}, u32[]{:S(2)}, u32[]{:S(2)}) collective-permute-start(f32[8,2176]{1,0:T(8,128)S(1)} %add_add_fusion.own_ref), channel_id=1, source_target_pairs={{0,3},{1,2},{2,1},{3,0},{4,7},{5,6},{6,5},{7,4},{8,11},{9,10},{10,... | collective-permute-start | bytes 208904 | tf_op jit(solution)/shard_map/ppermute | solution.py:272
  120.5 5.1 %collective-permute-start.47 = (f32[8,128]{1,0:T(8,128)S(1)}, f32[8,128]{1,0:T(8,128)S(1)}, u32[]{:S(2)}, u32[]{:S(2)}) collective-permute-start(f32[8,128]{1,0:T(8,128)S(1)} %add.51.own_ref), channel_id=1, source_target_pairs={{0,64},{32,96},{64,0},{96,32},{1,65},{33,97},{65,1},{97,33},{2,66}... | collective-permute-start | bytes 12296 | tf_op jit(solution)/shard_map/ppermute | solution.py:272
  122.4 4.8 %collective-permute-start.46 = (f32[8,128]{1,0:T(8,128)S(1)}, f32[8,128]{1,0:T(8,128)S(1)}, u32[]{:S(2)}, u32[]{:S(2)}) collective-permute-start(f32[8,128]{1,0:T(8,128)S(1)} %add.51.own_ref), channel_id=1, source_target_pairs={{0,96},{32,64},{64,32},{96,0},{1,97},{33,65},{65,33},{97,1},{2,98}... | collective-permute-start | bytes 12296 | tf_op jit(solution)/shard_map/ppermute | solution.py:272
  (19 other events, 58.7 us)

commit v7 on v6

--- a/solution.py
+++ b/solution.py
@@ -91,50 +91,21 @@
     scatter_products(u_ref[...], put, tiles_ref, keep_ref, send_ref, acc_ref, copies)
 
 
-def ray_vector(own_ref, left_ref, right_ref, far_ref, prev_ref, beta_ref):
-    total = (own_ref[...] + far_ref[...]) + (left_ref[...] + right_ref[...])
-    rows = prev_ref.shape[1]
-    alpha = jnp.sqrt(lane_sum(total[:, rows:]) + EPS)
-    u = total[:, :rows] / alpha - (alpha / beta_ref[:, :1]) * prev_ref[...]
-    return u, alpha
-
-
-def next_adjoint(
-    pattern_ref, counts_ref, own_ref, left_ref, right_ref, far_ref, prev_ref, beta_ref, tiles_ref,
-    keep_ref, send_ref, u_ref, alpha_ref, acc_ref,
-):
-    u, alpha = ray_vector(own_ref, left_ref, right_ref, far_ref, prev_ref, beta_ref)
-    u_ref[...] = u
-    alpha_ref[...] = wide(alpha)
-    put = slots_of(pattern_ref, counts_ref, BLK_DEV // 2 + 1, BLK_DEV // 2)
-    scatter_products(u, put, tiles_ref, keep_ref, send_ref, acc_ref)
-
-
-def last_norm(
-    own_ref, left_ref, right_ref, far_ref, prev_ref, beta_ref, out_ref, alpha_ref
-):
-    u, alpha = ray_vector(own_ref, left_ref, right_ref, far_ref, prev_ref, beta_ref)
-    alpha_ref[...] = wide(alpha)
-    out_ref[...] = fold_sq(u, 128)
-
-
 def split(value, digits):
     power = jnp.floor(jnp.log2(value))
     return power, value * jnp.exp2(-power) * digits
 
 
-def pack(keep_ref, other_ref, out_ref):
-    total = keep_ref[...] + other_ref[...]
-    width = out_ref.shape[1] - 128
-    body = total[:, :width]
+def encode(body, squares, out_ref):
+    width = body.shape[1]
     peak = jnp.maximum(jnp.max(jnp.abs(body), axis=1, keepdims=True), TINY)
     power, mantissa = split(peak, DIGITS)
     mantissa = jnp.floor(mantissa) + 1.0
     scale = mantissa * jnp.exp2(power) * (1.0 / DIGITS)
-    norm_power, norm = split(jnp.maximum(lane_sum(total[:, width:]), TINY), DIGITS)
+    norm_power, norm = split(jnp.maximum(squares, TINY), DIGITS)
     high = jnp.floor(norm)
     low = (norm - high) * DIGITS
-    lane = lax.broadcasted_iota(jnp.int32, (total.shape[0], 128), 1)
+    lane = lax.broadcasted_iota(jnp.int32, (body.shape[0], 128), 1)
     fields = jnp.zeros_like(lane).astype(F32)
     for at, field in enumerate((power, mantissa, norm_power, high, low)):
         fields = jnp.where(lane == at, field, fields)
@@ -146,7 +117,7 @@
     out_ref[:, width:] = code(fields)
 
 
-def unpack(ref):
+def decode(ref):
     width = ref.shape[1] - 128
     codes = ref[...].astype(jnp.int32).astype(F32)
     power, mantissa, norm_power, high, low = [codes[:, width + at : width + at + 1] for at in range(5)]
@@ -155,12 +126,54 @@
     return codes[:, :width] * (scale * (1.0 / CODES)), norm
 
 
+def decoded_sum(*refs):
+    own, left, right, far = [decode(ref) for ref in refs]
+    return [(own[at] + far[at]) + (left[at] + right[at]) for at in range(2)]
+
+
+def pack(keep_ref, other_ref, out_ref):
+    total = keep_ref[...] + other_ref[...]
+    width = total.shape[1] - 128
+    encode(total[:, :width], lane_sum(total[:, width:]), out_ref)
+
+
+def relay(own_ref, left_ref, right_ref, far_ref, out_ref):
+    body, squares = decoded_sum(own_ref, left_ref, right_ref, far_ref)
+    encode(body, squares, out_ref)
+
+
+def ray_vector(own_ref, left_ref, right_ref, far_ref, prev_ref, beta_ref):
+    total, squares = decoded_sum(own_ref, left_ref, right_ref, far_ref)
+    alpha = jnp.sqrt(squares + EPS)
+    u = total / alpha - (alpha / beta_ref[:, :1]) * prev_ref[...]
+    return u, alpha
+
+
+def next_adjoint(
+    pattern_ref, counts_ref, own_ref, left_ref, right_ref, far_ref, prev_ref, beta_ref, tiles_ref,
+    keep_ref, send_ref, u_ref, alpha_ref, acc_ref,
+):
+    u, alpha = ray_vector(own_ref, left_ref, right_ref, far_ref, prev_ref, beta_ref)
+    u_ref[...] = u
+    alpha_ref[...] = wide(alpha)
+    put = slots_of(pattern_ref, counts_ref, BLK_DEV // 2 + 1, BLK_DEV // 2)
+    scatter_products(u, put, tiles_ref, keep_ref, send_ref, acc_ref)
+
+
+def last_norm(
+    own_ref, left_ref, right_ref, far_ref, prev_ref, beta_ref, out_ref, alpha_ref
+):
+    u, alpha = ray_vector(own_ref, left_ref, right_ref, far_ref, prev_ref, beta_ref)
+    alpha_ref[...] = wide(alpha)
+    out_ref[...] = fold_sq(u, 128)
+
+
 def cell_vector(
     first, own_ref, left_ref, right_ref, far_ref, prev_ref, alpha_ref, v_ref, beta_ref
 ):
-    own, left, right, far = [unpack(ref) for ref in (own_ref, left_ref, right_ref, far_ref)]
-    beta = jnp.sqrt((own[1] + far[1]) + (left[1] + right[1]) + EPS)
-    v = ((own[0] + far[0]) + (left[0] + right[0])) / beta
+    total, squares = decoded_sum(own_ref, left_ref, right_ref, far_ref)
+    beta = jnp.sqrt(squares + EPS)
+    v = total / beta
     if not first:
         v = v - (beta / alpha_ref[:, :1]) * prev_ref[...]
     v_ref[...] = v
@@ -173,7 +186,7 @@
             out_ref[b, s] = tiles_ref[b, s].T
 
 
-def forward(pattern_ref, counts_ref, own_ref, other_ref, tiles_ref, out_ref, low_ref):
+def forward(pattern_ref, counts_ref, own_ref, other_ref, tiles_ref, out_ref, low_ref, sum_ref):
     bundles, slots, cells, rays = tiles_ref.shape
     width = own_ref.shape[1]
     own, other = own_ref[...], other_ref[...]
@@ -189,8 +202,8 @@
                 low_ref[:, pl.ds(at, cells)], tiles_ref[b, s], preferred_element_type=F32
             )
             acc = part if acc is None else acc + part
-        out_ref[:, b * rays : (b + 1) * rays] = acc
-    out_ref[:, bundles * rays :] = fold_sq(own, 128) + fold_sq(other, 128)
+        sum_ref[:, b * rays : (b + 1) * rays] = acc
+    encode(sum_ref[...], lane_sum(fold_sq(own, 128) + fold_sq(other, 128)), out_ref)
 
 
 def gather_up(*refs):
@@ -277,8 +290,10 @@
         return lax.ppermute(value, "core", [(0, 1), (1, 0)])
 
     def over_cell(partial):
-        own, left, right, far = lax.optimization_barrier(spread(partial, "x"))
-        return spread((own + far) + (left + right), "y")
+        summed, = call(
+            relay, [shape(rows + 128, jnp.int16)], [VMEM] * 4, spread(partial, "x")
+        )
+        return spread(summed, "y")
 
     halves = [shape(half + 128)] * 2
     store = [pltpu.VMEM((nrhs, 2 * (half + cells)), F32)]
@@ -310,8 +325,8 @@
         others.append(other)
         betas.append(beta)
         products, = call(
-            forward, [shape(rows + 128)], [SMEM] * 2 + [VMEM] * 3, (*slots_in, v, other, turned),
-            [pltpu.VMEM((nrhs, 2 * half + cells), BF16)],
+            forward, [shape(rows + 128, jnp.int16)], [SMEM] * 2 + [VMEM] * 3, (*slots_in, v, other, turned),
+            [pltpu.VMEM((nrhs, 2 * half + cells), BF16), pltpu.VMEM((nrhs, rows), F32)],
         )
         rows_in = over_cell(products)
         if step + 1 < ITERS:

time: 128 us -> 127 us (level)
  waiting for transfers between devices: 61.7 us -> 58.2 us
  Pallas kernels: 15.7 us -> 17.3 us
    ppermute x39, waiting for transfers between devices: 51 us -> 47.5 us  [spread(): lax.ppermute(value, axis, [(i, i ^ by) for i in range(n)])]
    pallas_call x20 -> x24, Pallas kernels: 15.7 us -> 17.3 us  [call(): pl.pallas_call(body, out_shape=outs, in_specs=specs, out_specs=[VMEM] * l...]
  transfers between devices with their start and end apart: 48 -> 48, of which waited for: 36 -> 35; matrix products, arithmetic and copies ran while one was open for 0% -> 0% of each run, Pallas kernels for 1% -> 1%
where the time goes in v7:
time: 127 us; the launch traced here: 126 us
  waiting for transfers between devices  58.2 us (46%)
  starting transfers between devices  50 us (39%)
  Pallas kernels  17.3 us (14%)
    ppermute x39, starting transfers between devices, spread(): lax.ppermute(value, axis, [(i, i ^ by) for i in range(n)])  49.2 us
    ppermute x39, waiting for transfers between devices, spread(): lax.ppermute(value, axis, [(i, i ^ by) for i in range(n)])  47.5 us
    pallas_call x24, Pallas kernels, call(): pl.pallas_call(body, out_shape=outs, in_specs=specs, out_specs=[VMEM] * l...  17.3 us
    ppermute x9, waiting for transfers between devices, swap(): return lax.ppermute(value, 'core', [(0, 1), (1, 0)])  10.7 us
  transfers between devices with their start and end apart: 48, of which 35 were waited for; matrix products, arithmetic and copies ran while one was open for 0% of the time, Pallas kernels for 1%

profile of v7, /device:TPU:0, one launch (start us, length us, event | category | flops | bytes accessed | tf_op | source)
XLA Modules:
  0.0 126.4 jit_solution(6822374307264614530)
XLA Ops:
  0.6 2.7 %shard_map.59 = (f32[8,4224]{1,0:T(8,128)S(1)}, f32[8,4224]{1,0:T(8,128)S(1)}, bf16[8,4,256,256]{3,2,1,0:T(8,128)(2,1)S(1)}) custom-call(s32[4,8]{1,0:T(4,128)} %bitcast.3, s32[1,8]{1,0:T(1,128)} %bitcast.11, f32[8,2048]{1,0:T(8,128)} %prev_ref.3, bf16[8,4,256,256]{3,2,1,0:T(8,128)(2,1)} %source_ref.1), custom_call_target="tpu_custom_call" | custom-call | tf_op jit(solution)/shard_map/pallas_call | solution.py:262
  5.0 4.0 %collective-permute-start.3 = (s16[8,4224]{1,0:T(8,128)(2,1)S(1)}, s16[8,4224]{1,0:T(8,128)(2,1)S(1)}, u32[]{:S(2)}, u32[]{:S(2)}) collective-permute-start(s16[8,4224]{1,0:T(8,128)(2,1)S(1)} %shard_map.60.own_ref), channel_id=1, source_target_pairs={{0,64},{32,96},{64,0},{96,32},{1,65},{33,97},{65,1},{97,33},{2,66}... | collective-permute-start | bytes 202760 | tf_op jit(solution)/shard_map/ppermute | solution.py:285
  11.5 3.0 %collective-permute-done.2.right_ref = s16[8,4224]{1,0:T(8,128)(2,1)S(1)} collective-permute-done((s16[8,4224]{1,0:T(8,128)(2,1)S(1)}, s16[8,4224]{1,0:T(8,128)(2,1)S(1)}, u32[]{:S(2)}, u32[]{:S(2)}) %collective-permute-start.2) | collective-permute-done | bytes 67616 | tf_op jit(solution)/shard_map/ppermute | solution.py:285
  17.5 3.1 %collective-permute-start.7 = (s16[8,2176]{1,0:T(8,128)(2,1)S(1)}, s16[8,2176]{1,0:T(8,128)(2,1)S(1)}, u32[]{:S(2)}, u32[]{:S(2)}) collective-permute-start(s16[8,2176]{1,0:T(8,128)(2,1)S(1)} %shard_map.63.own_ref), channel_id=1, source_target_pairs={{0,8},{4,12},{8,0},{12,4},{1,9},{5,13},{9,1},{13,5},{2,10},{6,14},... | collective-permute-start | bytes 104456 | tf_op jit(solution)/shard_map/ppermute | solution.py:285
  23.0 2.7 %collective-permute-done.6.right_ref = s16[8,2176]{1,0:T(8,128)(2,1)S(1)} collective-permute-done((s16[8,2176]{1,0:T(8,128)(2,1)S(1)}, s16[8,2176]{1,0:T(8,128)(2,1)S(1)}, u32[]{:S(2)}, u32[]{:S(2)}) %collective-permute-start.6) | collective-permute-done | bytes 34848 | tf_op jit(solution)/shard_map/ppermute | solution.py:285
  26.0 3.3 %collective-permute-start.10 = (s16[8,2176]{1,0:T(8,128)(2,1)S(1)}, s16[8,2176]{1,0:T(8,128)(2,1)S(1)}, u32[]{:S(2)}, u32[]{:S(2)}) collective-permute-start(s16[8,2176]{1,0:T(8,128)(2,1)S(1)} %shard_map.64.own_ref), channel_id=1, source_target_pairs={{0,2},{1,3},{2,0},{3,1},{4,6},{5,7},{6,4},{7,5},{8,10},{9,11},{10,... | collective-permute-start | bytes 104456 | tf_op jit(solution)/shard_map/ppermute | solution.py:285
  31.5 2.9 %collective-permute-done.9.right_ref = s16[8,2176]{1,0:T(8,128)(2,1)S(1)} collective-permute-done((s16[8,2176]{1,0:T(8,128)(2,1)S(1)}, s16[8,2176]{1,0:T(8,128)(2,1)S(1)}, u32[]{:S(2)}, u32[]{:S(2)}) %collective-permute-start.9) | collective-permute-done | bytes 34848 | tf_op jit(solution)/shard_map/ppermute | solution.py:285
  37.4 2.0 %collective-permute-start.14 = (s16[8,4224]{1,0:T(8,128)(2,1)S(1)}, s16[8,4224]{1,0:T(8,128)(2,1)S(1)}, u32[]{:S(2)}, u32[]{:S(2)}) collective-permute-start(s16[8,4224]{1,0:T(8,128)(2,1)S(1)} %shard_map.66.own_ref), channel_id=1, source_target_pairs={{0,64},{32,96},{64,0},{96,32},{1,65},{33,97},{65,1},{97,33},{2,66}... | collective-permute-start | bytes 202760 | tf_op jit(solution)/shard_map/ppermute | solution.py:285
  41.0 2.3 %collective-permute-done.14.far_ref = s16[8,4224]{1,0:T(8,128)(2,1)S(1)} collective-permute-done((s16[8,4224]{1,0:T(8,128)(2,1)S(1)}, s16[8,4224]{1,0:T(8,128)(2,1)S(1)}, u32[]{:S(2)}, u32[]{:S(2)}) %collective-permute-start.14) | collective-permute-done | bytes 67616 | tf_op jit(solution)/shard_map/ppermute | solution.py:285
  43.3 1.6 %collective-permute-done.13.right_ref = s16[8,4224]{1,0:T(8,128)(2,1)S(1)} collective-permute-done((s16[8,4224]{1,0:T(8,128)(2,1)S(1)}, s16[8,4224]{1,0:T(8,128)(2,1)S(1)}, u32[]{:S(2)}, u32[]{:S(2)}) %collective-permute-start.13) | collective-permute-done | bytes 67616 | tf_op jit(solution)/shard_map/ppermute | solution.py:285
  47.9 1.5 %collective-permute-start.18 = (s16[8,2176]{1,0:T(8,128)(2,1)S(1)}, s16[8,2176]{1,0:T(8,128)(2,1)S(1)}, u32[]{:S(2)}, u32[]{:S(2)}) collective-permute-start(s16[8,2176]{1,0:T(8,128)(2,1)S(1)} %shard_map.68.own_ref), channel_id=1, source_target_pairs={{0,8},{4,12},{8,0},{12,4},{1,9},{5,13},{9,1},{13,5},{2,10},{6,14},... | collective-permute-start | bytes 104456 | tf_op jit(solution)/shard_map/ppermute | solution.py:285
  51.5 2.0 %collective-permute-done.18.far_ref = s16[8,2176]{1,0:T(8,128)(2,1)S(1)} collective-permute-done((s16[8,2176]{1,0:T(8,128)(2,1)S(1)}, s16[8,2176]{1,0:T(8,128)(2,1)S(1)}, u32[]{:S(2)}, u32[]{:S(2)}) %collective-permute-start.18) | collective-permute-done | bytes 34848 | tf_op jit(solution)/shard_map/ppermute | solution.py:285
  54.9 1.6 %collective-permute-start.21 = (s16[8,2176]{1,0:T(8,128)(2,1)S(1)}, s16[8,2176]{1,0:T(8,128)(2,1)S(1)}, u32[]{:S(2)}, u32[]{:S(2)}) collective-permute-start(s16[8,2176]{1,0:T(8,128)(2,1)S(1)} %shard_map.69.own_ref), channel_id=1, source_target_pairs={{0,2},{1,3},{2,0},{3,1},{4,6},{5,7},{6,4},{7,5},{8,10},{9,11},{10,... | collective-permute-start | bytes 104456 | tf_op jit(solution)/shard_map/ppermute | solution.py:285
  58.4 2.1 %collective-permute-done.21.far_ref = s16[8,2176]{1,0:T(8,128)(2,1)S(1)} collective-permute-done((s16[8,2176]{1,0:T(8,128)(2,1)S(1)}, s16[8,2176]{1,0:T(8,128)(2,1)S(1)}, u32[]{:S(2)}, u32[]{:S(2)}) %collective-permute-start.21) | collective-permute-done | bytes 34848 | tf_op jit(solution)/shard_map/ppermute | solution.py:285
  64.6 1.9 %collective-permute-start.25 = (s16[8,4224]{1,0:T(8,128)(2,1)S(1)}, s16[8,4224]{1,0:T(8,128)(2,1)S(1)}, u32[]{:S(2)}, u32[]{:S(2)}) collective-permute-start(s16[8,4224]{1,0:T(8,128)(2,1)S(1)} %shard_map.71.own_ref), channel_id=1, source_target_pairs={{0,64},{32,96},{64,0},{96,32},{1,65},{33,97},{65,1},{97,33},{2,66}... | collective-permute-start | bytes 202760 | tf_op jit(solution)/shard_map/ppermute | solution.py:285
  68.2 2.3 %collective-permute-done.25.far_ref = s16[8,4224]{1,0:T(8,128)(2,1)S(1)} collective-permute-done((s16[8,4224]{1,0:T(8,128)(2,1)S(1)}, s16[8,4224]{1,0:T(8,128)(2,1)S(1)}, u32[]{:S(2)}, u32[]{:S(2)}) %collective-permute-start.25) | collective-permute-done | bytes 67616 | tf_op jit(solution)/shard_map/ppermute | solution.py:285
  70.5 1.5 %collective-permute-done.24.right_ref = s16[8,4224]{1,0:T(8,128)(2,1)S(1)} collective-permute-done((s16[8,4224]{1,0:T(8,128)(2,1)S(1)}, s16[8,4224]{1,0:T(8,128)(2,1)S(1)}, u32[]{:S(2)}, u32[]{:S(2)}) %collective-permute-start.24) | collective-permute-done | bytes 67616 | tf_op jit(solution)/shard_map/ppermute | solution.py:285
  75.0 2.3 %collective-permute-start.29 = (s16[8,2176]{1,0:T(8,128)(2,1)S(1)}, s16[8,2176]{1,0:T(8,128)(2,1)S(1)}, u32[]{:S(2)}, u32[]{:S(2)}) collective-permute-start(s16[8,2176]{1,0:T(8,128)(2,1)S(1)} %shard_map.73.own_ref), channel_id=1, source_target_pairs={{0,8},{4,12},{8,0},{12,4},{1,9},{5,13},{9,1},{13,5},{2,10},{6,14},... | collective-permute-start | bytes 104456 | tf_op jit(solution)/shard_map/ppermute | solution.py:285
  78.6 2.0 %collective-permute-done.29.far_ref = s16[8,2176]{1,0:T(8,128)(2,1)S(1)} collective-permute-done((s16[8,2176]{1,0:T(8,128)(2,1)S(1)}, s16[8,2176]{1,0:T(8,128)(2,1)S(1)}, u32[]{:S(2)}, u32[]{:S(2)}) %collective-permute-start.29) | collective-permute-done | bytes 34848 | tf_op jit(solution)/shard_map/ppermute | solution.py:285
  80.5 2.0 %collective-permute-done.28.right_ref = s16[8,2176]{1,0:T(8,128)(2,1)S(1)} collective-permute-done((s16[8,2176]{1,0:T(8,128)(2,1)S(1)}, s16[8,2176]{1,0:T(8,128)(2,1)S(1)}, u32[]{:S(2)}, u32[]{:S(2)}) %collective-permute-start.28) | collective-permute-done | bytes 34848 | tf_op jit(solution)/shard_map/ppermute | solution.py:285
  82.8 2.3 %collective-permute-start.32 = (s16[8,2176]{1,0:T(8,128)(2,1)S(1)}, s16[8,2176]{1,0:T(8,128)(2,1)S(1)}, u32[]{:S(2)}, u32[]{:S(2)}) collective-permute-start(s16[8,2176]{1,0:T(8,128)(2,1)S(1)} %shard_map.74.own_ref), channel_id=1, source_target_pairs={{0,2},{1,3},{2,0},{3,1},{4,6},{5,7},{6,4},{7,5},{8,10},{9,11},{10,... | collective-permute-start | bytes 104456 | tf_op jit(solution)/shard_map/ppermute | solution.py:285
  86.4 2.0 %collective-permute-done.32.far_ref = s16[8,2176]{1,0:T(8,128)(2,1)S(1)} collective-permute-done((s16[8,2176]{1,0:T(8,128)(2,1)S(1)}, s16[8,2176]{1,0:T(8,128)(2,1)S(1)}, u32[]{:S(2)}, u32[]{:S(2)}) %collective-permute-start.32) | collective-permute-done | bytes 34848 | tf_op jit(solution)/shard_map/ppermute | solution.py:285
  88.3 1.9 %collective-permute-done.31.right_ref = s16[8,2176]{1,0:T(8,128)(2,1)S(1)} collective-permute-done((s16[8,2176]{1,0:T(8,128)(2,1)S(1)}, s16[8,2176]{1,0:T(8,128)(2,1)S(1)}, u32[]{:S(2)}, u32[]{:S(2)}) %collective-permute-start.31) | collective-permute-done | bytes 34848 | tf_op jit(solution)/shard_map/ppermute | solution.py:285
  93.2 2.0 %collective-permute-start.36 = (s16[8,4224]{1,0:T(8,128)(2,1)S(1)}, s16[8,4224]{1,0:T(8,128)(2,1)S(1)}, u32[]{:S(2)}, u32[]{:S(2)}) collective-permute-start(s16[8,4224]{1,0:T(8,128)(2,1)S(1)} %shard_map.76.own_ref), channel_id=1, source_target_pairs={{0,64},{32,96},{64,0},{96,32},{1,65},{33,97},{65,1},{97,33},{2,66}... | collective-permute-start | bytes 202760 | tf_op jit(solution)/shard_map/ppermute | solution.py:285
  96.8 2.3 %collective-permute-done.36.far_ref = s16[8,4224]{1,0:T(8,128)(2,1)S(1)} collective-permute-done((s16[8,4224]{1,0:T(8,128)(2,1)S(1)}, s16[8,4224]{1,0:T(8,128)(2,1)S(1)}, u32[]{:S(2)}, u32[]{:S(2)}) %collective-permute-start.36) | collective-permute-done | bytes 67616 | tf_op jit(solution)/shard_map/ppermute | solution.py:285
  99.1 1.6 %collective-permute-done.35.right_ref = s16[8,4224]{1,0:T(8,128)(2,1)S(1)} collective-permute-done((s16[8,4224]{1,0:T(8,128)(2,1)S(1)}, s16[8,4224]{1,0:T(8,128)(2,1)S(1)}, u32[]{:S(2)}, u32[]{:S(2)}) %collective-permute-start.35) | collective-permute-done | bytes 67616 | tf_op jit(solution)/shard_map/ppermute | solution.py:285
  103.7 1.5 %collective-permute-start.40 = (s16[8,2176]{1,0:T(8,128)(2,1)S(1)}, s16[8,2176]{1,0:T(8,128)(2,1)S(1)}, u32[]{:S(2)}, u32[]{:S(2)}) collective-permute-start(s16[8,2176]{1,0:T(8,128)(2,1)S(1)} %shard_map.78.own_ref), channel_id=1, source_target_pairs={{0,8},{4,12},{8,0},{12,4},{1,9},{5,13},{9,1},{13,5},{2,10},{6,14},... | collective-permute-start | bytes 104456 | tf_op jit(solution)/shard_map/ppermute | solution.py:285
  107.3 2.0 %collective-permute-done.40.far_ref = s16[8,2176]{1,0:T(8,128)(2,1)S(1)} collective-permute-done((s16[8,2176]{1,0:T(8,128)(2,1)S(1)}, s16[8,2176]{1,0:T(8,128)(2,1)S(1)}, u32[]{:S(2)}, u32[]{:S(2)}) %collective-permute-start.40) | collective-permute-done | bytes 34848 | tf_op jit(solution)/shard_map/ppermute | solution.py:285
  110.7 1.6 %collective-permute-start.43 = (s16[8,2176]{1,0:T(8,128)(2,1)S(1)}, s16[8,2176]{1,0:T(8,128)(2,1)S(1)}, u32[]{:S(2)}, u32[]{:S(2)}) collective-permute-start(s16[8,2176]{1,0:T(8,128)(2,1)S(1)} %shard_map.79.own_ref), channel_id=1, source_target_pairs={{0,2},{1,3},{2,0},{3,1},{4,6},{5,7},{6,4},{7,5},{8,10},{9,11},{10,... | collective-permute-start | bytes 104456 | tf_op jit(solution)/shard_map/ppermute | solution.py:285
  114.2 2.1 %collective-permute-done.43.far_ref = s16[8,2176]{1,0:T(8,128)(2,1)S(1)} collective-permute-done((s16[8,2176]{1,0:T(8,128)(2,1)S(1)}, s16[8,2176]{1,0:T(8,128)(2,1)S(1)}, u32[]{:S(2)}, u32[]{:S(2)}) %collective-permute-start.43) | collective-permute-done | bytes 34848 | tf_op jit(solution)/shard_map/ppermute | solution.py:285
  118.8 1.9 %collective-permute-start.47 = (f32[8,128]{1,0:T(8,128)S(1)}, f32[8,128]{1,0:T(8,128)S(1)}, u32[]{:S(2)}, u32[]{:S(2)}) collective-permute-start(f32[8,128]{1,0:T(8,128)S(1)} %add.3.own_ref), channel_id=1, source_target_pairs={{0,64},{32,96},{64,0},{96,32},{1,65},{33,97},{65,1},{97,33},{2,66}... | collective-permute-start | bytes 12296 | tf_op jit(solution)/shard_map/ppermute | solution.py:285
  124.0 1.6 %collective-permute-done.46.right_ref = f32[8,128]{1,0:T(8,128)S(1)} collective-permute-done((f32[8,128]{1,0:T(8,128)S(1)}, f32[8,128]{1,0:T(8,128)S(1)}, u32[]{:S(2)}, u32[]{:S(2)}) %collective-permute-start.46) | collective-permute-done | bytes 4128 | tf_op jit(solution)/shard_map/ppermute | solution.py:285
  (95 shorter events, 55.8 us)
Async XLA Ops:
  5.0 6.5 %collective-permute-start.3 = (s16[8,4224]{1,0:T(8,128)(2,1)S(1)}, s16[8,4224]{1,0:T(8,128)(2,1)S(1)}, u32[]{:S(2)}, u32[]{:S(2)}) collective-permute-start(s16[8,4224]{1,0:T(8,128)(2,1)S(1)} %shard_map.60.own_ref), channel_id=1, source_target_pairs={{0,64},{32,96},{64,0},{96,32},{1,65},{33,97},{65,1},{97,33},{2,66}... | collective-permute-start | bytes 202760 | tf_op jit(solution)/shard_map/ppermute | solution.py:285
  9.0 5.5 %collective-permute-start.2 = (s16[8,4224]{1,0:T(8,128)(2,1)S(1)}, s16[8,4224]{1,0:T(8,128)(2,1)S(1)}, u32[]{:S(2)}, u32[]{:S(2)}) collective-permute-start(s16[8,4224]{1,0:T(8,128)(2,1)S(1)} %shard_map.60.own_ref), channel_id=1, source_target_pairs={{0,96},{32,64},{64,32},{96,0},{1,97},{33,65},{65,33},{97,1},{2,98}... | collective-permute-start | bytes 202760 | tf_op jit(solution)/shard_map/ppermute | solution.py:285
  9.7 4.8 %collective-permute-start.1 = (s16[8,4224]{1,0:T(8,128)(2,1)S(1)}, s16[8,4224]{1,0:T(8,128)(2,1)S(1)}, u32[]{:S(2)}, u32[]{:S(2)}) collective-permute-start(s16[8,4224]{1,0:T(8,128)(2,1)S(1)} %shard_map.60.own_ref), channel_id=1, source_target_pairs={{0,32},{32,0},{64,96},{96,64},{1,33},{33,1},{65,97},{97,65},{2,34}... | collective-permute-start | bytes 202760 | tf_op jit(solution)/shard_map/ppermute | solution.py:285
  17.5 5.5 %collective-permute-start.7 = (s16[8,2176]{1,0:T(8,128)(2,1)S(1)}, s16[8,2176]{1,0:T(8,128)(2,1)S(1)}, u32[]{:S(2)}, u32[]{:S(2)}) collective-permute-start(s16[8,2176]{1,0:T(8,128)(2,1)S(1)} %shard_map.63.own_ref), channel_id=1, source_target_pairs={{0,8},{4,12},{8,0},{12,4},{1,9},{5,13},{9,1},{13,5},{2,10},{6,14},... | collective-permute-start | bytes 104456 | tf_op jit(solution)/shard_map/ppermute | solution.py:285
  20.6 5.1 %collective-permute-start.6 = (s16[8,2176]{1,0:T(8,128)(2,1)S(1)}, s16[8,2176]{1,0:T(8,128)(2,1)S(1)}, u32[]{:S(2)}, u32[]{:S(2)}) collective-permute-start(s16[8,2176]{1,0:T(8,128)(2,1)S(1)} %shard_map.63.own_ref), channel_id=1, source_target_pairs={{0,12},{4,8},{8,4},{12,0},{1,13},{5,9},{9,5},{13,1},{2,14},{6,10},... | collective-permute-start | bytes 104456 | tf_op jit(solution)/shard_map/ppermute | solution.py:285
  26.0 5.5 %collective-permute-start.10 = (s16[8,2176]{1,0:T(8,128)(2,1)S(1)}, s16[8,2176]{1,0:T(8,128)(2,1)S(1)}, u32[]{:S(2)}, u32[]{:S(2)}) collective-permute-start(s16[8,2176]{1,0:T(8,128)(2,1)S(1)} %shard_map.64.own_ref), channel_id=1, source_target_pairs={{0,2},{1,3},{2,0},{3,1},{4,6},{5,7},{6,4},{7,5},{8,10},{9,11},{10,... | collective-permute-start | bytes 104456 | tf_op jit(solution)/shard_map/ppermute | solution.py:285
  29.3 5.1 %collective-permute-start.9 = (s16[8,2176]{1,0:T(8,128)(2,1)S(1)}, s16[8,2176]{1,0:T(8,128)(2,1)S(1)}, u32[]{:S(2)}, u32[]{:S(2)}) collective-permute-start(s16[8,2176]{1,0:T(8,128)(2,1)S(1)} %shard_map.64.own_ref), channel_id=1, source_target_pairs={{0,3},{1,2},{2,1},{3,0},{4,7},{5,6},{6,5},{7,4},{8,11},{9,10},{10,... | collective-permute-start | bytes 104456 | tf_op jit(solution)/shard_map/ppermute | solution.py:285
  30.3 4.1 %collective-permute-start.8 = (s16[8,2176]{1,0:T(8,128)(2,1)S(1)}, s16[8,2176]{1,0:T(8,128)(2,1)S(1)}, u32[]{:S(2)}, u32[]{:S(2)}) collective-permute-start(s16[8,2176]{1,0:T(8,128)(2,1)S(1)} %shard_map.64.own_ref), channel_id=1, source_target_pairs={{0,1},{1,0},{2,3},{3,2},{4,5},{5,4},{6,7},{7,6},{8,9},{9,8},{10,11... | collective-permute-start | bytes 104456 | tf_op jit(solution)/shard_map/ppermute | solution.py:285
  37.4 5.9 %collective-permute-start.14 = (s16[8,4224]{1,0:T(8,128)(2,1)S(1)}, s16[8,4224]{1,0:T(8,128)(2,1)S(1)}, u32[]{:S(2)}, u32[]{:S(2)}) collective-permute-start(s16[8,4224]{1,0:T(8,128)(2,1)S(1)} %shard_map.66.own_ref), channel_id=1, source_target_pairs={{0,64},{32,96},{64,0},{96,32},{1,65},{33,97},{65,1},{97,33},{2,66}... | collective-permute-start | bytes 202760 | tf_op jit(solution)/shard_map/ppermute | solution.py:285
  39.4 5.5 %collective-permute-start.13 = (s16[8,4224]{1,0:T(8,128)(2,1)S(1)}, s16[8,4224]{1,0:T(8,128)(2,1)S(1)}, u32[]{:S(2)}, u32[]{:S(2)}) collective-permute-start(s16[8,4224]{1,0:T(8,128)(2,1)S(1)} %shard_map.66.own_ref), channel_id=1, source_target_pairs={{0,96},{32,64},{64,32},{96,0},{1,97},{33,65},{65,33},{97,1},{2,98}... | collective-permute-start | bytes 202760 | tf_op jit(solution)/shard_map/ppermute | solution.py:285
  40.3 4.6 %collective-permute-start.12 = (s16[8,4224]{1,0:T(8,128)(2,1)S(1)}, s16[8,4224]{1,0:T(8,128)(2,1)S(1)}, u32[]{:S(2)}, u32[]{:S(2)}) collective-permute-start(s16[8,4224]{1,0:T(8,128)(2,1)S(1)} %shard_map.66.own_ref), channel_id=1, source_target_pairs={{0,32},{32,0},{64,96},{96,64},{1,33},{33,1},{65,97},{97,65},{2,34}... | collective-permute-start | bytes 202760 | tf_op jit(solution)/shard_map/ppermute | solution.py:285
  47.9 5.6 %collective-permute-start.18 = (s16[8,2176]{1,0:T(8,128)(2,1)S(1)}, s16[8,2176]{1,0:T(8,128)(2,1)S(1)}, u32[]{:S(2)}, u32[]{:S(2)}) collective-permute-start(s16[8,2176]{1,0:T(8,128)(2,1)S(1)} %shard_map.68.own_ref), channel_id=1, source_target_pairs={{0,8},{4,12},{8,0},{12,4},{1,9},{5,13},{9,1},{13,5},{2,10},{6,14},... | collective-permute-start | bytes 104456 | tf_op jit(solution)/shard_map/ppermute | solution.py:285
  49.4 5.1 %collective-permute-start.17 = (s16[8,2176]{1,0:T(8,128)(2,1)S(1)}, s16[8,2176]{1,0:T(8,128)(2,1)S(1)}, u32[]{:S(2)}, u32[]{:S(2)}) collective-permute-start(s16[8,2176]{1,0:T(8,128)(2,1)S(1)} %shard_map.68.own_ref), channel_id=1, source_target_pairs={{0,12},{4,8},{8,4},{12,0},{1,13},{5,9},{9,5},{13,1},{2,14},{6,10},... | collective-permute-start | bytes 104456 | tf_op jit(solution)/shard_map/ppermute | solution.py:285
  54.9 5.7 %collective-permute-start.21 = (s16[8,2176]{1,0:T(8,128)(2,1)S(1)}, s16[8,2176]{1,0:T(8,128)(2,1)S(1)}, u32[]{:S(2)}, u32[]{:S(2)}) collective-permute-start(s16[8,2176]{1,0:T(8,128)(2,1)S(1)} %shard_map.69.own_ref), channel_id=1, source_target_pairs={{0,2},{1,3},{2,0},{3,1},{4,6},{5,7},{6,4},{7,5},{8,10},{9,11},{10,... | collective-permute-start | bytes 104456 | tf_op jit(solution)/shard_map/ppermute | solution.py:285
  56.5 5.1 %collective-permute-start.20 = (s16[8,2176]{1,0:T(8,128)(2,1)S(1)}, s16[8,2176]{1,0:T(8,128)(2,1)S(1)}, u32[]{:S(2)}, u32[]{:S(2)}) collective-permute-start(s16[8,2176]{1,0:T(8,128)(2,1)S(1)} %shard_map.69.own_ref), channel_id=1, source_target_pairs={{0,3},{1,2},{2,1},{3,0},{4,7},{5,6},{6,5},{7,4},{8,11},{9,10},{10,... | collective-permute-start | bytes 104456 | tf_op jit(solution)/shard_map/ppermute | solution.py:285
  57.4 4.2 %collective-permute-start.19 = (s16[8,2176]{1,0:T(8,128)(2,1)S(1)}, s16[8,2176]{1,0:T(8,128)(2,1)S(1)}, u32[]{:S(2)}, u32[]{:S(2)}) collective-permute-start(s16[8,2176]{1,0:T(8,128)(2,1)S(1)} %shard_map.69.own_ref), channel_id=1, source_target_pairs={{0,1},{1,0},{2,3},{3,2},{4,5},{5,4},{6,7},{7,6},{8,9},{9,8},{10,11... | collective-permute-start | bytes 104456 | tf_op jit(solution)/shard_map/ppermute | solution.py:285
  64.6 5.9 %collective-permute-start.25 = (s16[8,4224]{1,0:T(8,128)(2,1)S(1)}, s16[8,4224]{1,0:T(8,128)(2,1)S(1)}, u32[]{:S(2)}, u32[]{:S(2)}) collective-permute-start(s16[8,4224]{1,0:T(8,128)(2,1)S(1)} %shard_map.71.own_ref), channel_id=1, source_target_pairs={{0,64},{32,96},{64,0},{96,32},{1,65},{33,97},{65,1},{97,33},{2,66}... | collective-permute-start | bytes 202760 | tf_op jit(solution)/shard_map/ppermute | solution.py:285
  66.5 5.5 %collective-permute-start.24 = (s16[8,4224]{1,0:T(8,128)(2,1)S(1)}, s16[8,4224]{1,0:T(8,128)(2,1)S(1)}, u32[]{:S(2)}, u32[]{:S(2)}) collective-permute-start(s16[8,4224]{1,0:T(8,128)(2,1)S(1)} %shard_map.71.own_ref), channel_id=1, source_target_pairs={{0,96},{32,64},{64,32},{96,0},{1,97},{33,65},{65,33},{97,1},{2,98}... | collective-permute-start | bytes 202760 | tf_op jit(solution)/shard_map/ppermute | solution.py:285
  67.7 4.3 %collective-permute-start.23 = (s16[8,4224]{1,0:T(8,128)(2,1)S(1)}, s16[8,4224]{1,0:T(8,128)(2,1)S(1)}, u32[]{:S(2)}, u32[]{:S(2)}) collective-permute-start(s16[8,4224]{1,0:T(8,128)(2,1)S(1)} %shard_map.71.own_ref), channel_id=1, source_target_pairs={{0,32},{32,0},{64,96},{96,64},{1,33},{33,1},{65,97},{97,65},{2,34}... | collective-permute-start | bytes 202760 | tf_op jit(solution)/shard_map/ppermute | solution.py:285
  75.0 5.5 %collective-permute-start.29 = (s16[8,2176]{1,0:T(8,128)(2,1)S(1)}, s16[8,2176]{1,0:T(8,128)(2,1)S(1)}, u32[]{:S(2)}, u32[]{:S(2)}) collective-permute-start(s16[8,2176]{1,0:T(8,128)(2,1)S(1)} %shard_map.73.own_ref), channel_id=1, source_target_pairs={{0,8},{4,12},{8,0},{12,4},{1,9},{5,13},{9,1},{13,5},{2,10},{6,14},... | collective-permute-start | bytes 104456 | tf_op jit(solution)/shard_map/ppermute | solution.py:285
  77.4 5.1 %collective-permute-start.28 = (s16[8,2176]{1,0:T(8,128)(2,1)S(1)}, s16[8,2176]{1,0:T(8,128)(2,1)S(1)}, u32[]{:S(2)}, u32[]{:S(2)}) collective-permute-start(s16[8,2176]{1,0:T(8,128)(2,1)S(1)} %shard_map.73.own_ref), channel_id=1, source_target_pairs={{0,12},{4,8},{8,4},{12,0},{1,13},{5,9},{9,5},{13,1},{2,14},{6,10},... | collective-permute-start | bytes 104456 | tf_op jit(solution)/shard_map/ppermute | solution.py:285
  82.8 5.5 %collective-permute-start.32 = (s16[8,2176]{1,0:T(8,128)(2,1)S(1)}, s16[8,2176]{1,0:T(8,128)(2,1)S(1)}, u32[]{:S(2)}, u32[]{:S(2)}) collective-permute-start(s16[8,2176]{1,0:T(8,128)(2,1)S(1)} %shard_map.74.own_ref), channel_id=1, source_target_pairs={{0,2},{1,3},{2,0},{3,1},{4,6},{5,7},{6,4},{7,5},{8,10},{9,11},{10,... | collective-permute-start | bytes 104456 | tf_op jit(solution)/shard_map/ppermute | solution.py:285
  85.1 5.1 %collective-permute-start.31 = (s16[8,2176]{1,0:T(8,128)(2,1)S(1)}, s16[8,2176]{1,0:T(8,128)(2,1)S(1)}, u32[]{:S(2)}, u32[]{:S(2)}) collective-permute-start(s16[8,2176]{1,0:T(8,128)(2,1)S(1)} %shard_map.74.own_ref), channel_id=1, source_target_pairs={{0,3},{1,2},{2,1},{3,0},{4,7},{5,6},{6,5},{7,4},{8,11},{9,10},{10,... | collective-permute-start | bytes 104456 | tf_op jit(solution)/shard_map/ppermute | solution.py:285
  93.2 5.9 %collective-permute-start.36 = (s16[8,4224]{1,0:T(8,128)(2,1)S(1)}, s16[8,4224]{1,0:T(8,128)(2,1)S(1)}, u32[]{:S(2)}, u32[]{:S(2)}) collective-permute-start(s16[8,4224]{1,0:T(8,128)(2,1)S(1)} %shard_map.76.own_ref), channel_id=1, source_target_pairs={{0,64},{32,96},{64,0},{96,32},{1,65},{33,97},{65,1},{97,33},{2,66}... | collective-permute-start | bytes 202760 | tf_op jit(solution)/shard_map/ppermute | solution.py:285
  95.2 5.5 %collective-permute-start.35 = (s16[8,4224]{1,0:T(8,128)(2,1)S(1)}, s16[8,4224]{1,0:T(8,128)(2,1)S(1)}, u32[]{:S(2)}, u32[]{:S(2)}) collective-permute-start(s16[8,4224]{1,0:T(8,128)(2,1)S(1)} %shard_map.76.own_ref), channel_id=1, source_target_pairs={{0,96},{32,64},{64,32},{96,0},{1,97},{33,65},{65,33},{97,1},{2,98}... | collective-permute-start | bytes 202760 | tf_op jit(solution)/shard_map/ppermute | solution.py:285
  96.4 4.3 %collective-permute-start.34 = (s16[8,4224]{1,0:T(8,128)(2,1)S(1)}, s16[8,4224]{1,0:T(8,128)(2,1)S(1)}, u32[]{:S(2)}, u32[]{:S(2)}) collective-permute-start(s16[8,4224]{1,0:T(8,128)(2,1)S(1)} %shard_map.76.own_ref), channel_id=1, source_target_pairs={{0,32},{32,0},{64,96},{96,64},{1,33},{33,1},{65,97},{97,65},{2,34}... | collective-permute-start | bytes 202760 | tf_op jit(solution)/shard_map/ppermute | solution.py:285
  103.7 5.6 %collective-permute-start.40 = (s16[8,2176]{1,0:T(8,128)(2,1)S(1)}, s16[8,2176]{1,0:T(8,128)(2,1)S(1)}, u32[]{:S(2)}, u32[]{:S(2)}) collective-permute-start(s16[8,2176]{1,0:T(8,128)(2,1)S(1)} %shard_map.78.own_ref), channel_id=1, source_target_pairs={{0,8},{4,12},{8,0},{12,4},{1,9},{5,13},{9,1},{13,5},{2,10},{6,14},... | collective-permute-start | bytes 104456 | tf_op jit(solution)/shard_map/ppermute | solution.py:285
  105.2 5.1 %collective-permute-start.39 = (s16[8,2176]{1,0:T(8,128)(2,1)S(1)}, s16[8,2176]{1,0:T(8,128)(2,1)S(1)}, u32[]{:S(2)}, u32[]{:S(2)}) collective-permute-start(s16[8,2176]{1,0:T(8,128)(2,1)S(1)} %shard_map.78.own_ref), channel_id=1, source_target_pairs={{0,12},{4,8},{8,4},{12,0},{1,13},{5,9},{9,5},{13,1},{2,14},{6,10},... | collective-permute-start | bytes 104456 | tf_op jit(solution)/shard_map/ppermute | solution.py:285
  110.7 5.7 %collective-permute-start.43 = (s16[8,2176]{1,0:T(8,128)(2,1)S(1)}, s16[8,2176]{1,0:T(8,128)(2,1)S(1)}, u32[]{:S(2)}, u32[]{:S(2)}) collective-permute-start(s16[8,2176]{1,0:T(8,128)(2,1)S(1)} %shard_map.79.own_ref), channel_id=1, source_target_pairs={{0,2},{1,3},{2,0},{3,1},{4,6},{5,7},{6,4},{7,5},{8,10},{9,11},{10,... | collective-permute-start | bytes 104456 | tf_op jit(solution)/shard_map/ppermute | solution.py:285
  112.3 5.1 %collective-permute-start.42 = (s16[8,2176]{1,0:T(8,128)(2,1)S(1)}, s16[8,2176]{1,0:T(8,128)(2,1)S(1)}, u32[]{:S(2)}, u32[]{:S(2)}) collective-permute-start(s16[8,2176]{1,0:T(8,128)(2,1)S(1)} %shard_map.79.own_ref), channel_id=1, source_target_pairs={{0,3},{1,2},{2,1},{3,0},{4,7},{5,6},{6,5},{7,4},{8,11},{9,10},{10,... | collective-permute-start | bytes 104456 | tf_op jit(solution)/shard_map/ppermute | solution.py:285
  118.8 5.1 %collective-permute-start.47 = (f32[8,128]{1,0:T(8,128)S(1)}, f32[8,128]{1,0:T(8,128)S(1)}, u32[]{:S(2)}, u32[]{:S(2)}) collective-permute-start(f32[8,128]{1,0:T(8,128)S(1)} %add.3.own_ref), channel_id=1, source_target_pairs={{0,64},{32,96},{64,0},{96,32},{1,65},{33,97},{65,1},{97,33},{2,66}... | collective-permute-start | bytes 12296 | tf_op jit(solution)/shard_map/ppermute | solution.py:285
  120.7 4.8 %collective-permute-start.46 = (f32[8,128]{1,0:T(8,128)S(1)}, f32[8,128]{1,0:T(8,128)S(1)}, u32[]{:S(2)}, u32[]{:S(2)}) collective-permute-start(f32[8,128]{1,0:T(8,128)S(1)} %add.3.own_ref), channel_id=1, source_target_pairs={{0,96},{32,64},{64,32},{96,0},{1,97},{33,65},{65,33},{97,1},{2,98}... | collective-permute-start | bytes 12296 | tf_op jit(solution)/shard_map/ppermute | solution.py:285
  (19 other events, 56.6 us)

commit v8 on v7

--- a/solution.py
+++ b/solution.py
@@ -8,6 +8,7 @@
 from jax.sharding import Mesh, PartitionSpec as P
 
 BLK_DEV = 32
+GROUP = 8
 ITERS = 4
 EPS = 1e-06
 TINY = 1e-30
@@ -48,6 +49,74 @@
         return jnp.where(s < counts_ref[0, b], at, dead)
 
     return block_of
+
+
+def fill_lists(pattern_ref, counts_ref, lists_ref):
+    slots, bundles = pattern_ref.shape
+    most = slots * bundles
+    blocks = BLK_DEV // 2
+    core = lax.axis_index("core")
+    for i in range(most):
+        for at, value in ((0, 0), (most, blocks), (2 * most, 0), (3 * most, blocks)):
+            lists_ref[at + i] = jnp.int32(value)
+    lengths = [jnp.int32(0), jnp.int32(0)]
+    for b in range(bundles):
+        for s in range(slots):
+            found = pattern_ref[s, b]
+            mine = (found // blocks == core).astype(jnp.int32)
+            live = (s < counts_ref[0, b]).astype(jnp.int32)
+            at = jnp.where(mine == 1, 2 * most + lengths[1], lengths[0])
+            at = jnp.where(live == 1, at, 4 * most + 2)
+            lists_ref[at] = jnp.int32(b * slots + s)
+            lists_ref[at + most] = found % blocks
+            lengths = [lengths[0] + live * (1 - mine), lengths[1] + live * mine]
+    lists_ref[4 * most] = lengths[0]
+    lists_ref[4 * most + 1] = lengths[1]
+
+
+def listed_products(lists_ref, mine, tiles_ref, one):
+    most = tiles_ref.shape[0]
+    base = 2 * most if mine else 0
+
+    def group(g, carry):
+        for i in range(GROUP):
+            at = base + g * GROUP + i
+            one(lists_ref[at], lists_ref[at + most])
+        return carry
+
+    length = lists_ref[4 * most + (1 if mine else 0)]
+    lax.fori_loop(0, (length + GROUP - 1) // GROUP, group, 0)
+
+
+def half_adjoint(lists_ref, mine, u, tiles_ref, out_ref, acc_ref, low_ref, slots):
+    cells = tiles_ref.shape[2]
+    rays = tiles_ref.shape[1]
+    half = out_ref.shape[1] - 128
+    acc_ref[...] = jnp.zeros_like(acc_ref)
+    low_ref[...] = u.astype(BF16)
+
+    def one(tile, block):
+        rows = low_ref[:, pl.ds(pl.multiple_of(tile // slots * rays, rays), rays)]
+        part = jnp.dot(rows, tiles_ref[tile], preferred_element_type=F32)
+        acc_ref[:, pl.ds(pl.multiple_of(block * cells, cells), cells)] += part
+
+    listed_products(lists_ref, mine, tiles_ref, one)
+    out_ref[:, :half] = acc_ref[:, :half]
+    out_ref[:, half:] = fold_sq(u, 128)
+
+
+def half_forward(lists_ref, mine, v, tiles_ref, sum_ref, low_ref, slots):
+    cells, rays = tiles_ref.shape[1:]
+    half = v.shape[1]
+    low_ref[:, :half] = v.astype(BF16)
+    low_ref[:, half:] = jnp.zeros((v.shape[0], cells), BF16)
+
+    def one(tile, block):
+        rows = low_ref[:, pl.ds(pl.multiple_of(block * cells, cells), cells)]
+        part = jnp.dot(rows, tiles_ref[tile], preferred_element_type=F32)
+        sum_ref[:, pl.ds(pl.multiple_of(tile // slots * rays, rays), rays)] += part
+
+    listed_products(lists_ref, mine, tiles_ref, one)
 
 
 def scatter_products(u, block_of, tiles_ref, keep_ref, send_ref, acc_ref, copies=None):
@@ -70,8 +139,8 @@
 
 
 def first_adjoint(
-    source_p_ref, source_c_ref, source_u_ref, source_ref, keep_ref, send_ref, tiles_ref, acc_ref,
-    pattern_ref, counts_ref, u_ref, sem,
+    source_p_ref, source_c_ref, source_u_ref, source_ref, keep_ref, send_ref, tiles_ref, lists_ref,
+    acc_ref, pattern_ref, counts_ref, u_ref, sem,
 ):
     bundles = source_ref.shape[0]
     small = ((source_p_ref, pattern_ref), (source_c_ref, counts_ref), (source_u_ref, u_ref))
@@ -87,6 +156,7 @@
         copy.start()
     for copy in first:
         copy.wait()
+    fill_lists(pattern_ref, counts_ref, lists_ref)
     put = slots_of(pattern_ref, counts_ref, BLK_DEV // 2 + 1, BLK_DEV // 2)
     scatter_products(u_ref[...], put, tiles_ref, keep_ref, send_ref, acc_ref, copies)
 
@@ -149,15 +219,18 @@
     return u, alpha
 
 
-def next_adjoint(
-    pattern_ref, counts_ref, own_ref, left_ref, right_ref, far_ref, prev_ref, beta_ref, tiles_ref,
-    keep_ref, send_ref, u_ref, alpha_ref, acc_ref,
+def adjoint_send(
+    slots, lists_ref, own_ref, left_ref, right_ref, far_ref, prev_ref, beta_ref, tiles_ref,
+    send_ref, u_ref, alpha_ref, acc_ref, low_ref,
 ):
     u, alpha = ray_vector(own_ref, left_ref, right_ref, far_ref, prev_ref, beta_ref)
     u_ref[...] = u
     alpha_ref[...] = wide(alpha)
-    put = slots_of(pattern_ref, counts_ref, BLK_DEV // 2 + 1, BLK_DEV // 2)
-    scatter_products(u, put, tiles_ref, keep_ref, send_ref, acc_ref)
+    half_adjoint(lists_ref, False, u, tiles_ref, send_ref, acc_ref, low_ref, slots)
+
+
+def adjoint_keep(slots, lists_ref, u_ref, tiles_ref, keep_ref, acc_ref, low_ref):
+    half_adjoint(lists_ref, True, u_ref[...], tiles_ref, keep_ref, acc_ref, low_ref, slots)
 
 
 def last_norm(
@@ -181,29 +254,23 @@
 
 
 def turn(tiles_ref, out_ref):
-    for b in range(tiles_ref.shape[0]):
-        for s in range(tiles_ref.shape[1]):
-            out_ref[b, s] = tiles_ref[b, s].T
-
-
-def forward(pattern_ref, counts_ref, own_ref, other_ref, tiles_ref, out_ref, low_ref, sum_ref):
-    bundles, slots, cells, rays = tiles_ref.shape
-    width = own_ref.shape[1]
-    own, other = own_ref[...], other_ref[...]
-    low_ref[:, :width] = own.astype(BF16)
-    low_ref[:, width : 2 * width] = other.astype(BF16)
-    low_ref[:, 2 * width :] = jnp.zeros((own.shape[0], cells), BF16)
-    get = slots_of(pattern_ref, counts_ref, BLK_DEV // 2, BLK_DEV)
-    for b in range(bundles):
-        acc = None
-        for s in range(slots):
-            at = pl.multiple_of(get(b, s) * cells, cells)
-            part = jnp.dot(
-                low_ref[:, pl.ds(at, cells)], tiles_ref[b, s], preferred_element_type=F32
-            )
-            acc = part if acc is None else acc + part
-        sum_ref[:, b * rays : (b + 1) * rays] = acc
-    encode(sum_ref[...], lane_sum(fold_sq(own, 128) + fold_sq(other, 128)), out_ref)
+    for tile in range(tiles_ref.shape[0]):
+        out_ref[tile] = tiles_ref[tile].T
+
+
+def forward_own(slots, lists_ref, own_ref, tiles_ref, part_ref, low_ref):
+    part_ref[...] = jnp.zeros_like(part_ref)
+    own = own_ref[...]
+    half_forward(lists_ref, True, own, tiles_ref, part_ref, low_ref, slots)
+    part_ref[:, part_ref.shape[1] - 128 :] = fold_sq(own, 128)
+
+
+def forward_other(slots, lists_ref, part_ref, other_ref, tiles_ref, out_ref, sum_ref, low_ref):
+    width = sum_ref.shape[1]
+    sum_ref[...] = part_ref[:, :width]
+    other = other_ref[...]
+    half_forward(lists_ref, False, other, tiles_ref, sum_ref, low_ref, slots)
+    encode(sum_ref[...], lane_sum(part_ref[:, width:] + fold_sq(other, 128)), out_ref)
 
 
 def gather_up(*refs):
@@ -258,12 +325,12 @@
     misfit_ref[...] = across[:, : misfit_ref.shape[1]]
 
 
-def call(body, outs, specs, args, scratch=()):
+def call(body, outs, specs, args, scratch=(), out_specs=None):
     return pl.pallas_call(
         body,
         out_shape=outs,
         in_specs=specs,
-        out_specs=[VMEM] * len(outs),
+        out_specs=out_specs or [VMEM] * len(outs),
         scratch_shapes=list(scratch),
         compiler_params=pltpu.CompilerParams(vmem_limit_bytes=12 << 20),
     )(*args)
@@ -274,6 +341,7 @@
     bundles, slots, rays, cells = tiles.shape
     blocks = BLK_DEV // 2
     half = blocks * cells
+    most = bundles * slots
     slots_in = (pattern.T, counts.T)
 
     def shape(columns, dtype=F32):
@@ -296,19 +364,25 @@
         return spread(summed, "y")
 
     halves = [shape(half + 128)] * 2
-    store = [pltpu.VMEM((nrhs, 2 * (half + cells)), F32)]
-    keep, send, tiles = call(
-        first_adjoint, halves + [jax.ShapeDtypeStruct(tiles.shape, tiles.dtype)],
+    keep, send, tiles, lists = call(
+        first_adjoint,
+        halves + [
+            jax.ShapeDtypeStruct(tiles.shape, tiles.dtype),
+            jax.ShapeDtypeStruct((4 * most + 3 + most,), jnp.int32),
+        ],
         [HBM] * 4,
         [pltpu.with_memory_space_constraint(z, pltpu.HBM) for z in (*slots_in, right_side, tiles)],
-        store + [
+        [
+            pltpu.VMEM((nrhs, 2 * (half + cells)), F32),
             pltpu.SMEM((slots, bundles), jnp.int32), pltpu.SMEM((1, bundles), jnp.int32),
             pltpu.VMEM(right_side.shape, F32), pltpu.SemaphoreType.DMA((bundles + 3,)),
         ],
+        [VMEM] * 3 + [SMEM],
     )
-    turned, = call(
-        turn, [jax.ShapeDtypeStruct((bundles, slots, cells, rays), tiles.dtype)], [VMEM], (tiles,)
-    )
+    tiles = tiles.reshape(most, rays, cells)
+    turned, = call(turn, [jax.ShapeDtypeStruct((most, cells, rays), tiles.dtype)], [VMEM], (tiles,))
+    adjoint_scratch = [pltpu.VMEM((nrhs, half + cells), F32), pltpu.VMEM((nrhs, rows), BF16)]
+    low = pltpu.VMEM((nrhs, half + cells), BF16)
     u = right_side
     owns, others, alphas, betas = [], [], [], []
     for step in range(ITERS):
@@ -324,15 +398,24 @@
         owns.append(v)
         others.append(other)
         betas.append(beta)
+        part, = call(
+            functools.partial(forward_own, slots), [shape(rows + 128)], [SMEM] + [VMEM] * 2,
+            (lists, v, turned), [low],
+        )
         products, = call(
-            forward, [shape(rows + 128, jnp.int16)], [SMEM] * 2 + [VMEM] * 3, (*slots_in, v, other, turned),
-            [pltpu.VMEM((nrhs, 2 * half + cells), BF16), pltpu.VMEM((nrhs, rows), F32)],
+            functools.partial(forward_other, slots), [shape(rows + 128, jnp.int16)],
+            [SMEM] + [VMEM] * 3, (lists, part, other, turned), [pltpu.VMEM((nrhs, rows), F32), low],
         )
         rows_in = over_cell(products)
         if step + 1 < ITERS:
-            keep, send, u, alpha = call(
-                next_adjoint, halves + [shape(rows), shape(128)], [SMEM] * 2 + [VMEM] * 7,
-                (*slots_in, *rows_in, u, beta, tiles), store,
+            send, u, alpha = call(
+                functools.partial(adjoint_send, slots),
+                [shape(half + 128), shape(rows), shape(128)], [SMEM] + [VMEM] * 7,
+                (lists, *rows_in, u, beta, tiles), adjoint_scratch,
+            )
+            keep, = call(
+                functools.partial(adjoint_keep, slots), [shape(half + 128)],
+                [SMEM] + [VMEM] * 2, (lists, u, tiles), adjoint_scratch,
             )
         else:
             squares, alpha = call(

time: 127 us -> 128 us (level)
  Pallas kernels: 17.3 us -> 24.6 us
  waiting for transfers between devices: 58.2 us -> 52.3 us
    pallas_call x24 -> x31, Pallas kernels: 17.3 us -> 24.6 us  [call(): pl.pallas_call(body, out_shape=outs, in_specs=specs, out_specs=out_specs...]
    ppermute x9, waiting for transfers between devices: 10.7 us -> 3.89 us  [swap(): return lax.ppermute(value, 'core', [(0, 1), (1, 0)])]
  transfers between devices with their start and end apart: 48 -> 48, of which waited for: 35 -> 37; matrix products, arithmetic and copies ran while one was open for 0% -> 0% of each run, Pallas kernels for 1% -> 7%
where the time goes in v8:
time: 128 us
  waiting for transfers between devices  52.3 us (41%)
  starting transfers between devices  50.1 us (39%)
  Pallas kernels  24.6 us (19%)
    ppermute x39, starting transfers between devices, spread(): lax.ppermute(value, axis, [(i, i ^ by) for i in range(n)])  49.2 us
    ppermute x39, waiting for transfers between devices, spread(): lax.ppermute(value, axis, [(i, i ^ by) for i in range(n)])  48.5 us
    pallas_call x31, Pallas kernels, call(): pl.pallas_call(body, out_shape=outs, in_specs=specs, out_specs=out_specs...  24.6 us
    ppermute x9, waiting for transfers between devices, swap(): return lax.ppermute(value, 'core', [(0, 1), (1, 0)])  3.89 us
  transfers between devices with their start and end apart: 48, of which 37 were waited for; matrix products, arithmetic and copies ran while one was open for 0% of the time, Pallas kernels for 7%

profile of v8, /device:TPU:0, one launch (start us, length us, event | category | flops | bytes accessed | tf_op | source)
XLA Modules:
  0.0 128.1 jit_solution(18244717182394788136)
XLA Ops:
  0.6 3.4 %shard_map.59 = (f32[8,4224]{1,0:T(8,128)S(1)}, f32[8,4224]{1,0:T(8,128)S(1)}, bf16[8,4,256,256]{3,2,1,0:T(8,128)(2,1)S(1)}, s32[163]{0:T(256)S(1)}) custom-call(s32[4,8]{1,0:T(4,128)} %bitcast.11, s32[1,8]{1,0:T(1,128)} %bitcast.12, f32[8,2048]{1,0:T(8,128)} %prev_ref.3, bf16[8,4,256,256]{3,2,1,0:T(8,128)(2,1)} %source_ref.1), custom_call_target="tpu_custom_call" | custom-call | tf_op jit(solution)/shard_map/pallas_call | solution.py:329
  5.6 4.0 %collective-permute-start.3 = (s16[8,4224]{1,0:T(8,128)(2,1)S(1)}, s16[8,4224]{1,0:T(8,128)(2,1)S(1)}, u32[]{:S(2)}, u32[]{:S(2)}) collective-permute-start(s16[8,4224]{1,0:T(8,128)(2,1)S(1)} %shard_map.60.own_ref), channel_id=1, source_target_pairs={{0,64},{32,96},{64,0},{96,32},{1,65},{33,97},{65,1},{97,33},{2,66}... | collective-permute-start | bytes 202760 | tf_op jit(solution)/shard_map/ppermute | solution.py:353
  10.7 1.4 %collective-permute-done.3.far_ref = s16[8,4224]{1,0:T(8,128)(2,1)S(1)} collective-permute-done((s16[8,4224]{1,0:T(8,128)(2,1)S(1)}, s16[8,4224]{1,0:T(8,128)(2,1)S(1)}, u32[]{:S(2)}, u32[]{:S(2)}) %collective-permute-start.3) | collective-permute-done | bytes 67616 | tf_op jit(solution)/shard_map/ppermute | solution.py:353
  12.1 3.0 %collective-permute-done.2.right_ref = s16[8,4224]{1,0:T(8,128)(2,1)S(1)} collective-permute-done((s16[8,4224]{1,0:T(8,128)(2,1)S(1)}, s16[8,4224]{1,0:T(8,128)(2,1)S(1)}, u32[]{:S(2)}, u32[]{:S(2)}) %collective-permute-start.2) | collective-permute-done | bytes 67616 | tf_op jit(solution)/shard_map/ppermute | solution.py:353
  18.9 3.1 %collective-permute-start.7 = (s16[8,2176]{1,0:T(8,128)(2,1)S(1)}, s16[8,2176]{1,0:T(8,128)(2,1)S(1)}, u32[]{:S(2)}, u32[]{:S(2)}) collective-permute-start(s16[8,2176]{1,0:T(8,128)(2,1)S(1)} %shard_map.64.own_ref), channel_id=1, source_target_pairs={{0,8},{4,12},{8,0},{12,4},{1,9},{5,13},{9,1},{13,5},{2,10},{6,14},... | collective-permute-start | bytes 104456 | tf_op jit(solution)/shard_map/ppermute | solution.py:353
  24.4 2.7 %collective-permute-done.6.right_ref = s16[8,2176]{1,0:T(8,128)(2,1)S(1)} collective-permute-done((s16[8,2176]{1,0:T(8,128)(2,1)S(1)}, s16[8,2176]{1,0:T(8,128)(2,1)S(1)}, u32[]{:S(2)}, u32[]{:S(2)}) %collective-permute-start.6) | collective-permute-done | bytes 34848 | tf_op jit(solution)/shard_map/ppermute | solution.py:353
  27.4 3.4 %collective-permute-start.10 = (s16[8,2176]{1,0:T(8,128)(2,1)S(1)}, s16[8,2176]{1,0:T(8,128)(2,1)S(1)}, u32[]{:S(2)}, u32[]{:S(2)}) collective-permute-start(s16[8,2176]{1,0:T(8,128)(2,1)S(1)} %shard_map.65.own_ref), channel_id=1, source_target_pairs={{0,2},{1,3},{2,0},{3,1},{4,6},{5,7},{6,4},{7,5},{8,10},{9,11},{10,... | collective-permute-start | bytes 104456 | tf_op jit(solution)/shard_map/ppermute | solution.py:353
  31.5 1.4 %collective-permute-done.10.far_ref = s16[8,2176]{1,0:T(8,128)(2,1)S(1)} collective-permute-done((s16[8,2176]{1,0:T(8,128)(2,1)S(1)}, s16[8,2176]{1,0:T(8,128)(2,1)S(1)}, u32[]{:S(2)}, u32[]{:S(2)}) %collective-permute-start.10) | collective-permute-done | bytes 34848 | tf_op jit(solution)/shard_map/ppermute | solution.py:353
  33.0 3.1 %collective-permute-done.9.right_ref = s16[8,2176]{1,0:T(8,128)(2,1)S(1)} collective-permute-done((s16[8,2176]{1,0:T(8,128)(2,1)S(1)}, s16[8,2176]{1,0:T(8,128)(2,1)S(1)}, u32[]{:S(2)}, u32[]{:S(2)}) %collective-permute-start.9) | collective-permute-done | bytes 34848 | tf_op jit(solution)/shard_map/ppermute | solution.py:353
  38.9 1.5 %collective-permute-start.14 = (s16[8,4224]{1,0:T(8,128)(2,1)S(1)}, s16[8,4224]{1,0:T(8,128)(2,1)S(1)}, u32[]{:S(2)}, u32[]{:S(2)}) collective-permute-start(s16[8,4224]{1,0:T(8,128)(2,1)S(1)} %shard_map.68.own_ref), channel_id=1, source_target_pairs={{0,64},{32,96},{64,0},{96,32},{1,65},{33,97},{65,1},{97,33},{2,66}... | collective-permute-start | bytes 202760 | tf_op jit(solution)/shard_map/ppermute | solution.py:353
  42.5 2.4 %collective-permute-done.14.far_ref = s16[8,4224]{1,0:T(8,128)(2,1)S(1)} collective-permute-done((s16[8,4224]{1,0:T(8,128)(2,1)S(1)}, s16[8,4224]{1,0:T(8,128)(2,1)S(1)}, u32[]{:S(2)}, u32[]{:S(2)}) %collective-permute-start.14) | collective-permute-done | bytes 67616 | tf_op jit(solution)/shard_map/ppermute | solution.py:353
  44.8 1.4 %collective-permute-done.13.right_ref = s16[8,4224]{1,0:T(8,128)(2,1)S(1)} collective-permute-done((s16[8,4224]{1,0:T(8,128)(2,1)S(1)}, s16[8,4224]{1,0:T(8,128)(2,1)S(1)}, u32[]{:S(2)}, u32[]{:S(2)}) %collective-permute-start.13) | collective-permute-done | bytes 67616 | tf_op jit(solution)/shard_map/ppermute | solution.py:353
  50.3 1.5 %collective-permute-start.17 = (s16[8,2176]{1,0:T(8,128)(2,1)S(1)}, s16[8,2176]{1,0:T(8,128)(2,1)S(1)}, u32[]{:S(2)}, u32[]{:S(2)}) collective-permute-start(s16[8,2176]{1,0:T(8,128)(2,1)S(1)} %shard_map.71.own_ref), channel_id=1, source_target_pairs={{0,12},{4,8},{8,4},{12,0},{1,13},{5,9},{9,5},{13,1},{2,14},{6,10},... | collective-permute-start | bytes 104456 | tf_op jit(solution)/shard_map/ppermute | solution.py:353
  52.6 2.1 %collective-permute-done.18.far_ref = s16[8,2176]{1,0:T(8,128)(2,1)S(1)} collective-permute-done((s16[8,2176]{1,0:T(8,128)(2,1)S(1)}, s16[8,2176]{1,0:T(8,128)(2,1)S(1)}, u32[]{:S(2)}, u32[]{:S(2)}) %collective-permute-start.18) | collective-permute-done | bytes 34848 | tf_op jit(solution)/shard_map/ppermute | solution.py:353
  56.0 2.1 %collective-permute-start.21 = (s16[8,2176]{1,0:T(8,128)(2,1)S(1)}, s16[8,2176]{1,0:T(8,128)(2,1)S(1)}, u32[]{:S(2)}, u32[]{:S(2)}) collective-permute-start(s16[8,2176]{1,0:T(8,128)(2,1)S(1)} %shard_map.72.own_ref), channel_id=1, source_target_pairs={{0,2},{1,3},{2,0},{3,1},{4,6},{5,7},{6,4},{7,5},{8,10},{9,11},{10,... | collective-permute-start | bytes 104456 | tf_op jit(solution)/shard_map/ppermute | solution.py:353
  59.6 2.3 %collective-permute-done.21.far_ref = s16[8,2176]{1,0:T(8,128)(2,1)S(1)} collective-permute-done((s16[8,2176]{1,0:T(8,128)(2,1)S(1)}, s16[8,2176]{1,0:T(8,128)(2,1)S(1)}, u32[]{:S(2)}, u32[]{:S(2)}) %collective-permute-start.21) | collective-permute-done | bytes 34848 | tf_op jit(solution)/shard_map/ppermute | solution.py:353
  61.9 1.4 %collective-permute-done.20.right_ref = s16[8,2176]{1,0:T(8,128)(2,1)S(1)} collective-permute-done((s16[8,2176]{1,0:T(8,128)(2,1)S(1)}, s16[8,2176]{1,0:T(8,128)(2,1)S(1)}, u32[]{:S(2)}, u32[]{:S(2)}) %collective-permute-start.20) | collective-permute-done | bytes 34848 | tf_op jit(solution)/shard_map/ppermute | solution.py:353
  67.3 1.6 %collective-permute-start.24 = (s16[8,4224]{1,0:T(8,128)(2,1)S(1)}, s16[8,4224]{1,0:T(8,128)(2,1)S(1)}, u32[]{:S(2)}, u32[]{:S(2)}) collective-permute-start(s16[8,4224]{1,0:T(8,128)(2,1)S(1)} %shard_map.75.own_ref), channel_id=1, source_target_pairs={{0,96},{32,64},{64,32},{96,0},{1,97},{33,65},{65,33},{97,1},{2,98}... | collective-permute-start | bytes 202760 | tf_op jit(solution)/shard_map/ppermute | solution.py:353
  69.7 2.4 %collective-permute-done.25.far_ref = s16[8,4224]{1,0:T(8,128)(2,1)S(1)} collective-permute-done((s16[8,4224]{1,0:T(8,128)(2,1)S(1)}, s16[8,4224]{1,0:T(8,128)(2,1)S(1)}, u32[]{:S(2)}, u32[]{:S(2)}) %collective-permute-start.25) | collective-permute-done | bytes 67616 | tf_op jit(solution)/shard_map/ppermute | solution.py:353
  76.5 1.6 %collective-permute-start.29 = (s16[8,2176]{1,0:T(8,128)(2,1)S(1)}, s16[8,2176]{1,0:T(8,128)(2,1)S(1)}, u32[]{:S(2)}, u32[]{:S(2)}) collective-permute-start(s16[8,2176]{1,0:T(8,128)(2,1)S(1)} %shard_map.78.own_ref), channel_id=1, source_target_pairs={{0,8},{4,12},{8,0},{12,4},{1,9},{5,13},{9,1},{13,5},{2,10},{6,14},... | collective-permute-start | bytes 104456 | tf_op jit(solution)/shard_map/ppermute | solution.py:353
  80.0 2.0 %collective-permute-done.29.far_ref = s16[8,2176]{1,0:T(8,128)(2,1)S(1)} collective-permute-done((s16[8,2176]{1,0:T(8,128)(2,1)S(1)}, s16[8,2176]{1,0:T(8,128)(2,1)S(1)}, u32[]{:S(2)}, u32[]{:S(2)}) %collective-permute-start.29) | collective-permute-done | bytes 34848 | tf_op jit(solution)/shard_map/ppermute | solution.py:353
  83.5 3.3 %collective-permute-start.32 = (s16[8,2176]{1,0:T(8,128)(2,1)S(1)}, s16[8,2176]{1,0:T(8,128)(2,1)S(1)}, u32[]{:S(2)}, u32[]{:S(2)}) collective-permute-start(s16[8,2176]{1,0:T(8,128)(2,1)S(1)} %shard_map.79.own_ref), channel_id=1, source_target_pairs={{0,2},{1,3},{2,0},{3,1},{4,6},{5,7},{6,4},{7,5},{8,10},{9,11},{10,... | collective-permute-start | bytes 104456 | tf_op jit(solution)/shard_map/ppermute | solution.py:353
  87.3 1.8 %collective-permute-done.32.far_ref = s16[8,2176]{1,0:T(8,128)(2,1)S(1)} collective-permute-done((s16[8,2176]{1,0:T(8,128)(2,1)S(1)}, s16[8,2176]{1,0:T(8,128)(2,1)S(1)}, u32[]{:S(2)}, u32[]{:S(2)}) %collective-permute-start.32) | collective-permute-done | bytes 34848 | tf_op jit(solution)/shard_map/ppermute | solution.py:353
  89.0 2.9 %collective-permute-done.31.right_ref = s16[8,2176]{1,0:T(8,128)(2,1)S(1)} collective-permute-done((s16[8,2176]{1,0:T(8,128)(2,1)S(1)}, s16[8,2176]{1,0:T(8,128)(2,1)S(1)}, u32[]{:S(2)}, u32[]{:S(2)}) %collective-permute-start.31) | collective-permute-done | bytes 34848 | tf_op jit(solution)/shard_map/ppermute | solution.py:353
  95.9 1.6 %collective-permute-start.35 = (s16[8,4224]{1,0:T(8,128)(2,1)S(1)}, s16[8,4224]{1,0:T(8,128)(2,1)S(1)}, u32[]{:S(2)}, u32[]{:S(2)}) collective-permute-start(s16[8,4224]{1,0:T(8,128)(2,1)S(1)} %shard_map.82.own_ref), channel_id=1, source_target_pairs={{0,96},{32,64},{64,32},{96,0},{1,97},{33,65},{65,33},{97,1},{2,98}... | collective-permute-start | bytes 202760 | tf_op jit(solution)/shard_map/ppermute | solution.py:353
  98.4 2.4 %collective-permute-done.36.far_ref = s16[8,4224]{1,0:T(8,128)(2,1)S(1)} collective-permute-done((s16[8,4224]{1,0:T(8,128)(2,1)S(1)}, s16[8,4224]{1,0:T(8,128)(2,1)S(1)}, u32[]{:S(2)}, u32[]{:S(2)}) %collective-permute-start.36) | collective-permute-done | bytes 67616 | tf_op jit(solution)/shard_map/ppermute | solution.py:353
  105.7 1.9 %collective-permute-start.39 = (s16[8,2176]{1,0:T(8,128)(2,1)S(1)}, s16[8,2176]{1,0:T(8,128)(2,1)S(1)}, u32[]{:S(2)}, u32[]{:S(2)}) collective-permute-start(s16[8,2176]{1,0:T(8,128)(2,1)S(1)} %shard_map.85.own_ref), channel_id=1, source_target_pairs={{0,12},{4,8},{8,4},{12,0},{1,13},{5,9},{9,5},{13,1},{2,14},{6,10},... | collective-permute-start | bytes 104456 | tf_op jit(solution)/shard_map/ppermute | solution.py:353
  108.6 2.0 %collective-permute-done.40.far_ref = s16[8,2176]{1,0:T(8,128)(2,1)S(1)} collective-permute-done((s16[8,2176]{1,0:T(8,128)(2,1)S(1)}, s16[8,2176]{1,0:T(8,128)(2,1)S(1)}, u32[]{:S(2)}, u32[]{:S(2)}) %collective-permute-start.40) | collective-permute-done | bytes 34848 | tf_op jit(solution)/shard_map/ppermute | solution.py:353
  111.8 2.2 %collective-permute-start.43 = (s16[8,2176]{1,0:T(8,128)(2,1)S(1)}, s16[8,2176]{1,0:T(8,128)(2,1)S(1)}, u32[]{:S(2)}, u32[]{:S(2)}) collective-permute-start(s16[8,2176]{1,0:T(8,128)(2,1)S(1)} %shard_map.86.own_ref), channel_id=1, source_target_pairs={{0,2},{1,3},{2,0},{3,1},{4,6},{5,7},{6,4},{7,5},{8,10},{9,11},{10,... | collective-permute-start | bytes 104456 | tf_op jit(solution)/shard_map/ppermute | solution.py:353
  115.4 2.0 %collective-permute-done.43.far_ref = s16[8,2176]{1,0:T(8,128)(2,1)S(1)} collective-permute-done((s16[8,2176]{1,0:T(8,128)(2,1)S(1)}, s16[8,2176]{1,0:T(8,128)(2,1)S(1)}, u32[]{:S(2)}, u32[]{:S(2)}) %collective-permute-start.43) | collective-permute-done | bytes 34848 | tf_op jit(solution)/shard_map/ppermute | solution.py:353
  117.4 1.8 %collective-permute-done.42.right_ref = s16[8,2176]{1,0:T(8,128)(2,1)S(1)} collective-permute-done((s16[8,2176]{1,0:T(8,128)(2,1)S(1)}, s16[8,2176]{1,0:T(8,128)(2,1)S(1)}, u32[]{:S(2)}, u32[]{:S(2)}) %collective-permute-start.42) | collective-permute-done | bytes 34848 | tf_op jit(solution)/shard_map/ppermute | solution.py:353
  121.8 1.8 %collective-permute-start.46 = (f32[8,128]{1,0:T(8,128)S(1)}, f32[8,128]{1,0:T(8,128)S(1)}, u32[]{:S(2)}, u32[]{:S(2)}) collective-permute-start(f32[8,128]{1,0:T(8,128)S(1)} %add.3.own_ref), channel_id=1, source_target_pairs={{0,96},{32,64},{64,32},{96,0},{1,97},{33,65},{65,33},{97,1},{2,98}... | collective-permute-start | bytes 12296 | tf_op jit(solution)/shard_map/ppermute | solution.py:353
  (98 shorter events, 55.7 us)
Async XLA Ops:
  5.6 6.5 %collective-permute-start.3 = (s16[8,4224]{1,0:T(8,128)(2,1)S(1)}, s16[8,4224]{1,0:T(8,128)(2,1)S(1)}, u32[]{:S(2)}, u32[]{:S(2)}) collective-permute-start(s16[8,4224]{1,0:T(8,128)(2,1)S(1)} %shard_map.60.own_ref), channel_id=1, source_target_pairs={{0,64},{32,96},{64,0},{96,32},{1,65},{33,97},{65,1},{97,33},{2,66}... | collective-permute-start | bytes 202760 | tf_op jit(solution)/shard_map/ppermute | solution.py:353
  9.6 5.5 %collective-permute-start.2 = (s16[8,4224]{1,0:T(8,128)(2,1)S(1)}, s16[8,4224]{1,0:T(8,128)(2,1)S(1)}, u32[]{:S(2)}, u32[]{:S(2)}) collective-permute-start(s16[8,4224]{1,0:T(8,128)(2,1)S(1)} %shard_map.60.own_ref), channel_id=1, source_target_pairs={{0,96},{32,64},{64,32},{96,0},{1,97},{33,65},{65,33},{97,1},{2,98}... | collective-permute-start | bytes 202760 | tf_op jit(solution)/shard_map/ppermute | solution.py:353
  10.3 4.8 %collective-permute-start.1 = (s16[8,4224]{1,0:T(8,128)(2,1)S(1)}, s16[8,4224]{1,0:T(8,128)(2,1)S(1)}, u32[]{:S(2)}, u32[]{:S(2)}) collective-permute-start(s16[8,4224]{1,0:T(8,128)(2,1)S(1)} %shard_map.60.own_ref), channel_id=1, source_target_pairs={{0,32},{32,0},{64,96},{96,64},{1,33},{33,1},{65,97},{97,65},{2,34}... | collective-permute-start | bytes 202760 | tf_op jit(solution)/shard_map/ppermute | solution.py:353
  18.9 5.5 %collective-permute-start.7 = (s16[8,2176]{1,0:T(8,128)(2,1)S(1)}, s16[8,2176]{1,0:T(8,128)(2,1)S(1)}, u32[]{:S(2)}, u32[]{:S(2)}) collective-permute-start(s16[8,2176]{1,0:T(8,128)(2,1)S(1)} %shard_map.64.own_ref), channel_id=1, source_target_pairs={{0,8},{4,12},{8,0},{12,4},{1,9},{5,13},{9,1},{13,5},{2,10},{6,14},... | collective-permute-start | bytes 104456 | tf_op jit(solution)/shard_map/ppermute | solution.py:353
  22.0 5.1 %collective-permute-start.6 = (s16[8,2176]{1,0:T(8,128)(2,1)S(1)}, s16[8,2176]{1,0:T(8,128)(2,1)S(1)}, u32[]{:S(2)}, u32[]{:S(2)}) collective-permute-start(s16[8,2176]{1,0:T(8,128)(2,1)S(1)} %shard_map.64.own_ref), channel_id=1, source_target_pairs={{0,12},{4,8},{8,4},{12,0},{1,13},{5,9},{9,5},{13,1},{2,14},{6,10},... | collective-permute-start | bytes 104456 | tf_op jit(solution)/shard_map/ppermute | solution.py:353
  27.4 5.5 %collective-permute-start.10 = (s16[8,2176]{1,0:T(8,128)(2,1)S(1)}, s16[8,2176]{1,0:T(8,128)(2,1)S(1)}, u32[]{:S(2)}, u32[]{:S(2)}) collective-permute-start(s16[8,2176]{1,0:T(8,128)(2,1)S(1)} %shard_map.65.own_ref), channel_id=1, source_target_pairs={{0,2},{1,3},{2,0},{3,1},{4,6},{5,7},{6,4},{7,5},{8,10},{9,11},{10,... | collective-permute-start | bytes 104456 | tf_op jit(solution)/shard_map/ppermute | solution.py:353
  30.9 5.1 %collective-permute-start.9 = (s16[8,2176]{1,0:T(8,128)(2,1)S(1)}, s16[8,2176]{1,0:T(8,128)(2,1)S(1)}, u32[]{:S(2)}, u32[]{:S(2)}) collective-permute-start(s16[8,2176]{1,0:T(8,128)(2,1)S(1)} %shard_map.65.own_ref), channel_id=1, source_target_pairs={{0,3},{1,2},{2,1},{3,0},{4,7},{5,6},{6,5},{7,4},{8,11},{9,10},{10,... | collective-permute-start | bytes 104456 | tf_op jit(solution)/shard_map/ppermute | solution.py:353
  38.9 6.0 %collective-permute-start.14 = (s16[8,4224]{1,0:T(8,128)(2,1)S(1)}, s16[8,4224]{1,0:T(8,128)(2,1)S(1)}, u32[]{:S(2)}, u32[]{:S(2)}) collective-permute-start(s16[8,4224]{1,0:T(8,128)(2,1)S(1)} %shard_map.68.own_ref), channel_id=1, source_target_pairs={{0,64},{32,96},{64,0},{96,32},{1,65},{33,97},{65,1},{97,33},{2,66}... | collective-permute-start | bytes 202760 | tf_op jit(solution)/shard_map/ppermute | solution.py:353
  40.4 5.8 %collective-permute-start.13 = (s16[8,4224]{1,0:T(8,128)(2,1)S(1)}, s16[8,4224]{1,0:T(8,128)(2,1)S(1)}, u32[]{:S(2)}, u32[]{:S(2)}) collective-permute-start(s16[8,4224]{1,0:T(8,128)(2,1)S(1)} %shard_map.68.own_ref), channel_id=1, source_target_pairs={{0,96},{32,64},{64,32},{96,0},{1,97},{33,65},{65,33},{97,1},{2,98}... | collective-permute-start | bytes 202760 | tf_op jit(solution)/shard_map/ppermute | solution.py:353
  41.1 5.1 %collective-permute-start.12 = (s16[8,4224]{1,0:T(8,128)(2,1)S(1)}, s16[8,4224]{1,0:T(8,128)(2,1)S(1)}, u32[]{:S(2)}, u32[]{:S(2)}) collective-permute-start(s16[8,4224]{1,0:T(8,128)(2,1)S(1)} %shard_map.68.own_ref), channel_id=1, source_target_pairs={{0,32},{32,0},{64,96},{96,64},{1,33},{33,1},{65,97},{97,65},{2,34}... | collective-permute-start | bytes 202760 | tf_op jit(solution)/shard_map/ppermute | solution.py:353
  49.1 5.6 %collective-permute-start.18 = (s16[8,2176]{1,0:T(8,128)(2,1)S(1)}, s16[8,2176]{1,0:T(8,128)(2,1)S(1)}, u32[]{:S(2)}, u32[]{:S(2)}) collective-permute-start(s16[8,2176]{1,0:T(8,128)(2,1)S(1)} %shard_map.71.own_ref), channel_id=1, source_target_pairs={{0,8},{4,12},{8,0},{12,4},{1,9},{5,13},{9,1},{13,5},{2,10},{6,14},... | collective-permute-start | bytes 104456 | tf_op jit(solution)/shard_map/ppermute | solution.py:353
  50.3 5.1 %collective-permute-start.17 = (s16[8,2176]{1,0:T(8,128)(2,1)S(1)}, s16[8,2176]{1,0:T(8,128)(2,1)S(1)}, u32[]{:S(2)}, u32[]{:S(2)}) collective-permute-start(s16[8,2176]{1,0:T(8,128)(2,1)S(1)} %shard_map.71.own_ref), channel_id=1, source_target_pairs={{0,12},{4,8},{8,4},{12,0},{1,13},{5,9},{9,5},{13,1},{2,14},{6,10},... | collective-permute-start | bytes 104456 | tf_op jit(solution)/shard_map/ppermute | solution.py:353
  56.0 5.8 %collective-permute-start.21 = (s16[8,2176]{1,0:T(8,128)(2,1)S(1)}, s16[8,2176]{1,0:T(8,128)(2,1)S(1)}, u32[]{:S(2)}, u32[]{:S(2)}) collective-permute-start(s16[8,2176]{1,0:T(8,128)(2,1)S(1)} %shard_map.72.own_ref), channel_id=1, source_target_pairs={{0,2},{1,3},{2,0},{3,1},{4,6},{5,7},{6,4},{7,5},{8,10},{9,11},{10,... | collective-permute-start | bytes 104456 | tf_op jit(solution)/shard_map/ppermute | solution.py:353
  58.1 5.1 %collective-permute-start.20 = (s16[8,2176]{1,0:T(8,128)(2,1)S(1)}, s16[8,2176]{1,0:T(8,128)(2,1)S(1)}, u32[]{:S(2)}, u32[]{:S(2)}) collective-permute-start(s16[8,2176]{1,0:T(8,128)(2,1)S(1)} %shard_map.72.own_ref), channel_id=1, source_target_pairs={{0,3},{1,2},{2,1},{3,0},{4,7},{5,6},{6,5},{7,4},{8,11},{9,10},{10,... | collective-permute-start | bytes 104456 | tf_op jit(solution)/shard_map/ppermute | solution.py:353
  58.6 4.7 %collective-permute-start.19 = (s16[8,2176]{1,0:T(8,128)(2,1)S(1)}, s16[8,2176]{1,0:T(8,128)(2,1)S(1)}, u32[]{:S(2)}, u32[]{:S(2)}) collective-permute-start(s16[8,2176]{1,0:T(8,128)(2,1)S(1)} %shard_map.72.own_ref), channel_id=1, source_target_pairs={{0,1},{1,0},{2,3},{3,2},{4,5},{5,4},{6,7},{7,6},{8,9},{9,8},{10,11... | collective-permute-start | bytes 104456 | tf_op jit(solution)/shard_map/ppermute | solution.py:353
  66.1 6.0 %collective-permute-start.25 = (s16[8,4224]{1,0:T(8,128)(2,1)S(1)}, s16[8,4224]{1,0:T(8,128)(2,1)S(1)}, u32[]{:S(2)}, u32[]{:S(2)}) collective-permute-start(s16[8,4224]{1,0:T(8,128)(2,1)S(1)} %shard_map.75.own_ref), channel_id=1, source_target_pairs={{0,64},{32,96},{64,0},{96,32},{1,65},{33,97},{65,1},{97,33},{2,66}... | collective-permute-start | bytes 202760 | tf_op jit(solution)/shard_map/ppermute | solution.py:353
  67.3 6.2 %collective-permute-start.24 = (s16[8,4224]{1,0:T(8,128)(2,1)S(1)}, s16[8,4224]{1,0:T(8,128)(2,1)S(1)}, u32[]{:S(2)}, u32[]{:S(2)}) collective-permute-start(s16[8,4224]{1,0:T(8,128)(2,1)S(1)} %shard_map.75.own_ref), channel_id=1, source_target_pairs={{0,96},{32,64},{64,32},{96,0},{1,97},{33,65},{65,33},{97,1},{2,98}... | collective-permute-start | bytes 202760 | tf_op jit(solution)/shard_map/ppermute | solution.py:353
  68.8 4.6 %collective-permute-start.23 = (s16[8,4224]{1,0:T(8,128)(2,1)S(1)}, s16[8,4224]{1,0:T(8,128)(2,1)S(1)}, u32[]{:S(2)}, u32[]{:S(2)}) collective-permute-start(s16[8,4224]{1,0:T(8,128)(2,1)S(1)} %shard_map.75.own_ref), channel_id=1, source_target_pairs={{0,32},{32,0},{64,96},{96,64},{1,33},{33,1},{65,97},{97,65},{2,34}... | collective-permute-start | bytes 202760 | tf_op jit(solution)/shard_map/ppermute | solution.py:353
  76.5 5.5 %collective-permute-start.29 = (s16[8,2176]{1,0:T(8,128)(2,1)S(1)}, s16[8,2176]{1,0:T(8,128)(2,1)S(1)}, u32[]{:S(2)}, u32[]{:S(2)}) collective-permute-start(s16[8,2176]{1,0:T(8,128)(2,1)S(1)} %shard_map.78.own_ref), channel_id=1, source_target_pairs={{0,8},{4,12},{8,0},{12,4},{1,9},{5,13},{9,1},{13,5},{2,10},{6,14},... | collective-permute-start | bytes 104456 | tf_op jit(solution)/shard_map/ppermute | solution.py:353
  78.1 5.1 %collective-permute-start.28 = (s16[8,2176]{1,0:T(8,128)(2,1)S(1)}, s16[8,2176]{1,0:T(8,128)(2,1)S(1)}, u32[]{:S(2)}, u32[]{:S(2)}) collective-permute-start(s16[8,2176]{1,0:T(8,128)(2,1)S(1)} %shard_map.78.own_ref), channel_id=1, source_target_pairs={{0,12},{4,8},{8,4},{12,0},{1,13},{5,9},{9,5},{13,1},{2,14},{6,10},... | collective-permute-start | bytes 104456 | tf_op jit(solution)/shard_map/ppermute | solution.py:353
  83.5 5.5 %collective-permute-start.32 = (s16[8,2176]{1,0:T(8,128)(2,1)S(1)}, s16[8,2176]{1,0:T(8,128)(2,1)S(1)}, u32[]{:S(2)}, u32[]{:S(2)}) collective-permute-start(s16[8,2176]{1,0:T(8,128)(2,1)S(1)} %shard_map.79.own_ref), channel_id=1, source_target_pairs={{0,2},{1,3},{2,0},{3,1},{4,6},{5,7},{6,4},{7,5},{8,10},{9,11},{10,... | collective-permute-start | bytes 104456 | tf_op jit(solution)/shard_map/ppermute | solution.py:353
  86.8 5.1 %collective-permute-start.31 = (s16[8,2176]{1,0:T(8,128)(2,1)S(1)}, s16[8,2176]{1,0:T(8,128)(2,1)S(1)}, u32[]{:S(2)}, u32[]{:S(2)}) collective-permute-start(s16[8,2176]{1,0:T(8,128)(2,1)S(1)} %shard_map.79.own_ref), channel_id=1, source_target_pairs={{0,3},{1,2},{2,1},{3,0},{4,7},{5,6},{6,5},{7,4},{8,11},{9,10},{10,... | collective-permute-start | bytes 104456 | tf_op jit(solution)/shard_map/ppermute | solution.py:353
  87.3 4.7 %collective-permute-start.30 = (s16[8,2176]{1,0:T(8,128)(2,1)S(1)}, s16[8,2176]{1,0:T(8,128)(2,1)S(1)}, u32[]{:S(2)}, u32[]{:S(2)}) collective-permute-start(s16[8,2176]{1,0:T(8,128)(2,1)S(1)} %shard_map.79.own_ref), channel_id=1, source_target_pairs={{0,1},{1,0},{2,3},{3,2},{4,5},{5,4},{6,7},{7,6},{8,9},{9,8},{10,11... | collective-permute-start | bytes 104456 | tf_op jit(solution)/shard_map/ppermute | solution.py:353
  94.8 6.0 %collective-permute-start.36 = (s16[8,4224]{1,0:T(8,128)(2,1)S(1)}, s16[8,4224]{1,0:T(8,128)(2,1)S(1)}, u32[]{:S(2)}, u32[]{:S(2)}) collective-permute-start(s16[8,4224]{1,0:T(8,128)(2,1)S(1)} %shard_map.82.own_ref), channel_id=1, source_target_pairs={{0,64},{32,96},{64,0},{96,32},{1,65},{33,97},{65,1},{97,33},{2,66}... | collective-permute-start | bytes 202760 | tf_op jit(solution)/shard_map/ppermute | solution.py:353
  95.9 6.2 %collective-permute-start.35 = (s16[8,4224]{1,0:T(8,128)(2,1)S(1)}, s16[8,4224]{1,0:T(8,128)(2,1)S(1)}, u32[]{:S(2)}, u32[]{:S(2)}) collective-permute-start(s16[8,4224]{1,0:T(8,128)(2,1)S(1)} %shard_map.82.own_ref), channel_id=1, source_target_pairs={{0,96},{32,64},{64,32},{96,0},{1,97},{33,65},{65,33},{97,1},{2,98}... | collective-permute-start | bytes 202760 | tf_op jit(solution)/shard_map/ppermute | solution.py:353
  105.0 5.5 %collective-permute-start.40 = (s16[8,2176]{1,0:T(8,128)(2,1)S(1)}, s16[8,2176]{1,0:T(8,128)(2,1)S(1)}, u32[]{:S(2)}, u32[]{:S(2)}) collective-permute-start(s16[8,2176]{1,0:T(8,128)(2,1)S(1)} %shard_map.85.own_ref), channel_id=1, source_target_pairs={{0,8},{4,12},{8,0},{12,4},{1,9},{5,13},{9,1},{13,5},{2,10},{6,14},... | collective-permute-start | bytes 104456 | tf_op jit(solution)/shard_map/ppermute | solution.py:353
  105.7 5.2 %collective-permute-start.39 = (s16[8,2176]{1,0:T(8,128)(2,1)S(1)}, s16[8,2176]{1,0:T(8,128)(2,1)S(1)}, u32[]{:S(2)}, u32[]{:S(2)}) collective-permute-start(s16[8,2176]{1,0:T(8,128)(2,1)S(1)} %shard_map.85.own_ref), channel_id=1, source_target_pairs={{0,12},{4,8},{8,4},{12,0},{1,13},{5,9},{9,5},{13,1},{2,14},{6,10},... | collective-permute-start | bytes 104456 | tf_op jit(solution)/shard_map/ppermute | solution.py:353
  111.8 5.6 %collective-permute-start.43 = (s16[8,2176]{1,0:T(8,128)(2,1)S(1)}, s16[8,2176]{1,0:T(8,128)(2,1)S(1)}, u32[]{:S(2)}, u32[]{:S(2)}) collective-permute-start(s16[8,2176]{1,0:T(8,128)(2,1)S(1)} %shard_map.86.own_ref), channel_id=1, source_target_pairs={{0,2},{1,3},{2,0},{3,1},{4,6},{5,7},{6,4},{7,5},{8,10},{9,11},{10,... | collective-permute-start | bytes 104456 | tf_op jit(solution)/shard_map/ppermute | solution.py:353
  114.0 5.1 %collective-permute-start.42 = (s16[8,2176]{1,0:T(8,128)(2,1)S(1)}, s16[8,2176]{1,0:T(8,128)(2,1)S(1)}, u32[]{:S(2)}, u32[]{:S(2)}) collective-permute-start(s16[8,2176]{1,0:T(8,128)(2,1)S(1)} %shard_map.86.own_ref), channel_id=1, source_target_pairs={{0,3},{1,2},{2,1},{3,0},{4,7},{5,6},{6,5},{7,4},{8,11},{9,10},{10,... | collective-permute-start | bytes 104456 | tf_op jit(solution)/shard_map/ppermute | solution.py:353
  114.5 4.7 %collective-permute-start.41 = (s16[8,2176]{1,0:T(8,128)(2,1)S(1)}, s16[8,2176]{1,0:T(8,128)(2,1)S(1)}, u32[]{:S(2)}, u32[]{:S(2)}) collective-permute-start(s16[8,2176]{1,0:T(8,128)(2,1)S(1)} %shard_map.86.own_ref), channel_id=1, source_target_pairs={{0,1},{1,0},{2,3},{3,2},{4,5},{5,4},{6,7},{7,6},{8,9},{9,8},{10,11... | collective-permute-start | bytes 104456 | tf_op jit(solution)/shard_map/ppermute | solution.py:353
  120.6 5.1 %collective-permute-start.47 = (f32[8,128]{1,0:T(8,128)S(1)}, f32[8,128]{1,0:T(8,128)S(1)}, u32[]{:S(2)}, u32[]{:S(2)}) collective-permute-start(f32[8,128]{1,0:T(8,128)S(1)} %add.3.own_ref), channel_id=1, source_target_pairs={{0,64},{32,96},{64,0},{96,32},{1,65},{33,97},{65,1},{97,33},{2,66}... | collective-permute-start | bytes 12296 | tf_op jit(solution)/shard_map/ppermute | solution.py:353
  121.8 4.8 %collective-permute-start.46 = (f32[8,128]{1,0:T(8,128)S(1)}, f32[8,128]{1,0:T(8,128)S(1)}, u32[]{:S(2)}, u32[]{:S(2)}) collective-permute-start(f32[8,128]{1,0:T(8,128)S(1)} %add.3.own_ref), channel_id=1, source_target_pairs={{0,96},{32,64},{64,32},{96,0},{1,97},{33,65},{65,33},{97,1},{2,98}... | collective-permute-start | bytes 12296 | tf_op jit(solution)/shard_map/ppermute | solution.py:353
  (17 other events, 56.9 us)

commit v9 on v8

--- a/solution.py
+++ b/solution.py
@@ -8,7 +8,8 @@
 from jax.sharding import Mesh, PartitionSpec as P
 
 BLK_DEV = 32
-GROUP = 8
+HEAD = 20
+GROUP = 4
 ITERS = 4
 EPS = 1e-06
 TINY = 1e-30
@@ -78,14 +79,18 @@
     most = tiles_ref.shape[0]
     base = 2 * most if mine else 0
 
+    def run(first, count):
+        for i in range(count):
+            one(lists_ref[first + i], lists_ref[first + i + most])
+
     def group(g, carry):
-        for i in range(GROUP):
-            at = base + g * GROUP + i
-            one(lists_ref[at], lists_ref[at + most])
+        run(base + HEAD + g * GROUP, GROUP)
         return carry
 
-    length = lists_ref[4 * most + (1 if mine else 0)]
-    lax.fori_loop(0, (length + GROUP - 1) // GROUP, group, 0)
+    run(base, min(HEAD, most))
+    if HEAD < most:
+        rest = jnp.maximum(lists_ref[4 * most + (1 if mine else 0)] - HEAD, 0)
+        lax.fori_loop(0, (rest + GROUP - 1) // GROUP, group, 0)
 
 
 def half_adjoint(lists_ref, mine, u, tiles_ref, out_ref, acc_ref, low_ref, slots):
@@ -139,8 +144,8 @@
 
 
 def first_adjoint(
-    source_p_ref, source_c_ref, source_u_ref, source_ref, keep_ref, send_ref, tiles_ref, lists_ref,
-    acc_ref, pattern_ref, counts_ref, u_ref, sem,
+    source_p_ref, source_c_ref, source_u_ref, source_ref, keep_ref, send_ref, tiles_ref, acc_ref,
+    pattern_ref, counts_ref, u_ref, sem,
 ):
     bundles = source_ref.shape[0]
     small = ((source_p_ref, pattern_ref), (source_c_ref, counts_ref), (source_u_ref, u_ref))
@@ -156,7 +161,6 @@
         copy.start()
     for copy in first:
         copy.wait()
-    fill_lists(pattern_ref, counts_ref, lists_ref)
     put = slots_of(pattern_ref, counts_ref, BLK_DEV // 2 + 1, BLK_DEV // 2)
     scatter_products(u_ref[...], put, tiles_ref, keep_ref, send_ref, acc_ref, copies)
 
@@ -253,7 +257,8 @@
     beta_ref[...] = wide(beta)
 
 
-def turn(tiles_ref, out_ref):
+def turn(pattern_ref, counts_ref, tiles_ref, out_ref, lists_ref):
+    fill_lists(pattern_ref, counts_ref, lists_ref)
     for tile in range(tiles_ref.shape[0]):
         out_ref[tile] = tiles_ref[tile].T
 
@@ -364,12 +369,8 @@
         return spread(summed, "y")
 
     halves = [shape(half + 128)] * 2
-    keep, send, tiles, lists = call(
-        first_adjoint,
-        halves + [
-            jax.ShapeDtypeStruct(tiles.shape, tiles.dtype),
-            jax.ShapeDtypeStruct((4 * most + 3 + most,), jnp.int32),
-        ],
+    keep, send, tiles = call(
+        first_adjoint, halves + [jax.ShapeDtypeStruct(tiles.shape, tiles.dtype)],
         [HBM] * 4,
         [pltpu.with_memory_space_constraint(z, pltpu.HBM) for z in (*slots_in, right_side, tiles)],
         [
@@ -377,10 +378,16 @@
             pltpu.SMEM((slots, bundles), jnp.int32), pltpu.SMEM((1, bundles), jnp.int32),
             pltpu.VMEM(right_side.shape, F32), pltpu.SemaphoreType.DMA((bundles + 3,)),
         ],
-        [VMEM] * 3 + [SMEM],
     )
     tiles = tiles.reshape(most, rays, cells)
-    turned, = call(turn, [jax.ShapeDtypeStruct((most, cells, rays), tiles.dtype)], [VMEM], (tiles,))
+    turned, lists = call(
+        turn,
+        [
+            jax.ShapeDtypeStruct((most, cells, rays), tiles.dtype),
+            jax.ShapeDtypeStruct((5 * most + 3,), jnp.int32),
+        ],
+        [SMEM] * 2 + [VMEM], (*slots_in, tiles), (), [VMEM, SMEM],
+    )
     adjoint_scratch = [pltpu.VMEM((nrhs, half + cells), F32), pltpu.VMEM((nrhs, rows), BF16)]
     low = pltpu.VMEM((nrhs, half + cells), BF16)
     u = right_side
@@ -390,9 +397,12 @@
         packed, = call(
             pack, [shape(half + 128, jnp.int16)], [VMEM] * 2, (keep, swap(send))
         )
+        moved = spread(packed, "z")
+        if step == 0:
+            moved, turned, lists = lax.optimization_barrier((moved, turned, lists))
         v, beta = call(
             functools.partial(cell_vector, step == 0), [shape(half), shape(128)], [VMEM] * 6,
-            (*spread(packed, "z"), *prev),
+            (*moved, *prev),
         )
         other = swap(v)
         owns.append(v)

time: 128 us -> 125 us (0.977)
  waiting for transfers between devices: 52.3 us -> 49.4 us
    ppermute x39, waiting for transfers between devices: 48.5 us -> 44.9 us  [spread(): lax.ppermute(value, axis, [(i, i ^ by) for i in range(n)])]
  transfers between devices with their start and end apart: 48 -> 48, of which waited for: 37 -> 34; matrix products, arithmetic and copies ran while one was open for 0% -> 0% of each run, Pallas kernels for 7% -> 8%
where the time goes in v9:
time: 125 us
  starting transfers between devices  50 us (40%)
  waiting for transfers between devices  49.4 us (40%)
  Pallas kernels  24.6 us (20%)
    ppermute x39, starting transfers between devices, spread(): lax.ppermute(value, axis, [(i, i ^ by) for i in range(n)])  49.2 us
    ppermute x39, waiting for transfers between devices, spread(): lax.ppermute(value, axis, [(i, i ^ by) for i in range(n)])  44.9 us
    pallas_call x31, Pallas kernels, call(): pl.pallas_call(body, out_shape=outs, in_specs=specs, out_specs=out_specs...  24.6 us
    ppermute x9, waiting for transfers between devices, swap(): return lax.ppermute(value, 'core', [(0, 1), (1, 0)])  4.51 us
  transfers between devices with their start and end apart: 48, of which 34 were waited for; matrix products, arithmetic and copies ran while one was open for 0% of the time, Pallas kernels for 8%

profile of v9, /device:TPU:0, one launch (start us, length us, event | category | flops | bytes accessed | tf_op | source)
XLA Modules:
  0.0 125.1 jit_solution(941448872878605630)
XLA Ops:
  0.7 2.7 %shard_map.59 = (f32[8,4224]{1,0:T(8,128)S(1)}, f32[8,4224]{1,0:T(8,128)S(1)}, bf16[8,4,256,256]{3,2,1,0:T(8,128)(2,1)S(1)}) custom-call(s32[4,8]{1,0:T(4,128)} %bitcast.11, s32[1,8]{1,0:T(1,128)} %bitcast.13, f32[8,2048]{1,0:T(8,128)} %prev_ref.3, bf16[8,4,256,256]{3,2,1,0:T(8,128)(2,1)} %source_ref.1), custom_call_target="tpu_custom_call" | custom-call | tf_op jit(solution)/shard_map/pallas_call | solution.py:334
  5.0 4.0 %collective-permute-start.3 = (s16[8,4224]{1,0:T(8,128)(2,1)S(1)}, s16[8,4224]{1,0:T(8,128)(2,1)S(1)}, u32[]{:S(2)}, u32[]{:S(2)}) collective-permute-start(s16[8,4224]{1,0:T(8,128)(2,1)S(1)} %shard_map.60.own_ref), channel_id=1, source_target_pairs={{0,64},{32,96},{64,0},{96,32},{1,65},{33,97},{65,1},{97,33},{2,66}... | collective-permute-start | bytes 202760 | tf_op jit(solution)/shard_map/ppermute | solution.py:358
  10.0 2.6 %shard_map.61 = (bf16[32,256,256]{2,1,0:T(8,128)(2,1)S(1)}, s32[163]{0:T(256)S(1)}) custom-call(s32[4,8]{1,0:T(4,128)S(1)} %bitcast.12, s32[1,8]{1,0:T(1,128)S(1)} %bitcast.14, bf16[32,256,256]{2,1,0:T(8,128)(2,1)S(1)} %bitcast.4), custom_call_target="tpu_custom_call" | custom-call | tf_op jit(solution)/shard_map/pallas_call | solution.py:334
  12.6 1.9 %collective-permute-done.2.right_ref = s16[8,4224]{1,0:T(8,128)(2,1)S(1)} collective-permute-done((s16[8,4224]{1,0:T(8,128)(2,1)S(1)}, s16[8,4224]{1,0:T(8,128)(2,1)S(1)}, u32[]{:S(2)}, u32[]{:S(2)}) %collective-permute-start.2) | collective-permute-done | bytes 67616 | tf_op jit(solution)/shard_map/ppermute | solution.py:358
  17.3 3.1 %collective-permute-start.7 = (s16[8,2176]{1,0:T(8,128)(2,1)S(1)}, s16[8,2176]{1,0:T(8,128)(2,1)S(1)}, u32[]{:S(2)}, u32[]{:S(2)}) collective-permute-start(s16[8,2176]{1,0:T(8,128)(2,1)S(1)} %shard_map.64.own_ref), channel_id=1, source_target_pairs={{0,8},{4,12},{8,0},{12,4},{1,9},{5,13},{9,1},{13,5},{2,10},{6,14},... | collective-permute-start | bytes 104456 | tf_op jit(solution)/shard_map/ppermute | solution.py:358
  22.8 2.7 %collective-permute-done.6.right_ref = s16[8,2176]{1,0:T(8,128)(2,1)S(1)} collective-permute-done((s16[8,2176]{1,0:T(8,128)(2,1)S(1)}, s16[8,2176]{1,0:T(8,128)(2,1)S(1)}, u32[]{:S(2)}, u32[]{:S(2)}) %collective-permute-start.6) | collective-permute-done | bytes 34848 | tf_op jit(solution)/shard_map/ppermute | solution.py:358
  25.8 3.3 %collective-permute-start.10 = (s16[8,2176]{1,0:T(8,128)(2,1)S(1)}, s16[8,2176]{1,0:T(8,128)(2,1)S(1)}, u32[]{:S(2)}, u32[]{:S(2)}) collective-permute-start(s16[8,2176]{1,0:T(8,128)(2,1)S(1)} %shard_map.65.own_ref), channel_id=1, source_target_pairs={{0,2},{1,3},{2,0},{3,1},{4,6},{5,7},{6,4},{7,5},{8,10},{9,11},{10,... | collective-permute-start | bytes 104456 | tf_op jit(solution)/shard_map/ppermute | solution.py:358
  31.4 2.9 %collective-permute-done.9.right_ref = s16[8,2176]{1,0:T(8,128)(2,1)S(1)} collective-permute-done((s16[8,2176]{1,0:T(8,128)(2,1)S(1)}, s16[8,2176]{1,0:T(8,128)(2,1)S(1)}, u32[]{:S(2)}, u32[]{:S(2)}) %collective-permute-start.9) | collective-permute-done | bytes 34848 | tf_op jit(solution)/shard_map/ppermute | solution.py:358
  37.0 2.0 %collective-permute-start.14 = (s16[8,4224]{1,0:T(8,128)(2,1)S(1)}, s16[8,4224]{1,0:T(8,128)(2,1)S(1)}, u32[]{:S(2)}, u32[]{:S(2)}) collective-permute-start(s16[8,4224]{1,0:T(8,128)(2,1)S(1)} %shard_map.68.own_ref), channel_id=1, source_target_pairs={{0,64},{32,96},{64,0},{96,32},{1,65},{33,97},{65,1},{97,33},{2,66}... | collective-permute-start | bytes 202760 | tf_op jit(solution)/shard_map/ppermute | solution.py:358
  40.6 2.3 %collective-permute-done.14.far_ref = s16[8,4224]{1,0:T(8,128)(2,1)S(1)} collective-permute-done((s16[8,4224]{1,0:T(8,128)(2,1)S(1)}, s16[8,4224]{1,0:T(8,128)(2,1)S(1)}, u32[]{:S(2)}, u32[]{:S(2)}) %collective-permute-start.14) | collective-permute-done | bytes 67616 | tf_op jit(solution)/shard_map/ppermute | solution.py:358
  42.9 1.6 %collective-permute-done.13.right_ref = s16[8,4224]{1,0:T(8,128)(2,1)S(1)} collective-permute-done((s16[8,4224]{1,0:T(8,128)(2,1)S(1)}, s16[8,4224]{1,0:T(8,128)(2,1)S(1)}, u32[]{:S(2)}, u32[]{:S(2)}) %collective-permute-start.13) | collective-permute-done | bytes 67616 | tf_op jit(solution)/shard_map/ppermute | solution.py:358
  47.3 1.5 %collective-permute-start.18 = (s16[8,2176]{1,0:T(8,128)(2,1)S(1)}, s16[8,2176]{1,0:T(8,128)(2,1)S(1)}, u32[]{:S(2)}, u32[]{:S(2)}) collective-permute-start(s16[8,2176]{1,0:T(8,128)(2,1)S(1)} %shard_map.71.own_ref), channel_id=1, source_target_pairs={{0,8},{4,12},{8,0},{12,4},{1,9},{5,13},{9,1},{13,5},{2,10},{6,14},... | collective-permute-start | bytes 104456 | tf_op jit(solution)/shard_map/ppermute | solution.py:358
  50.9 2.0 %collective-permute-done.18.far_ref = s16[8,2176]{1,0:T(8,128)(2,1)S(1)} collective-permute-done((s16[8,2176]{1,0:T(8,128)(2,1)S(1)}, s16[8,2176]{1,0:T(8,128)(2,1)S(1)}, u32[]{:S(2)}, u32[]{:S(2)}) %collective-permute-start.18) | collective-permute-done | bytes 34848 | tf_op jit(solution)/shard_map/ppermute | solution.py:358
  54.3 1.6 %collective-permute-start.21 = (s16[8,2176]{1,0:T(8,128)(2,1)S(1)}, s16[8,2176]{1,0:T(8,128)(2,1)S(1)}, u32[]{:S(2)}, u32[]{:S(2)}) collective-permute-start(s16[8,2176]{1,0:T(8,128)(2,1)S(1)} %shard_map.72.own_ref), channel_id=1, source_target_pairs={{0,2},{1,3},{2,0},{3,1},{4,6},{5,7},{6,4},{7,5},{8,10},{9,11},{10,... | collective-permute-start | bytes 104456 | tf_op jit(solution)/shard_map/ppermute | solution.py:358
  57.8 2.1 %collective-permute-done.21.far_ref = s16[8,2176]{1,0:T(8,128)(2,1)S(1)} collective-permute-done((s16[8,2176]{1,0:T(8,128)(2,1)S(1)}, s16[8,2176]{1,0:T(8,128)(2,1)S(1)}, u32[]{:S(2)}, u32[]{:S(2)}) %collective-permute-start.21) | collective-permute-done | bytes 34848 | tf_op jit(solution)/shard_map/ppermute | solution.py:358
  63.8 1.9 %collective-permute-start.25 = (s16[8,4224]{1,0:T(8,128)(2,1)S(1)}, s16[8,4224]{1,0:T(8,128)(2,1)S(1)}, u32[]{:S(2)}, u32[]{:S(2)}) collective-permute-start(s16[8,4224]{1,0:T(8,128)(2,1)S(1)} %shard_map.75.own_ref), channel_id=1, source_target_pairs={{0,64},{32,96},{64,0},{96,32},{1,65},{33,97},{65,1},{97,33},{2,66}... | collective-permute-start | bytes 202760 | tf_op jit(solution)/shard_map/ppermute | solution.py:358
  67.4 2.3 %collective-permute-done.25.far_ref = s16[8,4224]{1,0:T(8,128)(2,1)S(1)} collective-permute-done((s16[8,4224]{1,0:T(8,128)(2,1)S(1)}, s16[8,4224]{1,0:T(8,128)(2,1)S(1)}, u32[]{:S(2)}, u32[]{:S(2)}) %collective-permute-start.25) | collective-permute-done | bytes 67616 | tf_op jit(solution)/shard_map/ppermute | solution.py:358
  74.0 2.3 %collective-permute-start.29 = (s16[8,2176]{1,0:T(8,128)(2,1)S(1)}, s16[8,2176]{1,0:T(8,128)(2,1)S(1)}, u32[]{:S(2)}, u32[]{:S(2)}) collective-permute-start(s16[8,2176]{1,0:T(8,128)(2,1)S(1)} %shard_map.78.own_ref), channel_id=1, source_target_pairs={{0,8},{4,12},{8,0},{12,4},{1,9},{5,13},{9,1},{13,5},{2,10},{6,14},... | collective-permute-start | bytes 104456 | tf_op jit(solution)/shard_map/ppermute | solution.py:358
  77.6 2.0 %collective-permute-done.29.far_ref = s16[8,2176]{1,0:T(8,128)(2,1)S(1)} collective-permute-done((s16[8,2176]{1,0:T(8,128)(2,1)S(1)}, s16[8,2176]{1,0:T(8,128)(2,1)S(1)}, u32[]{:S(2)}, u32[]{:S(2)}) %collective-permute-start.29) | collective-permute-done | bytes 34848 | tf_op jit(solution)/shard_map/ppermute | solution.py:358
  79.5 2.0 %collective-permute-done.28.right_ref = s16[8,2176]{1,0:T(8,128)(2,1)S(1)} collective-permute-done((s16[8,2176]{1,0:T(8,128)(2,1)S(1)}, s16[8,2176]{1,0:T(8,128)(2,1)S(1)}, u32[]{:S(2)}, u32[]{:S(2)}) %collective-permute-start.28) | collective-permute-done | bytes 34848 | tf_op jit(solution)/shard_map/ppermute | solution.py:358
  81.8 2.3 %collective-permute-start.32 = (s16[8,2176]{1,0:T(8,128)(2,1)S(1)}, s16[8,2176]{1,0:T(8,128)(2,1)S(1)}, u32[]{:S(2)}, u32[]{:S(2)}) collective-permute-start(s16[8,2176]{1,0:T(8,128)(2,1)S(1)} %shard_map.79.own_ref), channel_id=1, source_target_pairs={{0,2},{1,3},{2,0},{3,1},{4,6},{5,7},{6,4},{7,5},{8,10},{9,11},{10,... | collective-permute-start | bytes 104456 | tf_op jit(solution)/shard_map/ppermute | solution.py:358
  85.4 2.0 %collective-permute-done.32.far_ref = s16[8,2176]{1,0:T(8,128)(2,1)S(1)} collective-permute-done((s16[8,2176]{1,0:T(8,128)(2,1)S(1)}, s16[8,2176]{1,0:T(8,128)(2,1)S(1)}, u32[]{:S(2)}, u32[]{:S(2)}) %collective-permute-start.32) | collective-permute-done | bytes 34848 | tf_op jit(solution)/shard_map/ppermute | solution.py:358
  87.3 1.9 %collective-permute-done.31.right_ref = s16[8,2176]{1,0:T(8,128)(2,1)S(1)} collective-permute-done((s16[8,2176]{1,0:T(8,128)(2,1)S(1)}, s16[8,2176]{1,0:T(8,128)(2,1)S(1)}, u32[]{:S(2)}, u32[]{:S(2)}) %collective-permute-start.31) | collective-permute-done | bytes 34848 | tf_op jit(solution)/shard_map/ppermute | solution.py:358
  92.0 2.0 %collective-permute-start.36 = (s16[8,4224]{1,0:T(8,128)(2,1)S(1)}, s16[8,4224]{1,0:T(8,128)(2,1)S(1)}, u32[]{:S(2)}, u32[]{:S(2)}) collective-permute-start(s16[8,4224]{1,0:T(8,128)(2,1)S(1)} %shard_map.82.own_ref), channel_id=1, source_target_pairs={{0,64},{32,96},{64,0},{96,32},{1,65},{33,97},{65,1},{97,33},{2,66}... | collective-permute-start | bytes 202760 | tf_op jit(solution)/shard_map/ppermute | solution.py:358
  95.6 2.3 %collective-permute-done.36.far_ref = s16[8,4224]{1,0:T(8,128)(2,1)S(1)} collective-permute-done((s16[8,4224]{1,0:T(8,128)(2,1)S(1)}, s16[8,4224]{1,0:T(8,128)(2,1)S(1)}, u32[]{:S(2)}, u32[]{:S(2)}) %collective-permute-start.36) | collective-permute-done | bytes 67616 | tf_op jit(solution)/shard_map/ppermute | solution.py:358
  97.9 1.6 %collective-permute-done.35.right_ref = s16[8,4224]{1,0:T(8,128)(2,1)S(1)} collective-permute-done((s16[8,4224]{1,0:T(8,128)(2,1)S(1)}, s16[8,4224]{1,0:T(8,128)(2,1)S(1)}, u32[]{:S(2)}, u32[]{:S(2)}) %collective-permute-start.35) | collective-permute-done | bytes 67616 | tf_op jit(solution)/shard_map/ppermute | solution.py:358
  102.3 1.5 %collective-permute-start.40 = (s16[8,2176]{1,0:T(8,128)(2,1)S(1)}, s16[8,2176]{1,0:T(8,128)(2,1)S(1)}, u32[]{:S(2)}, u32[]{:S(2)}) collective-permute-start(s16[8,2176]{1,0:T(8,128)(2,1)S(1)} %shard_map.85.own_ref), channel_id=1, source_target_pairs={{0,8},{4,12},{8,0},{12,4},{1,9},{5,13},{9,1},{13,5},{2,10},{6,14},... | collective-permute-start | bytes 104456 | tf_op jit(solution)/shard_map/ppermute | solution.py:358
  105.8 2.0 %collective-permute-done.40.far_ref = s16[8,2176]{1,0:T(8,128)(2,1)S(1)} collective-permute-done((s16[8,2176]{1,0:T(8,128)(2,1)S(1)}, s16[8,2176]{1,0:T(8,128)(2,1)S(1)}, u32[]{:S(2)}, u32[]{:S(2)}) %collective-permute-start.40) | collective-permute-done | bytes 34848 | tf_op jit(solution)/shard_map/ppermute | solution.py:358
  109.3 1.6 %collective-permute-start.43 = (s16[8,2176]{1,0:T(8,128)(2,1)S(1)}, s16[8,2176]{1,0:T(8,128)(2,1)S(1)}, u32[]{:S(2)}, u32[]{:S(2)}) collective-permute-start(s16[8,2176]{1,0:T(8,128)(2,1)S(1)} %shard_map.86.own_ref), channel_id=1, source_target_pairs={{0,2},{1,3},{2,0},{3,1},{4,6},{5,7},{6,4},{7,5},{8,10},{9,11},{10,... | collective-permute-start | bytes 104456 | tf_op jit(solution)/shard_map/ppermute | solution.py:358
  112.8 2.1 %collective-permute-done.43.far_ref = s16[8,2176]{1,0:T(8,128)(2,1)S(1)} collective-permute-done((s16[8,2176]{1,0:T(8,128)(2,1)S(1)}, s16[8,2176]{1,0:T(8,128)(2,1)S(1)}, u32[]{:S(2)}, u32[]{:S(2)}) %collective-permute-start.43) | collective-permute-done | bytes 34848 | tf_op jit(solution)/shard_map/ppermute | solution.py:358
  117.5 1.8 %collective-permute-start.47 = (f32[8,128]{1,0:T(8,128)S(1)}, f32[8,128]{1,0:T(8,128)S(1)}, u32[]{:S(2)}, u32[]{:S(2)}) collective-permute-start(f32[8,128]{1,0:T(8,128)S(1)} %add.3.own_ref), channel_id=1, source_target_pairs={{0,64},{32,96},{64,0},{96,32},{1,65},{33,97},{65,1},{97,33},{2,66}... | collective-permute-start | bytes 12296 | tf_op jit(solution)/shard_map/ppermute | solution.py:358
  122.6 1.5 %collective-permute-done.46.right_ref = f32[8,128]{1,0:T(8,128)S(1)} collective-permute-done((f32[8,128]{1,0:T(8,128)S(1)}, f32[8,128]{1,0:T(8,128)S(1)}, u32[]{:S(2)}, u32[]{:S(2)}) %collective-permute-start.46) | collective-permute-done | bytes 4128 | tf_op jit(solution)/shard_map/ppermute | solution.py:358
  (102 shorter events, 54.7 us)
Async XLA Ops:
  5.0 7.7 %collective-permute-start.3 = (s16[8,4224]{1,0:T(8,128)(2,1)S(1)}, s16[8,4224]{1,0:T(8,128)(2,1)S(1)}, u32[]{:S(2)}, u32[]{:S(2)}) collective-permute-start(s16[8,4224]{1,0:T(8,128)(2,1)S(1)} %shard_map.60.own_ref), channel_id=1, source_target_pairs={{0,64},{32,96},{64,0},{96,32},{1,65},{33,97},{65,1},{97,33},{2,66}... | collective-permute-start | bytes 202760 | tf_op jit(solution)/shard_map/ppermute | solution.py:358
  9.0 5.5 %collective-permute-start.2 = (s16[8,4224]{1,0:T(8,128)(2,1)S(1)}, s16[8,4224]{1,0:T(8,128)(2,1)S(1)}, u32[]{:S(2)}, u32[]{:S(2)}) collective-permute-start(s16[8,4224]{1,0:T(8,128)(2,1)S(1)} %shard_map.60.own_ref), channel_id=1, source_target_pairs={{0,96},{32,64},{64,32},{96,0},{1,97},{33,65},{65,33},{97,1},{2,98}... | collective-permute-start | bytes 202760 | tf_op jit(solution)/shard_map/ppermute | solution.py:358
  9.7 4.8 %collective-permute-start.1 = (s16[8,4224]{1,0:T(8,128)(2,1)S(1)}, s16[8,4224]{1,0:T(8,128)(2,1)S(1)}, u32[]{:S(2)}, u32[]{:S(2)}) collective-permute-start(s16[8,4224]{1,0:T(8,128)(2,1)S(1)} %shard_map.60.own_ref), channel_id=1, source_target_pairs={{0,32},{32,0},{64,96},{96,64},{1,33},{33,1},{65,97},{97,65},{2,34}... | collective-permute-start | bytes 202760 | tf_op jit(solution)/shard_map/ppermute | solution.py:358
  17.3 5.5 %collective-permute-start.7 = (s16[8,2176]{1,0:T(8,128)(2,1)S(1)}, s16[8,2176]{1,0:T(8,128)(2,1)S(1)}, u32[]{:S(2)}, u32[]{:S(2)}) collective-permute-start(s16[8,2176]{1,0:T(8,128)(2,1)S(1)} %shard_map.64.own_ref), channel_id=1, source_target_pairs={{0,8},{4,12},{8,0},{12,4},{1,9},{5,13},{9,1},{13,5},{2,10},{6,14},... | collective-permute-start | bytes 104456 | tf_op jit(solution)/shard_map/ppermute | solution.py:358
  20.4 5.1 %collective-permute-start.6 = (s16[8,2176]{1,0:T(8,128)(2,1)S(1)}, s16[8,2176]{1,0:T(8,128)(2,1)S(1)}, u32[]{:S(2)}, u32[]{:S(2)}) collective-permute-start(s16[8,2176]{1,0:T(8,128)(2,1)S(1)} %shard_map.64.own_ref), channel_id=1, source_target_pairs={{0,12},{4,8},{8,4},{12,0},{1,13},{5,9},{9,5},{13,1},{2,14},{6,10},... | collective-permute-start | bytes 104456 | tf_op jit(solution)/shard_map/ppermute | solution.py:358
  25.8 5.5 %collective-permute-start.10 = (s16[8,2176]{1,0:T(8,128)(2,1)S(1)}, s16[8,2176]{1,0:T(8,128)(2,1)S(1)}, u32[]{:S(2)}, u32[]{:S(2)}) collective-permute-start(s16[8,2176]{1,0:T(8,128)(2,1)S(1)} %shard_map.65.own_ref), channel_id=1, source_target_pairs={{0,2},{1,3},{2,0},{3,1},{4,6},{5,7},{6,4},{7,5},{8,10},{9,11},{10,... | collective-permute-start | bytes 104456 | tf_op jit(solution)/shard_map/ppermute | solution.py:358
  29.1 5.1 %collective-permute-start.9 = (s16[8,2176]{1,0:T(8,128)(2,1)S(1)}, s16[8,2176]{1,0:T(8,128)(2,1)S(1)}, u32[]{:S(2)}, u32[]{:S(2)}) collective-permute-start(s16[8,2176]{1,0:T(8,128)(2,1)S(1)} %shard_map.65.own_ref), channel_id=1, source_target_pairs={{0,3},{1,2},{2,1},{3,0},{4,7},{5,6},{6,5},{7,4},{8,11},{9,10},{10,... | collective-permute-start | bytes 104456 | tf_op jit(solution)/shard_map/ppermute | solution.py:358
  30.2 4.1 %collective-permute-start.8 = (s16[8,2176]{1,0:T(8,128)(2,1)S(1)}, s16[8,2176]{1,0:T(8,128)(2,1)S(1)}, u32[]{:S(2)}, u32[]{:S(2)}) collective-permute-start(s16[8,2176]{1,0:T(8,128)(2,1)S(1)} %shard_map.65.own_ref), channel_id=1, source_target_pairs={{0,1},{1,0},{2,3},{3,2},{4,5},{5,4},{6,7},{7,6},{8,9},{9,8},{10,11... | collective-permute-start | bytes 104456 | tf_op jit(solution)/shard_map/ppermute | solution.py:358
  37.0 5.9 %collective-permute-start.14 = (s16[8,4224]{1,0:T(8,128)(2,1)S(1)}, s16[8,4224]{1,0:T(8,128)(2,1)S(1)}, u32[]{:S(2)}, u32[]{:S(2)}) collective-permute-start(s16[8,4224]{1,0:T(8,128)(2,1)S(1)} %shard_map.68.own_ref), channel_id=1, source_target_pairs={{0,64},{32,96},{64,0},{96,32},{1,65},{33,97},{65,1},{97,33},{2,66}... | collective-permute-start | bytes 202760 | tf_op jit(solution)/shard_map/ppermute | solution.py:358
  39.0 5.5 %collective-permute-start.13 = (s16[8,4224]{1,0:T(8,128)(2,1)S(1)}, s16[8,4224]{1,0:T(8,128)(2,1)S(1)}, u32[]{:S(2)}, u32[]{:S(2)}) collective-permute-start(s16[8,4224]{1,0:T(8,128)(2,1)S(1)} %shard_map.68.own_ref), channel_id=1, source_target_pairs={{0,96},{32,64},{64,32},{96,0},{1,97},{33,65},{65,33},{97,1},{2,98}... | collective-permute-start | bytes 202760 | tf_op jit(solution)/shard_map/ppermute | solution.py:358
  39.9 4.6 %collective-permute-start.12 = (s16[8,4224]{1,0:T(8,128)(2,1)S(1)}, s16[8,4224]{1,0:T(8,128)(2,1)S(1)}, u32[]{:S(2)}, u32[]{:S(2)}) collective-permute-start(s16[8,4224]{1,0:T(8,128)(2,1)S(1)} %shard_map.68.own_ref), channel_id=1, source_target_pairs={{0,32},{32,0},{64,96},{96,64},{1,33},{33,1},{65,97},{97,65},{2,34}... | collective-permute-start | bytes 202760 | tf_op jit(solution)/shard_map/ppermute | solution.py:358
  47.3 5.5 %collective-permute-start.18 = (s16[8,2176]{1,0:T(8,128)(2,1)S(1)}, s16[8,2176]{1,0:T(8,128)(2,1)S(1)}, u32[]{:S(2)}, u32[]{:S(2)}) collective-permute-start(s16[8,2176]{1,0:T(8,128)(2,1)S(1)} %shard_map.71.own_ref), channel_id=1, source_target_pairs={{0,8},{4,12},{8,0},{12,4},{1,9},{5,13},{9,1},{13,5},{2,10},{6,14},... | collective-permute-start | bytes 104456 | tf_op jit(solution)/shard_map/ppermute | solution.py:358
  48.8 5.1 %collective-permute-start.17 = (s16[8,2176]{1,0:T(8,128)(2,1)S(1)}, s16[8,2176]{1,0:T(8,128)(2,1)S(1)}, u32[]{:S(2)}, u32[]{:S(2)}) collective-permute-start(s16[8,2176]{1,0:T(8,128)(2,1)S(1)} %shard_map.71.own_ref), channel_id=1, source_target_pairs={{0,12},{4,8},{8,4},{12,0},{1,13},{5,9},{9,5},{13,1},{2,14},{6,10},... | collective-permute-start | bytes 104456 | tf_op jit(solution)/shard_map/ppermute | solution.py:358
  54.3 5.7 %collective-permute-start.21 = (s16[8,2176]{1,0:T(8,128)(2,1)S(1)}, s16[8,2176]{1,0:T(8,128)(2,1)S(1)}, u32[]{:S(2)}, u32[]{:S(2)}) collective-permute-start(s16[8,2176]{1,0:T(8,128)(2,1)S(1)} %shard_map.72.own_ref), channel_id=1, source_target_pairs={{0,2},{1,3},{2,0},{3,1},{4,6},{5,7},{6,4},{7,5},{8,10},{9,11},{10,... | collective-permute-start | bytes 104456 | tf_op jit(solution)/shard_map/ppermute | solution.py:358
  55.9 5.1 %collective-permute-start.20 = (s16[8,2176]{1,0:T(8,128)(2,1)S(1)}, s16[8,2176]{1,0:T(8,128)(2,1)S(1)}, u32[]{:S(2)}, u32[]{:S(2)}) collective-permute-start(s16[8,2176]{1,0:T(8,128)(2,1)S(1)} %shard_map.72.own_ref), channel_id=1, source_target_pairs={{0,3},{1,2},{2,1},{3,0},{4,7},{5,6},{6,5},{7,4},{8,11},{9,10},{10,... | collective-permute-start | bytes 104456 | tf_op jit(solution)/shard_map/ppermute | solution.py:358
  56.9 4.2 %collective-permute-start.19 = (s16[8,2176]{1,0:T(8,128)(2,1)S(1)}, s16[8,2176]{1,0:T(8,128)(2,1)S(1)}, u32[]{:S(2)}, u32[]{:S(2)}) collective-permute-start(s16[8,2176]{1,0:T(8,128)(2,1)S(1)} %shard_map.72.own_ref), channel_id=1, source_target_pairs={{0,1},{1,0},{2,3},{3,2},{4,5},{5,4},{6,7},{7,6},{8,9},{9,8},{10,11... | collective-permute-start | bytes 104456 | tf_op jit(solution)/shard_map/ppermute | solution.py:358
  63.8 5.9 %collective-permute-start.25 = (s16[8,4224]{1,0:T(8,128)(2,1)S(1)}, s16[8,4224]{1,0:T(8,128)(2,1)S(1)}, u32[]{:S(2)}, u32[]{:S(2)}) collective-permute-start(s16[8,4224]{1,0:T(8,128)(2,1)S(1)} %shard_map.75.own_ref), channel_id=1, source_target_pairs={{0,64},{32,96},{64,0},{96,32},{1,65},{33,97},{65,1},{97,33},{2,66}... | collective-permute-start | bytes 202760 | tf_op jit(solution)/shard_map/ppermute | solution.py:358
  65.7 5.5 %collective-permute-start.24 = (s16[8,4224]{1,0:T(8,128)(2,1)S(1)}, s16[8,4224]{1,0:T(8,128)(2,1)S(1)}, u32[]{:S(2)}, u32[]{:S(2)}) collective-permute-start(s16[8,4224]{1,0:T(8,128)(2,1)S(1)} %shard_map.75.own_ref), channel_id=1, source_target_pairs={{0,96},{32,64},{64,32},{96,0},{1,97},{33,65},{65,33},{97,1},{2,98}... | collective-permute-start | bytes 202760 | tf_op jit(solution)/shard_map/ppermute | solution.py:358
  66.9 4.3 %collective-permute-start.23 = (s16[8,4224]{1,0:T(8,128)(2,1)S(1)}, s16[8,4224]{1,0:T(8,128)(2,1)S(1)}, u32[]{:S(2)}, u32[]{:S(2)}) collective-permute-start(s16[8,4224]{1,0:T(8,128)(2,1)S(1)} %shard_map.75.own_ref), channel_id=1, source_target_pairs={{0,32},{32,0},{64,96},{96,64},{1,33},{33,1},{65,97},{97,65},{2,34}... | collective-permute-start | bytes 202760 | tf_op jit(solution)/shard_map/ppermute | solution.py:358
  74.0 5.5 %collective-permute-start.29 = (s16[8,2176]{1,0:T(8,128)(2,1)S(1)}, s16[8,2176]{1,0:T(8,128)(2,1)S(1)}, u32[]{:S(2)}, u32[]{:S(2)}) collective-permute-start(s16[8,2176]{1,0:T(8,128)(2,1)S(1)} %shard_map.78.own_ref), channel_id=1, source_target_pairs={{0,8},{4,12},{8,0},{12,4},{1,9},{5,13},{9,1},{13,5},{2,10},{6,14},... | collective-permute-start | bytes 104456 | tf_op jit(solution)/shard_map/ppermute | solution.py:358
  76.4 5.1 %collective-permute-start.28 = (s16[8,2176]{1,0:T(8,128)(2,1)S(1)}, s16[8,2176]{1,0:T(8,128)(2,1)S(1)}, u32[]{:S(2)}, u32[]{:S(2)}) collective-permute-start(s16[8,2176]{1,0:T(8,128)(2,1)S(1)} %shard_map.78.own_ref), channel_id=1, source_target_pairs={{0,12},{4,8},{8,4},{12,0},{1,13},{5,9},{9,5},{13,1},{2,14},{6,10},... | collective-permute-start | bytes 104456 | tf_op jit(solution)/shard_map/ppermute | solution.py:358
  81.8 5.5 %collective-permute-start.32 = (s16[8,2176]{1,0:T(8,128)(2,1)S(1)}, s16[8,2176]{1,0:T(8,128)(2,1)S(1)}, u32[]{:S(2)}, u32[]{:S(2)}) collective-permute-start(s16[8,2176]{1,0:T(8,128)(2,1)S(1)} %shard_map.79.own_ref), channel_id=1, source_target_pairs={{0,2},{1,3},{2,0},{3,1},{4,6},{5,7},{6,4},{7,5},{8,10},{9,11},{10,... | collective-permute-start | bytes 104456 | tf_op jit(solution)/shard_map/ppermute | solution.py:358
  84.1 5.1 %collective-permute-start.31 = (s16[8,2176]{1,0:T(8,128)(2,1)S(1)}, s16[8,2176]{1,0:T(8,128)(2,1)S(1)}, u32[]{:S(2)}, u32[]{:S(2)}) collective-permute-start(s16[8,2176]{1,0:T(8,128)(2,1)S(1)} %shard_map.79.own_ref), channel_id=1, source_target_pairs={{0,3},{1,2},{2,1},{3,0},{4,7},{5,6},{6,5},{7,4},{8,11},{9,10},{10,... | collective-permute-start | bytes 104456 | tf_op jit(solution)/shard_map/ppermute | solution.py:358
  92.0 5.9 %collective-permute-start.36 = (s16[8,4224]{1,0:T(8,128)(2,1)S(1)}, s16[8,4224]{1,0:T(8,128)(2,1)S(1)}, u32[]{:S(2)}, u32[]{:S(2)}) collective-permute-start(s16[8,4224]{1,0:T(8,128)(2,1)S(1)} %shard_map.82.own_ref), channel_id=1, source_target_pairs={{0,64},{32,96},{64,0},{96,32},{1,65},{33,97},{65,1},{97,33},{2,66}... | collective-permute-start | bytes 202760 | tf_op jit(solution)/shard_map/ppermute | solution.py:358
  94.0 5.5 %collective-permute-start.35 = (s16[8,4224]{1,0:T(8,128)(2,1)S(1)}, s16[8,4224]{1,0:T(8,128)(2,1)S(1)}, u32[]{:S(2)}, u32[]{:S(2)}) collective-permute-start(s16[8,4224]{1,0:T(8,128)(2,1)S(1)} %shard_map.82.own_ref), channel_id=1, source_target_pairs={{0,96},{32,64},{64,32},{96,0},{1,97},{33,65},{65,33},{97,1},{2,98}... | collective-permute-start | bytes 202760 | tf_op jit(solution)/shard_map/ppermute | solution.py:358
  95.2 4.3 %collective-permute-start.34 = (s16[8,4224]{1,0:T(8,128)(2,1)S(1)}, s16[8,4224]{1,0:T(8,128)(2,1)S(1)}, u32[]{:S(2)}, u32[]{:S(2)}) collective-permute-start(s16[8,4224]{1,0:T(8,128)(2,1)S(1)} %shard_map.82.own_ref), channel_id=1, source_target_pairs={{0,32},{32,0},{64,96},{96,64},{1,33},{33,1},{65,97},{97,65},{2,34}... | collective-permute-start | bytes 202760 | tf_op jit(solution)/shard_map/ppermute | solution.py:358
  102.3 5.5 %collective-permute-start.40 = (s16[8,2176]{1,0:T(8,128)(2,1)S(1)}, s16[8,2176]{1,0:T(8,128)(2,1)S(1)}, u32[]{:S(2)}, u32[]{:S(2)}) collective-permute-start(s16[8,2176]{1,0:T(8,128)(2,1)S(1)} %shard_map.85.own_ref), channel_id=1, source_target_pairs={{0,8},{4,12},{8,0},{12,4},{1,9},{5,13},{9,1},{13,5},{2,10},{6,14},... | collective-permute-start | bytes 104456 | tf_op jit(solution)/shard_map/ppermute | solution.py:358
  103.8 5.1 %collective-permute-start.39 = (s16[8,2176]{1,0:T(8,128)(2,1)S(1)}, s16[8,2176]{1,0:T(8,128)(2,1)S(1)}, u32[]{:S(2)}, u32[]{:S(2)}) collective-permute-start(s16[8,2176]{1,0:T(8,128)(2,1)S(1)} %shard_map.85.own_ref), channel_id=1, source_target_pairs={{0,12},{4,8},{8,4},{12,0},{1,13},{5,9},{9,5},{13,1},{2,14},{6,10},... | collective-permute-start | bytes 104456 | tf_op jit(solution)/shard_map/ppermute | solution.py:358
  109.3 5.7 %collective-permute-start.43 = (s16[8,2176]{1,0:T(8,128)(2,1)S(1)}, s16[8,2176]{1,0:T(8,128)(2,1)S(1)}, u32[]{:S(2)}, u32[]{:S(2)}) collective-permute-start(s16[8,2176]{1,0:T(8,128)(2,1)S(1)} %shard_map.86.own_ref), channel_id=1, source_target_pairs={{0,2},{1,3},{2,0},{3,1},{4,6},{5,7},{6,4},{7,5},{8,10},{9,11},{10,... | collective-permute-start | bytes 104456 | tf_op jit(solution)/shard_map/ppermute | solution.py:358
  110.9 5.1 %collective-permute-start.42 = (s16[8,2176]{1,0:T(8,128)(2,1)S(1)}, s16[8,2176]{1,0:T(8,128)(2,1)S(1)}, u32[]{:S(2)}, u32[]{:S(2)}) collective-permute-start(s16[8,2176]{1,0:T(8,128)(2,1)S(1)} %shard_map.86.own_ref), channel_id=1, source_target_pairs={{0,3},{1,2},{2,1},{3,0},{4,7},{5,6},{6,5},{7,4},{8,11},{9,10},{10,... | collective-permute-start | bytes 104456 | tf_op jit(solution)/shard_map/ppermute | solution.py:358
  117.5 5.1 %collective-permute-start.47 = (f32[8,128]{1,0:T(8,128)S(1)}, f32[8,128]{1,0:T(8,128)S(1)}, u32[]{:S(2)}, u32[]{:S(2)}) collective-permute-start(f32[8,128]{1,0:T(8,128)S(1)} %add.3.own_ref), channel_id=1, source_target_pairs={{0,64},{32,96},{64,0},{96,32},{1,65},{33,97},{65,1},{97,33},{2,66}... | collective-permute-start | bytes 12296 | tf_op jit(solution)/shard_map/ppermute | solution.py:358
  119.3 4.8 %collective-permute-start.46 = (f32[8,128]{1,0:T(8,128)S(1)}, f32[8,128]{1,0:T(8,128)S(1)}, u32[]{:S(2)}, u32[]{:S(2)}) collective-permute-start(f32[8,128]{1,0:T(8,128)S(1)} %add.3.own_ref), channel_id=1, source_target_pairs={{0,96},{32,64},{64,32},{96,0},{1,97},{33,65},{65,33},{97,1},{2,98}... | collective-permute-start | bytes 12296 | tf_op jit(solution)/shard_map/ppermute | solution.py:358
  (19 other events, 72.7 us)

commit v10 on v9

--- a/solution.py
+++ b/solution.py
@@ -33,6 +33,16 @@
         piece = x[:, at : at + width]
         total = piece * piece if total is None else total + piece * piece
     return total
+
+
+def two_parts(x):
+    return jnp.concatenate([x, x - x.astype(BF16).astype(F32)], axis=0).astype(BF16)
+
+
+def product(rows, tile):
+    both = jnp.dot(rows, tile, preferred_element_type=F32)
+    half = both.shape[0] // 2
+    return both[:half] + both[half:]
 
 
 def wide(x):
@@ -98,11 +108,11 @@
     rays = tiles_ref.shape[1]
     half = out_ref.shape[1] - 128
     acc_ref[...] = jnp.zeros_like(acc_ref)
-    low_ref[...] = u.astype(BF16)
+    low_ref[...] = two_parts(u)
 
     def one(tile, block):
         rows = low_ref[:, pl.ds(pl.multiple_of(tile // slots * rays, rays), rays)]
-        part = jnp.dot(rows, tiles_ref[tile], preferred_element_type=F32)
+        part = product(rows, tiles_ref[tile])
         acc_ref[:, pl.ds(pl.multiple_of(block * cells, cells), cells)] += part
 
     listed_products(lists_ref, mine, tiles_ref, one)
@@ -113,12 +123,12 @@
 def half_forward(lists_ref, mine, v, tiles_ref, sum_ref, low_ref, slots):
     cells, rays = tiles_ref.shape[1:]
     half = v.shape[1]
-    low_ref[:, :half] = v.astype(BF16)
-    low_ref[:, half:] = jnp.zeros((v.shape[0], cells), BF16)
+    low_ref[:, :half] = two_parts(v)
+    low_ref[:, half:] = jnp.zeros((low_ref.shape[0], cells), BF16)
 
     def one(tile, block):
         rows = low_ref[:, pl.ds(pl.multiple_of(block * cells, cells), cells)]
-        part = jnp.dot(rows, tiles_ref[tile], preferred_element_type=F32)
+        part = product(rows, tiles_ref[tile])
         sum_ref[:, pl.ds(pl.multiple_of(tile // slots * rays, rays), rays)] += part
 
     listed_products(lists_ref, mine, tiles_ref, one)
@@ -128,13 +138,13 @@
     bundles, slots, rays, cells = tiles_ref.shape
     half = keep_ref.shape[1] - 128
     acc_ref[...] = jnp.zeros_like(acc_ref)
-    low = u.astype(BF16)
+    low = two_parts(u)
     for b in range(bundles):
         if copies:
             copies[b].wait()
         rows = low[:, b * rays : (b + 1) * rays]
         for s in range(slots):
-            part = jnp.dot(rows, tiles_ref[b, s], preferred_element_type=F32)
+            part = product(rows, tiles_ref[b, s])
             at = pl.multiple_of(block_of(b, s) * cells, cells)
             acc_ref[:, pl.ds(at, cells)] += part
     squares = fold_sq(u, 128)
@@ -388,8 +398,8 @@
         ],
         [SMEM] * 2 + [VMEM], (*slots_in, tiles), (), [VMEM, SMEM],
     )
-    adjoint_scratch = [pltpu.VMEM((nrhs, half + cells), F32), pltpu.VMEM((nrhs, rows), BF16)]
-    low = pltpu.VMEM((nrhs, half + cells), BF16)
+    adjoint_scratch = [pltpu.VMEM((nrhs, half + cells), F32), pltpu.VMEM((2 * nrhs, rows), BF16)]
+    low = pltpu.VMEM((2 * nrhs, half + cells), BF16)
     u = right_side
     owns, others, alphas, betas = [], [], [], []
     for step in range(ITERS):

time: 125 us -> 125 us (level)
  no operation moved by 1% of the time
where the time goes in v10:
time: 125 us
  starting transfers between devices  50 us (40%)
  waiting for transfers between devices  49.4 us (40%)
  Pallas kernels  24.7 us (20%)
    ppermute x39, starting transfers between devices, spread(): lax.ppermute(value, axis, [(i, i ^ by) for i in range(n)])  49.2 us
    ppermute x39, waiting for transfers between devices, spread(): lax.ppermute(value, axis, [(i, i ^ by) for i in range(n)])  44.9 us
    pallas_call x31, Pallas kernels, call(): pl.pallas_call(body, out_shape=outs, in_specs=specs, out_specs=out_specs...  24.7 us
    ppermute x9, waiting for transfers between devices, swap(): return lax.ppermute(value, 'core', [(0, 1), (1, 0)])  4.5 us
  transfers between devices with their start and end apart: 48, of which 34 were waited for; matrix products, arithmetic and copies ran while one was open for 0% of the time, Pallas kernels for 8%

profile of v10, /device:TPU:0, one launch (start us, length us, event | category | flops | bytes accessed | tf_op | source)
XLA Modules:
  0.0 125.1 jit_solution(12205968523736013669)
XLA Ops:
  0.7 2.7 %shard_map.59 = (f32[8,4224]{1,0:T(8,128)S(1)}, f32[8,4224]{1,0:T(8,128)S(1)}, bf16[8,4,256,256]{3,2,1,0:T(8,128)(2,1)S(1)}) custom-call(s32[4,8]{1,0:T(4,128)} %bitcast.11, s32[1,8]{1,0:T(1,128)} %bitcast.13, f32[8,2048]{1,0:T(8,128)} %prev_ref.3, bf16[8,4,256,256]{3,2,1,0:T(8,128)(2,1)} %source_ref.1), custom_call_target="tpu_custom_call" | custom-call | tf_op jit(solution)/shard_map/pallas_call | solution.py:344
  5.0 4.0 %collective-permute-start.3 = (s16[8,4224]{1,0:T(8,128)(2,1)S(1)}, s16[8,4224]{1,0:T(8,128)(2,1)S(1)}, u32[]{:S(2)}, u32[]{:S(2)}) collective-permute-start(s16[8,4224]{1,0:T(8,128)(2,1)S(1)} %shard_map.60.own_ref), channel_id=1, source_target_pairs={{0,64},{32,96},{64,0},{96,32},{1,65},{33,97},{65,1},{97,33},{2,66}... | collective-permute-start | bytes 202760 | tf_op jit(solution)/shard_map/ppermute | solution.py:368
  10.1 2.6 %shard_map.61 = (bf16[32,256,256]{2,1,0:T(8,128)(2,1)S(1)}, s32[163]{0:T(256)S(1)}) custom-call(s32[4,8]{1,0:T(4,128)S(1)} %bitcast.12, s32[1,8]{1,0:T(1,128)S(1)} %bitcast.14, bf16[32,256,256]{2,1,0:T(8,128)(2,1)S(1)} %bitcast.4), custom_call_target="tpu_custom_call" | custom-call | tf_op jit(solution)/shard_map/pallas_call | solution.py:344
  12.7 1.9 %collective-permute-done.2.right_ref = s16[8,4224]{1,0:T(8,128)(2,1)S(1)} collective-permute-done((s16[8,4224]{1,0:T(8,128)(2,1)S(1)}, s16[8,4224]{1,0:T(8,128)(2,1)S(1)}, u32[]{:S(2)}, u32[]{:S(2)}) %collective-permute-start.2) | collective-permute-done | bytes 67616 | tf_op jit(solution)/shard_map/ppermute | solution.py:368
  17.3 3.1 %collective-permute-start.7 = (s16[8,2176]{1,0:T(8,128)(2,1)S(1)}, s16[8,2176]{1,0:T(8,128)(2,1)S(1)}, u32[]{:S(2)}, u32[]{:S(2)}) collective-permute-start(s16[8,2176]{1,0:T(8,128)(2,1)S(1)} %shard_map.64.own_ref), channel_id=1, source_target_pairs={{0,8},{4,12},{8,0},{12,4},{1,9},{5,13},{9,1},{13,5},{2,10},{6,14},... | collective-permute-start | bytes 104456 | tf_op jit(solution)/shard_map/ppermute | solution.py:368
  22.8 2.7 %collective-permute-done.6.right_ref = s16[8,2176]{1,0:T(8,128)(2,1)S(1)} collective-permute-done((s16[8,2176]{1,0:T(8,128)(2,1)S(1)}, s16[8,2176]{1,0:T(8,128)(2,1)S(1)}, u32[]{:S(2)}, u32[]{:S(2)}) %collective-permute-start.6) | collective-permute-done | bytes 34848 | tf_op jit(solution)/shard_map/ppermute | solution.py:368
  25.9 3.3 %collective-permute-start.10 = (s16[8,2176]{1,0:T(8,128)(2,1)S(1)}, s16[8,2176]{1,0:T(8,128)(2,1)S(1)}, u32[]{:S(2)}, u32[]{:S(2)}) collective-permute-start(s16[8,2176]{1,0:T(8,128)(2,1)S(1)} %shard_map.65.own_ref), channel_id=1, source_target_pairs={{0,2},{1,3},{2,0},{3,1},{4,6},{5,7},{6,4},{7,5},{8,10},{9,11},{10,... | collective-permute-start | bytes 104456 | tf_op jit(solution)/shard_map/ppermute | solution.py:368
  31.4 2.9 %collective-permute-done.9.right_ref = s16[8,2176]{1,0:T(8,128)(2,1)S(1)} collective-permute-done((s16[8,2176]{1,0:T(8,128)(2,1)S(1)}, s16[8,2176]{1,0:T(8,128)(2,1)S(1)}, u32[]{:S(2)}, u32[]{:S(2)}) %collective-permute-start.9) | collective-permute-done | bytes 34848 | tf_op jit(solution)/shard_map/ppermute | solution.py:368
  37.1 1.9 %collective-permute-start.14 = (s16[8,4224]{1,0:T(8,128)(2,1)S(1)}, s16[8,4224]{1,0:T(8,128)(2,1)S(1)}, u32[]{:S(2)}, u32[]{:S(2)}) collective-permute-start(s16[8,4224]{1,0:T(8,128)(2,1)S(1)} %shard_map.68.own_ref), channel_id=1, source_target_pairs={{0,64},{32,96},{64,0},{96,32},{1,65},{33,97},{65,1},{97,33},{2,66}... | collective-permute-start | bytes 202760 | tf_op jit(solution)/shard_map/ppermute | solution.py:368
  40.6 2.3 %collective-permute-done.14.far_ref = s16[8,4224]{1,0:T(8,128)(2,1)S(1)} collective-permute-done((s16[8,4224]{1,0:T(8,128)(2,1)S(1)}, s16[8,4224]{1,0:T(8,128)(2,1)S(1)}, u32[]{:S(2)}, u32[]{:S(2)}) %collective-permute-start.14) | collective-permute-done | bytes 67616 | tf_op jit(solution)/shard_map/ppermute | solution.py:368
  43.0 1.6 %collective-permute-done.13.right_ref = s16[8,4224]{1,0:T(8,128)(2,1)S(1)} collective-permute-done((s16[8,4224]{1,0:T(8,128)(2,1)S(1)}, s16[8,4224]{1,0:T(8,128)(2,1)S(1)}, u32[]{:S(2)}, u32[]{:S(2)}) %collective-permute-start.13) | collective-permute-done | bytes 67616 | tf_op jit(solution)/shard_map/ppermute | solution.py:368
  47.3 1.5 %collective-permute-start.18 = (s16[8,2176]{1,0:T(8,128)(2,1)S(1)}, s16[8,2176]{1,0:T(8,128)(2,1)S(1)}, u32[]{:S(2)}, u32[]{:S(2)}) collective-permute-start(s16[8,2176]{1,0:T(8,128)(2,1)S(1)} %shard_map.71.own_ref), channel_id=1, source_target_pairs={{0,8},{4,12},{8,0},{12,4},{1,9},{5,13},{9,1},{13,5},{2,10},{6,14},... | collective-permute-start | bytes 104456 | tf_op jit(solution)/shard_map/ppermute | solution.py:368
  50.9 2.0 %collective-permute-done.18.far_ref = s16[8,2176]{1,0:T(8,128)(2,1)S(1)} collective-permute-done((s16[8,2176]{1,0:T(8,128)(2,1)S(1)}, s16[8,2176]{1,0:T(8,128)(2,1)S(1)}, u32[]{:S(2)}, u32[]{:S(2)}) %collective-permute-start.18) | collective-permute-done | bytes 34848 | tf_op jit(solution)/shard_map/ppermute | solution.py:368
  54.3 1.6 %collective-permute-start.21 = (s16[8,2176]{1,0:T(8,128)(2,1)S(1)}, s16[8,2176]{1,0:T(8,128)(2,1)S(1)}, u32[]{:S(2)}, u32[]{:S(2)}) collective-permute-start(s16[8,2176]{1,0:T(8,128)(2,1)S(1)} %shard_map.72.own_ref), channel_id=1, source_target_pairs={{0,2},{1,3},{2,0},{3,1},{4,6},{5,7},{6,4},{7,5},{8,10},{9,11},{10,... | collective-permute-start | bytes 104456 | tf_op jit(solution)/shard_map/ppermute | solution.py:368
  57.9 2.1 %collective-permute-done.21.far_ref = s16[8,2176]{1,0:T(8,128)(2,1)S(1)} collective-permute-done((s16[8,2176]{1,0:T(8,128)(2,1)S(1)}, s16[8,2176]{1,0:T(8,128)(2,1)S(1)}, u32[]{:S(2)}, u32[]{:S(2)}) %collective-permute-start.21) | collective-permute-done | bytes 34848 | tf_op jit(solution)/shard_map/ppermute | solution.py:368
  63.9 1.9 %collective-permute-start.25 = (s16[8,4224]{1,0:T(8,128)(2,1)S(1)}, s16[8,4224]{1,0:T(8,128)(2,1)S(1)}, u32[]{:S(2)}, u32[]{:S(2)}) collective-permute-start(s16[8,4224]{1,0:T(8,128)(2,1)S(1)} %shard_map.75.own_ref), channel_id=1, source_target_pairs={{0,64},{32,96},{64,0},{96,32},{1,65},{33,97},{65,1},{97,33},{2,66}... | collective-permute-start | bytes 202760 | tf_op jit(solution)/shard_map/ppermute | solution.py:368
  67.4 2.3 %collective-permute-done.25.far_ref = s16[8,4224]{1,0:T(8,128)(2,1)S(1)} collective-permute-done((s16[8,4224]{1,0:T(8,128)(2,1)S(1)}, s16[8,4224]{1,0:T(8,128)(2,1)S(1)}, u32[]{:S(2)}, u32[]{:S(2)}) %collective-permute-start.25) | collective-permute-done | bytes 67616 | tf_op jit(solution)/shard_map/ppermute | solution.py:368
  74.1 2.4 %collective-permute-start.29 = (s16[8,2176]{1,0:T(8,128)(2,1)S(1)}, s16[8,2176]{1,0:T(8,128)(2,1)S(1)}, u32[]{:S(2)}, u32[]{:S(2)}) collective-permute-start(s16[8,2176]{1,0:T(8,128)(2,1)S(1)} %shard_map.78.own_ref), channel_id=1, source_target_pairs={{0,8},{4,12},{8,0},{12,4},{1,9},{5,13},{9,1},{13,5},{2,10},{6,14},... | collective-permute-start | bytes 104456 | tf_op jit(solution)/shard_map/ppermute | solution.py:368
  77.6 2.0 %collective-permute-done.29.far_ref = s16[8,2176]{1,0:T(8,128)(2,1)S(1)} collective-permute-done((s16[8,2176]{1,0:T(8,128)(2,1)S(1)}, s16[8,2176]{1,0:T(8,128)(2,1)S(1)}, u32[]{:S(2)}, u32[]{:S(2)}) %collective-permute-start.29) | collective-permute-done | bytes 34848 | tf_op jit(solution)/shard_map/ppermute | solution.py:368
  79.6 2.0 %collective-permute-done.28.right_ref = s16[8,2176]{1,0:T(8,128)(2,1)S(1)} collective-permute-done((s16[8,2176]{1,0:T(8,128)(2,1)S(1)}, s16[8,2176]{1,0:T(8,128)(2,1)S(1)}, u32[]{:S(2)}, u32[]{:S(2)}) %collective-permute-start.28) | collective-permute-done | bytes 34848 | tf_op jit(solution)/shard_map/ppermute | solution.py:368
  81.9 2.3 %collective-permute-start.32 = (s16[8,2176]{1,0:T(8,128)(2,1)S(1)}, s16[8,2176]{1,0:T(8,128)(2,1)S(1)}, u32[]{:S(2)}, u32[]{:S(2)}) collective-permute-start(s16[8,2176]{1,0:T(8,128)(2,1)S(1)} %shard_map.79.own_ref), channel_id=1, source_target_pairs={{0,2},{1,3},{2,0},{3,1},{4,6},{5,7},{6,4},{7,5},{8,10},{9,11},{10,... | collective-permute-start | bytes 104456 | tf_op jit(solution)/shard_map/ppermute | solution.py:368
  85.4 2.0 %collective-permute-done.32.far_ref = s16[8,2176]{1,0:T(8,128)(2,1)S(1)} collective-permute-done((s16[8,2176]{1,0:T(8,128)(2,1)S(1)}, s16[8,2176]{1,0:T(8,128)(2,1)S(1)}, u32[]{:S(2)}, u32[]{:S(2)}) %collective-permute-start.32) | collective-permute-done | bytes 34848 | tf_op jit(solution)/shard_map/ppermute | solution.py:368
  87.4 1.9 %collective-permute-done.31.right_ref = s16[8,2176]{1,0:T(8,128)(2,1)S(1)} collective-permute-done((s16[8,2176]{1,0:T(8,128)(2,1)S(1)}, s16[8,2176]{1,0:T(8,128)(2,1)S(1)}, u32[]{:S(2)}, u32[]{:S(2)}) %collective-permute-start.31) | collective-permute-done | bytes 34848 | tf_op jit(solution)/shard_map/ppermute | solution.py:368
  92.1 1.9 %collective-permute-start.36 = (s16[8,4224]{1,0:T(8,128)(2,1)S(1)}, s16[8,4224]{1,0:T(8,128)(2,1)S(1)}, u32[]{:S(2)}, u32[]{:S(2)}) collective-permute-start(s16[8,4224]{1,0:T(8,128)(2,1)S(1)} %shard_map.82.own_ref), channel_id=1, source_target_pairs={{0,64},{32,96},{64,0},{96,32},{1,65},{33,97},{65,1},{97,33},{2,66}... | collective-permute-start | bytes 202760 | tf_op jit(solution)/shard_map/ppermute | solution.py:368
  95.7 2.3 %collective-permute-done.36.far_ref = s16[8,4224]{1,0:T(8,128)(2,1)S(1)} collective-permute-done((s16[8,4224]{1,0:T(8,128)(2,1)S(1)}, s16[8,4224]{1,0:T(8,128)(2,1)S(1)}, u32[]{:S(2)}, u32[]{:S(2)}) %collective-permute-start.36) | collective-permute-done | bytes 67616 | tf_op jit(solution)/shard_map/ppermute | solution.py:368
  98.0 1.5 %collective-permute-done.35.right_ref = s16[8,4224]{1,0:T(8,128)(2,1)S(1)} collective-permute-done((s16[8,4224]{1,0:T(8,128)(2,1)S(1)}, s16[8,4224]{1,0:T(8,128)(2,1)S(1)}, u32[]{:S(2)}, u32[]{:S(2)}) %collective-permute-start.35) | collective-permute-done | bytes 67616 | tf_op jit(solution)/shard_map/ppermute | solution.py:368
  102.3 1.5 %collective-permute-start.40 = (s16[8,2176]{1,0:T(8,128)(2,1)S(1)}, s16[8,2176]{1,0:T(8,128)(2,1)S(1)}, u32[]{:S(2)}, u32[]{:S(2)}) collective-permute-start(s16[8,2176]{1,0:T(8,128)(2,1)S(1)} %shard_map.85.own_ref), channel_id=1, source_target_pairs={{0,8},{4,12},{8,0},{12,4},{1,9},{5,13},{9,1},{13,5},{2,10},{6,14},... | collective-permute-start | bytes 104456 | tf_op jit(solution)/shard_map/ppermute | solution.py:368
  105.9 2.0 %collective-permute-done.40.far_ref = s16[8,2176]{1,0:T(8,128)(2,1)S(1)} collective-permute-done((s16[8,2176]{1,0:T(8,128)(2,1)S(1)}, s16[8,2176]{1,0:T(8,128)(2,1)S(1)}, u32[]{:S(2)}, u32[]{:S(2)}) %collective-permute-start.40) | collective-permute-done | bytes 34848 | tf_op jit(solution)/shard_map/ppermute | solution.py:368
  109.3 1.6 %collective-permute-start.43 = (s16[8,2176]{1,0:T(8,128)(2,1)S(1)}, s16[8,2176]{1,0:T(8,128)(2,1)S(1)}, u32[]{:S(2)}, u32[]{:S(2)}) collective-permute-start(s16[8,2176]{1,0:T(8,128)(2,1)S(1)} %shard_map.86.own_ref), channel_id=1, source_target_pairs={{0,2},{1,3},{2,0},{3,1},{4,6},{5,7},{6,4},{7,5},{8,10},{9,11},{10,... | collective-permute-start | bytes 104456 | tf_op jit(solution)/shard_map/ppermute | solution.py:368
  112.9 2.1 %collective-permute-done.43.far_ref = s16[8,2176]{1,0:T(8,128)(2,1)S(1)} collective-permute-done((s16[8,2176]{1,0:T(8,128)(2,1)S(1)}, s16[8,2176]{1,0:T(8,128)(2,1)S(1)}, u32[]{:S(2)}, u32[]{:S(2)}) %collective-permute-start.43) | collective-permute-done | bytes 34848 | tf_op jit(solution)/shard_map/ppermute | solution.py:368
  117.5 1.8 %collective-permute-start.47 = (f32[8,128]{1,0:T(8,128)S(1)}, f32[8,128]{1,0:T(8,128)S(1)}, u32[]{:S(2)}, u32[]{:S(2)}) collective-permute-start(f32[8,128]{1,0:T(8,128)S(1)} %add.3.own_ref), channel_id=1, source_target_pairs={{0,64},{32,96},{64,0},{96,32},{1,65},{33,97},{65,1},{97,33},{2,66}... | collective-permute-start | bytes 12296 | tf_op jit(solution)/shard_map/ppermute | solution.py:368
  122.7 1.5 %collective-permute-done.46.right_ref = f32[8,128]{1,0:T(8,128)S(1)} collective-permute-done((f32[8,128]{1,0:T(8,128)S(1)}, f32[8,128]{1,0:T(8,128)S(1)}, u32[]{:S(2)}, u32[]{:S(2)}) %collective-permute-start.46) | collective-permute-done | bytes 4128 | tf_op jit(solution)/shard_map/ppermute | solution.py:368
  (102 shorter events, 54.7 us)
Async XLA Ops:
  5.0 7.7 %collective-permute-start.3 = (s16[8,4224]{1,0:T(8,128)(2,1)S(1)}, s16[8,4224]{1,0:T(8,128)(2,1)S(1)}, u32[]{:S(2)}, u32[]{:S(2)}) collective-permute-start(s16[8,4224]{1,0:T(8,128)(2,1)S(1)} %shard_map.60.own_ref), channel_id=1, source_target_pairs={{0,64},{32,96},{64,0},{96,32},{1,65},{33,97},{65,1},{97,33},{2,66}... | collective-permute-start | bytes 202760 | tf_op jit(solution)/shard_map/ppermute | solution.py:368
  9.0 5.5 %collective-permute-start.2 = (s16[8,4224]{1,0:T(8,128)(2,1)S(1)}, s16[8,4224]{1,0:T(8,128)(2,1)S(1)}, u32[]{:S(2)}, u32[]{:S(2)}) collective-permute-start(s16[8,4224]{1,0:T(8,128)(2,1)S(1)} %shard_map.60.own_ref), channel_id=1, source_target_pairs={{0,96},{32,64},{64,32},{96,0},{1,97},{33,65},{65,33},{97,1},{2,98}... | collective-permute-start | bytes 202760 | tf_op jit(solution)/shard_map/ppermute | solution.py:368
  9.8 4.8 %collective-permute-start.1 = (s16[8,4224]{1,0:T(8,128)(2,1)S(1)}, s16[8,4224]{1,0:T(8,128)(2,1)S(1)}, u32[]{:S(2)}, u32[]{:S(2)}) collective-permute-start(s16[8,4224]{1,0:T(8,128)(2,1)S(1)} %shard_map.60.own_ref), channel_id=1, source_target_pairs={{0,32},{32,0},{64,96},{96,64},{1,33},{33,1},{65,97},{97,65},{2,34}... | collective-permute-start | bytes 202760 | tf_op jit(solution)/shard_map/ppermute | solution.py:368
  17.3 5.5 %collective-permute-start.7 = (s16[8,2176]{1,0:T(8,128)(2,1)S(1)}, s16[8,2176]{1,0:T(8,128)(2,1)S(1)}, u32[]{:S(2)}, u32[]{:S(2)}) collective-permute-start(s16[8,2176]{1,0:T(8,128)(2,1)S(1)} %shard_map.64.own_ref), channel_id=1, source_target_pairs={{0,8},{4,12},{8,0},{12,4},{1,9},{5,13},{9,1},{13,5},{2,10},{6,14},... | collective-permute-start | bytes 104456 | tf_op jit(solution)/shard_map/ppermute | solution.py:368
  20.4 5.1 %collective-permute-start.6 = (s16[8,2176]{1,0:T(8,128)(2,1)S(1)}, s16[8,2176]{1,0:T(8,128)(2,1)S(1)}, u32[]{:S(2)}, u32[]{:S(2)}) collective-permute-start(s16[8,2176]{1,0:T(8,128)(2,1)S(1)} %shard_map.64.own_ref), channel_id=1, source_target_pairs={{0,12},{4,8},{8,4},{12,0},{1,13},{5,9},{9,5},{13,1},{2,14},{6,10},... | collective-permute-start | bytes 104456 | tf_op jit(solution)/shard_map/ppermute | solution.py:368
  25.9 5.5 %collective-permute-start.10 = (s16[8,2176]{1,0:T(8,128)(2,1)S(1)}, s16[8,2176]{1,0:T(8,128)(2,1)S(1)}, u32[]{:S(2)}, u32[]{:S(2)}) collective-permute-start(s16[8,2176]{1,0:T(8,128)(2,1)S(1)} %shard_map.65.own_ref), channel_id=1, source_target_pairs={{0,2},{1,3},{2,0},{3,1},{4,6},{5,7},{6,4},{7,5},{8,10},{9,11},{10,... | collective-permute-start | bytes 104456 | tf_op jit(solution)/shard_map/ppermute | solution.py:368
  29.1 5.1 %collective-permute-start.9 = (s16[8,2176]{1,0:T(8,128)(2,1)S(1)}, s16[8,2176]{1,0:T(8,128)(2,1)S(1)}, u32[]{:S(2)}, u32[]{:S(2)}) collective-permute-start(s16[8,2176]{1,0:T(8,128)(2,1)S(1)} %shard_map.65.own_ref), channel_id=1, source_target_pairs={{0,3},{1,2},{2,1},{3,0},{4,7},{5,6},{6,5},{7,4},{8,11},{9,10},{10,... | collective-permute-start | bytes 104456 | tf_op jit(solution)/shard_map/ppermute | solution.py:368
  30.2 4.1 %collective-permute-start.8 = (s16[8,2176]{1,0:T(8,128)(2,1)S(1)}, s16[8,2176]{1,0:T(8,128)(2,1)S(1)}, u32[]{:S(2)}, u32[]{:S(2)}) collective-permute-start(s16[8,2176]{1,0:T(8,128)(2,1)S(1)} %shard_map.65.own_ref), channel_id=1, source_target_pairs={{0,1},{1,0},{2,3},{3,2},{4,5},{5,4},{6,7},{7,6},{8,9},{9,8},{10,11... | collective-permute-start | bytes 104456 | tf_op jit(solution)/shard_map/ppermute | solution.py:368
  37.1 5.9 %collective-permute-start.14 = (s16[8,4224]{1,0:T(8,128)(2,1)S(1)}, s16[8,4224]{1,0:T(8,128)(2,1)S(1)}, u32[]{:S(2)}, u32[]{:S(2)}) collective-permute-start(s16[8,4224]{1,0:T(8,128)(2,1)S(1)} %shard_map.68.own_ref), channel_id=1, source_target_pairs={{0,64},{32,96},{64,0},{96,32},{1,65},{33,97},{65,1},{97,33},{2,66}... | collective-permute-start | bytes 202760 | tf_op jit(solution)/shard_map/ppermute | solution.py:368
  39.0 5.5 %collective-permute-start.13 = (s16[8,4224]{1,0:T(8,128)(2,1)S(1)}, s16[8,4224]{1,0:T(8,128)(2,1)S(1)}, u32[]{:S(2)}, u32[]{:S(2)}) collective-permute-start(s16[8,4224]{1,0:T(8,128)(2,1)S(1)} %shard_map.68.own_ref), channel_id=1, source_target_pairs={{0,96},{32,64},{64,32},{96,0},{1,97},{33,65},{65,33},{97,1},{2,98}... | collective-permute-start | bytes 202760 | tf_op jit(solution)/shard_map/ppermute | solution.py:368
  40.0 4.5 %collective-permute-start.12 = (s16[8,4224]{1,0:T(8,128)(2,1)S(1)}, s16[8,4224]{1,0:T(8,128)(2,1)S(1)}, u32[]{:S(2)}, u32[]{:S(2)}) collective-permute-start(s16[8,4224]{1,0:T(8,128)(2,1)S(1)} %shard_map.68.own_ref), channel_id=1, source_target_pairs={{0,32},{32,0},{64,96},{96,64},{1,33},{33,1},{65,97},{97,65},{2,34}... | collective-permute-start | bytes 202760 | tf_op jit(solution)/shard_map/ppermute | solution.py:368
  47.3 5.5 %collective-permute-start.18 = (s16[8,2176]{1,0:T(8,128)(2,1)S(1)}, s16[8,2176]{1,0:T(8,128)(2,1)S(1)}, u32[]{:S(2)}, u32[]{:S(2)}) collective-permute-start(s16[8,2176]{1,0:T(8,128)(2,1)S(1)} %shard_map.71.own_ref), channel_id=1, source_target_pairs={{0,8},{4,12},{8,0},{12,4},{1,9},{5,13},{9,1},{13,5},{2,10},{6,14},... | collective-permute-start | bytes 104456 | tf_op jit(solution)/shard_map/ppermute | solution.py:368
  48.9 5.1 %collective-permute-start.17 = (s16[8,2176]{1,0:T(8,128)(2,1)S(1)}, s16[8,2176]{1,0:T(8,128)(2,1)S(1)}, u32[]{:S(2)}, u32[]{:S(2)}) collective-permute-start(s16[8,2176]{1,0:T(8,128)(2,1)S(1)} %shard_map.71.own_ref), channel_id=1, source_target_pairs={{0,12},{4,8},{8,4},{12,0},{1,13},{5,9},{9,5},{13,1},{2,14},{6,10},... | collective-permute-start | bytes 104456 | tf_op jit(solution)/shard_map/ppermute | solution.py:368
  54.3 5.7 %collective-permute-start.21 = (s16[8,2176]{1,0:T(8,128)(2,1)S(1)}, s16[8,2176]{1,0:T(8,128)(2,1)S(1)}, u32[]{:S(2)}, u32[]{:S(2)}) collective-permute-start(s16[8,2176]{1,0:T(8,128)(2,1)S(1)} %shard_map.72.own_ref), channel_id=1, source_target_pairs={{0,2},{1,3},{2,0},{3,1},{4,6},{5,7},{6,4},{7,5},{8,10},{9,11},{10,... | collective-permute-start | bytes 104456 | tf_op jit(solution)/shard_map/ppermute | solution.py:368
  55.9 5.1 %collective-permute-start.20 = (s16[8,2176]{1,0:T(8,128)(2,1)S(1)}, s16[8,2176]{1,0:T(8,128)(2,1)S(1)}, u32[]{:S(2)}, u32[]{:S(2)}) collective-permute-start(s16[8,2176]{1,0:T(8,128)(2,1)S(1)} %shard_map.72.own_ref), channel_id=1, source_target_pairs={{0,3},{1,2},{2,1},{3,0},{4,7},{5,6},{6,5},{7,4},{8,11},{9,10},{10,... | collective-permute-start | bytes 104456 | tf_op jit(solution)/shard_map/ppermute | solution.py:368
  56.9 4.2 %collective-permute-start.19 = (s16[8,2176]{1,0:T(8,128)(2,1)S(1)}, s16[8,2176]{1,0:T(8,128)(2,1)S(1)}, u32[]{:S(2)}, u32[]{:S(2)}) collective-permute-start(s16[8,2176]{1,0:T(8,128)(2,1)S(1)} %shard_map.72.own_ref), channel_id=1, source_target_pairs={{0,1},{1,0},{2,3},{3,2},{4,5},{5,4},{6,7},{7,6},{8,9},{9,8},{10,11... | collective-permute-start | bytes 104456 | tf_op jit(solution)/shard_map/ppermute | solution.py:368
  63.9 5.9 %collective-permute-start.25 = (s16[8,4224]{1,0:T(8,128)(2,1)S(1)}, s16[8,4224]{1,0:T(8,128)(2,1)S(1)}, u32[]{:S(2)}, u32[]{:S(2)}) collective-permute-start(s16[8,4224]{1,0:T(8,128)(2,1)S(1)} %shard_map.75.own_ref), channel_id=1, source_target_pairs={{0,64},{32,96},{64,0},{96,32},{1,65},{33,97},{65,1},{97,33},{2,66}... | collective-permute-start | bytes 202760 | tf_op jit(solution)/shard_map/ppermute | solution.py:368
  65.8 5.5 %collective-permute-start.24 = (s16[8,4224]{1,0:T(8,128)(2,1)S(1)}, s16[8,4224]{1,0:T(8,128)(2,1)S(1)}, u32[]{:S(2)}, u32[]{:S(2)}) collective-permute-start(s16[8,4224]{1,0:T(8,128)(2,1)S(1)} %shard_map.75.own_ref), channel_id=1, source_target_pairs={{0,96},{32,64},{64,32},{96,0},{1,97},{33,65},{65,33},{97,1},{2,98}... | collective-permute-start | bytes 202760 | tf_op jit(solution)/shard_map/ppermute | solution.py:368
  67.0 4.3 %collective-permute-start.23 = (s16[8,4224]{1,0:T(8,128)(2,1)S(1)}, s16[8,4224]{1,0:T(8,128)(2,1)S(1)}, u32[]{:S(2)}, u32[]{:S(2)}) collective-permute-start(s16[8,4224]{1,0:T(8,128)(2,1)S(1)} %shard_map.75.own_ref), channel_id=1, source_target_pairs={{0,32},{32,0},{64,96},{96,64},{1,33},{33,1},{65,97},{97,65},{2,34}... | collective-permute-start | bytes 202760 | tf_op jit(solution)/shard_map/ppermute | solution.py:368
  74.1 5.5 %collective-permute-start.29 = (s16[8,2176]{1,0:T(8,128)(2,1)S(1)}, s16[8,2176]{1,0:T(8,128)(2,1)S(1)}, u32[]{:S(2)}, u32[]{:S(2)}) collective-permute-start(s16[8,2176]{1,0:T(8,128)(2,1)S(1)} %shard_map.78.own_ref), channel_id=1, source_target_pairs={{0,8},{4,12},{8,0},{12,4},{1,9},{5,13},{9,1},{13,5},{2,10},{6,14},... | collective-permute-start | bytes 104456 | tf_op jit(solution)/shard_map/ppermute | solution.py:368
  76.4 5.1 %collective-permute-start.28 = (s16[8,2176]{1,0:T(8,128)(2,1)S(1)}, s16[8,2176]{1,0:T(8,128)(2,1)S(1)}, u32[]{:S(2)}, u32[]{:S(2)}) collective-permute-start(s16[8,2176]{1,0:T(8,128)(2,1)S(1)} %shard_map.78.own_ref), channel_id=1, source_target_pairs={{0,12},{4,8},{8,4},{12,0},{1,13},{5,9},{9,5},{13,1},{2,14},{6,10},... | collective-permute-start | bytes 104456 | tf_op jit(solution)/shard_map/ppermute | solution.py:368
  81.9 5.5 %collective-permute-start.32 = (s16[8,2176]{1,0:T(8,128)(2,1)S(1)}, s16[8,2176]{1,0:T(8,128)(2,1)S(1)}, u32[]{:S(2)}, u32[]{:S(2)}) collective-permute-start(s16[8,2176]{1,0:T(8,128)(2,1)S(1)} %shard_map.79.own_ref), channel_id=1, source_target_pairs={{0,2},{1,3},{2,0},{3,1},{4,6},{5,7},{6,4},{7,5},{8,10},{9,11},{10,... | collective-permute-start | bytes 104456 | tf_op jit(solution)/shard_map/ppermute | solution.py:368
  84.2 5.1 %collective-permute-start.31 = (s16[8,2176]{1,0:T(8,128)(2,1)S(1)}, s16[8,2176]{1,0:T(8,128)(2,1)S(1)}, u32[]{:S(2)}, u32[]{:S(2)}) collective-permute-start(s16[8,2176]{1,0:T(8,128)(2,1)S(1)} %shard_map.79.own_ref), channel_id=1, source_target_pairs={{0,3},{1,2},{2,1},{3,0},{4,7},{5,6},{6,5},{7,4},{8,11},{9,10},{10,... | collective-permute-start | bytes 104456 | tf_op jit(solution)/shard_map/ppermute | solution.py:368
  92.1 5.9 %collective-permute-start.36 = (s16[8,4224]{1,0:T(8,128)(2,1)S(1)}, s16[8,4224]{1,0:T(8,128)(2,1)S(1)}, u32[]{:S(2)}, u32[]{:S(2)}) collective-permute-start(s16[8,4224]{1,0:T(8,128)(2,1)S(1)} %shard_map.82.own_ref), channel_id=1, source_target_pairs={{0,64},{32,96},{64,0},{96,32},{1,65},{33,97},{65,1},{97,33},{2,66}... | collective-permute-start | bytes 202760 | tf_op jit(solution)/shard_map/ppermute | solution.py:368
  94.0 5.5 %collective-permute-start.35 = (s16[8,4224]{1,0:T(8,128)(2,1)S(1)}, s16[8,4224]{1,0:T(8,128)(2,1)S(1)}, u32[]{:S(2)}, u32[]{:S(2)}) collective-permute-start(s16[8,4224]{1,0:T(8,128)(2,1)S(1)} %shard_map.82.own_ref), channel_id=1, source_target_pairs={{0,96},{32,64},{64,32},{96,0},{1,97},{33,65},{65,33},{97,1},{2,98}... | collective-permute-start | bytes 202760 | tf_op jit(solution)/shard_map/ppermute | solution.py:368
  95.3 4.3 %collective-permute-start.34 = (s16[8,4224]{1,0:T(8,128)(2,1)S(1)}, s16[8,4224]{1,0:T(8,128)(2,1)S(1)}, u32[]{:S(2)}, u32[]{:S(2)}) collective-permute-start(s16[8,4224]{1,0:T(8,128)(2,1)S(1)} %shard_map.82.own_ref), channel_id=1, source_target_pairs={{0,32},{32,0},{64,96},{96,64},{1,33},{33,1},{65,97},{97,65},{2,34}... | collective-permute-start | bytes 202760 | tf_op jit(solution)/shard_map/ppermute | solution.py:368
  102.3 5.5 %collective-permute-start.40 = (s16[8,2176]{1,0:T(8,128)(2,1)S(1)}, s16[8,2176]{1,0:T(8,128)(2,1)S(1)}, u32[]{:S(2)}, u32[]{:S(2)}) collective-permute-start(s16[8,2176]{1,0:T(8,128)(2,1)S(1)} %shard_map.85.own_ref), channel_id=1, source_target_pairs={{0,8},{4,12},{8,0},{12,4},{1,9},{5,13},{9,1},{13,5},{2,10},{6,14},... | collective-permute-start | bytes 104456 | tf_op jit(solution)/shard_map/ppermute | solution.py:368
  103.9 5.1 %collective-permute-start.39 = (s16[8,2176]{1,0:T(8,128)(2,1)S(1)}, s16[8,2176]{1,0:T(8,128)(2,1)S(1)}, u32[]{:S(2)}, u32[]{:S(2)}) collective-permute-start(s16[8,2176]{1,0:T(8,128)(2,1)S(1)} %shard_map.85.own_ref), channel_id=1, source_target_pairs={{0,12},{4,8},{8,4},{12,0},{1,13},{5,9},{9,5},{13,1},{2,14},{6,10},... | collective-permute-start | bytes 104456 | tf_op jit(solution)/shard_map/ppermute | solution.py:368
  109.3 5.7 %collective-permute-start.43 = (s16[8,2176]{1,0:T(8,128)(2,1)S(1)}, s16[8,2176]{1,0:T(8,128)(2,1)S(1)}, u32[]{:S(2)}, u32[]{:S(2)}) collective-permute-start(s16[8,2176]{1,0:T(8,128)(2,1)S(1)} %shard_map.86.own_ref), channel_id=1, source_target_pairs={{0,2},{1,3},{2,0},{3,1},{4,6},{5,7},{6,4},{7,5},{8,10},{9,11},{10,... | collective-permute-start | bytes 104456 | tf_op jit(solution)/shard_map/ppermute | solution.py:368
  111.0 5.1 %collective-permute-start.42 = (s16[8,2176]{1,0:T(8,128)(2,1)S(1)}, s16[8,2176]{1,0:T(8,128)(2,1)S(1)}, u32[]{:S(2)}, u32[]{:S(2)}) collective-permute-start(s16[8,2176]{1,0:T(8,128)(2,1)S(1)} %shard_map.86.own_ref), channel_id=1, source_target_pairs={{0,3},{1,2},{2,1},{3,0},{4,7},{5,6},{6,5},{7,4},{8,11},{9,10},{10,... | collective-permute-start | bytes 104456 | tf_op jit(solution)/shard_map/ppermute | solution.py:368
  117.5 5.1 %collective-permute-start.47 = (f32[8,128]{1,0:T(8,128)S(1)}, f32[8,128]{1,0:T(8,128)S(1)}, u32[]{:S(2)}, u32[]{:S(2)}) collective-permute-start(f32[8,128]{1,0:T(8,128)S(1)} %add.3.own_ref), channel_id=1, source_target_pairs={{0,64},{32,96},{64,0},{96,32},{1,65},{33,97},{65,1},{97,33},{2,66}... | collective-permute-start | bytes 12296 | tf_op jit(solution)/shard_map/ppermute | solution.py:368
  119.4 4.8 %collective-permute-start.46 = (f32[8,128]{1,0:T(8,128)S(1)}, f32[8,128]{1,0:T(8,128)S(1)}, u32[]{:S(2)}, u32[]{:S(2)}) collective-permute-start(f32[8,128]{1,0:T(8,128)S(1)} %add.3.own_ref), channel_id=1, source_target_pairs={{0,96},{32,64},{64,32},{96,0},{1,97},{33,65},{65,33},{97,1},{2,98}... | collective-permute-start | bytes 12296 | tf_op jit(solution)/shard_map/ppermute | solution.py:368
  (19 other events, 72.8 us)

commit v11 on v10

--- a/solution.py
+++ b/solution.py
@@ -8,8 +8,8 @@
 from jax.sharding import Mesh, PartitionSpec as P
 
 BLK_DEV = 32
-HEAD = 20
-GROUP = 4
+HEAD = 18
+GROUP = 2
 ITERS = 4
 EPS = 1e-06
 TINY = 1e-30

time: 125 us -> 125 us (level)
  no operation moved by 1% of the time
where the time goes in v11:
time: 125 us
  starting transfers between devices  50 us (40%)
  waiting for transfers between devices  49.7 us (40%)
  Pallas kernels  24.2 us (19%)
    ppermute x39, starting transfers between devices, spread(): lax.ppermute(value, axis, [(i, i ^ by) for i in range(n)])  49.2 us
    ppermute x39, waiting for transfers between devices, spread(): lax.ppermute(value, axis, [(i, i ^ by) for i in range(n)])  45 us
    pallas_call x31, Pallas kernels, call(): pl.pallas_call(body, out_shape=outs, in_specs=specs, out_specs=out_specs...  24.2 us
    ppermute x9, waiting for transfers between devices, swap(): return lax.ppermute(value, 'core', [(0, 1), (1, 0)])  4.74 us
  transfers between devices with their start and end apart: 48, of which 34 were waited for; matrix products, arithmetic and copies ran while one was open for 0% of the time, Pallas kernels for 8%

profile of v11, /device:TPU:0, one launch (start us, length us, event | category | flops | bytes accessed | tf_op | source)
XLA Modules:
  0.0 125.0 jit_solution(13159506391546171894)
XLA Ops:
  0.7 2.8 %shard_map.59 = (f32[8,4224]{1,0:T(8,128)S(1)}, f32[8,4224]{1,0:T(8,128)S(1)}, bf16[8,4,256,256]{3,2,1,0:T(8,128)(2,1)S(1)}) custom-call(s32[4,8]{1,0:T(4,128)} %bitcast.11, s32[1,8]{1,0:T(1,128)} %bitcast.13, f32[8,2048]{1,0:T(8,128)} %prev_ref.3, bf16[8,4,256,256]{3,2,1,0:T(8,128)(2,1)} %source_ref.1), custom_call_target="tpu_custom_call" | custom-call | tf_op jit(solution)/shard_map/pallas_call | solution.py:344
  5.0 4.0 %collective-permute-start.3 = (s16[8,4224]{1,0:T(8,128)(2,1)S(1)}, s16[8,4224]{1,0:T(8,128)(2,1)S(1)}, u32[]{:S(2)}, u32[]{:S(2)}) collective-permute-start(s16[8,4224]{1,0:T(8,128)(2,1)S(1)} %shard_map.60.own_ref), channel_id=1, source_target_pairs={{0,64},{32,96},{64,0},{96,32},{1,65},{33,97},{65,1},{97,33},{2,66}... | collective-permute-start | bytes 202760 | tf_op jit(solution)/shard_map/ppermute | solution.py:368
  10.1 2.6 %shard_map.61 = (bf16[32,256,256]{2,1,0:T(8,128)(2,1)S(1)}, s32[163]{0:T(256)S(1)}) custom-call(s32[4,8]{1,0:T(4,128)S(1)} %bitcast.12, s32[1,8]{1,0:T(1,128)S(1)} %bitcast.14, bf16[32,256,256]{2,1,0:T(8,128)(2,1)S(1)} %bitcast.4), custom_call_target="tpu_custom_call" | custom-call | tf_op jit(solution)/shard_map/pallas_call | solution.py:344
  12.7 1.9 %collective-permute-done.2.right_ref = s16[8,4224]{1,0:T(8,128)(2,1)S(1)} collective-permute-done((s16[8,4224]{1,0:T(8,128)(2,1)S(1)}, s16[8,4224]{1,0:T(8,128)(2,1)S(1)}, u32[]{:S(2)}, u32[]{:S(2)}) %collective-permute-start.2) | collective-permute-done | bytes 67616 | tf_op jit(solution)/shard_map/ppermute | solution.py:368
  17.3 3.1 %collective-permute-start.7 = (s16[8,2176]{1,0:T(8,128)(2,1)S(1)}, s16[8,2176]{1,0:T(8,128)(2,1)S(1)}, u32[]{:S(2)}, u32[]{:S(2)}) collective-permute-start(s16[8,2176]{1,0:T(8,128)(2,1)S(1)} %shard_map.64.own_ref), channel_id=1, source_target_pairs={{0,8},{4,12},{8,0},{12,4},{1,9},{5,13},{9,1},{13,5},{2,10},{6,14},... | collective-permute-start | bytes 104456 | tf_op jit(solution)/shard_map/ppermute | solution.py:368
  22.8 2.7 %collective-permute-done.6.right_ref = s16[8,2176]{1,0:T(8,128)(2,1)S(1)} collective-permute-done((s16[8,2176]{1,0:T(8,128)(2,1)S(1)}, s16[8,2176]{1,0:T(8,128)(2,1)S(1)}, u32[]{:S(2)}, u32[]{:S(2)}) %collective-permute-start.6) | collective-permute-done | bytes 34848 | tf_op jit(solution)/shard_map/ppermute | solution.py:368
  25.8 3.3 %collective-permute-start.10 = (s16[8,2176]{1,0:T(8,128)(2,1)S(1)}, s16[8,2176]{1,0:T(8,128)(2,1)S(1)}, u32[]{:S(2)}, u32[]{:S(2)}) collective-permute-start(s16[8,2176]{1,0:T(8,128)(2,1)S(1)} %shard_map.65.own_ref), channel_id=1, source_target_pairs={{0,2},{1,3},{2,0},{3,1},{4,6},{5,7},{6,4},{7,5},{8,10},{9,11},{10,... | collective-permute-start | bytes 104456 | tf_op jit(solution)/shard_map/ppermute | solution.py:368
  31.3 2.9 %collective-permute-done.9.right_ref = s16[8,2176]{1,0:T(8,128)(2,1)S(1)} collective-permute-done((s16[8,2176]{1,0:T(8,128)(2,1)S(1)}, s16[8,2176]{1,0:T(8,128)(2,1)S(1)}, u32[]{:S(2)}, u32[]{:S(2)}) %collective-permute-start.9) | collective-permute-done | bytes 34848 | tf_op jit(solution)/shard_map/ppermute | solution.py:368
  37.0 2.0 %collective-permute-start.14 = (s16[8,4224]{1,0:T(8,128)(2,1)S(1)}, s16[8,4224]{1,0:T(8,128)(2,1)S(1)}, u32[]{:S(2)}, u32[]{:S(2)}) collective-permute-start(s16[8,4224]{1,0:T(8,128)(2,1)S(1)} %shard_map.68.own_ref), channel_id=1, source_target_pairs={{0,64},{32,96},{64,0},{96,32},{1,65},{33,97},{65,1},{97,33},{2,66}... | collective-permute-start | bytes 202760 | tf_op jit(solution)/shard_map/ppermute | solution.py:368
  40.6 2.3 %collective-permute-done.14.far_ref = s16[8,4224]{1,0:T(8,128)(2,1)S(1)} collective-permute-done((s16[8,4224]{1,0:T(8,128)(2,1)S(1)}, s16[8,4224]{1,0:T(8,128)(2,1)S(1)}, u32[]{:S(2)}, u32[]{:S(2)}) %collective-permute-start.14) | collective-permute-done | bytes 67616 | tf_op jit(solution)/shard_map/ppermute | solution.py:368
  42.9 1.6 %collective-permute-done.13.right_ref = s16[8,4224]{1,0:T(8,128)(2,1)S(1)} collective-permute-done((s16[8,4224]{1,0:T(8,128)(2,1)S(1)}, s16[8,4224]{1,0:T(8,128)(2,1)S(1)}, u32[]{:S(2)}, u32[]{:S(2)}) %collective-permute-start.13) | collective-permute-done | bytes 67616 | tf_op jit(solution)/shard_map/ppermute | solution.py:368
  47.2 1.5 %collective-permute-start.18 = (s16[8,2176]{1,0:T(8,128)(2,1)S(1)}, s16[8,2176]{1,0:T(8,128)(2,1)S(1)}, u32[]{:S(2)}, u32[]{:S(2)}) collective-permute-start(s16[8,2176]{1,0:T(8,128)(2,1)S(1)} %shard_map.71.own_ref), channel_id=1, source_target_pairs={{0,8},{4,12},{8,0},{12,4},{1,9},{5,13},{9,1},{13,5},{2,10},{6,14},... | collective-permute-start | bytes 104456 | tf_op jit(solution)/shard_map/ppermute | solution.py:368
  50.8 2.0 %collective-permute-done.18.far_ref = s16[8,2176]{1,0:T(8,128)(2,1)S(1)} collective-permute-done((s16[8,2176]{1,0:T(8,128)(2,1)S(1)}, s16[8,2176]{1,0:T(8,128)(2,1)S(1)}, u32[]{:S(2)}, u32[]{:S(2)}) %collective-permute-start.18) | collective-permute-done | bytes 34848 | tf_op jit(solution)/shard_map/ppermute | solution.py:368
  54.2 1.6 %collective-permute-start.21 = (s16[8,2176]{1,0:T(8,128)(2,1)S(1)}, s16[8,2176]{1,0:T(8,128)(2,1)S(1)}, u32[]{:S(2)}, u32[]{:S(2)}) collective-permute-start(s16[8,2176]{1,0:T(8,128)(2,1)S(1)} %shard_map.72.own_ref), channel_id=1, source_target_pairs={{0,2},{1,3},{2,0},{3,1},{4,6},{5,7},{6,4},{7,5},{8,10},{9,11},{10,... | collective-permute-start | bytes 104456 | tf_op jit(solution)/shard_map/ppermute | solution.py:368
  57.8 2.1 %collective-permute-done.21.far_ref = s16[8,2176]{1,0:T(8,128)(2,1)S(1)} collective-permute-done((s16[8,2176]{1,0:T(8,128)(2,1)S(1)}, s16[8,2176]{1,0:T(8,128)(2,1)S(1)}, u32[]{:S(2)}, u32[]{:S(2)}) %collective-permute-start.21) | collective-permute-done | bytes 34848 | tf_op jit(solution)/shard_map/ppermute | solution.py:368
  63.7 1.9 %collective-permute-start.25 = (s16[8,4224]{1,0:T(8,128)(2,1)S(1)}, s16[8,4224]{1,0:T(8,128)(2,1)S(1)}, u32[]{:S(2)}, u32[]{:S(2)}) collective-permute-start(s16[8,4224]{1,0:T(8,128)(2,1)S(1)} %shard_map.75.own_ref), channel_id=1, source_target_pairs={{0,64},{32,96},{64,0},{96,32},{1,65},{33,97},{65,1},{97,33},{2,66}... | collective-permute-start | bytes 202760 | tf_op jit(solution)/shard_map/ppermute | solution.py:368
  67.3 2.3 %collective-permute-done.25.far_ref = s16[8,4224]{1,0:T(8,128)(2,1)S(1)} collective-permute-done((s16[8,4224]{1,0:T(8,128)(2,1)S(1)}, s16[8,4224]{1,0:T(8,128)(2,1)S(1)}, u32[]{:S(2)}, u32[]{:S(2)}) %collective-permute-start.25) | collective-permute-done | bytes 67616 | tf_op jit(solution)/shard_map/ppermute | solution.py:368
  69.6 1.6 %collective-permute-done.24.right_ref = s16[8,4224]{1,0:T(8,128)(2,1)S(1)} collective-permute-done((s16[8,4224]{1,0:T(8,128)(2,1)S(1)}, s16[8,4224]{1,0:T(8,128)(2,1)S(1)}, u32[]{:S(2)}, u32[]{:S(2)}) %collective-permute-start.24) | collective-permute-done | bytes 67616 | tf_op jit(solution)/shard_map/ppermute | solution.py:368
  73.9 2.3 %collective-permute-start.29 = (s16[8,2176]{1,0:T(8,128)(2,1)S(1)}, s16[8,2176]{1,0:T(8,128)(2,1)S(1)}, u32[]{:S(2)}, u32[]{:S(2)}) collective-permute-start(s16[8,2176]{1,0:T(8,128)(2,1)S(1)} %shard_map.78.own_ref), channel_id=1, source_target_pairs={{0,8},{4,12},{8,0},{12,4},{1,9},{5,13},{9,1},{13,5},{2,10},{6,14},... | collective-permute-start | bytes 104456 | tf_op jit(solution)/shard_map/ppermute | solution.py:368
  77.5 2.0 %collective-permute-done.29.far_ref = s16[8,2176]{1,0:T(8,128)(2,1)S(1)} collective-permute-done((s16[8,2176]{1,0:T(8,128)(2,1)S(1)}, s16[8,2176]{1,0:T(8,128)(2,1)S(1)}, u32[]{:S(2)}, u32[]{:S(2)}) %collective-permute-start.29) | collective-permute-done | bytes 34848 | tf_op jit(solution)/shard_map/ppermute | solution.py:368
  79.4 2.0 %collective-permute-done.28.right_ref = s16[8,2176]{1,0:T(8,128)(2,1)S(1)} collective-permute-done((s16[8,2176]{1,0:T(8,128)(2,1)S(1)}, s16[8,2176]{1,0:T(8,128)(2,1)S(1)}, u32[]{:S(2)}, u32[]{:S(2)}) %collective-permute-start.28) | collective-permute-done | bytes 34848 | tf_op jit(solution)/shard_map/ppermute | solution.py:368
  81.7 2.3 %collective-permute-start.32 = (s16[8,2176]{1,0:T(8,128)(2,1)S(1)}, s16[8,2176]{1,0:T(8,128)(2,1)S(1)}, u32[]{:S(2)}, u32[]{:S(2)}) collective-permute-start(s16[8,2176]{1,0:T(8,128)(2,1)S(1)} %shard_map.79.own_ref), channel_id=1, source_target_pairs={{0,2},{1,3},{2,0},{3,1},{4,6},{5,7},{6,4},{7,5},{8,10},{9,11},{10,... | collective-permute-start | bytes 104456 | tf_op jit(solution)/shard_map/ppermute | solution.py:368
  85.3 2.0 %collective-permute-done.32.far_ref = s16[8,2176]{1,0:T(8,128)(2,1)S(1)} collective-permute-done((s16[8,2176]{1,0:T(8,128)(2,1)S(1)}, s16[8,2176]{1,0:T(8,128)(2,1)S(1)}, u32[]{:S(2)}, u32[]{:S(2)}) %collective-permute-start.32) | collective-permute-done | bytes 34848 | tf_op jit(solution)/shard_map/ppermute | solution.py:368
  87.2 1.9 %collective-permute-done.31.right_ref = s16[8,2176]{1,0:T(8,128)(2,1)S(1)} collective-permute-done((s16[8,2176]{1,0:T(8,128)(2,1)S(1)}, s16[8,2176]{1,0:T(8,128)(2,1)S(1)}, u32[]{:S(2)}, u32[]{:S(2)}) %collective-permute-start.31) | collective-permute-done | bytes 34848 | tf_op jit(solution)/shard_map/ppermute | solution.py:368
  91.9 2.0 %collective-permute-start.36 = (s16[8,4224]{1,0:T(8,128)(2,1)S(1)}, s16[8,4224]{1,0:T(8,128)(2,1)S(1)}, u32[]{:S(2)}, u32[]{:S(2)}) collective-permute-start(s16[8,4224]{1,0:T(8,128)(2,1)S(1)} %shard_map.82.own_ref), channel_id=1, source_target_pairs={{0,64},{32,96},{64,0},{96,32},{1,65},{33,97},{65,1},{97,33},{2,66}... | collective-permute-start | bytes 202760 | tf_op jit(solution)/shard_map/ppermute | solution.py:368
  95.4 2.3 %collective-permute-done.36.far_ref = s16[8,4224]{1,0:T(8,128)(2,1)S(1)} collective-permute-done((s16[8,4224]{1,0:T(8,128)(2,1)S(1)}, s16[8,4224]{1,0:T(8,128)(2,1)S(1)}, u32[]{:S(2)}, u32[]{:S(2)}) %collective-permute-start.36) | collective-permute-done | bytes 67616 | tf_op jit(solution)/shard_map/ppermute | solution.py:368
  97.8 1.6 %collective-permute-done.35.right_ref = s16[8,4224]{1,0:T(8,128)(2,1)S(1)} collective-permute-done((s16[8,4224]{1,0:T(8,128)(2,1)S(1)}, s16[8,4224]{1,0:T(8,128)(2,1)S(1)}, u32[]{:S(2)}, u32[]{:S(2)}) %collective-permute-start.35) | collective-permute-done | bytes 67616 | tf_op jit(solution)/shard_map/ppermute | solution.py:368
  105.7 2.0 %collective-permute-done.40.far_ref = s16[8,2176]{1,0:T(8,128)(2,1)S(1)} collective-permute-done((s16[8,2176]{1,0:T(8,128)(2,1)S(1)}, s16[8,2176]{1,0:T(8,128)(2,1)S(1)}, u32[]{:S(2)}, u32[]{:S(2)}) %collective-permute-start.40) | collective-permute-done | bytes 34848 | tf_op jit(solution)/shard_map/ppermute | solution.py:368
  109.1 1.6 %collective-permute-start.43 = (s16[8,2176]{1,0:T(8,128)(2,1)S(1)}, s16[8,2176]{1,0:T(8,128)(2,1)S(1)}, u32[]{:S(2)}, u32[]{:S(2)}) collective-permute-start(s16[8,2176]{1,0:T(8,128)(2,1)S(1)} %shard_map.86.own_ref), channel_id=1, source_target_pairs={{0,2},{1,3},{2,0},{3,1},{4,6},{5,7},{6,4},{7,5},{8,10},{9,11},{10,... | collective-permute-start | bytes 104456 | tf_op jit(solution)/shard_map/ppermute | solution.py:368
  112.6 2.1 %collective-permute-done.43.far_ref = s16[8,2176]{1,0:T(8,128)(2,1)S(1)} collective-permute-done((s16[8,2176]{1,0:T(8,128)(2,1)S(1)}, s16[8,2176]{1,0:T(8,128)(2,1)S(1)}, u32[]{:S(2)}, u32[]{:S(2)}) %collective-permute-start.43) | collective-permute-done | bytes 34848 | tf_op jit(solution)/shard_map/ppermute | solution.py:368
  117.3 2.0 %collective-permute-start.47 = (f32[8,128]{1,0:T(8,128)S(1)}, f32[8,128]{1,0:T(8,128)S(1)}, u32[]{:S(2)}, u32[]{:S(2)}) collective-permute-start(f32[8,128]{1,0:T(8,128)S(1)} %add.3.own_ref), channel_id=1, source_target_pairs={{0,64},{32,96},{64,0},{96,32},{1,65},{33,97},{65,1},{97,33},{2,66}... | collective-permute-start | bytes 12296 | tf_op jit(solution)/shard_map/ppermute | solution.py:368
  122.4 1.7 %collective-permute-done.46.right_ref = f32[8,128]{1,0:T(8,128)S(1)} collective-permute-done((f32[8,128]{1,0:T(8,128)S(1)}, f32[8,128]{1,0:T(8,128)S(1)}, u32[]{:S(2)}, u32[]{:S(2)}) %collective-permute-start.46) | collective-permute-done | bytes 4128 | tf_op jit(solution)/shard_map/ppermute | solution.py:368
  (102 shorter events, 54.3 us)
Async XLA Ops:
  5.0 7.7 %collective-permute-start.3 = (s16[8,4224]{1,0:T(8,128)(2,1)S(1)}, s16[8,4224]{1,0:T(8,128)(2,1)S(1)}, u32[]{:S(2)}, u32[]{:S(2)}) collective-permute-start(s16[8,4224]{1,0:T(8,128)(2,1)S(1)} %shard_map.60.own_ref), channel_id=1, source_target_pairs={{0,64},{32,96},{64,0},{96,32},{1,65},{33,97},{65,1},{97,33},{2,66}... | collective-permute-start | bytes 202760 | tf_op jit(solution)/shard_map/ppermute | solution.py:368
  9.0 5.5 %collective-permute-start.2 = (s16[8,4224]{1,0:T(8,128)(2,1)S(1)}, s16[8,4224]{1,0:T(8,128)(2,1)S(1)}, u32[]{:S(2)}, u32[]{:S(2)}) collective-permute-start(s16[8,4224]{1,0:T(8,128)(2,1)S(1)} %shard_map.60.own_ref), channel_id=1, source_target_pairs={{0,96},{32,64},{64,32},{96,0},{1,97},{33,65},{65,33},{97,1},{2,98}... | collective-permute-start | bytes 202760 | tf_op jit(solution)/shard_map/ppermute | solution.py:368
  9.7 4.8 %collective-permute-start.1 = (s16[8,4224]{1,0:T(8,128)(2,1)S(1)}, s16[8,4224]{1,0:T(8,128)(2,1)S(1)}, u32[]{:S(2)}, u32[]{:S(2)}) collective-permute-start(s16[8,4224]{1,0:T(8,128)(2,1)S(1)} %shard_map.60.own_ref), channel_id=1, source_target_pairs={{0,32},{32,0},{64,96},{96,64},{1,33},{33,1},{65,97},{97,65},{2,34}... | collective-permute-start | bytes 202760 | tf_op jit(solution)/shard_map/ppermute | solution.py:368
  17.3 5.5 %collective-permute-start.7 = (s16[8,2176]{1,0:T(8,128)(2,1)S(1)}, s16[8,2176]{1,0:T(8,128)(2,1)S(1)}, u32[]{:S(2)}, u32[]{:S(2)}) collective-permute-start(s16[8,2176]{1,0:T(8,128)(2,1)S(1)} %shard_map.64.own_ref), channel_id=1, source_target_pairs={{0,8},{4,12},{8,0},{12,4},{1,9},{5,13},{9,1},{13,5},{2,10},{6,14},... | collective-permute-start | bytes 104456 | tf_op jit(solution)/shard_map/ppermute | solution.py:368
  20.4 5.1 %collective-permute-start.6 = (s16[8,2176]{1,0:T(8,128)(2,1)S(1)}, s16[8,2176]{1,0:T(8,128)(2,1)S(1)}, u32[]{:S(2)}, u32[]{:S(2)}) collective-permute-start(s16[8,2176]{1,0:T(8,128)(2,1)S(1)} %shard_map.64.own_ref), channel_id=1, source_target_pairs={{0,12},{4,8},{8,4},{12,0},{1,13},{5,9},{9,5},{13,1},{2,14},{6,10},... | collective-permute-start | bytes 104456 | tf_op jit(solution)/shard_map/ppermute | solution.py:368
  25.8 5.5 %collective-permute-start.10 = (s16[8,2176]{1,0:T(8,128)(2,1)S(1)}, s16[8,2176]{1,0:T(8,128)(2,1)S(1)}, u32[]{:S(2)}, u32[]{:S(2)}) collective-permute-start(s16[8,2176]{1,0:T(8,128)(2,1)S(1)} %shard_map.65.own_ref), channel_id=1, source_target_pairs={{0,2},{1,3},{2,0},{3,1},{4,6},{5,7},{6,4},{7,5},{8,10},{9,11},{10,... | collective-permute-start | bytes 104456 | tf_op jit(solution)/shard_map/ppermute | solution.py:368
  29.1 5.1 %collective-permute-start.9 = (s16[8,2176]{1,0:T(8,128)(2,1)S(1)}, s16[8,2176]{1,0:T(8,128)(2,1)S(1)}, u32[]{:S(2)}, u32[]{:S(2)}) collective-permute-start(s16[8,2176]{1,0:T(8,128)(2,1)S(1)} %shard_map.65.own_ref), channel_id=1, source_target_pairs={{0,3},{1,2},{2,1},{3,0},{4,7},{5,6},{6,5},{7,4},{8,11},{9,10},{10,... | collective-permute-start | bytes 104456 | tf_op jit(solution)/shard_map/ppermute | solution.py:368
  30.2 4.1 %collective-permute-start.8 = (s16[8,2176]{1,0:T(8,128)(2,1)S(1)}, s16[8,2176]{1,0:T(8,128)(2,1)S(1)}, u32[]{:S(2)}, u32[]{:S(2)}) collective-permute-start(s16[8,2176]{1,0:T(8,128)(2,1)S(1)} %shard_map.65.own_ref), channel_id=1, source_target_pairs={{0,1},{1,0},{2,3},{3,2},{4,5},{5,4},{6,7},{7,6},{8,9},{9,8},{10,11... | collective-permute-start | bytes 104456 | tf_op jit(solution)/shard_map/ppermute | solution.py:368
  37.0 5.9 %collective-permute-start.14 = (s16[8,4224]{1,0:T(8,128)(2,1)S(1)}, s16[8,4224]{1,0:T(8,128)(2,1)S(1)}, u32[]{:S(2)}, u32[]{:S(2)}) collective-permute-start(s16[8,4224]{1,0:T(8,128)(2,1)S(1)} %shard_map.68.own_ref), channel_id=1, source_target_pairs={{0,64},{32,96},{64,0},{96,32},{1,65},{33,97},{65,1},{97,33},{2,66}... | collective-permute-start | bytes 202760 | tf_op jit(solution)/shard_map/ppermute | solution.py:368
  38.9 5.5 %collective-permute-start.13 = (s16[8,4224]{1,0:T(8,128)(2,1)S(1)}, s16[8,4224]{1,0:T(8,128)(2,1)S(1)}, u32[]{:S(2)}, u32[]{:S(2)}) collective-permute-start(s16[8,4224]{1,0:T(8,128)(2,1)S(1)} %shard_map.68.own_ref), channel_id=1, source_target_pairs={{0,96},{32,64},{64,32},{96,0},{1,97},{33,65},{65,33},{97,1},{2,98}... | collective-permute-start | bytes 202760 | tf_op jit(solution)/shard_map/ppermute | solution.py:368
  39.9 4.6 %collective-permute-start.12 = (s16[8,4224]{1,0:T(8,128)(2,1)S(1)}, s16[8,4224]{1,0:T(8,128)(2,1)S(1)}, u32[]{:S(2)}, u32[]{:S(2)}) collective-permute-start(s16[8,4224]{1,0:T(8,128)(2,1)S(1)} %shard_map.68.own_ref), channel_id=1, source_target_pairs={{0,32},{32,0},{64,96},{96,64},{1,33},{33,1},{65,97},{97,65},{2,34}... | collective-permute-start | bytes 202760 | tf_op jit(solution)/shard_map/ppermute | solution.py:368
  47.2 5.5 %collective-permute-start.18 = (s16[8,2176]{1,0:T(8,128)(2,1)S(1)}, s16[8,2176]{1,0:T(8,128)(2,1)S(1)}, u32[]{:S(2)}, u32[]{:S(2)}) collective-permute-start(s16[8,2176]{1,0:T(8,128)(2,1)S(1)} %shard_map.71.own_ref), channel_id=1, source_target_pairs={{0,8},{4,12},{8,0},{12,4},{1,9},{5,13},{9,1},{13,5},{2,10},{6,14},... | collective-permute-start | bytes 104456 | tf_op jit(solution)/shard_map/ppermute | solution.py:368
  48.8 5.1 %collective-permute-start.17 = (s16[8,2176]{1,0:T(8,128)(2,1)S(1)}, s16[8,2176]{1,0:T(8,128)(2,1)S(1)}, u32[]{:S(2)}, u32[]{:S(2)}) collective-permute-start(s16[8,2176]{1,0:T(8,128)(2,1)S(1)} %shard_map.71.own_ref), channel_id=1, source_target_pairs={{0,12},{4,8},{8,4},{12,0},{1,13},{5,9},{9,5},{13,1},{2,14},{6,10},... | collective-permute-start | bytes 104456 | tf_op jit(solution)/shard_map/ppermute | solution.py:368
  54.2 5.7 %collective-permute-start.21 = (s16[8,2176]{1,0:T(8,128)(2,1)S(1)}, s16[8,2176]{1,0:T(8,128)(2,1)S(1)}, u32[]{:S(2)}, u32[]{:S(2)}) collective-permute-start(s16[8,2176]{1,0:T(8,128)(2,1)S(1)} %shard_map.72.own_ref), channel_id=1, source_target_pairs={{0,2},{1,3},{2,0},{3,1},{4,6},{5,7},{6,4},{7,5},{8,10},{9,11},{10,... | collective-permute-start | bytes 104456 | tf_op jit(solution)/shard_map/ppermute | solution.py:368
  55.8 5.1 %collective-permute-start.20 = (s16[8,2176]{1,0:T(8,128)(2,1)S(1)}, s16[8,2176]{1,0:T(8,128)(2,1)S(1)}, u32[]{:S(2)}, u32[]{:S(2)}) collective-permute-start(s16[8,2176]{1,0:T(8,128)(2,1)S(1)} %shard_map.72.own_ref), channel_id=1, source_target_pairs={{0,3},{1,2},{2,1},{3,0},{4,7},{5,6},{6,5},{7,4},{8,11},{9,10},{10,... | collective-permute-start | bytes 104456 | tf_op jit(solution)/shard_map/ppermute | solution.py:368
  56.8 4.2 %collective-permute-start.19 = (s16[8,2176]{1,0:T(8,128)(2,1)S(1)}, s16[8,2176]{1,0:T(8,128)(2,1)S(1)}, u32[]{:S(2)}, u32[]{:S(2)}) collective-permute-start(s16[8,2176]{1,0:T(8,128)(2,1)S(1)} %shard_map.72.own_ref), channel_id=1, source_target_pairs={{0,1},{1,0},{2,3},{3,2},{4,5},{5,4},{6,7},{7,6},{8,9},{9,8},{10,11... | collective-permute-start | bytes 104456 | tf_op jit(solution)/shard_map/ppermute | solution.py:368
  63.7 5.9 %collective-permute-start.25 = (s16[8,4224]{1,0:T(8,128)(2,1)S(1)}, s16[8,4224]{1,0:T(8,128)(2,1)S(1)}, u32[]{:S(2)}, u32[]{:S(2)}) collective-permute-start(s16[8,4224]{1,0:T(8,128)(2,1)S(1)} %shard_map.75.own_ref), channel_id=1, source_target_pairs={{0,64},{32,96},{64,0},{96,32},{1,65},{33,97},{65,1},{97,33},{2,66}... | collective-permute-start | bytes 202760 | tf_op jit(solution)/shard_map/ppermute | solution.py:368
  65.6 5.5 %collective-permute-start.24 = (s16[8,4224]{1,0:T(8,128)(2,1)S(1)}, s16[8,4224]{1,0:T(8,128)(2,1)S(1)}, u32[]{:S(2)}, u32[]{:S(2)}) collective-permute-start(s16[8,4224]{1,0:T(8,128)(2,1)S(1)} %shard_map.75.own_ref), channel_id=1, source_target_pairs={{0,96},{32,64},{64,32},{96,0},{1,97},{33,65},{65,33},{97,1},{2,98}... | collective-permute-start | bytes 202760 | tf_op jit(solution)/shard_map/ppermute | solution.py:368
  66.9 4.3 %collective-permute-start.23 = (s16[8,4224]{1,0:T(8,128)(2,1)S(1)}, s16[8,4224]{1,0:T(8,128)(2,1)S(1)}, u32[]{:S(2)}, u32[]{:S(2)}) collective-permute-start(s16[8,4224]{1,0:T(8,128)(2,1)S(1)} %shard_map.75.own_ref), channel_id=1, source_target_pairs={{0,32},{32,0},{64,96},{96,64},{1,33},{33,1},{65,97},{97,65},{2,34}... | collective-permute-start | bytes 202760 | tf_op jit(solution)/shard_map/ppermute | solution.py:368
  73.9 5.5 %collective-permute-start.29 = (s16[8,2176]{1,0:T(8,128)(2,1)S(1)}, s16[8,2176]{1,0:T(8,128)(2,1)S(1)}, u32[]{:S(2)}, u32[]{:S(2)}) collective-permute-start(s16[8,2176]{1,0:T(8,128)(2,1)S(1)} %shard_map.78.own_ref), channel_id=1, source_target_pairs={{0,8},{4,12},{8,0},{12,4},{1,9},{5,13},{9,1},{13,5},{2,10},{6,14},... | collective-permute-start | bytes 104456 | tf_op jit(solution)/shard_map/ppermute | solution.py:368
  76.3 5.1 %collective-permute-start.28 = (s16[8,2176]{1,0:T(8,128)(2,1)S(1)}, s16[8,2176]{1,0:T(8,128)(2,1)S(1)}, u32[]{:S(2)}, u32[]{:S(2)}) collective-permute-start(s16[8,2176]{1,0:T(8,128)(2,1)S(1)} %shard_map.78.own_ref), channel_id=1, source_target_pairs={{0,12},{4,8},{8,4},{12,0},{1,13},{5,9},{9,5},{13,1},{2,14},{6,10},... | collective-permute-start | bytes 104456 | tf_op jit(solution)/shard_map/ppermute | solution.py:368
  81.7 5.5 %collective-permute-start.32 = (s16[8,2176]{1,0:T(8,128)(2,1)S(1)}, s16[8,2176]{1,0:T(8,128)(2,1)S(1)}, u32[]{:S(2)}, u32[]{:S(2)}) collective-permute-start(s16[8,2176]{1,0:T(8,128)(2,1)S(1)} %shard_map.79.own_ref), channel_id=1, source_target_pairs={{0,2},{1,3},{2,0},{3,1},{4,6},{5,7},{6,4},{7,5},{8,10},{9,11},{10,... | collective-permute-start | bytes 104456 | tf_op jit(solution)/shard_map/ppermute | solution.py:368
  84.0 5.1 %collective-permute-start.31 = (s16[8,2176]{1,0:T(8,128)(2,1)S(1)}, s16[8,2176]{1,0:T(8,128)(2,1)S(1)}, u32[]{:S(2)}, u32[]{:S(2)}) collective-permute-start(s16[8,2176]{1,0:T(8,128)(2,1)S(1)} %shard_map.79.own_ref), channel_id=1, source_target_pairs={{0,3},{1,2},{2,1},{3,0},{4,7},{5,6},{6,5},{7,4},{8,11},{9,10},{10,... | collective-permute-start | bytes 104456 | tf_op jit(solution)/shard_map/ppermute | solution.py:368
  91.9 5.9 %collective-permute-start.36 = (s16[8,4224]{1,0:T(8,128)(2,1)S(1)}, s16[8,4224]{1,0:T(8,128)(2,1)S(1)}, u32[]{:S(2)}, u32[]{:S(2)}) collective-permute-start(s16[8,4224]{1,0:T(8,128)(2,1)S(1)} %shard_map.82.own_ref), channel_id=1, source_target_pairs={{0,64},{32,96},{64,0},{96,32},{1,65},{33,97},{65,1},{97,33},{2,66}... | collective-permute-start | bytes 202760 | tf_op jit(solution)/shard_map/ppermute | solution.py:368
  93.8 5.5 %collective-permute-start.35 = (s16[8,4224]{1,0:T(8,128)(2,1)S(1)}, s16[8,4224]{1,0:T(8,128)(2,1)S(1)}, u32[]{:S(2)}, u32[]{:S(2)}) collective-permute-start(s16[8,4224]{1,0:T(8,128)(2,1)S(1)} %shard_map.82.own_ref), channel_id=1, source_target_pairs={{0,96},{32,64},{64,32},{96,0},{1,97},{33,65},{65,33},{97,1},{2,98}... | collective-permute-start | bytes 202760 | tf_op jit(solution)/shard_map/ppermute | solution.py:368
  95.0 4.3 %collective-permute-start.34 = (s16[8,4224]{1,0:T(8,128)(2,1)S(1)}, s16[8,4224]{1,0:T(8,128)(2,1)S(1)}, u32[]{:S(2)}, u32[]{:S(2)}) collective-permute-start(s16[8,4224]{1,0:T(8,128)(2,1)S(1)} %shard_map.82.own_ref), channel_id=1, source_target_pairs={{0,32},{32,0},{64,96},{96,64},{1,33},{33,1},{65,97},{97,65},{2,34}... | collective-permute-start | bytes 202760 | tf_op jit(solution)/shard_map/ppermute | solution.py:368
  102.1 5.5 %collective-permute-start.40 = (s16[8,2176]{1,0:T(8,128)(2,1)S(1)}, s16[8,2176]{1,0:T(8,128)(2,1)S(1)}, u32[]{:S(2)}, u32[]{:S(2)}) collective-permute-start(s16[8,2176]{1,0:T(8,128)(2,1)S(1)} %shard_map.85.own_ref), channel_id=1, source_target_pairs={{0,8},{4,12},{8,0},{12,4},{1,9},{5,13},{9,1},{13,5},{2,10},{6,14},... | collective-permute-start | bytes 104456 | tf_op jit(solution)/shard_map/ppermute | solution.py:368
  103.6 5.1 %collective-permute-start.39 = (s16[8,2176]{1,0:T(8,128)(2,1)S(1)}, s16[8,2176]{1,0:T(8,128)(2,1)S(1)}, u32[]{:S(2)}, u32[]{:S(2)}) collective-permute-start(s16[8,2176]{1,0:T(8,128)(2,1)S(1)} %shard_map.85.own_ref), channel_id=1, source_target_pairs={{0,12},{4,8},{8,4},{12,0},{1,13},{5,9},{9,5},{13,1},{2,14},{6,10},... | collective-permute-start | bytes 104456 | tf_op jit(solution)/shard_map/ppermute | solution.py:368
  109.1 5.7 %collective-permute-start.43 = (s16[8,2176]{1,0:T(8,128)(2,1)S(1)}, s16[8,2176]{1,0:T(8,128)(2,1)S(1)}, u32[]{:S(2)}, u32[]{:S(2)}) collective-permute-start(s16[8,2176]{1,0:T(8,128)(2,1)S(1)} %shard_map.86.own_ref), channel_id=1, source_target_pairs={{0,2},{1,3},{2,0},{3,1},{4,6},{5,7},{6,4},{7,5},{8,10},{9,11},{10,... | collective-permute-start | bytes 104456 | tf_op jit(solution)/shard_map/ppermute | solution.py:368
  110.7 5.1 %collective-permute-start.42 = (s16[8,2176]{1,0:T(8,128)(2,1)S(1)}, s16[8,2176]{1,0:T(8,128)(2,1)S(1)}, u32[]{:S(2)}, u32[]{:S(2)}) collective-permute-start(s16[8,2176]{1,0:T(8,128)(2,1)S(1)} %shard_map.86.own_ref), channel_id=1, source_target_pairs={{0,3},{1,2},{2,1},{3,0},{4,7},{5,6},{6,5},{7,4},{8,11},{9,10},{10,... | collective-permute-start | bytes 104456 | tf_op jit(solution)/shard_map/ppermute | solution.py:368
  117.3 5.1 %collective-permute-start.47 = (f32[8,128]{1,0:T(8,128)S(1)}, f32[8,128]{1,0:T(8,128)S(1)}, u32[]{:S(2)}, u32[]{:S(2)}) collective-permute-start(f32[8,128]{1,0:T(8,128)S(1)} %add.3.own_ref), channel_id=1, source_target_pairs={{0,64},{32,96},{64,0},{96,32},{1,65},{33,97},{65,1},{97,33},{2,66}... | collective-permute-start | bytes 12296 | tf_op jit(solution)/shard_map/ppermute | solution.py:368
  119.2 4.8 %collective-permute-start.46 = (f32[8,128]{1,0:T(8,128)S(1)}, f32[8,128]{1,0:T(8,128)S(1)}, u32[]{:S(2)}, u32[]{:S(2)}) collective-permute-start(f32[8,128]{1,0:T(8,128)S(1)} %add.3.own_ref), channel_id=1, source_target_pairs={{0,96},{32,64},{64,32},{96,0},{1,97},{33,65},{65,33},{97,1},{2,98}... | collective-permute-start | bytes 12296 | tf_op jit(solution)/shard_map/ppermute | solution.py:368
  (19 other events, 72.9 us)

commit v12 on v10

--- a/solution.py
+++ b/solution.py
@@ -8,7 +8,7 @@
 from jax.sharding import Mesh, PartitionSpec as P
 
 BLK_DEV = 32
-HEAD = 20
+HEAD = 16
 GROUP = 4
 ITERS = 4
 EPS = 1e-06

time: 125 us -> 125 us (level)
  transfers between devices with their start and end apart: 48 -> 48, of which waited for: 34 -> 35; matrix products, arithmetic and copies ran while one was open for 0% -> 0% of each run, Pallas kernels for 8% -> 8%
where the time goes in v12:
time: 125 us
  waiting for transfers between devices  50.1 us (40%)
  starting transfers between devices  50 us (40%)
  Pallas kernels  23.7 us (19%)
    ppermute x39, starting transfers between devices, spread(): lax.ppermute(value, axis, [(i, i ^ by) for i in range(n)])  49.3 us
    ppermute x39, waiting for transfers between devices, spread(): lax.ppermute(value, axis, [(i, i ^ by) for i in range(n)])  45.1 us
    pallas_call x31, Pallas kernels, call(): pl.pallas_call(body, out_shape=outs, in_specs=specs, out_specs=out_specs...  23.7 us
    ppermute x9, waiting for transfers between devices, swap(): return lax.ppermute(value, 'core', [(0, 1), (1, 0)])  4.99 us
  transfers between devices with their start and end apart: 48, of which 35 were waited for; matrix products, arithmetic and copies ran while one was open for 0% of the time, Pallas kernels for 8%

profile of v12, /device:TPU:0, one launch (start us, length us, event | category | flops | bytes accessed | tf_op | source)
XLA Modules:
  0.0 124.8 jit_solution(8719280175230425273)
XLA Ops:
  0.7 2.8 %shard_map.59 = (f32[8,4224]{1,0:T(8,128)S(1)}, f32[8,4224]{1,0:T(8,128)S(1)}, bf16[8,4,256,256]{3,2,1,0:T(8,128)(2,1)S(1)}) custom-call(s32[4,8]{1,0:T(4,128)} %bitcast.11, s32[1,8]{1,0:T(1,128)} %bitcast.13, f32[8,2048]{1,0:T(8,128)} %prev_ref.3, bf16[8,4,256,256]{3,2,1,0:T(8,128)(2,1)} %source_ref.1), custom_call_target="tpu_custom_call" | custom-call | tf_op jit(solution)/shard_map/pallas_call | solution.py:344
  5.0 4.0 %collective-permute-start.3 = (s16[8,4224]{1,0:T(8,128)(2,1)S(1)}, s16[8,4224]{1,0:T(8,128)(2,1)S(1)}, u32[]{:S(2)}, u32[]{:S(2)}) collective-permute-start(s16[8,4224]{1,0:T(8,128)(2,1)S(1)} %shard_map.60.own_ref), channel_id=1, source_target_pairs={{0,64},{32,96},{64,0},{96,32},{1,65},{33,97},{65,1},{97,33},{2,66}... | collective-permute-start | bytes 202760 | tf_op jit(solution)/shard_map/ppermute | solution.py:368
  10.1 2.6 %shard_map.61 = (bf16[32,256,256]{2,1,0:T(8,128)(2,1)S(1)}, s32[163]{0:T(256)S(1)}) custom-call(s32[4,8]{1,0:T(4,128)S(1)} %bitcast.12, s32[1,8]{1,0:T(1,128)S(1)} %bitcast.14, bf16[32,256,256]{2,1,0:T(8,128)(2,1)S(1)} %bitcast.4), custom_call_target="tpu_custom_call" | custom-call | tf_op jit(solution)/shard_map/pallas_call | solution.py:344
  12.7 1.9 %collective-permute-done.2.right_ref = s16[8,4224]{1,0:T(8,128)(2,1)S(1)} collective-permute-done((s16[8,4224]{1,0:T(8,128)(2,1)S(1)}, s16[8,4224]{1,0:T(8,128)(2,1)S(1)}, u32[]{:S(2)}, u32[]{:S(2)}) %collective-permute-start.2) | collective-permute-done | bytes 67616 | tf_op jit(solution)/shard_map/ppermute | solution.py:368
  17.3 3.1 %collective-permute-start.7 = (s16[8,2176]{1,0:T(8,128)(2,1)S(1)}, s16[8,2176]{1,0:T(8,128)(2,1)S(1)}, u32[]{:S(2)}, u32[]{:S(2)}) collective-permute-start(s16[8,2176]{1,0:T(8,128)(2,1)S(1)} %shard_map.64.own_ref), channel_id=1, source_target_pairs={{0,8},{4,12},{8,0},{12,4},{1,9},{5,13},{9,1},{13,5},{2,10},{6,14},... | collective-permute-start | bytes 104456 | tf_op jit(solution)/shard_map/ppermute | solution.py:368
  22.8 2.7 %collective-permute-done.6.right_ref = s16[8,2176]{1,0:T(8,128)(2,1)S(1)} collective-permute-done((s16[8,2176]{1,0:T(8,128)(2,1)S(1)}, s16[8,2176]{1,0:T(8,128)(2,1)S(1)}, u32[]{:S(2)}, u32[]{:S(2)}) %collective-permute-start.6) | collective-permute-done | bytes 34848 | tf_op jit(solution)/shard_map/ppermute | solution.py:368
  25.8 3.3 %collective-permute-start.10 = (s16[8,2176]{1,0:T(8,128)(2,1)S(1)}, s16[8,2176]{1,0:T(8,128)(2,1)S(1)}, u32[]{:S(2)}, u32[]{:S(2)}) collective-permute-start(s16[8,2176]{1,0:T(8,128)(2,1)S(1)} %shard_map.65.own_ref), channel_id=1, source_target_pairs={{0,2},{1,3},{2,0},{3,1},{4,6},{5,7},{6,4},{7,5},{8,10},{9,11},{10,... | collective-permute-start | bytes 104456 | tf_op jit(solution)/shard_map/ppermute | solution.py:368
  31.3 2.9 %collective-permute-done.9.right_ref = s16[8,2176]{1,0:T(8,128)(2,1)S(1)} collective-permute-done((s16[8,2176]{1,0:T(8,128)(2,1)S(1)}, s16[8,2176]{1,0:T(8,128)(2,1)S(1)}, u32[]{:S(2)}, u32[]{:S(2)}) %collective-permute-start.9) | collective-permute-done | bytes 34848 | tf_op jit(solution)/shard_map/ppermute | solution.py:368
  36.9 1.9 %collective-permute-start.14 = (s16[8,4224]{1,0:T(8,128)(2,1)S(1)}, s16[8,4224]{1,0:T(8,128)(2,1)S(1)}, u32[]{:S(2)}, u32[]{:S(2)}) collective-permute-start(s16[8,4224]{1,0:T(8,128)(2,1)S(1)} %shard_map.68.own_ref), channel_id=1, source_target_pairs={{0,64},{32,96},{64,0},{96,32},{1,65},{33,97},{65,1},{97,33},{2,66}... | collective-permute-start | bytes 202760 | tf_op jit(solution)/shard_map/ppermute | solution.py:368
  40.5 2.3 %collective-permute-done.14.far_ref = s16[8,4224]{1,0:T(8,128)(2,1)S(1)} collective-permute-done((s16[8,4224]{1,0:T(8,128)(2,1)S(1)}, s16[8,4224]{1,0:T(8,128)(2,1)S(1)}, u32[]{:S(2)}, u32[]{:S(2)}) %collective-permute-start.14) | collective-permute-done | bytes 67616 | tf_op jit(solution)/shard_map/ppermute | solution.py:368
  42.8 1.5 %collective-permute-done.13.right_ref = s16[8,4224]{1,0:T(8,128)(2,1)S(1)} collective-permute-done((s16[8,4224]{1,0:T(8,128)(2,1)S(1)}, s16[8,4224]{1,0:T(8,128)(2,1)S(1)}, u32[]{:S(2)}, u32[]{:S(2)}) %collective-permute-start.13) | collective-permute-done | bytes 67616 | tf_op jit(solution)/shard_map/ppermute | solution.py:368
  47.1 1.7 %collective-permute-start.18 = (s16[8,2176]{1,0:T(8,128)(2,1)S(1)}, s16[8,2176]{1,0:T(8,128)(2,1)S(1)}, u32[]{:S(2)}, u32[]{:S(2)}) collective-permute-start(s16[8,2176]{1,0:T(8,128)(2,1)S(1)} %shard_map.71.own_ref), channel_id=1, source_target_pairs={{0,8},{4,12},{8,0},{12,4},{1,9},{5,13},{9,1},{13,5},{2,10},{6,14},... | collective-permute-start | bytes 104456 | tf_op jit(solution)/shard_map/ppermute | solution.py:368
  50.7 2.0 %collective-permute-done.18.far_ref = s16[8,2176]{1,0:T(8,128)(2,1)S(1)} collective-permute-done((s16[8,2176]{1,0:T(8,128)(2,1)S(1)}, s16[8,2176]{1,0:T(8,128)(2,1)S(1)}, u32[]{:S(2)}, u32[]{:S(2)}) %collective-permute-start.18) | collective-permute-done | bytes 34848 | tf_op jit(solution)/shard_map/ppermute | solution.py:368
  57.8 2.3 %collective-permute-done.21.far_ref = s16[8,2176]{1,0:T(8,128)(2,1)S(1)} collective-permute-done((s16[8,2176]{1,0:T(8,128)(2,1)S(1)}, s16[8,2176]{1,0:T(8,128)(2,1)S(1)}, u32[]{:S(2)}, u32[]{:S(2)}) %collective-permute-start.21) | collective-permute-done | bytes 34848 | tf_op jit(solution)/shard_map/ppermute | solution.py:368
  63.6 1.9 %collective-permute-start.25 = (s16[8,4224]{1,0:T(8,128)(2,1)S(1)}, s16[8,4224]{1,0:T(8,128)(2,1)S(1)}, u32[]{:S(2)}, u32[]{:S(2)}) collective-permute-start(s16[8,4224]{1,0:T(8,128)(2,1)S(1)} %shard_map.75.own_ref), channel_id=1, source_target_pairs={{0,64},{32,96},{64,0},{96,32},{1,65},{33,97},{65,1},{97,33},{2,66}... | collective-permute-start | bytes 202760 | tf_op jit(solution)/shard_map/ppermute | solution.py:368
  67.1 2.3 %collective-permute-done.25.far_ref = s16[8,4224]{1,0:T(8,128)(2,1)S(1)} collective-permute-done((s16[8,4224]{1,0:T(8,128)(2,1)S(1)}, s16[8,4224]{1,0:T(8,128)(2,1)S(1)}, u32[]{:S(2)}, u32[]{:S(2)}) %collective-permute-start.25) | collective-permute-done | bytes 67616 | tf_op jit(solution)/shard_map/ppermute | solution.py:368
  69.5 1.5 %collective-permute-done.24.right_ref = s16[8,4224]{1,0:T(8,128)(2,1)S(1)} collective-permute-done((s16[8,4224]{1,0:T(8,128)(2,1)S(1)}, s16[8,4224]{1,0:T(8,128)(2,1)S(1)}, u32[]{:S(2)}, u32[]{:S(2)}) %collective-permute-start.24) | collective-permute-done | bytes 67616 | tf_op jit(solution)/shard_map/ppermute | solution.py:368
  73.7 2.5 %collective-permute-start.29 = (s16[8,2176]{1,0:T(8,128)(2,1)S(1)}, s16[8,2176]{1,0:T(8,128)(2,1)S(1)}, u32[]{:S(2)}, u32[]{:S(2)}) collective-permute-start(s16[8,2176]{1,0:T(8,128)(2,1)S(1)} %shard_map.78.own_ref), channel_id=1, source_target_pairs={{0,8},{4,12},{8,0},{12,4},{1,9},{5,13},{9,1},{13,5},{2,10},{6,14},... | collective-permute-start | bytes 104456 | tf_op jit(solution)/shard_map/ppermute | solution.py:368
  77.3 1.9 %collective-permute-done.29.far_ref = s16[8,2176]{1,0:T(8,128)(2,1)S(1)} collective-permute-done((s16[8,2176]{1,0:T(8,128)(2,1)S(1)}, s16[8,2176]{1,0:T(8,128)(2,1)S(1)}, u32[]{:S(2)}, u32[]{:S(2)}) %collective-permute-start.29) | collective-permute-done | bytes 34848 | tf_op jit(solution)/shard_map/ppermute | solution.py:368
  79.3 2.2 %collective-permute-done.28.right_ref = s16[8,2176]{1,0:T(8,128)(2,1)S(1)} collective-permute-done((s16[8,2176]{1,0:T(8,128)(2,1)S(1)}, s16[8,2176]{1,0:T(8,128)(2,1)S(1)}, u32[]{:S(2)}, u32[]{:S(2)}) %collective-permute-start.28) | collective-permute-done | bytes 34848 | tf_op jit(solution)/shard_map/ppermute | solution.py:368
  81.7 2.1 %collective-permute-start.32 = (s16[8,2176]{1,0:T(8,128)(2,1)S(1)}, s16[8,2176]{1,0:T(8,128)(2,1)S(1)}, u32[]{:S(2)}, u32[]{:S(2)}) collective-permute-start(s16[8,2176]{1,0:T(8,128)(2,1)S(1)} %shard_map.79.own_ref), channel_id=1, source_target_pairs={{0,2},{1,3},{2,0},{3,1},{4,6},{5,7},{6,4},{7,5},{8,10},{9,11},{10,... | collective-permute-start | bytes 104456 | tf_op jit(solution)/shard_map/ppermute | solution.py:368
  85.3 2.0 %collective-permute-done.32.far_ref = s16[8,2176]{1,0:T(8,128)(2,1)S(1)} collective-permute-done((s16[8,2176]{1,0:T(8,128)(2,1)S(1)}, s16[8,2176]{1,0:T(8,128)(2,1)S(1)}, u32[]{:S(2)}, u32[]{:S(2)}) %collective-permute-start.32) | collective-permute-done | bytes 34848 | tf_op jit(solution)/shard_map/ppermute | solution.py:368
  87.2 1.7 %collective-permute-done.31.right_ref = s16[8,2176]{1,0:T(8,128)(2,1)S(1)} collective-permute-done((s16[8,2176]{1,0:T(8,128)(2,1)S(1)}, s16[8,2176]{1,0:T(8,128)(2,1)S(1)}, u32[]{:S(2)}, u32[]{:S(2)}) %collective-permute-start.31) | collective-permute-done | bytes 34848 | tf_op jit(solution)/shard_map/ppermute | solution.py:368
  91.7 1.9 %collective-permute-start.36 = (s16[8,4224]{1,0:T(8,128)(2,1)S(1)}, s16[8,4224]{1,0:T(8,128)(2,1)S(1)}, u32[]{:S(2)}, u32[]{:S(2)}) collective-permute-start(s16[8,4224]{1,0:T(8,128)(2,1)S(1)} %shard_map.82.own_ref), channel_id=1, source_target_pairs={{0,64},{32,96},{64,0},{96,32},{1,65},{33,97},{65,1},{97,33},{2,66}... | collective-permute-start | bytes 202760 | tf_op jit(solution)/shard_map/ppermute | solution.py:368
  95.2 2.3 %collective-permute-done.36.far_ref = s16[8,4224]{1,0:T(8,128)(2,1)S(1)} collective-permute-done((s16[8,4224]{1,0:T(8,128)(2,1)S(1)}, s16[8,4224]{1,0:T(8,128)(2,1)S(1)}, u32[]{:S(2)}, u32[]{:S(2)}) %collective-permute-start.36) | collective-permute-done | bytes 67616 | tf_op jit(solution)/shard_map/ppermute | solution.py:368
  97.6 1.5 %collective-permute-done.35.right_ref = s16[8,4224]{1,0:T(8,128)(2,1)S(1)} collective-permute-done((s16[8,4224]{1,0:T(8,128)(2,1)S(1)}, s16[8,4224]{1,0:T(8,128)(2,1)S(1)}, u32[]{:S(2)}, u32[]{:S(2)}) %collective-permute-start.35) | collective-permute-done | bytes 67616 | tf_op jit(solution)/shard_map/ppermute | solution.py:368
  101.8 1.9 %collective-permute-start.40 = (s16[8,2176]{1,0:T(8,128)(2,1)S(1)}, s16[8,2176]{1,0:T(8,128)(2,1)S(1)}, u32[]{:S(2)}, u32[]{:S(2)}) collective-permute-start(s16[8,2176]{1,0:T(8,128)(2,1)S(1)} %shard_map.85.own_ref), channel_id=1, source_target_pairs={{0,8},{4,12},{8,0},{12,4},{1,9},{5,13},{9,1},{13,5},{2,10},{6,14},... | collective-permute-start | bytes 104456 | tf_op jit(solution)/shard_map/ppermute | solution.py:368
  105.4 2.0 %collective-permute-done.40.far_ref = s16[8,2176]{1,0:T(8,128)(2,1)S(1)} collective-permute-done((s16[8,2176]{1,0:T(8,128)(2,1)S(1)}, s16[8,2176]{1,0:T(8,128)(2,1)S(1)}, u32[]{:S(2)}, u32[]{:S(2)}) %collective-permute-start.40) | collective-permute-done | bytes 34848 | tf_op jit(solution)/shard_map/ppermute | solution.py:368
  107.4 1.5 %collective-permute-done.39.right_ref = s16[8,2176]{1,0:T(8,128)(2,1)S(1)} collective-permute-done((s16[8,2176]{1,0:T(8,128)(2,1)S(1)}, s16[8,2176]{1,0:T(8,128)(2,1)S(1)}, u32[]{:S(2)}, u32[]{:S(2)}) %collective-permute-start.39) | collective-permute-done | bytes 34848 | tf_op jit(solution)/shard_map/ppermute | solution.py:368
  112.7 2.2 %collective-permute-done.43.far_ref = s16[8,2176]{1,0:T(8,128)(2,1)S(1)} collective-permute-done((s16[8,2176]{1,0:T(8,128)(2,1)S(1)}, s16[8,2176]{1,0:T(8,128)(2,1)S(1)}, u32[]{:S(2)}, u32[]{:S(2)}) %collective-permute-start.43) | collective-permute-done | bytes 34848 | tf_op jit(solution)/shard_map/ppermute | solution.py:368
  117.2 1.9 %collective-permute-start.47 = (f32[8,128]{1,0:T(8,128)S(1)}, f32[8,128]{1,0:T(8,128)S(1)}, u32[]{:S(2)}, u32[]{:S(2)}) collective-permute-start(f32[8,128]{1,0:T(8,128)S(1)} %add.3.own_ref), channel_id=1, source_target_pairs={{0,64},{32,96},{64,0},{96,32},{1,65},{33,97},{65,1},{97,33},{2,66}... | collective-permute-start | bytes 12296 | tf_op jit(solution)/shard_map/ppermute | solution.py:368
  122.3 1.6 %collective-permute-done.46.right_ref = f32[8,128]{1,0:T(8,128)S(1)} collective-permute-done((f32[8,128]{1,0:T(8,128)S(1)}, f32[8,128]{1,0:T(8,128)S(1)}, u32[]{:S(2)}, u32[]{:S(2)}) %collective-permute-start.46) | collective-permute-done | bytes 4128 | tf_op jit(solution)/shard_map/ppermute | solution.py:368
  (102 shorter events, 53.8 us)
Async XLA Ops:
  5.0 7.7 %collective-permute-start.3 = (s16[8,4224]{1,0:T(8,128)(2,1)S(1)}, s16[8,4224]{1,0:T(8,128)(2,1)S(1)}, u32[]{:S(2)}, u32[]{:S(2)}) collective-permute-start(s16[8,4224]{1,0:T(8,128)(2,1)S(1)} %shard_map.60.own_ref), channel_id=1, source_target_pairs={{0,64},{32,96},{64,0},{96,32},{1,65},{33,97},{65,1},{97,33},{2,66}... | collective-permute-start | bytes 202760 | tf_op jit(solution)/shard_map/ppermute | solution.py:368
  9.0 5.5 %collective-permute-start.2 = (s16[8,4224]{1,0:T(8,128)(2,1)S(1)}, s16[8,4224]{1,0:T(8,128)(2,1)S(1)}, u32[]{:S(2)}, u32[]{:S(2)}) collective-permute-start(s16[8,4224]{1,0:T(8,128)(2,1)S(1)} %shard_map.60.own_ref), channel_id=1, source_target_pairs={{0,96},{32,64},{64,32},{96,0},{1,97},{33,65},{65,33},{97,1},{2,98}... | collective-permute-start | bytes 202760 | tf_op jit(solution)/shard_map/ppermute | solution.py:368
  9.7 4.8 %collective-permute-start.1 = (s16[8,4224]{1,0:T(8,128)(2,1)S(1)}, s16[8,4224]{1,0:T(8,128)(2,1)S(1)}, u32[]{:S(2)}, u32[]{:S(2)}) collective-permute-start(s16[8,4224]{1,0:T(8,128)(2,1)S(1)} %shard_map.60.own_ref), channel_id=1, source_target_pairs={{0,32},{32,0},{64,96},{96,64},{1,33},{33,1},{65,97},{97,65},{2,34}... | collective-permute-start | bytes 202760 | tf_op jit(solution)/shard_map/ppermute | solution.py:368
  17.3 5.5 %collective-permute-start.7 = (s16[8,2176]{1,0:T(8,128)(2,1)S(1)}, s16[8,2176]{1,0:T(8,128)(2,1)S(1)}, u32[]{:S(2)}, u32[]{:S(2)}) collective-permute-start(s16[8,2176]{1,0:T(8,128)(2,1)S(1)} %shard_map.64.own_ref), channel_id=1, source_target_pairs={{0,8},{4,12},{8,0},{12,4},{1,9},{5,13},{9,1},{13,5},{2,10},{6,14},... | collective-permute-start | bytes 104456 | tf_op jit(solution)/shard_map/ppermute | solution.py:368
  20.3 5.1 %collective-permute-start.6 = (s16[8,2176]{1,0:T(8,128)(2,1)S(1)}, s16[8,2176]{1,0:T(8,128)(2,1)S(1)}, u32[]{:S(2)}, u32[]{:S(2)}) collective-permute-start(s16[8,2176]{1,0:T(8,128)(2,1)S(1)} %shard_map.64.own_ref), channel_id=1, source_target_pairs={{0,12},{4,8},{8,4},{12,0},{1,13},{5,9},{9,5},{13,1},{2,14},{6,10},... | collective-permute-start | bytes 104456 | tf_op jit(solution)/shard_map/ppermute | solution.py:368
  25.8 5.5 %collective-permute-start.10 = (s16[8,2176]{1,0:T(8,128)(2,1)S(1)}, s16[8,2176]{1,0:T(8,128)(2,1)S(1)}, u32[]{:S(2)}, u32[]{:S(2)}) collective-permute-start(s16[8,2176]{1,0:T(8,128)(2,1)S(1)} %shard_map.65.own_ref), channel_id=1, source_target_pairs={{0,2},{1,3},{2,0},{3,1},{4,6},{5,7},{6,4},{7,5},{8,10},{9,11},{10,... | collective-permute-start | bytes 104456 | tf_op jit(solution)/shard_map/ppermute | solution.py:368
  29.1 5.1 %collective-permute-start.9 = (s16[8,2176]{1,0:T(8,128)(2,1)S(1)}, s16[8,2176]{1,0:T(8,128)(2,1)S(1)}, u32[]{:S(2)}, u32[]{:S(2)}) collective-permute-start(s16[8,2176]{1,0:T(8,128)(2,1)S(1)} %shard_map.65.own_ref), channel_id=1, source_target_pairs={{0,3},{1,2},{2,1},{3,0},{4,7},{5,6},{6,5},{7,4},{8,11},{9,10},{10,... | collective-permute-start | bytes 104456 | tf_op jit(solution)/shard_map/ppermute | solution.py:368
  36.9 5.9 %collective-permute-start.14 = (s16[8,4224]{1,0:T(8,128)(2,1)S(1)}, s16[8,4224]{1,0:T(8,128)(2,1)S(1)}, u32[]{:S(2)}, u32[]{:S(2)}) collective-permute-start(s16[8,4224]{1,0:T(8,128)(2,1)S(1)} %shard_map.68.own_ref), channel_id=1, source_target_pairs={{0,64},{32,96},{64,0},{96,32},{1,65},{33,97},{65,1},{97,33},{2,66}... | collective-permute-start | bytes 202760 | tf_op jit(solution)/shard_map/ppermute | solution.py:368
  38.9 5.5 %collective-permute-start.13 = (s16[8,4224]{1,0:T(8,128)(2,1)S(1)}, s16[8,4224]{1,0:T(8,128)(2,1)S(1)}, u32[]{:S(2)}, u32[]{:S(2)}) collective-permute-start(s16[8,4224]{1,0:T(8,128)(2,1)S(1)} %shard_map.68.own_ref), channel_id=1, source_target_pairs={{0,96},{32,64},{64,32},{96,0},{1,97},{33,65},{65,33},{97,1},{2,98}... | collective-permute-start | bytes 202760 | tf_op jit(solution)/shard_map/ppermute | solution.py:368
  39.8 4.6 %collective-permute-start.12 = (s16[8,4224]{1,0:T(8,128)(2,1)S(1)}, s16[8,4224]{1,0:T(8,128)(2,1)S(1)}, u32[]{:S(2)}, u32[]{:S(2)}) collective-permute-start(s16[8,4224]{1,0:T(8,128)(2,1)S(1)} %shard_map.68.own_ref), channel_id=1, source_target_pairs={{0,32},{32,0},{64,96},{96,64},{1,33},{33,1},{65,97},{97,65},{2,34}... | collective-permute-start | bytes 202760 | tf_op jit(solution)/shard_map/ppermute | solution.py:368
  47.1 5.5 %collective-permute-start.18 = (s16[8,2176]{1,0:T(8,128)(2,1)S(1)}, s16[8,2176]{1,0:T(8,128)(2,1)S(1)}, u32[]{:S(2)}, u32[]{:S(2)}) collective-permute-start(s16[8,2176]{1,0:T(8,128)(2,1)S(1)} %shard_map.71.own_ref), channel_id=1, source_target_pairs={{0,8},{4,12},{8,0},{12,4},{1,9},{5,13},{9,1},{13,5},{2,10},{6,14},... | collective-permute-start | bytes 104456 | tf_op jit(solution)/shard_map/ppermute | solution.py:368
  48.8 5.1 %collective-permute-start.17 = (s16[8,2176]{1,0:T(8,128)(2,1)S(1)}, s16[8,2176]{1,0:T(8,128)(2,1)S(1)}, u32[]{:S(2)}, u32[]{:S(2)}) collective-permute-start(s16[8,2176]{1,0:T(8,128)(2,1)S(1)} %shard_map.71.own_ref), channel_id=1, source_target_pairs={{0,12},{4,8},{8,4},{12,0},{1,13},{5,9},{9,5},{13,1},{2,14},{6,10},... | collective-permute-start | bytes 104456 | tf_op jit(solution)/shard_map/ppermute | solution.py:368
  49.8 4.2 %collective-permute-start.16 = (s16[8,2176]{1,0:T(8,128)(2,1)S(1)}, s16[8,2176]{1,0:T(8,128)(2,1)S(1)}, u32[]{:S(2)}, u32[]{:S(2)}) collective-permute-start(s16[8,2176]{1,0:T(8,128)(2,1)S(1)} %shard_map.71.own_ref), channel_id=1, source_target_pairs={{0,4},{4,0},{8,12},{12,8},{1,5},{5,1},{9,13},{13,9},{2,6},{6,2},{1... | collective-permute-start | bytes 104456 | tf_op jit(solution)/shard_map/ppermute | solution.py:368
  54.3 5.9 %collective-permute-start.21 = (s16[8,2176]{1,0:T(8,128)(2,1)S(1)}, s16[8,2176]{1,0:T(8,128)(2,1)S(1)}, u32[]{:S(2)}, u32[]{:S(2)}) collective-permute-start(s16[8,2176]{1,0:T(8,128)(2,1)S(1)} %shard_map.72.own_ref), channel_id=1, source_target_pairs={{0,2},{1,3},{2,0},{3,1},{4,6},{5,7},{6,4},{7,5},{8,10},{9,11},{10,... | collective-permute-start | bytes 104456 | tf_op jit(solution)/shard_map/ppermute | solution.py:368
  55.7 5.1 %collective-permute-start.20 = (s16[8,2176]{1,0:T(8,128)(2,1)S(1)}, s16[8,2176]{1,0:T(8,128)(2,1)S(1)}, u32[]{:S(2)}, u32[]{:S(2)}) collective-permute-start(s16[8,2176]{1,0:T(8,128)(2,1)S(1)} %shard_map.72.own_ref), channel_id=1, source_target_pairs={{0,3},{1,2},{2,1},{3,0},{4,7},{5,6},{6,5},{7,4},{8,11},{9,10},{10,... | collective-permute-start | bytes 104456 | tf_op jit(solution)/shard_map/ppermute | solution.py:368
  56.7 4.2 %collective-permute-start.19 = (s16[8,2176]{1,0:T(8,128)(2,1)S(1)}, s16[8,2176]{1,0:T(8,128)(2,1)S(1)}, u32[]{:S(2)}, u32[]{:S(2)}) collective-permute-start(s16[8,2176]{1,0:T(8,128)(2,1)S(1)} %shard_map.72.own_ref), channel_id=1, source_target_pairs={{0,1},{1,0},{2,3},{3,2},{4,5},{5,4},{6,7},{7,6},{8,9},{9,8},{10,11... | collective-permute-start | bytes 104456 | tf_op jit(solution)/shard_map/ppermute | solution.py:368
  63.6 5.9 %collective-permute-start.25 = (s16[8,4224]{1,0:T(8,128)(2,1)S(1)}, s16[8,4224]{1,0:T(8,128)(2,1)S(1)}, u32[]{:S(2)}, u32[]{:S(2)}) collective-permute-start(s16[8,4224]{1,0:T(8,128)(2,1)S(1)} %shard_map.75.own_ref), channel_id=1, source_target_pairs={{0,64},{32,96},{64,0},{96,32},{1,65},{33,97},{65,1},{97,33},{2,66}... | collective-permute-start | bytes 202760 | tf_op jit(solution)/shard_map/ppermute | solution.py:368
  65.5 5.5 %collective-permute-start.24 = (s16[8,4224]{1,0:T(8,128)(2,1)S(1)}, s16[8,4224]{1,0:T(8,128)(2,1)S(1)}, u32[]{:S(2)}, u32[]{:S(2)}) collective-permute-start(s16[8,4224]{1,0:T(8,128)(2,1)S(1)} %shard_map.75.own_ref), channel_id=1, source_target_pairs={{0,96},{32,64},{64,32},{96,0},{1,97},{33,65},{65,33},{97,1},{2,98}... | collective-permute-start | bytes 202760 | tf_op jit(solution)/shard_map/ppermute | solution.py:368
  66.7 4.3 %collective-permute-start.23 = (s16[8,4224]{1,0:T(8,128)(2,1)S(1)}, s16[8,4224]{1,0:T(8,128)(2,1)S(1)}, u32[]{:S(2)}, u32[]{:S(2)}) collective-permute-start(s16[8,4224]{1,0:T(8,128)(2,1)S(1)} %shard_map.75.own_ref), channel_id=1, source_target_pairs={{0,32},{32,0},{64,96},{96,64},{1,33},{33,1},{65,97},{97,65},{2,34}... | collective-permute-start | bytes 202760 | tf_op jit(solution)/shard_map/ppermute | solution.py:368
  73.7 5.5 %collective-permute-start.29 = (s16[8,2176]{1,0:T(8,128)(2,1)S(1)}, s16[8,2176]{1,0:T(8,128)(2,1)S(1)}, u32[]{:S(2)}, u32[]{:S(2)}) collective-permute-start(s16[8,2176]{1,0:T(8,128)(2,1)S(1)} %shard_map.78.own_ref), channel_id=1, source_target_pairs={{0,8},{4,12},{8,0},{12,4},{1,9},{5,13},{9,1},{13,5},{2,10},{6,14},... | collective-permute-start | bytes 104456 | tf_op jit(solution)/shard_map/ppermute | solution.py:368
  76.3 5.1 %collective-permute-start.28 = (s16[8,2176]{1,0:T(8,128)(2,1)S(1)}, s16[8,2176]{1,0:T(8,128)(2,1)S(1)}, u32[]{:S(2)}, u32[]{:S(2)}) collective-permute-start(s16[8,2176]{1,0:T(8,128)(2,1)S(1)} %shard_map.78.own_ref), channel_id=1, source_target_pairs={{0,12},{4,8},{8,4},{12,0},{1,13},{5,9},{9,5},{13,1},{2,14},{6,10},... | collective-permute-start | bytes 104456 | tf_op jit(solution)/shard_map/ppermute | solution.py:368
  81.7 5.5 %collective-permute-start.32 = (s16[8,2176]{1,0:T(8,128)(2,1)S(1)}, s16[8,2176]{1,0:T(8,128)(2,1)S(1)}, u32[]{:S(2)}, u32[]{:S(2)}) collective-permute-start(s16[8,2176]{1,0:T(8,128)(2,1)S(1)} %shard_map.79.own_ref), channel_id=1, source_target_pairs={{0,2},{1,3},{2,0},{3,1},{4,6},{5,7},{6,4},{7,5},{8,10},{9,11},{10,... | collective-permute-start | bytes 104456 | tf_op jit(solution)/shard_map/ppermute | solution.py:368
  83.8 5.1 %collective-permute-start.31 = (s16[8,2176]{1,0:T(8,128)(2,1)S(1)}, s16[8,2176]{1,0:T(8,128)(2,1)S(1)}, u32[]{:S(2)}, u32[]{:S(2)}) collective-permute-start(s16[8,2176]{1,0:T(8,128)(2,1)S(1)} %shard_map.79.own_ref), channel_id=1, source_target_pairs={{0,3},{1,2},{2,1},{3,0},{4,7},{5,6},{6,5},{7,4},{8,11},{9,10},{10,... | collective-permute-start | bytes 104456 | tf_op jit(solution)/shard_map/ppermute | solution.py:368
  91.7 5.9 %collective-permute-start.36 = (s16[8,4224]{1,0:T(8,128)(2,1)S(1)}, s16[8,4224]{1,0:T(8,128)(2,1)S(1)}, u32[]{:S(2)}, u32[]{:S(2)}) collective-permute-start(s16[8,4224]{1,0:T(8,128)(2,1)S(1)} %shard_map.82.own_ref), channel_id=1, source_target_pairs={{0,64},{32,96},{64,0},{96,32},{1,65},{33,97},{65,1},{97,33},{2,66}... | collective-permute-start | bytes 202760 | tf_op jit(solution)/shard_map/ppermute | solution.py:368
  93.6 5.5 %collective-permute-start.35 = (s16[8,4224]{1,0:T(8,128)(2,1)S(1)}, s16[8,4224]{1,0:T(8,128)(2,1)S(1)}, u32[]{:S(2)}, u32[]{:S(2)}) collective-permute-start(s16[8,4224]{1,0:T(8,128)(2,1)S(1)} %shard_map.82.own_ref), channel_id=1, source_target_pairs={{0,96},{32,64},{64,32},{96,0},{1,97},{33,65},{65,33},{97,1},{2,98}... | collective-permute-start | bytes 202760 | tf_op jit(solution)/shard_map/ppermute | solution.py:368
  94.8 4.3 %collective-permute-start.34 = (s16[8,4224]{1,0:T(8,128)(2,1)S(1)}, s16[8,4224]{1,0:T(8,128)(2,1)S(1)}, u32[]{:S(2)}, u32[]{:S(2)}) collective-permute-start(s16[8,4224]{1,0:T(8,128)(2,1)S(1)} %shard_map.82.own_ref), channel_id=1, source_target_pairs={{0,32},{32,0},{64,96},{96,64},{1,33},{33,1},{65,97},{97,65},{2,34}... | collective-permute-start | bytes 202760 | tf_op jit(solution)/shard_map/ppermute | solution.py:368
  101.8 5.5 %collective-permute-start.40 = (s16[8,2176]{1,0:T(8,128)(2,1)S(1)}, s16[8,2176]{1,0:T(8,128)(2,1)S(1)}, u32[]{:S(2)}, u32[]{:S(2)}) collective-permute-start(s16[8,2176]{1,0:T(8,128)(2,1)S(1)} %shard_map.85.own_ref), channel_id=1, source_target_pairs={{0,8},{4,12},{8,0},{12,4},{1,9},{5,13},{9,1},{13,5},{2,10},{6,14},... | collective-permute-start | bytes 104456 | tf_op jit(solution)/shard_map/ppermute | solution.py:368
  103.7 5.1 %collective-permute-start.39 = (s16[8,2176]{1,0:T(8,128)(2,1)S(1)}, s16[8,2176]{1,0:T(8,128)(2,1)S(1)}, u32[]{:S(2)}, u32[]{:S(2)}) collective-permute-start(s16[8,2176]{1,0:T(8,128)(2,1)S(1)} %shard_map.85.own_ref), channel_id=1, source_target_pairs={{0,12},{4,8},{8,4},{12,0},{1,13},{5,9},{9,5},{13,1},{2,14},{6,10},... | collective-permute-start | bytes 104456 | tf_op jit(solution)/shard_map/ppermute | solution.py:368
  109.2 5.7 %collective-permute-start.43 = (s16[8,2176]{1,0:T(8,128)(2,1)S(1)}, s16[8,2176]{1,0:T(8,128)(2,1)S(1)}, u32[]{:S(2)}, u32[]{:S(2)}) collective-permute-start(s16[8,2176]{1,0:T(8,128)(2,1)S(1)} %shard_map.86.own_ref), channel_id=1, source_target_pairs={{0,2},{1,3},{2,0},{3,1},{4,6},{5,7},{6,4},{7,5},{8,10},{9,11},{10,... | collective-permute-start | bytes 104456 | tf_op jit(solution)/shard_map/ppermute | solution.py:368
  110.4 5.1 %collective-permute-start.42 = (s16[8,2176]{1,0:T(8,128)(2,1)S(1)}, s16[8,2176]{1,0:T(8,128)(2,1)S(1)}, u32[]{:S(2)}, u32[]{:S(2)}) collective-permute-start(s16[8,2176]{1,0:T(8,128)(2,1)S(1)} %shard_map.86.own_ref), channel_id=1, source_target_pairs={{0,3},{1,2},{2,1},{3,0},{4,7},{5,6},{6,5},{7,4},{8,11},{9,10},{10,... | collective-permute-start | bytes 104456 | tf_op jit(solution)/shard_map/ppermute | solution.py:368
  117.2 5.1 %collective-permute-start.47 = (f32[8,128]{1,0:T(8,128)S(1)}, f32[8,128]{1,0:T(8,128)S(1)}, u32[]{:S(2)}, u32[]{:S(2)}) collective-permute-start(f32[8,128]{1,0:T(8,128)S(1)} %add.3.own_ref), channel_id=1, source_target_pairs={{0,64},{32,96},{64,0},{96,32},{1,65},{33,97},{65,1},{97,33},{2,66}... | collective-permute-start | bytes 12296 | tf_op jit(solution)/shard_map/ppermute | solution.py:368
  119.1 4.8 %collective-permute-start.46 = (f32[8,128]{1,0:T(8,128)S(1)}, f32[8,128]{1,0:T(8,128)S(1)}, u32[]{:S(2)}, u32[]{:S(2)}) collective-permute-start(f32[8,128]{1,0:T(8,128)S(1)} %add.3.own_ref), channel_id=1, source_target_pairs={{0,96},{32,64},{64,32},{96,0},{1,97},{33,65},{65,33},{97,1},{2,98}... | collective-permute-start | bytes 12296 | tf_op jit(solution)/shard_map/ppermute | solution.py:368
  (19 other events, 73.2 us)
